TPU v7x, 32 devices: a whole 2x2x4 slice. The times are simulated.
32 devices in a mesh: dp: 4 (over y, core), ctx: 8 (over z, x).
Axes of the slice: x: 2, y: 2, z: 4, core: 2. Of those that a mesh axis runs over, the one named last changes fastest.
Arguments:
- tokens: bfloat16 [8192, 2048], P(('dp', 'ctx')), may hold values from -6 to 6
- lengths: int32 [4, 3], P('dp'), may hold values from 1 to 1536, 2048 in all within a row
- w_qkv: float32 [2048, 6144], P(('dp', 'ctx')), may hold values from -0.125 to 0.125
- b_qkv: float32 [6144], P(('dp', 'ctx')), may hold values from -1.8 to 1.8
- w_out: float32 [2048, 2048], P(('dp', 'ctx')), may hold values from -0.5 to 0.5
- b_out: float32 [2048], P(('dp', 'ctx')), may hold values from -1.8 to 1.8
- w_fc1: float32 [2048, 8192], P(('dp', 'ctx')), may hold values from -0.125 to 0.125
- b_fc1: float32 [8192], P(('dp', 'ctx')), may hold values from -1.8 to 1.8
- w_fc2: float32 [8192, 2048], P(('dp', 'ctx')), may hold values from -0.0625 to 0.0625
- b_fc2: float32 [2048], P(('dp', 'ctx')), may hold values from -1.8 to 1.8
- ln_gain: float32 [2048], P(('dp', 'ctx')), may hold values from 0.5 to 1.5
- ln_shift: float32 [2048], P(('dp', 'ctx')), may hold values from -1.8 to 1.8
- cotangent: bfloat16 [8192, 2048], P(('dp', 'ctx')), may hold values from -6 to 6
Outputs:
- block_out: bfloat16 [8192, 2048], P(('dp', 'ctx'))
- grad_tokens: bfloat16 [8192, 2048], P(('dp', 'ctx'))
- grad_w_qkv: float32 [2048, 6144], P(('dp', 'ctx'))
- grad_b_qkv: float32 [6144], P(('dp', 'ctx'))
- grad_w_out: float32 [2048, 2048], P(('dp', 'ctx'))
- grad_b_out: float32 [2048], P(('dp', 'ctx'))
- grad_w_fc1: float32 [2048, 8192], P(('dp', 'ctx'))
- grad_b_fc1: float32 [8192], P(('dp', 'ctx'))
- grad_w_fc2: float32 [8192, 2048], P(('dp', 'ctx'))
- grad_b_fc2: float32 [2048], P(('dp', 'ctx'))
- grad_ln_gain: float32 [2048], P(('dp', 'ctx'))
- grad_ln_shift: float32 [2048], P(('dp', 'ctx'))
Inputs may be any that keep to these rules, and one draw needn't show every extreme that they name: Each row holds the lengths of the sequences of one group in order; they sum to 2048 and the longest is exactly 1536.
All inputs are finite; a program needn't handle non-finite values.
Results may differ from a plain program's by a relative error of at most 0.014.
Values may be sent and summed in bfloat16 or wider, within the bound.
A program may use at most 256 MiB of HBM per device.

v0:
```python
import math

import jax
import jax.numpy as jnp
from jax import lax
from jax.sharding import PartitionSpec as P

D = 2048
HEADS = 32
HEAD_DIM = 64
ROT = 32
FF = 8192


EPS = 1e-05
GELU_COEF = math.sqrt(2.0 / math.pi)
NEGATIVE = -1e30


def norm_parts(inputs, gain, shift):
    mean = jnp.mean(inputs, axis=-1, keepdims=True)
    centred = inputs - mean
    var = jnp.mean(centred * centred, axis=-1, keepdims=True)
    scaled = lax.rsqrt(var + EPS)
    normed = centred * scaled
    return (normed, scaled, normed * gain + shift)


def norm_back(d_hidden, normed, scaled, gain32):
    grad_gain = jnp.sum(d_hidden * normed, axis=0)
    grad_shift = jnp.sum(d_hidden, axis=0)
    d_normed = d_hidden * gain32
    d_inputs = scaled * (
        d_normed
        - jnp.mean(d_normed, axis=-1, keepdims=True)
        - normed * jnp.mean(d_normed * normed, axis=-1, keepdims=True)
    )
    return (grad_gain, grad_shift, d_inputs)


def gelu_tanh(pre):
    return 0.5 * pre * (1.0 + jnp.tanh(GELU_COEF * (pre + 0.044715 * pre * pre * pre)))


def gelu_slope(pre):
    tangent = jnp.tanh(GELU_COEF * (pre + 0.044715 * pre * pre * pre))
    return 0.5 * (1.0 + tangent) + 0.5 * pre * (1.0 - tangent * tangent) * GELU_COEF * (
        1.0 + 3.0 * 0.044715 * pre * pre
    )


def rotary_tables(positions):
    half = ROT // 2
    freq = jnp.exp(jnp.arange(half, dtype=jnp.float32) * (-2.0 * math.log(10000.0) / ROT))
    angle = positions.astype(jnp.float32)[:, None] * freq[None, :]
    return (jnp.cos(angle)[:, None, :], jnp.sin(angle)[:, None, :])


def rotate(heads, cosine, sine):
    half = ROT // 2
    first = heads[..., :half]
    second = heads[..., half:ROT]
    return jnp.concatenate(
        [first * cosine - second * sine, second * cosine + first * sine, heads[..., ROT:]], axis=-1
    )


def rotate_back(grads, cosine, sine):
    half = ROT // 2
    first = grads[..., :half]
    second = grads[..., half:ROT]
    return jnp.concatenate(
        [first * cosine + second * sine, second * cosine - first * sine, grads[..., ROT:]], axis=-1
    )


def segment_info(lengths_row, rows):
    ends = jnp.cumsum(lengths_row)
    starts = ends - lengths_row
    seg = jnp.sum((rows[:, None] >= ends[None, :]).astype(jnp.int32), axis=1)
    onehot = seg[:, None] == jnp.arange(lengths_row.shape[0], dtype=jnp.int32)[None, :]
    first_rows = jnp.sum(jnp.where(onehot, starts[None, :], 0), axis=1)
    return (seg, rows - first_rows)


def attend_forward(query, key_all, value_all, query_seg, query_rows, key_seg, key_rows, width):
    count = key_all.shape[0] // width
    rows = query.shape[0]
    heads = query.shape[1]
    score_scale = 1.0 / math.sqrt(HEAD_DIM)

    def absorb(carry, item):
        running_max, denominator, weighted = carry
        key_piece, value_piece, seg_piece, row_piece = item
        allowed = (
            (query_seg[:, None] == seg_piece[None, :]) & (row_piece[None, :] <= query_rows[:, None])
        )[None]
        scores = (
            jnp.einsum("ihd,jhd->hij", query, key_piece, preferred_element_type=jnp.float32)
            * score_scale
        )
        scores = jnp.where(allowed, scores, NEGATIVE)
        new_max = jnp.maximum(running_max, jnp.max(scores, axis=2))
        factor = jnp.exp(running_max - new_max)
        weights = jnp.where(allowed, jnp.exp(scores - new_max[:, :, None]), 0.0)
        denominator = denominator * factor + jnp.sum(weights, axis=2)
        weighted = weighted * factor.T[:, :, None] + jnp.einsum(
            "hij,jhd->ihd",
            weights.astype(jnp.bfloat16),
            value_piece,
            preferred_element_type=jnp.float32,
        )
        return ((new_max, denominator, weighted), None)

    start_carry = (
        jnp.full((heads, rows), NEGATIVE, jnp.float32),
        jnp.zeros((heads, rows), jnp.float32),
        jnp.zeros((rows, heads, HEAD_DIM), jnp.float32),
    )
    items = (
        key_all.reshape(count, width, heads, HEAD_DIM),
        value_all.reshape(count, width, heads, HEAD_DIM),
        key_seg.reshape(count, width),
        key_rows.reshape(count, width),
    )
    (running_max, denominator, weighted), _ = lax.scan(absorb, start_carry, items)
    log_total = running_max + jnp.log(denominator)
    return (weighted / denominator.T[:, :, None], log_total)


def attend_backward(
    query,
    d_attended,
    delta,
    log_total,
    key_all,
    value_all,
    query_seg,
    query_rows,
    key_seg,
    key_rows,
    width,
):
    count = key_all.shape[0] // width
    heads = query.shape[1]
    score_scale = 1.0 / math.sqrt(HEAD_DIM)

    def key_step(d_query, item):
        key_block, value_block, seg_block, row_block = item
        allowed = (
            (query_seg[:, None] == seg_block[None, :]) & (row_block[None, :] <= query_rows[:, None])
        )[None]
        scores = (
            jnp.einsum("ihd,jhd->hij", query, key_block, preferred_element_type=jnp.float32)
            * score_scale
        )
        probs = jnp.where(allowed, jnp.exp(scores - log_total[:, :, None]), 0.0)
        d_probs = jnp.einsum(
            "ihd,jhd->hij", d_attended, value_block, preferred_element_type=jnp.float32
        )
        d_scores = (probs * (d_probs - delta[:, :, None])).astype(jnp.bfloat16)
        d_query = (
            d_query
            + jnp.einsum("hij,jhd->ihd", d_scores, key_block, preferred_element_type=jnp.float32)
            * score_scale
        )
        d_key = (
            jnp.einsum("hij,ihd->jhd", d_scores, query, preferred_element_type=jnp.float32)
            * score_scale
        )
        d_value = jnp.einsum(
            "hij,ihd->jhd",
            probs.astype(jnp.bfloat16),
            d_attended,
            preferred_element_type=jnp.float32,
        )
        return (d_query, (d_key, d_value))

    items = (
        key_all.reshape(count, width, heads, HEAD_DIM),
        value_all.reshape(count, width, heads, HEAD_DIM),
        key_seg.reshape(count, width),
        key_rows.reshape(count, width),
    )
    d_query, (key_terms, value_terms) = lax.scan(
        key_step, jnp.zeros(query.shape, jnp.float32), items
    )
    total = key_all.shape[0]
    return (
        d_query,
        key_terms.reshape(total, heads, HEAD_DIM),
        value_terms.reshape(total, heads, HEAD_DIM),
    )


def causal_forward(query, keys, values, seg, rows, width):
    count = query.shape[0] // width
    results = []
    logs = []
    for block in range(count):
        lower = block * width
        upper = lower + width
        result, log_total = attend_forward(
            query[lower:upper],
            keys[:upper],
            values[:upper],
            seg[lower:upper],
            rows[lower:upper],
            seg[:upper],
            rows[:upper],
            width,
        )
        results.append(result)
        logs.append(log_total)
    return (jnp.concatenate(results, axis=0), jnp.concatenate(logs, axis=1))


def causal_backward(query, d_attended, delta, log_total, keys, values, seg, rows, width):
    total = query.shape[0]
    count = total // width
    query_parts = []
    key_sum = jnp.zeros(keys.shape, jnp.float32)
    value_sum = jnp.zeros(values.shape, jnp.float32)
    for block in range(count):
        lower = block * width
        upper = lower + width
        d_query, key_terms, value_terms = attend_backward(
            query[lower:upper],
            d_attended[lower:upper],
            delta[:, lower:upper],
            log_total[:, lower:upper],
            keys[:upper],
            values[:upper],
            seg[lower:upper],
            rows[lower:upper],
            seg[:upper],
            rows[:upper],
            width,
        )
        query_parts.append(d_query)
        padding = ((0, total - upper), (0, 0), (0, 0))
        key_sum = key_sum + jnp.pad(key_terms, padding)
        value_sum = value_sum + jnp.pad(value_terms, padding)
    return (jnp.concatenate(query_parts, axis=0), key_sum, value_sum)


def fetch_shared(w_out, b_qkv, b_out, b_fc2, ln_gain, ln_shift):
    return (
        lax.all_gather(w_out.astype(jnp.bfloat16), ("dp", "ctx"), axis=0, tiled=True),
        lax.all_gather(b_qkv.astype(jnp.bfloat16), ("dp", "ctx"), axis=0, tiled=True),
        lax.all_gather(b_out.astype(jnp.bfloat16), ("dp", "ctx"), axis=0, tiled=True),
        lax.all_gather(b_fc2.astype(jnp.bfloat16), ("dp", "ctx"), axis=0, tiled=True),
        lax.all_gather(ln_gain.astype(jnp.bfloat16), ("dp", "ctx"), axis=0, tiled=True),
        lax.all_gather(ln_shift.astype(jnp.bfloat16), ("dp", "ctx"), axis=0, tiled=True),
    )


def return_shared(grad_w_out, grad_b_qkv, grad_b_fc2, grad_gain, grad_shift):
    return (
        lax.psum_scatter(grad_w_out, ("dp", "ctx"), scatter_dimension=0, tiled=True),
        lax.psum_scatter(grad_b_qkv, ("dp", "ctx"), scatter_dimension=0, tiled=True),
        lax.psum_scatter(grad_b_fc2, ("dp", "ctx"), scatter_dimension=0, tiled=True),
        lax.psum_scatter(grad_gain, ("dp", "ctx"), scatter_dimension=0, tiled=True),
        lax.psum_scatter(grad_shift, ("dp", "ctx"), scatter_dimension=0, tiled=True),
    )


def fetch_heads(w_qkv, w_fc1, b_fc1, w_fc2):
    dp_count = lax.axis_size("dp")
    ctx_count = lax.axis_size("ctx")
    rows_piece = w_qkv.shape[0]
    head_width = D // ctx_count
    unit = FF // (dp_count * ctx_count)
    qkv_piece = w_qkv.astype(jnp.bfloat16).reshape(rows_piece, 3, ctx_count, head_width)
    fc1_piece = w_fc1.astype(jnp.bfloat16).reshape(rows_piece, dp_count, ctx_count, unit)
    qkv_sent, fc1_sent = (
        lax.all_to_all(qkv_piece, "ctx", split_axis=2, concat_axis=0, tiled=True),
        lax.all_to_all(fc1_piece, "ctx", split_axis=2, concat_axis=0, tiled=True),
    )
    qkv_cols, fc1_cols, fc2_rows, fc1_bias = (
        lax.all_gather(qkv_sent, "dp", axis=0, tiled=True),
        lax.all_gather(fc1_sent, "dp", axis=0, tiled=True),
        lax.all_gather(w_fc2.astype(jnp.bfloat16), "dp", axis=0, tiled=True),
        lax.all_gather(b_fc1.astype(jnp.bfloat16), "dp", axis=0, tiled=True),
    )
    return (
        qkv_cols.reshape(D, 3 * head_width),
        fc1_cols.reshape(D, dp_count * unit),
        fc2_rows,
        fc1_bias,
    )


def head_plan(
    tokens,
    lengths,
    w_qkv,
    b_qkv,
    w_out,
    b_out,
    w_fc1,
    b_fc1,
    w_fc2,
    b_fc2,
    ln_gain,
    ln_shift,
    cotangent,
):
    rows_here = tokens.shape[0]
    rows_piece = w_qkv.shape[0]
    dp_count = lax.axis_size("dp")
    ctx_count = lax.axis_size("ctx")
    group = rows_here * ctx_count
    width = min(512, group)
    head_width = D // ctx_count
    local_heads = HEADS // ctx_count
    unit = FF // (dp_count * ctx_count)
    here = lax.axis_index("ctx")
    group_rows = jnp.arange(group, dtype=jnp.int32)
    seg, positions = segment_info(lengths[0], group_rows)
    cosine, sine = rotary_tables(positions)
    out_weight, qkv_bias, out_bias, fc2_bias, gain_low, shift_low = fetch_shared(
        w_out, b_qkv, b_out, b_fc2, ln_gain, ln_shift
    )
    qkv_cols, fc1_cols, fc2_rows, fc1_bias = fetch_heads(w_qkv, w_fc1, b_fc1, w_fc2)
    gain32 = gain_low.astype(jnp.float32)
    inputs = tokens.astype(jnp.float32)
    normed, scaled, hidden32 = norm_parts(inputs, gain32, shift_low.astype(jnp.float32))
    hidden = hidden32.astype(jnp.bfloat16)
    hidden_group, dy_group = (
        lax.all_gather(hidden, "ctx", axis=0, tiled=True),
        lax.all_gather(cotangent, "ctx", axis=0, tiled=True),
    )
    bias_cols = lax.dynamic_slice_in_dim(
        qkv_bias.reshape(3, D), here * head_width, head_width, 1
    ).reshape(3 * head_width)
    qkv = jnp.dot(hidden_group, qkv_cols, preferred_element_type=jnp.float32) + bias_cols.astype(
        jnp.float32
    )
    shape = (group, local_heads, HEAD_DIM)
    query = rotate(qkv[:, :head_width].reshape(shape), cosine, sine).astype(jnp.bfloat16)
    keys = rotate(qkv[:, head_width : 2 * head_width].reshape(shape), cosine, sine).astype(
        jnp.bfloat16
    )
    values = qkv[:, 2 * head_width :].reshape(shape).astype(jnp.bfloat16)
    attended32, log_total = causal_forward(query, keys, values, seg, group_rows, width)
    attended = attended32.reshape(group, head_width).astype(jnp.bfloat16)
    out_rows = lax.dynamic_slice_in_dim(out_weight, here * head_width, head_width, 0)
    pre = jnp.dot(hidden_group, fc1_cols, preferred_element_type=jnp.float32) + fc1_bias.astype(
        jnp.float32
    )
    act = gelu_tanh(pre).astype(jnp.bfloat16)
    branches = lax.psum_scatter(
        (
            jnp.dot(attended, out_rows, preferred_element_type=jnp.float32)
            + jnp.dot(act, fc2_rows, preferred_element_type=jnp.float32)
        ).astype(jnp.bfloat16),
        "ctx",
        scatter_dimension=0,
        tiled=True,
    ).astype(jnp.float32)
    block_out = (
        inputs + branches + out_bias.astype(jnp.float32) + fc2_bias.astype(jnp.float32)
    ).astype(jnp.bfloat16)
    back_qkv, back_fc1, back_fc2, back_rows = (qkv_cols, fc1_cols, fc2_rows, out_rows)
    grad_out32 = cotangent.astype(jnp.float32)
    grad_b_fc2 = jnp.sum(grad_out32, axis=0)
    grad_fc2_part = jnp.einsum("tf,td->fd", act, dy_group, preferred_element_type=jnp.float32)
    d_act = jnp.einsum("td,fd->tf", dy_group, back_fc2, preferred_element_type=jnp.float32)
    d_pre = (d_act * gelu_slope(pre)).astype(jnp.bfloat16)
    grad_fc1_part = jnp.einsum("td,tf->df", hidden_group, d_pre, preferred_element_type=jnp.float32)
    grad_bfc1_part = jnp.sum(d_pre.astype(jnp.float32), axis=0)
    grad_out_rows = jnp.einsum("tc,td->cd", attended, dy_group, preferred_element_type=jnp.float32)
    grad_w_out = lax.dynamic_update_slice_in_dim(
        jnp.zeros((D, D), jnp.float32), grad_out_rows, here * head_width, 0
    )
    d_attended = (
        jnp.einsum("td,cd->tc", dy_group, back_rows, preferred_element_type=jnp.float32)
        .astype(jnp.bfloat16)
        .reshape(shape)
    )
    delta = jnp.sum(d_attended.astype(jnp.float32) * attended32, axis=2).T
    d_query, d_keys, d_values = causal_backward(
        query, d_attended, delta, log_total, keys, values, seg, group_rows, width
    )
    d_query = rotate_back(d_query, cosine, sine).reshape(group, head_width)
    d_keys = rotate_back(d_keys, cosine, sine).reshape(group, head_width)
    d_qkv = jnp.concatenate([d_query, d_keys, d_values.reshape(group, head_width)], axis=1).astype(
        jnp.bfloat16
    )
    grad_qkv_part = jnp.einsum("td,tc->dc", hidden_group, d_qkv, preferred_element_type=jnp.float32)
    bias_part = jnp.sum(d_qkv.astype(jnp.float32), axis=0).reshape(3, head_width)
    grad_b_qkv = lax.dynamic_update_slice_in_dim(
        jnp.zeros((3, D), jnp.float32), bias_part, here * head_width, 1
    ).reshape(3 * D)
    d_hidden = lax.psum_scatter(
        (
            jnp.einsum("tc,dc->td", d_qkv, back_qkv, preferred_element_type=jnp.float32)
            + jnp.einsum("tf,df->td", d_pre, back_fc1, preferred_element_type=jnp.float32)
        ).astype(jnp.bfloat16),
        "ctx",
        scatter_dimension=0,
        tiled=True,
    ).astype(jnp.float32)
    grad_gain, grad_shift, d_inputs = norm_back(d_hidden, normed, scaled, gain32)
    grad_tokens = (grad_out32 + d_inputs).astype(jnp.bfloat16)
    owned_qkv, owned_fc1, owned_fc2, owned_bfc1 = (
        lax.psum_scatter(
            grad_qkv_part.reshape(D, 3, 1, head_width).astype(jnp.bfloat16),
            "dp",
            scatter_dimension=0,
            tiled=True,
        ).astype(jnp.float32),
        lax.psum_scatter(
            grad_fc1_part.reshape(D, dp_count, 1, unit).astype(jnp.bfloat16),
            "dp",
            scatter_dimension=0,
            tiled=True,
        ).astype(jnp.float32),
        lax.psum_scatter(
            grad_fc2_part.astype(jnp.bfloat16), "dp", scatter_dimension=0, tiled=True
        ).astype(jnp.float32),
        lax.psum_scatter(
            grad_bfc1_part.astype(jnp.bfloat16), "dp", scatter_dimension=0, tiled=True
        ).astype(jnp.float32),
    )
    split_qkv, split_fc1 = (
        lax.all_to_all(
            owned_qkv.astype(jnp.bfloat16), "ctx", split_axis=0, concat_axis=2, tiled=True
        ).astype(owned_qkv.dtype),
        lax.all_to_all(
            owned_fc1.astype(jnp.bfloat16), "ctx", split_axis=0, concat_axis=2, tiled=True
        ).astype(owned_fc1.dtype),
    )
    owned_shared = return_shared(grad_w_out, grad_b_qkv, grad_b_fc2, grad_gain, grad_shift)
    return (
        block_out,
        grad_tokens,
        split_qkv.reshape(rows_piece, 3 * D),
        owned_shared[1],
        owned_shared[0],
        owned_shared[2],
        split_fc1.reshape(rows_piece, FF),
        owned_bfc1,
        owned_fc2,
        owned_shared[2],
        owned_shared[3],
        owned_shared[4],
    )


def body(
    tokens,
    lengths,
    w_qkv,
    b_qkv,
    w_out,
    b_out,
    w_fc1,
    b_fc1,
    w_fc2,
    b_fc2,
    ln_gain,
    ln_shift,
    cotangent,
):
    return head_plan(
        tokens,
        lengths,
        w_qkv,
        b_qkv,
        w_out,
        b_out,
        w_fc1,
        b_fc1,
        w_fc2,
        b_fc2,
        ln_gain,
        ln_shift,
        cotangent,
    )


def solution(mesh):
    in_specs = (
        P(("dp", "ctx"), None),
        P("dp", None),
        P(("dp", "ctx"), None),
        P(("dp", "ctx")),
        P(("dp", "ctx"), None),
        P(("dp", "ctx")),
        P(("dp", "ctx"), None),
        P(("dp", "ctx")),
        P(("dp", "ctx"), None),
        P(("dp", "ctx")),
        P(("dp", "ctx")),
        P(("dp", "ctx")),
        P(("dp", "ctx"), None),
    )
    out_specs = (
        P(("dp", "ctx"), None),
        P(("dp", "ctx"), None),
        P(("dp", "ctx"), None),
        P(("dp", "ctx")),
        P(("dp", "ctx"), None),
        P(("dp", "ctx")),
        P(("dp", "ctx"), None),
        P(("dp", "ctx")),
        P(("dp", "ctx"), None),
        P(("dp", "ctx")),
        P(("dp", "ctx")),
        P(("dp", "ctx")),
    )
    return jax.shard_map(body, mesh=mesh, in_specs=in_specs, out_specs=out_specs, check_vma=False)
```

profile of v0, /device:TPU:0, one launch (start us, length us, event | category | flops | bytes accessed | tf_op | source)
XLA Modules:
  0.0 1700.6 jit_solution(7679369070642188737)
XLA Ops:
  9.2 27.2 %all_to_all.54 = bf16[64,3,8,256]{3,0,1,2:T(8,128)(2,1)S(1)} all-to-all(bf16[64,3,8,256]{3,0,1,2:T(8,128)(2,1)S(1)} %copy.255), channel_id=1, replica_groups=mesh['dp'=4,'ctx'=8] {'ctx'}, dimensions={2} | all-to-all | bytes 1572864 | tf_op jit(solution)/shard_map/all_to_all | solution.py:277
  38.3 28.8 %all_to_all.55 = bf16[64,4,8,256]{3,1,0,2:T(4,128)(2,1)S(1)} all-to-all(bf16[64,4,8,256]{3,1,0,2:T(4,128)(2,1)S(1)} %copy.267), channel_id=1, replica_groups=mesh['dp'=4,'ctx'=8] {'ctx'}, dimensions={2} | all-to-all | bytes 2097152 | tf_op jit(solution)/shard_map/all_to_all | solution.py:278
  69.7 40.0 %all-reduce.20 = (bf16[2048]{0:T(1024)(128)(2,1)S(1)}, bf16[2048]{0:T(1024)(128)(2,1)S(1)}, bf16[3,2048]{1,0:T(4,128)(2,1)S(1)}, bf16[2048]{0:T(1024)(128)(2,1)}, bf16[2048]{0:T(1024)(128)(2,1)}) all-reduce(bf16[2048]{0:T(1024)(128)(2,1)S(1)} %dynamic-update-slice.1, ...), channel_id=1, replica_groups=mesh['dp'=4,'ctx'=8] {'dp','ctx'}, use_global_device_ids=true, to_apply=%add.7 | all-reduce | flops 14336 | bytes 57344
  118.0 5.2 all-gather
  127.8 3.2 copy.257
  131.1 7.0 copy.269
  138.2 98.8 %all-gather.8.cloned.1.call-done = bf16[2048,2048]{1,0:T(8,128)(2,1)} async-done(((bf16[256,2048]{1,0:T(8,128)(2,1)}), bf16[2048,2048]{1,0:T(8,128)(2,1)}) %all-gather.8.cloned.1.call-update) | async-done | bytes 8388624 | tf_op jit(solution)/shard_map/all_gather | solution.py:331
  236.9 9.1 broadcast_add_fusion
  246.2 2.6 fusion.207
  270.1 18.3 %while.103 = (s32[]{:T(128)}, f32[4,512]{1,0:T(4,128)S(1)}, f32[4,512]{1,0:T(4,128)S(1)}, f32[512,4,64]{0,2,1:T(8,128)}, s32[512]{0:T(512)S(1)}, /*index=5*/s32[...) while((s32[]{:T(128)}, f32[4,512]{1,0:T(4,128)S(1)}, ...), condition=%wide.region_14.15_spmd.clone, body=%wide.region_11.14_spmd.clone.sunk | while | flops 283258880 | bytes 19808468 | solution.py:126
  288.4 14.9 fusion.213
  303.4 94.5 %all-gather.18.cloned.1.call-done = bf16[2048,2048]{1,0:T(8,128)(2,1)} async-done(((bf16[256,2048]{1,0:T(8,128)(2,1)}), bf16[2048,2048]{1,0:T(8,128)(2,1)}) %all-gather.18.cloned.1.call-update) | async-done | bytes 8388624 | tf_op jit(solution)/shard_map/all_gather | solution.py:332
  397.9 20.2 %fusion.212 = (bf16[1024]{0:T(1024)(128)(2,1)}, bf16[2048,1024]{1,0:T(8,128)(2,1)S(1)}) fusion(f32[2048,1024]{1,0:T(8,128)} %fusion.213, f32[1024]{0:T(1024)S(1)} %bitcast.591, bf16[2048,2048]{1,0:T(8,128)(2,1)} %all-gather.18.cloned.1.call-done, bf16[1024,2048]{1,0:T(8,128)(2,1)} %all-gather.16.cloned.1.call-done), kind=kOutput, calls=%fused_computation.317 | convolution fusion | flops 8633973760 | bytes 25171968 | tf_op jit(solution)/shard_map/td,fd->tf/dot_general | solution.py:369
  418.1 14.4 convolution_convert_fusion.1
  432.5 7.6 copy.288
  447.6 25.7 %while.104 = (s32[]{:T(128)}, f32[4,512]{1,0:T(4,128)S(1)}, f32[4,512]{1,0:T(4,128)S(1)}, f32[512,4,64]{0,2,1:T(8,128)}, s32[512]{0:T(512)S(1)}, /*index=5*/s32[...) while((s32[]{:T(128)}, f32[4,512]{1,0:T(4,128)S(1)}, ...), condition=%wide.region_18.19_spmd.clone, body=%wide.region_15.18_spmd.clone.sunk | while | flops 283258880 | bytes 19808468 | solution.py:126
  473.3 9.2 while.102
  487.1 4.3 fusion.188
  491.4 6.4 fusion.169
  505.1 132.0 %while.107 = (s32[]{:T(128)}, f32[512,4,64]{0,2,1:T(8,128)}, f32[4,512,4,64]{1,0,3,2:T(4,128)}, f32[4,512,4,64]{1,0,3,2:T(4,128)}, bf16[4,512,4,64]{1,3,2,0:T(8,...) while((s32[]{:T(128)}, f32[512,4,64]{0,2,1:T(8,128)}, ...), condition=%wide.region_26.27_spmd.clone, body=%wide.region_25.26_spmd.clone.sunk | while | flops 682885120 | bytes 27828416 | solution.py:185
  516.0 11.1 dynamic_update_slice.52
  527.1 11.1 dynamic_update_slice.53
  549.0 11.1 dynamic_update_slice.52
  560.1 11.1 dynamic_update_slice.53
  582.0 11.1 dynamic_update_slice.52
  593.0 11.1 dynamic_update_slice.53
  614.9 11.1 dynamic_update_slice.52
  626.0 11.1 dynamic_update_slice.53
  637.1 90.0 %while.106 = (s32[]{:T(128)}, f32[512,4,64]{0,2,1:T(8,128)}, f32[3,512,4,64]{1,0,3,2:T(4,128)}, f32[3,512,4,64]{1,0,3,2:T(4,128)}, bf16[3,512,4,64]{1,3,2,0:T(8,...) while((s32[]{:T(128)}, f32[512,4,64]{0,2,1:T(8,128)}, ...), condition=%wide.region_24.25_spmd.clone, body=%wide.region_23.24_spmd.clone.sunk | while | flops 682885120 | bytes 32022776 | solution.py:185
  645.0 11.1 dynamic_update_slice.50
  656.1 11.1 dynamic_update_slice.51
  675.0 11.1 dynamic_update_slice.50
  686.1 11.1 dynamic_update_slice.51
  705.0 11.1 dynamic_update_slice.50
  716.1 11.1 dynamic_update_slice.51
  727.2 53.9 %while.105 = (s32[]{:T(128)}, f32[512,4,64]{0,2,1:T(8,128)}, f32[2,512,4,64]{1,0,3,2:T(2,128)}, f32[2,512,4,64]{1,0,3,2:T(2,128)}, bf16[2,512,4,64]{1,3,2,0:T(8,...) while((s32[]{:T(128)}, f32[512,4,64]{0,2,1:T(8,128)}, ...), condition=%wide.region_22.23_spmd.clone, body=%wide.region_21.22_spmd.clone.sunk | while | flops 682885120 | bytes 35168556 | solution.py:185
  733.7 10.3 dynamic_update_slice.48
  744.0 10.3 dynamic_update_slice.49
  760.5 10.3 dynamic_update_slice.48
  770.8 10.3 dynamic_update_slice.49
  788.9 2.7 reshape.763
  795.8 2.8 reshape.767
  798.6 4.1 reshape.766
  807.7 10.6 convolution_convert_fusion.2
  818.4 7.2 copy.285
  826.2 17.3 %convolution_convert_fusion = bf16[1024,2048]{1,0:T(8,128)(2,1)} fusion(bf16[2048,2048]{1,0:T(8,128)(2,1)} %all-gather.18.cloned.1.call-done, f32[2048,1024]{1,0:T(8,128)} %fusion.213, f32[1024]{0:T(1024)S(1)} %bitcast.592), kind=kOutput, calls=%fused_computation.182 | convolution fusion | flops 8613003264 | bytes 20975616 | tf_op jit(solution)/shard_map/tf,td->fd/dot_general | solution.py:368
  845.1 12.5 fusion.205
  857.7 14.4 add_convert_fusion
  873.8 16.8 fusion.206
  890.6 12.0 add_convert_fusion.1
  902.9 8.7 broadcast_in_dim.240
  911.7 7.1 convolution_dynamic-update-slice_fusion
  920.7 56.6 %all-reduce.24.cloned.1.call-done = (bf16[2048,3,1,256]{3,1,2,0:T(4,128)(2,1)}, bf16[2048,4,1,256]{3,1,2,0:T(4,128)(2,1)}) async-done(((bf16[2048,3,1,256]{3,1,2,0:T(4,128)(2,1)}, bf16[2048,4,1,256]{3,1,2,0:T(4,128)(2,1)}), (bf16[2048,3,1,256]{3,1,2,0:T(4,128)(2,1)}, bf16[2048,4,1,256]{3,1,2,0:T(4,128)(2,1)})) %all-reduce.24.cloned.1.call-update) | async-done | bytes 7340048
  979.9 5.5 all-to-all-start.2
  988.0 23.1 %all-to-all-done.2 = bf16[512,3,1,256]{3,1,2,0:T(4,128)(2,1)S(1)} async-done(((bf16[512,3,1,256]{3,1,2,0:T(4,128)(2,1)}), bf16[512,3,1,256]{3,1,2,0:T(4,128)(2,1)S(1)}, u32[]{:S(2)}, u32[]{:S(2)}) %all-to-all-start.2) | async-done | bytes 786464 | tf_op jit(solution)/shard_map/all_to_all | solution.py:428
  1011.1 4.3 all-to-all-start.3
  1016.1 6.2 all-reduce.16
  1027.2 23.0 %all-to-all-done.3 = bf16[512,4,1,256]{3,1,2,0:T(4,128)(2,1)} async-done(((bf16[512,4,1,256]{3,1,2,0:T(4,128)(2,1)}), bf16[512,4,1,256]{3,1,2,0:T(4,128)(2,1)}, u32[]{:S(2)}, u32[]{:S(2)}) %all-to-all-start.3) | async-done | bytes 1048608 | tf_op jit(solution)/shard_map/all_to_all | solution.py:431
  1054.6 2.9 convert_element_type.304
  1057.5 122.9 %reduce-scatter.7.cloned.1.call-done = bf16[256,2048]{1,0:T(8,128)(2,1)} async-done(((bf16[2048,2048]{1,0:T(8,128)(2,1)}), bf16[256,2048]{1,0:T(8,128)(2,1)}) %reduce-scatter.7.cloned.1.call-update) | async-done | bytes 1048592 | tf_op jit(solution)/shard_map/reduce_scatter | solution.py:396
  1182.8 149.2 %reduce-scatter.5.cloned.1.call-done = bf16[256,2048]{1,0:T(8,128)(2,1)} async-done(((bf16[2048,2048]{1,0:T(8,128)(2,1)}), bf16[256,2048]{1,0:T(8,128)(2,1)}) %reduce-scatter.5.cloned.1.call-update) | async-done | bytes 1048592 | tf_op jit(solution)/shard_map/reduce_scatter | solution.py:353
  1332.0 4.5 convert_reduce_fusion.3
  1336.5 51.3 %all-reduce.19 = (f32[6144]{0:T(1024)S(1)}, f32[2048]{0:T(1024)S(1)}, f32[2048]{0:T(1024)S(1)}, f32[2048]{0:T(1024)S(1)}) all-reduce(f32[6144]{0:T(1024)S(1)} %reshape.770, f32[2048]{0:T(1024)S(1)} %get-tuple-element.1396, f32[2048]{0:T(1024)S(1)} %get-tuple-element.1197, ...), channel_id=5, replica_groups=mesh['dp'=4,'ctx'=8] {'dp','ctx'}, use_global_device_ids=true, to_apply=%region_32.33.clone | all-reduce | flops 12288 | bytes 98304
  1389.6 303.5 %reduce-scatter.9.cloned.1.call-done = f32[64,2048]{1,0:T(8,128)} async-done(((f32[2048,2048]{1,0:T(8,128)}), f32[64,2048]{1,0:T(8,128)}) %reduce-scatter.9.cloned.1.call-update) | async-done | bytes 524304 | tf_op jit(solution)/shard_map/reduce_scatter | solution.py:260
  (555 shorter events, 231.6 us)
Async XLA Ops:
  7.2 30.3 %copy-start.28 = (f32[64,8192]{1,0:T(8,128)S(1)}, f32[64,8192]{1,0:T(8,128)}, u32[]{:S(2)}) copy-start(f32[64,8192]{1,0:T(8,128)} %param.31) | copy-start | bytes 6291460
  7.2 120.7 %all-gather.10.cloned.1.call-start = ((), (), s32[]{:S(2)}) async-start(), calls=%async_computation.9 | async-start | bytes 3932160 | tf_op jit(solution)/shard_map/all_gather | solution.py:281
  37.4 93.7 %all-gather.14.cloned.1.call-start = ((), (), s32[]{:S(2)}) async-start(), calls=%async_computation.11 | async-start | bytes 5242880 | tf_op jit(solution)/shard_map/all_gather | solution.py:282
  37.8 30.6 %copy-start.79 = (f32[192]{0:T(256)S(1)}, f32[192]{0:T(256)}, u32[]{:S(2)}) copy-start(f32[192]{0:T(256)} %param.28) | copy-start | bytes 2308
  37.8 30.6 %copy-start.81 = (f32[64]{0:T(128)S(1)}, f32[64]{0:T(128)}, u32[]{:S(2)}) copy-start(f32[64]{0:T(128)} %param.30) | copy-start | bytes 772
  37.9 30.6 %copy-start.82 = (f32[64]{0:T(128)S(1)}, f32[64]{0:T(128)}, u32[]{:S(2)}) copy-start(f32[64]{0:T(128)} %param.34) | copy-start | bytes 772
  37.9 30.6 %copy-start.83 = (f32[64]{0:T(128)S(1)}, f32[64]{0:T(128)}, u32[]{:S(2)}) copy-start(f32[64]{0:T(128)} %param.35) | copy-start | bytes 772
  37.9 30.6 %copy-start.84 = (f32[64]{0:T(128)S(1)}, f32[64]{0:T(128)}, u32[]{:S(2)}) copy-start(f32[64]{0:T(128)} %param.36) | copy-start | bytes 772
  37.9 71.8 %copy-start.4 = (bf16[256,2048]{1,0:T(8,128)(2,1)S(1)}, bf16[256,2048]{1,0:T(8,128)(2,1)}, u32[]{:S(2)}) copy-start(bf16[256,2048]{1,0:T(8,128)(2,1)} %param.25) | copy-start | bytes 3145732
  67.2 45.4 %copy-start.29 = (f32[256,2048]{1,0:T(8,128)S(1)}, f32[256,2048]{1,0:T(8,128)}, u32[]{:S(2)}) copy-start(f32[256,2048]{1,0:T(8,128)} %param.33) | copy-start | bytes 6291460
  68.3 168.6 %all-gather.8.cloned.1.call-start = ((), (), s32[]{:S(2)}) async-start(), calls=%async_computation.8 | async-start | bytes 9437184 | tf_op jit(solution)/shard_map/all_gather | solution.py:331
  112.5 190.9 %all-gather.16.cloned.1.call-start = ((), (), s32[]{:S(2)}) async-start(), calls=%async_computation.12 | async-start | bytes 5242880 | tf_op jit(solution)/shard_map/all_gather | solution.py:283
  113.7 284.2 %all-gather.18.cloned.1.call-start = ((), (), s32[]{:S(2)}) async-start(), calls=%async_computation.14 | async-start | bytes 9437184 | tf_op jit(solution)/shard_map/all_gather | solution.py:332
  114.3 377.2 %all-gather.12.cloned.1.call-start = ((), (), s32[]{:S(2)}) async-start(), calls=%async_computation.10 | async-start | bytes 8650752 | tf_op jit(solution)/shard_map/all_gather | solution.py:249
  115.1 862.2 %all-reduce.24.cloned.1.call-start = ((), (), s32[]{:S(2)}) async-start(), calls=%async_computation.18 | async-start | bytes 16777216
  116.3 11.5 copy-start.52
  127.5 126.2 %copy-start.33 = (f32[2048,16]{0,1:T(8,128)}, f32[2048,16]{0,1:T(8,128)S(1)}, u32[]{:S(2)}) copy-start(f32[2048,16]{0,1:T(8,128)S(1)} %get-tuple-element.1414) | copy-start | bytes 393220
  131.1 105.8 %copy-start.25 = (bf16[2048,3,1,256]{0,3,1,2:T(8,128)(2,1)}, bf16[2048,3,1,256]{0,3,1,2:T(8,128)(2,1)S(1)}, u32[]{:S(2)}) copy-start(bf16[2048,3,1,256]{0,3,1,2:T(8,128)(2,1)S(1)} %copy.257) | copy-start | bytes 9437188
  262.9 7.2 copy-start.51
  262.9 7.2 copy-start.53
  262.9 7.2 copy-start.59
  262.9 7.2 copy-start.61
  288.4 14.9 copy-start
  288.4 14.9 copy-start.2
  288.4 109.5 %copy-start.76 = (f32[4,1,256]{2,1,0:T(1,128)S(1)}, f32[4,1,256]{2,1,0:T(1,128)}, u32[]{:S(2)}) copy-start(f32[4,1,256]{2,1,0:T(1,128)} %convert_element_type.313) | copy-start | bytes 12292
  418.1 14.4 copy-start.88
  432.5 7.6 copy-start.17
  447.5 25.8 %copy-start.38 = (f32[4,512]{1,0:T(4,128)S(1)}, f32[4,512]{1,0:T(4,128)}, u32[]{:S(2)}) copy-start(f32[4,512]{1,0:T(4,128)} %custom-call) | copy-start | bytes 24580
  447.5 25.8 %copy-start.41 = (bf16[2,512,4,64]{1,3,2,0:T(8,128)(2,1)S(1)}, bf16[2,512,4,64]{1,3,2,0:T(8,128)(2,1)}, u32[]{:S(2)}) copy-start(bf16[2,512,4,64]{1,3,2,0:T(8,128)(2,1)} %copy.260) | copy-start | bytes 1572868
  447.5 25.8 %copy-start.49 = (f32[4,512]{1,0:T(4,128)S(1)}, f32[4,512]{1,0:T(4,128)}, u32[]{:S(2)}) copy-start(f32[4,512]{1,0:T(4,128)} %custom-call.1) | copy-start | bytes 24580
  447.5 25.8 %copy-start.57 = (s32[512]{0:T(512)S(1)}, s32[512]{0:T(512)}, u32[]{:S(2)}) copy-start(s32[512]{0:T(512)} %iota_add_fusion.2) | copy-start | bytes 6148
  447.5 25.8 %copy-start.58 = (s32[512]{0:T(512)S(1)}, s32[512]{0:T(512)}, u32[]{:S(2)}) copy-start(s32[512]{0:T(512)} %get-tuple-element.2153) | copy-start | bytes 6148
  447.5 25.8 %copy-start.65 = (s32[2,512]{1,0:T(2,128)S(1)}, s32[2,512]{1,0:T(2,128)}, u32[]{:S(2)}) copy-start(s32[2,512]{1,0:T(2,128)} %slice.256) | copy-start | bytes 12292
  447.5 25.8 %copy-start.66 = (s32[2,512]{1,0:T(2,128)S(1)}, s32[2,512]{1,0:T(2,128)}, u32[]{:S(2)}) copy-start(s32[2,512]{1,0:T(2,128)} %slice.308) | copy-start | bytes 12292
  483.7 7.8 copy-start.30
  491.4 7.4 copy-start.12
  505.1 132.0 %copy-start.1 = (bf16[512,4,64]{0,2,1:T(8,128)(2,1)S(1)}, bf16[512,4,64]{0,2,1:T(8,128)(2,1)}, u32[]{:S(2)}) copy-start(bf16[512,4,64]{0,2,1:T(8,128)(2,1)} %copy-done) | copy-start | bytes 786436
  505.1 132.0 %copy-start.3 = (bf16[3,512,4,64]{1,3,2,0:T(8,128)(2,1)S(1)}, bf16[3,512,4,64]{1,3,2,0:T(8,128)(2,1)}, u32[]{:S(2)}) copy-start(bf16[3,512,4,64]{1,3,2,0:T(8,128)(2,1)} %copy-done.2) | copy-start | bytes 2359300
  505.1 132.0 %copy-start.56 = (bf16[512,256]{0,1:T(8,128)(2,1)S(1)}, bf16[512,256]{0,1:T(8,128)(2,1)}, u32[]{:S(2)}) copy-start(bf16[512,256]{0,1:T(8,128)(2,1)} %get-tuple-element.1400) | copy-start | bytes 786436
  505.1 132.0 %copy-start.60 = (s32[512]{0:T(512)S(1)}, s32[512]{0:T(512)}, u32[]{:S(2)}) copy-start(s32[512]{0:T(512)} %iota_add_fusion.1) | copy-start | bytes 6148
  505.1 132.0 %copy-start.62 = (s32[512]{0:T(512)S(1)}, s32[512]{0:T(512)}, u32[]{:S(2)}) copy-start(s32[512]{0:T(512)} %get-tuple-element.2105) | copy-start | bytes 6148
  727.2 53.9 %copy-start.10 = (f32[512,4,64]{0,2,1:T(8,128)S(1)}, f32[512,4,64]{0,2,1:T(8,128)}, u32[]{:S(2)}) copy-start(f32[512,4,64]{0,2,1:T(8,128)} %get-tuple-element.495) | copy-start | bytes 1572868
  727.2 53.9 %copy-start.32 = (f32[512,4,64]{0,2,1:T(8,128)S(1)}, f32[512,4,64]{0,2,1:T(8,128)}, u32[]{:S(2)}) copy-start(f32[512,4,64]{0,2,1:T(8,128)} %fusion.183) | copy-start | bytes 1572868
  732.4 22.0 %copy-start.7 = (f32[512,4,64]{0,2,1:T(8,128)}, f32[512,4,64]{0,2,1:T(8,128)S(1)}, u32[]{:S(2)}) copy-start(f32[512,4,64]{0,2,1:T(8,128)S(1)} %fusion.366) | copy-start | bytes 1572868 | tf_op jit(solution)/shard_map/while
  759.2 22.0 %copy-start.7 = (f32[512,4,64]{0,2,1:T(8,128)}, f32[512,4,64]{0,2,1:T(8,128)S(1)}, u32[]{:S(2)}) copy-start(f32[512,4,64]{0,2,1:T(8,128)S(1)} %fusion.366) | copy-start | bytes 1572868 | tf_op jit(solution)/shard_map/while
  807.2 11.2 copy-start.19
  807.7 10.6 copy-start.22
  825.6 229.0 %reduce-scatter.11.cloned.1.call-start = ((), (), s32[]{:S(2)}) async-start(), calls=%async_computation.17 | async-start | bytes 5242880 | tf_op jit(solution)/shard_map/reduce_scatter | solution.py:420
  843.6 336.9 %reduce-scatter.7.cloned.1.call-start = ((), (), s32[]{:S(2)}) async-start(), calls=%async_computation.15 | async-start | bytes 9437184 | tf_op jit(solution)/shard_map/reduce_scatter | solution.py:396
  845.1 12.5 copy-start.18
  845.1 12.5 copy-start.89
  872.1 459.9 %reduce-scatter.5.cloned.1.call-start = ((), (), s32[]{:S(2)}) async-start(), calls=%async_computation.13 | async-start | bytes 9437184 | tf_op jit(solution)/shard_map/reduce_scatter | solution.py:353
  902.6 790.5 %reduce-scatter.9.cloned.1.call-start = ((), (), s32[]{:S(2)}) async-start(), calls=%async_computation.16 | async-start | bytes 17301504 | tf_op jit(solution)/shard_map/reduce_scatter | solution.py:260
  977.3 38.7 %copy-start.75 = (bf16[2048]{0:T(1024)(128)(2,1)S(1)}, bf16[2048]{0:T(1024)(128)(2,1)}, u32[]{:S(2)}) copy-start(bf16[2048]{0:T(1024)(128)(2,1)} %get-tuple-element.1358) | copy-start | bytes 12292
  977.3 38.7 %copy-start.74 = (bf16[2048]{0:T(1024)(128)(2,1)S(1)}, bf16[2048]{0:T(1024)(128)(2,1)}, u32[]{:S(2)}) copy-start(bf16[2048]{0:T(1024)(128)(2,1)} %get-tuple-element.1359) | copy-start | bytes 12292
  977.3 38.7 %copy-start.78 = (bf16[1024]{0:T(1024)(128)(2,1)S(1)}, bf16[1024]{0:T(1024)(128)(2,1)}, u32[]{:S(2)}) copy-start(bf16[1024]{0:T(1024)(128)(2,1)} %get-tuple-element.1426) | copy-start | bytes 6148
  979.9 31.2 %all-to-all-start.2 = ((bf16[512,3,1,256]{3,1,2,0:T(4,128)(2,1)}), bf16[512,3,1,256]{3,1,2,0:T(4,128)(2,1)S(1)}, u32[]{:S(2)}, u32[]{:S(2)}) async-start(bf16[512,3,1,256]{3,1,2,0:T(4,128)(2,1)} %constant_dynamic-slice_fusion.13), calls=%async_computation.4 | async-start | bytes 2097152 | tf_op jit(solution)/shard_map/all_to_all | solution.py:428
  1011.1 39.1 %all-to-all-start.3 = ((bf16[512,4,1,256]{3,1,2,0:T(4,128)(2,1)}), bf16[512,4,1,256]{3,1,2,0:T(4,128)(2,1)}, u32[]{:S(2)}, u32[]{:S(2)}) async-start(bf16[512,4,1,256]{3,1,2,0:T(4,128)(2,1)} %constant_dynamic-slice_fusion.12), calls=%async_computation.6 | async-start | bytes 2097152 | tf_op jit(solution)/shard_map/all_to_all | solution.py:431
  1053.0 127.4 %copy-start.5 = (bf16[256,2048]{1,0:T(8,128)(2,1)S(1)}, bf16[256,2048]{1,0:T(8,128)(2,1)}, u32[]{:S(2)}) copy-start(bf16[256,2048]{1,0:T(8,128)(2,1)} %param.25) | copy-start | bytes 3145732
  1053.0 127.4 %copy-start.68 = (f32[2048]{0:T(1024)S(1)}, f32[2048]{0:T(1024)}, u32[]{:S(2)}) copy-start(f32[2048]{0:T(1024)} %copy-done.67) | copy-start | bytes 24580
  1053.0 127.4 %copy-start.71 = (f32[256]{0:T(256)S(1)}, f32[256]{0:T(256)}, u32[]{:S(2)}) copy-start(f32[256]{0:T(256)} %copy-done.70) | copy-start | bytes 3076
  1053.1 127.4 %copy-start.73 = (f32[256]{0:T(256)S(1)}, f32[256]{0:T(256)}, u32[]{:S(2)}) copy-start(f32[256]{0:T(256)} %copy-done.72) | copy-start | bytes 3076
  1054.6 277.4 %copy-start.21 = (bf16[256,2048]{1,0:T(8,128)(2,1)S(1)}, bf16[256,2048]{1,0:T(8,128)(2,1)}, u32[]{:S(2)}) copy-start(bf16[256,2048]{1,0:T(8,128)(2,1)} %param.37) | copy-start | bytes 3145732
  1387.8 305.8 %copy-start.87 = (f32[64]{0:T(128)}, f32[64]{0:T(128)S(1)}, u32[]{:S(2)}) copy-start(f32[64]{0:T(128)S(1)} %dynamic-slice.7) | copy-start | bytes 772
  (61 other events, 146.5 us)
Sparse Core Ops, SparseCore 0:
  37.5 27.5 all-gather.9
  68.5 33.7 all-gather.13
  112.6 124.2 all-gather.7
  238.3 32.6 all-gather.15
  273.0 124.8 all-gather.17
  400.7 75.5 all-gather.11
  825.7 151.5 all-reduce.23
  979.8 44.7 reduce-scatter.10
  1028.7 151.6 reduce-scatter.6
  1183.9 148.0 reduce-scatter.4
  1335.0 358.1 reduce-scatter.8
where the time goes:
time: 1710 us; the launch traced here: 1700 us
  waiting for transfers between devices  872 us (51%)
  local copies, waits for them, and re-layouts  322 us (19%)
  matrix products  263 us (15%)
  blocking collectives  159 us (9%)
  other arithmetic  55.6 us (3%)
    reduce_scatter x1, waiting for transfers between devices, return_shared(): lax.psum_scatter(grad_w_out, ('dp', 'ctx'), scatter_dimension=0, tiled=True)  304 us
    dynamic_update_slice x36, local copies, waits for them, and re-layouts, attend_backward(): lax.scan(key_step, jnp.zeros(query.shape, jnp.float32), items)  206 us
    reduce_scatter x1, waiting for transfers between devices, head_plan(): lax.psum_scatter((jnp.dot(attended, out_rows, preferred_element_type=jnp....  149 us
    reduce_scatter x1, waiting for transfers between devices, head_plan(): lax.psum_scatter((jnp.einsum('tc,dc->td', d_qkv, back_qkv, preferred_elem...  123 us
    all_gather x1, waiting for transfers between devices, head_plan(): lax.all_gather(hidden, 'ctx', axis=0, tiled=True)  98.8 us
    unnamed x3, blocking collectives  97.4 us
    all_gather x1, waiting for transfers between devices, head_plan(): lax.all_gather(cotangent, 'ctx', axis=0, tiled=True)  94.5 us
    unnamed x12, waiting for transfers between devices  57.3 us
  transfers between devices with their start and end apart: 13, of which 8 were waited for; matrix products, arithmetic and copies ran while one was open for 17% of the time, Pallas kernels for 0%

commit v1 on v0

--- a/solution.py
+++ b/solution.py
@@ -244,28 +244,39 @@
     return (jnp.concatenate(query_parts, axis=0), key_sum, value_sum)
 
 
-def fetch_shared(w_out, b_qkv, b_out, b_fc2, ln_gain, ln_shift):
-    return (
-        lax.all_gather(w_out.astype(jnp.bfloat16), ("dp", "ctx"), axis=0, tiled=True),
-        lax.all_gather(b_qkv.astype(jnp.bfloat16), ("dp", "ctx"), axis=0, tiled=True),
-        lax.all_gather(b_out.astype(jnp.bfloat16), ("dp", "ctx"), axis=0, tiled=True),
-        lax.all_gather(b_fc2.astype(jnp.bfloat16), ("dp", "ctx"), axis=0, tiled=True),
-        lax.all_gather(ln_gain.astype(jnp.bfloat16), ("dp", "ctx"), axis=0, tiled=True),
-        lax.all_gather(ln_shift.astype(jnp.bfloat16), ("dp", "ctx"), axis=0, tiled=True),
-    )
-
-
-def return_shared(grad_w_out, grad_b_qkv, grad_b_fc2, grad_gain, grad_shift):
-    return (
-        lax.psum_scatter(grad_w_out, ("dp", "ctx"), scatter_dimension=0, tiled=True),
-        lax.psum_scatter(grad_b_qkv, ("dp", "ctx"), scatter_dimension=0, tiled=True),
-        lax.psum_scatter(grad_b_fc2, ("dp", "ctx"), scatter_dimension=0, tiled=True),
-        lax.psum_scatter(grad_gain, ("dp", "ctx"), scatter_dimension=0, tiled=True),
-        lax.psum_scatter(grad_shift, ("dp", "ctx"), scatter_dimension=0, tiled=True),
-    )
-
-
-def fetch_heads(w_qkv, w_fc1, b_fc1, w_fc2):
+def block_moves(n_dp, n_ctx):
+    count = n_dp * n_ctx
+    return [(f, (f % n_dp) * n_ctx + f // n_dp) for f in range(count)]
+
+
+def fetch_out_rows(w_out):
+    n_dp = lax.axis_size("dp")
+    n_ctx = lax.axis_size("ctx")
+    moved = lax.ppermute(w_out.astype(jnp.bfloat16), ("dp", "ctx"), perm=block_moves(n_dp, n_ctx))
+    return lax.all_gather(moved, "dp", axis=0, tiled=True)
+
+
+def return_out_rows(grad_out_rows):
+    n_dp = lax.axis_size("dp")
+    n_ctx = lax.axis_size("ctx")
+    part = lax.psum_scatter(grad_out_rows, "dp", scatter_dimension=0, tiled=True)
+    back = [(b, a) for a, b in block_moves(n_dp, n_ctx)]
+    return lax.ppermute(part, ("dp", "ctx"), perm=back)
+
+
+def fetch_small(b_qkv, b_out, b_fc2, ln_gain, ln_shift, b_fc1):
+    pieces = (b_qkv, b_out, b_fc2, ln_gain, ln_shift, b_fc1)
+    packed = jnp.concatenate([p.astype(jnp.bfloat16) for p in pieces])
+    table = lax.all_gather(packed, ("dp", "ctx"), axis=0, tiled=False)
+    result = []
+    offset = 0
+    for p in pieces:
+        result.append(table[:, offset : offset + p.shape[0]])
+        offset += p.shape[0]
+    return result
+
+
+def fetch_heads(w_qkv, w_fc1, w_fc2):
     dp_count = lax.axis_size("dp")
     ctx_count = lax.axis_size("ctx")
     rows_piece = w_qkv.shape[0]
@@ -277,17 +288,15 @@
         lax.all_to_all(qkv_piece, "ctx", split_axis=2, concat_axis=0, tiled=True),
         lax.all_to_all(fc1_piece, "ctx", split_axis=2, concat_axis=0, tiled=True),
     )
-    qkv_cols, fc1_cols, fc2_rows, fc1_bias = (
+    qkv_cols, fc1_cols, fc2_rows = (
         lax.all_gather(qkv_sent, "dp", axis=0, tiled=True),
         lax.all_gather(fc1_sent, "dp", axis=0, tiled=True),
         lax.all_gather(w_fc2.astype(jnp.bfloat16), "dp", axis=0, tiled=True),
-        lax.all_gather(b_fc1.astype(jnp.bfloat16), "dp", axis=0, tiled=True),
     )
     return (
         qkv_cols.reshape(D, 3 * head_width),
         fc1_cols.reshape(D, dp_count * unit),
         fc2_rows,
-        fc1_bias,
     )
 
 
@@ -310,6 +319,7 @@
     rows_piece = w_qkv.shape[0]
     dp_count = lax.axis_size("dp")
     ctx_count = lax.axis_size("ctx")
+    count = dp_count * ctx_count
     group = rows_here * ctx_count
     width = min(512, group)
     head_width = D // ctx_count
@@ -319,10 +329,19 @@
     group_rows = jnp.arange(group, dtype=jnp.int32)
     seg, positions = segment_info(lengths[0], group_rows)
     cosine, sine = rotary_tables(positions)
-    out_weight, qkv_bias, out_bias, fc2_bias, gain_low, shift_low = fetch_shared(
-        w_out, b_qkv, b_out, b_fc2, ln_gain, ln_shift
-    )
-    qkv_cols, fc1_cols, fc2_rows, fc1_bias = fetch_heads(w_qkv, w_fc1, b_fc1, w_fc2)
+    qkv_bias, out_bias, fc2_bias, gain_low, shift_low, fc1_table = fetch_small(
+        b_qkv, b_out, b_fc2, ln_gain, ln_shift, b_fc1
+    )
+    qkv_bias = qkv_bias.reshape(3 * D)
+    out_bias = out_bias.reshape(D)
+    fc2_bias = fc2_bias.reshape(D)
+    gain_low = gain_low.reshape(D)
+    shift_low = shift_low.reshape(D)
+    fc1_bias = lax.dynamic_index_in_dim(
+        fc1_table.reshape(dp_count, ctx_count, unit), here, 1, keepdims=False
+    ).reshape(dp_count * unit)
+    out_rows = fetch_out_rows(w_out)
+    qkv_cols, fc1_cols, fc2_rows = fetch_heads(w_qkv, w_fc1, w_fc2)
     gain32 = gain_low.astype(jnp.float32)
     inputs = tokens.astype(jnp.float32)
     normed, scaled, hidden32 = norm_parts(inputs, gain32, shift_low.astype(jnp.float32))
@@ -345,7 +364,6 @@
     values = qkv[:, 2 * head_width :].reshape(shape).astype(jnp.bfloat16)
     attended32, log_total = causal_forward(query, keys, values, seg, group_rows, width)
     attended = attended32.reshape(group, head_width).astype(jnp.bfloat16)
-    out_rows = lax.dynamic_slice_in_dim(out_weight, here * head_width, head_width, 0)
     pre = jnp.dot(hidden_group, fc1_cols, preferred_element_type=jnp.float32) + fc1_bias.astype(
         jnp.float32
     )
@@ -362,20 +380,17 @@
     block_out = (
         inputs + branches + out_bias.astype(jnp.float32) + fc2_bias.astype(jnp.float32)
     ).astype(jnp.bfloat16)
-    back_qkv, back_fc1, back_fc2, back_rows = (qkv_cols, fc1_cols, fc2_rows, out_rows)
     grad_out32 = cotangent.astype(jnp.float32)
     grad_b_fc2 = jnp.sum(grad_out32, axis=0)
     grad_fc2_part = jnp.einsum("tf,td->fd", act, dy_group, preferred_element_type=jnp.float32)
-    d_act = jnp.einsum("td,fd->tf", dy_group, back_fc2, preferred_element_type=jnp.float32)
+    d_act = jnp.einsum("td,fd->tf", dy_group, fc2_rows, preferred_element_type=jnp.float32)
     d_pre = (d_act * gelu_slope(pre)).astype(jnp.bfloat16)
     grad_fc1_part = jnp.einsum("td,tf->df", hidden_group, d_pre, preferred_element_type=jnp.float32)
     grad_bfc1_part = jnp.sum(d_pre.astype(jnp.float32), axis=0)
     grad_out_rows = jnp.einsum("tc,td->cd", attended, dy_group, preferred_element_type=jnp.float32)
-    grad_w_out = lax.dynamic_update_slice_in_dim(
-        jnp.zeros((D, D), jnp.float32), grad_out_rows, here * head_width, 0
-    )
+    owned_w_out = return_out_rows(grad_out_rows)
     d_attended = (
-        jnp.einsum("td,cd->tc", dy_group, back_rows, preferred_element_type=jnp.float32)
+        jnp.einsum("td,cd->tc", dy_group, out_rows, preferred_element_type=jnp.float32)
         .astype(jnp.bfloat16)
         .reshape(shape)
     )
@@ -390,13 +405,10 @@
     )
     grad_qkv_part = jnp.einsum("td,tc->dc", hidden_group, d_qkv, preferred_element_type=jnp.float32)
     bias_part = jnp.sum(d_qkv.astype(jnp.float32), axis=0).reshape(3, head_width)
-    grad_b_qkv = lax.dynamic_update_slice_in_dim(
-        jnp.zeros((3, D), jnp.float32), bias_part, here * head_width, 1
-    ).reshape(3 * D)
     d_hidden = lax.psum_scatter(
         (
-            jnp.einsum("tc,dc->td", d_qkv, back_qkv, preferred_element_type=jnp.float32)
-            + jnp.einsum("tf,df->td", d_pre, back_fc1, preferred_element_type=jnp.float32)
+            jnp.einsum("tc,dc->td", d_qkv, qkv_cols, preferred_element_type=jnp.float32)
+            + jnp.einsum("tf,df->td", d_pre, fc1_cols, preferred_element_type=jnp.float32)
         ).astype(jnp.bfloat16),
         "ctx",
         scatter_dimension=0,
@@ -404,48 +416,59 @@
     ).astype(jnp.float32)
     grad_gain, grad_shift, d_inputs = norm_back(d_hidden, normed, scaled, gain32)
     grad_tokens = (grad_out32 + d_inputs).astype(jnp.bfloat16)
-    owned_qkv, owned_fc1, owned_fc2, owned_bfc1 = (
-        lax.psum_scatter(
-            grad_qkv_part.reshape(D, 3, 1, head_width).astype(jnp.bfloat16),
-            "dp",
-            scatter_dimension=0,
-            tiled=True,
-        ).astype(jnp.float32),
-        lax.psum_scatter(
-            grad_fc1_part.reshape(D, dp_count, 1, unit).astype(jnp.bfloat16),
-            "dp",
-            scatter_dimension=0,
-            tiled=True,
-        ).astype(jnp.float32),
-        lax.psum_scatter(
-            grad_fc2_part.astype(jnp.bfloat16), "dp", scatter_dimension=0, tiled=True
-        ).astype(jnp.float32),
-        lax.psum_scatter(
-            grad_bfc1_part.astype(jnp.bfloat16), "dp", scatter_dimension=0, tiled=True
-        ).astype(jnp.float32),
-    )
+    weight_parts = jnp.concatenate([grad_qkv_part, grad_fc1_part], axis=1).astype(jnp.bfloat16)
+    owned_parts = lax.psum_scatter(weight_parts, "dp", scatter_dimension=0, tiled=True)
+    owned_qkv = owned_parts[:, : 3 * head_width].reshape(-1, 3, 1, head_width)
+    owned_fc1 = owned_parts[:, 3 * head_width :].reshape(-1, dp_count, 1, unit)
+    owned_fc2 = lax.psum_scatter(
+        grad_fc2_part.astype(jnp.bfloat16), "dp", scatter_dimension=0, tiled=True
+    ).astype(jnp.float32)
     split_qkv, split_fc1 = (
-        lax.all_to_all(
-            owned_qkv.astype(jnp.bfloat16), "ctx", split_axis=0, concat_axis=2, tiled=True
-        ).astype(owned_qkv.dtype),
-        lax.all_to_all(
-            owned_fc1.astype(jnp.bfloat16), "ctx", split_axis=0, concat_axis=2, tiled=True
-        ).astype(owned_fc1.dtype),
-    )
-    owned_shared = return_shared(grad_w_out, grad_b_qkv, grad_b_fc2, grad_gain, grad_shift)
+        lax.all_to_all(owned_qkv, "ctx", split_axis=0, concat_axis=2, tiled=True).astype(
+            jnp.float32
+        ),
+        lax.all_to_all(owned_fc1, "ctx", split_axis=0, concat_axis=2, tiled=True).astype(
+            jnp.float32
+        ),
+    )
+    full_bqkv = lax.dynamic_update_slice_in_dim(
+        jnp.zeros((3, D), jnp.float32), bias_part, here * head_width, 1
+    )
+    full_bfc1 = lax.dynamic_update_slice_in_dim(
+        jnp.zeros((dp_count, ctx_count, unit), jnp.float32),
+        grad_bfc1_part.reshape(dp_count, 1, unit),
+        here,
+        1,
+    )
+    small = jnp.concatenate(
+        [
+            full_bqkv.reshape(count, -1),
+            grad_b_fc2.reshape(count, -1),
+            grad_gain.reshape(count, -1),
+            grad_shift.reshape(count, -1),
+            full_bfc1.reshape(count, -1),
+        ],
+        axis=1,
+    )
+    owned_small = lax.psum_scatter(small, ("dp", "ctx"), scatter_dimension=0, tiled=True)[0]
+    cuts = [0, 3 * D // count, D // count, D // count, D // count, FF // count]
+    bounds = [sum(cuts[: i + 1]) for i in range(len(cuts))]
+    owned_bqkv, owned_bout, owned_gain, owned_shift, owned_bfc1 = [
+        owned_small[bounds[i] : bounds[i + 1]] for i in range(5)
+    ]
     return (
         block_out,
         grad_tokens,
         split_qkv.reshape(rows_piece, 3 * D),
-        owned_shared[1],
-        owned_shared[0],
-        owned_shared[2],
+        owned_bqkv,
+        owned_w_out,
+        owned_bout,
         split_fc1.reshape(rows_piece, FF),
         owned_bfc1,
         owned_fc2,
-        owned_shared[2],
-        owned_shared[3],
-        owned_shared[4],
+        owned_bout,
+        owned_gain,
+        owned_shift,
     )
 
 

time: 1710 us -> 1380 us (0.81)
  waiting for transfers between devices: 872 us -> 626 us
  blocking collectives: 159 us -> 95.5 us
  local copies, waits for them, and re-layouts: 322 us -> 292 us
    reduce_scatter x2 -> x3, waiting for transfers between devices: 426 us -> 155 us  [the longest x1 154 us: head_plan(): lax.psum_scatter((jnp.einsum('tc,dc->td', d_qkv, qkv_cols, preferred_elem...]
    unnamed x12 -> x13, waiting for transfers between devices: 57.3 us -> 118 us
    unnamed x3 -> x1, blocking collectives: 97.4 us -> 39.5 us
    all_gather x1, waiting for transfers between devices: 94.5 us -> 48.6 us  [head_plan(): lax.all_gather(cotangent, 'ctx', axis=0, tiled=True)]
  transfers between devices with their start and end apart: 13 -> 16, of which waited for: 8 -> 8; matrix products, arithmetic and copies ran while one was open for 17% -> 39% of each run, Pallas kernels for 0% -> 0%
where the time goes in v1:
time: 1380 us; the launch traced here: 1360 us
  waiting for transfers between devices  626 us (45%)
  local copies, waits for them, and re-layouts  292 us (21%)
  matrix products  260 us (19%)
  blocking collectives  95.5 us (7%)
  other arithmetic  56.9 us (4%)
  between operations  15.9 us (1%)
  starting transfers between devices  14.7 us (1%)
    dynamic_update_slice x36, local copies, waits for them, and re-layouts, attend_backward(): lax.scan(key_step, jnp.zeros(query.shape, jnp.float32), items)  195 us
    reduce_scatter x1, waiting for transfers between devices, head_plan(): lax.psum_scatter((jnp.einsum('tc,dc->td', d_qkv, qkv_cols, preferred_elem...  154 us
    reduce_scatter x1, waiting for transfers between devices, head_plan(): lax.psum_scatter((jnp.dot(attended, out_rows, preferred_element_type=jnp....  149 us
    unnamed x13, waiting for transfers between devices  118 us
    all_gather x1, waiting for transfers between devices, head_plan(): lax.all_gather(hidden, 'ctx', axis=0, tiled=True)  108 us
    all_gather x1, waiting for transfers between devices, head_plan(): lax.all_gather(cotangent, 'ctx', axis=0, tiled=True)  48.6 us
    unnamed x1, blocking collectives  39.5 us
    all_to_all x1, blocking collectives, fetch_heads(): lax.all_to_all(fc1_piece, 'ctx', split_axis=2, concat_axis=0, tiled=True)  28.8 us
  transfers between devices with their start and end apart: 16, of which 8 were waited for; matrix products, arithmetic and copies ran while one was open for 39% of the time, Pallas kernels for 0%

profile of v1, /device:TPU:0, one launch (start us, length us, event | category | flops | bytes accessed | tf_op | source)
XLA Modules:
  0.0 1362.2 jit_solution(17555270084745351379)
XLA Ops:
  9.2 27.2 %all_to_all.54 = bf16[64,3,8,256]{3,0,1,2:T(8,128)(2,1)S(1)} all-to-all(bf16[64,3,8,256]{3,0,1,2:T(8,128)(2,1)S(1)} %copy.255), channel_id=1, replica_groups=mesh['dp'=4,'ctx'=8] {'ctx'}, dimensions={2} | all-to-all | bytes 1572864 | tf_op jit(solution)/shard_map/all_to_all | solution.py:288
  38.3 28.8 %all_to_all.55 = bf16[64,4,8,256]{3,1,0,2:T(4,128)(2,1)S(1)} all-to-all(bf16[64,4,8,256]{3,1,0,2:T(4,128)(2,1)S(1)} %copy.267), channel_id=1, replica_groups=mesh['dp'=4,'ctx'=8] {'ctx'}, dimensions={2} | all-to-all | bytes 2097152 | tf_op jit(solution)/shard_map/all_to_all | solution.py:289
  68.9 39.5 %all-reduce.6 = bf16[22528]{0:T(1024)(128)(2,1)S(1)} all-reduce(bf16[22528]{0:T(1024)(128)(2,1)S(1)} %dynamic-update-slice), channel_id=2, replica_groups=mesh['dp'=4,'ctx'=8] {'dp','ctx'}, use_global_device_ids=true, to_apply=%add.6 | all-reduce | flops 22528 | bytes 90112
  122.9 3.4 copy.257
  126.3 7.0 copy.269
  133.3 108.5 %all-gather.8.cloned.1.call-done = bf16[2048,2048]{1,0:T(8,128)(2,1)} async-done(((bf16[256,2048]{1,0:T(8,128)(2,1)}), bf16[2048,2048]{1,0:T(8,128)(2,1)}) %all-gather.8.cloned.1.call-update) | async-done | bytes 8388624 | tf_op jit(solution)/shard_map/all_gather | solution.py:350
  241.8 9.1 broadcast_add_fusion
  277.3 9.3 while.102
  288.2 25.7 %while.104 = (s32[]{:T(128)}, f32[4,512]{1,0:T(4,128)S(1)}, f32[4,512]{1,0:T(4,128)S(1)}, f32[512,4,64]{0,2,1:T(8,128)}, s32[512]{0:T(512)S(1)}, /*index=5*/s32[...) while((s32[]{:T(128)}, f32[4,512]{1,0:T(4,128)S(1)}, ...), condition=%wide.region_18.19_spmd.clone, body=%wide.region_15.18_spmd.clone.sunk | while | flops 283258880 | bytes 19808468 | solution.py:126
  313.9 13.9 %while.103 = (s32[]{:T(128)}, f32[4,512]{1,0:T(4,128)S(1)}, f32[4,512]{1,0:T(4,128)S(1)}, f32[512,4,64]{0,2,1:T(8,128)S(1)}, s32[512]{0:T(512)S(1)}, /*index=5*/...) while((s32[]{:T(128)}, f32[4,512]{1,0:T(4,128)S(1)}, ...), condition=%wide.region_14.15_spmd.clone, body=%wide.region_11.14_spmd.clone.sunk | while | flops 283258880 | bytes 15614109 | solution.py:126
  332.2 4.3 fusion.188
  336.5 48.6 %all-gather.18.cloned.1.call-done = bf16[2048,2048]{1,0:T(8,128)(2,1)} async-done(((bf16[256,2048]{1,0:T(8,128)(2,1)}), bf16[2048,2048]{1,0:T(8,128)(2,1)}) %all-gather.18.cloned.1.call-update) | async-done | bytes 8388624 | tf_op jit(solution)/shard_map/all_gather | solution.py:351
  385.1 6.3 fusion.169
  392.4 128.3 %while.107 = (s32[]{:T(128)}, f32[512,4,64]{0,2,1:T(8,128)}, f32[4,512,4,64]{1,0,3,2:T(4,128)}, f32[4,512,4,64]{1,0,3,2:T(4,128)}, bf16[4,512,4,64]{1,3,2,0:T(8,...) while((s32[]{:T(128)}, f32[512,4,64]{0,2,1:T(8,128)}, ...), condition=%wide.region_26.27_spmd.clone, body=%wide.region_25.26_spmd.clone.sunk | while | flops 682885120 | bytes 27828416 | solution.py:185
  402.5 11.1 dynamic_update_slice.51
  413.6 11.1 dynamic_update_slice.52
  434.5 11.1 dynamic_update_slice.51
  445.6 11.1 dynamic_update_slice.52
  466.5 11.1 dynamic_update_slice.51
  477.6 11.1 dynamic_update_slice.52
  498.5 11.1 dynamic_update_slice.51
  509.6 11.1 dynamic_update_slice.52
  520.6 90.8 %while.106 = (s32[]{:T(128)}, f32[512,4,64]{0,2,1:T(8,128)}, f32[3,512,4,64]{1,0,3,2:T(4,128)}, f32[3,512,4,64]{1,0,3,2:T(4,128)}, bf16[3,512,4,64]{1,3,2,0:T(8,...) while((s32[]{:T(128)}, f32[512,4,64]{0,2,1:T(8,128)}, ...), condition=%wide.region_24.25_spmd.clone, body=%wide.region_23.24_spmd.clone.sunk | while | flops 682885120 | bytes 32022776 | solution.py:185
  523.7 2.7 fusion.378
  528.8 11.1 dynamic_update_slice.49
  539.9 11.0 dynamic_update_slice.50
  553.9 2.7 fusion.378
  559.0 11.1 dynamic_update_slice.49
  570.1 11.0 dynamic_update_slice.50
  584.2 2.7 fusion.378
  589.3 11.1 dynamic_update_slice.49
  600.4 11.0 dynamic_update_slice.50
  611.5 44.8 %while.105 = (s32[]{:T(128)}, f32[512,4,64]{0,2,1:T(8,128)S(1)}, f32[2,512,4,64]{1,0,3,2:T(2,128)}, f32[2,512,4,64]{1,0,3,2:T(2,128)}, bf16[2,512,4,64]{1,3,2,0:...) while((s32[]{:T(128)}, f32[512,4,64]{0,2,1:T(8,128)S(1)}, ...), condition=%wide.region_22.23_spmd.clone, body=%wide.region_21.22_spmd.clone.sunk | while | flops 682885120 | bytes 39362864 | solution.py:185
  617.7 10.3 dynamic_update_slice.47
  628.1 4.8 dynamic_update_slice.48
  640.1 10.3 dynamic_update_slice.47
  650.4 4.8 dynamic_update_slice.48
  656.3 3.8 reshape.801
  660.1 3.9 reshape.800
  665.9 3.7 multiply_convert_fusion.1
  674.4 3.9 reshape.796
  678.3 2.9 reshape.797
  691.9 13.3 fusion.208
  705.2 20.2 %convert_reduce_fusion = (f32[1024]{0:T(1024)S(1)}, bf16[2048,1024]{1,0:T(8,128)(2,1)S(1)}) fusion(f32[2048,1024]{1,0:T(8,128)} %fusion.208, f32[1024]{0:T(1024)S(1)} %bitcast.602, bf16[2048,2048]{1,0:T(8,128)(2,1)} %all-gather.18.cloned.1.call-done, bf16[1024,2048]{1,0:T(8,128)(2,1)} %all-gather.16.cloned.1.call-done), kind=kOutput, calls=%fused_computation.176 | convolution fusion | flops 8636070912 | bytes 25174016 | tf_op jit(solution)/shard_map/td,fd->tf/dot_general | solution.py:386
  725.5 13.1 convolution_convert_fusion.1
  738.6 10.4 convolution_convert_fusion.2
  748.9 5.9 pad_maximum_fusion
  758.3 8.3 fusion.209
  766.7 16.7 %convolution_convert_fusion = bf16[1024,2048]{1,0:T(8,128)(2,1)} fusion(bf16[2048,2048]{1,0:T(8,128)(2,1)} %all-gather.18.cloned.1.call-done, f32[2048,1024]{1,0:T(8,128)} %fusion.208, f32[1024]{0:T(1024)S(1)} %bitcast.603), kind=kOutput, calls=%fused_computation.184 | convolution fusion | flops 8613003264 | bytes 20975616 | tf_op jit(solution)/shard_map/tf,td->fd/dot_general | solution.py:385
  784.7 12.6 fusion.201
  797.2 14.0 %add_convert_fusion = bf16[2048,2048]{1,0:T(8,128)(2,1)} fusion(f32[2048,2048]{1,0:T(8,128)} %fusion.201, bf16[2048,1024]{1,0:T(8,128)(2,1)S(1)} %copy-done.91, bf16[2048,1024]{0,1:T(8,128)(2,1)S(1)} %bitcast.549), kind=kOutput, calls=%fused_computation.165 | convolution fusion | flops 8598323200 | bytes 33554432 | tf_op jit(solution)/shard_map/tf,df->td/dot_general | solution.py:411
  811.4 16.8 %fusion.202 = f32[2048,2048]{1,0:T(8,128)} fusion(bf16[1024,2048]{1,0:T(8,128)(2,1)} %all-gather.16.cloned.1.call-done, f32[2048,1024]{1,0:T(8,128)} %fusion.208, f32[1024]{0:T(1024)S(1)} %bitcast.604), kind=kOutput, calls=%fused_computation.315 | convolution fusion | flops 8610906112 | bytes 29364224 | tf_op jit(solution)/shard_map/dot_general | solution.py:374
  828.1 12.3 add_convert_fusion.1
  843.1 3.9 all-to-all-start.2
  851.7 21.4 %all-to-all-done.2 = bf16[512,3,1,256]{3,1,2,0:T(4,128)(2,1)S(1)} async-done(((bf16[512,3,1,256]{3,1,2,0:T(4,128)(2,1)}), bf16[512,3,1,256]{3,1,2,0:T(4,128)(2,1)S(1)}, u32[]{:S(2)}, u32[]{:S(2)}) %all-to-all-start.2) | async-done | bytes 786464 | tf_op jit(solution)/shard_map/all_to_all | solution.py:427
  873.0 4.3 all-to-all-start.3
  877.4 5.4 collective-permute-start.1
  884.7 15.7 %reduce-scatter.14.cloned.1.call-done = bf16[256,2048]{1,0:T(8,128)(2,1)} async-done(((bf16[1024,2048]{1,0:T(8,128)(2,1)}), bf16[256,2048]{1,0:T(8,128)(2,1)}) %reduce-scatter.14.cloned.1.call-update) | async-done | bytes 1048592 | tf_op jit(solution)/shard_map/reduce_scatter | solution.py:423
  900.4 2.8 convert_element_type.303
  905.9 9.9 all-to-all-done.3
  917.1 154.5 %reduce-scatter.8.cloned.1.call-done = bf16[256,2048]{1,0:T(8,128)(2,1)} async-done(((bf16[2048,2048]{1,0:T(8,128)(2,1)}), bf16[256,2048]{1,0:T(8,128)(2,1)}) %reduce-scatter.8.cloned.1.call-update) | async-done | bytes 1048592 | tf_op jit(solution)/shard_map/reduce_scatter | solution.py:408
  1073.9 149.4 %reduce-scatter.6.cloned.1.call-done = bf16[256,2048]{1,0:T(8,128)(2,1)} async-done(((bf16[2048,2048]{1,0:T(8,128)(2,1)}), bf16[256,2048]{1,0:T(8,128)(2,1)}) %reduce-scatter.6.cloned.1.call-update) | async-done | bytes 1048592 | tf_op jit(solution)/shard_map/reduce_scatter | solution.py:371
  1223.3 4.5 convert_reduce_fusion.4
  1231.7 117.0 %all-reduce.10.cloned.1.call-done = f32[32,640]{1,0:T(8,128)} async-done(((f32[32,640]{1,0:T(8,128)}), f32[32,640]{1,0:T(8,128)}) %all-reduce.10.cloned.1.call-update) | async-done | bytes 81936
  (558 shorter events, 217.8 us)
Async XLA Ops:
  7.2 30.3 %copy-start.28 = (f32[64,8192]{1,0:T(8,128)S(1)}, f32[64,8192]{1,0:T(8,128)}, u32[]{:S(2)}) copy-start(f32[64,8192]{1,0:T(8,128)} %param.31) | copy-start | bytes 6291460
  7.2 115.7 %all-gather.10.cloned.1.call-start = ((), (), s32[]{:S(2)}) async-start(), calls=%async_computation.10 | async-start | bytes 3932160 | tf_op jit(solution)/shard_map/all_gather | solution.py:292
  37.4 88.9 %all-gather.14.cloned.1.call-start = ((), (), s32[]{:S(2)}) async-start(), calls=%async_computation.12 | async-start | bytes 5242880 | tf_op jit(solution)/shard_map/all_gather | solution.py:293
  37.8 30.6 %copy-start.83 = (f32[192]{0:T(256)S(1)}, f32[192]{0:T(256)}, u32[]{:S(2)}) copy-start(f32[192]{0:T(256)} %param.28) | copy-start | bytes 2308
  37.8 30.6 %copy-start.85 = (f32[64]{0:T(128)S(1)}, f32[64]{0:T(128)}, u32[]{:S(2)}) copy-start(f32[64]{0:T(128)} %param.30) | copy-start | bytes 772
  37.8 30.6 %copy-start.84 = (f32[256]{0:T(256)S(1)}, f32[256]{0:T(256)}, u32[]{:S(2)}) copy-start(f32[256]{0:T(256)} %param.32) | copy-start | bytes 3076
  37.9 30.6 %copy-start.86 = (f32[64]{0:T(128)S(1)}, f32[64]{0:T(128)}, u32[]{:S(2)}) copy-start(f32[64]{0:T(128)} %param.34) | copy-start | bytes 772
  37.9 30.6 %copy-start.87 = (f32[64]{0:T(128)S(1)}, f32[64]{0:T(128)}, u32[]{:S(2)}) copy-start(f32[64]{0:T(128)} %param.35) | copy-start | bytes 772
  37.9 30.6 %copy-start.88 = (f32[64]{0:T(128)S(1)}, f32[64]{0:T(128)}, u32[]{:S(2)}) copy-start(f32[64]{0:T(128)} %param.36) | copy-start | bytes 772
  37.9 71.4 %copy-start = (bf16[256,2048]{1,0:T(8,128)(2,1)S(1)}, bf16[256,2048]{1,0:T(8,128)(2,1)}, u32[]{:S(2)}) copy-start(bf16[256,2048]{1,0:T(8,128)(2,1)} %param.25) | copy-start | bytes 3145732
  68.3 46.3 %copy-start.29 = (f32[256,2048]{1,0:T(8,128)S(1)}, f32[256,2048]{1,0:T(8,128)}, u32[]{:S(2)}) copy-start(f32[256,2048]{1,0:T(8,128)} %param.33) | copy-start | bytes 6291460
  68.4 173.4 %all-gather.8.cloned.1.call-start = ((), (), s32[]{:S(2)}) async-start(), calls=%async_computation.9 | async-start | bytes 9437184 | tf_op jit(solution)/shard_map/all_gather | solution.py:350
  111.4 225.1 %all-gather.12.cloned.1.call-start = ((), (), s32[]{:S(2)}) async-start(), calls=%async_computation.11 | async-start | bytes 1310720 | tf_op jit(solution)/shard_map/all_gather | solution.py:256
  112.6 0.7 collective-permute-start
  114.0 271.1 %all-gather.18.cloned.1.call-start = ((), (), s32[]{:S(2)}) async-start(), calls=%async_computation.15 | async-start | bytes 9437184 | tf_op jit(solution)/shard_map/all_gather | solution.py:351
  114.6 590.6 %all-gather.16.cloned.1.call-start = ((), (), s32[]{:S(2)}) async-start(), calls=%async_computation.13 | async-start | bytes 5242880 | tf_op jit(solution)/shard_map/all_gather | solution.py:294
  115.8 724.6 %reduce-scatter.10.cloned.1.call-start = ((), (), s32[]{:S(2)}) async-start(), calls=%async_computation.17 | async-start | bytes 9175040 | tf_op jit(solution)/shard_map/reduce_scatter | solution.py:420
  122.6 133.9 %copy-start.35 = (f32[2048,16]{0,1:T(8,128)}, f32[2048,16]{0,1:T(8,128)S(1)}, u32[]{:S(2)}) copy-start(f32[2048,16]{0,1:T(8,128)S(1)} %get-tuple-element.1410) | copy-start | bytes 393220
  122.9 209.3 %copy-start.24 = (pred[512,512]{0,1:T(8,128)(4,1)}, pred[512,512]{0,1:T(8,128)(4,1)S(1)}, u32[]{:S(2)}) copy-start(pred[512,512]{0,1:T(8,128)(4,1)S(1)} %compare_and_fusion.6) | copy-start | bytes 786436
  126.3 115.5 %copy-start.23 = (bf16[2048,3,1,256]{0,3,1,2:T(8,128)(2,1)}, bf16[2048,3,1,256]{0,3,1,2:T(8,128)(2,1)S(1)}, u32[]{:S(2)}) copy-start(bf16[2048,3,1,256]{0,3,1,2:T(8,128)(2,1)S(1)} %copy.257) | copy-start | bytes 9437188
  267.9 9.3 copy-start.64
  267.9 9.3 copy-start.69
  277.2 10.9 copy-start.54
  277.2 10.9 copy-start.57
  277.2 10.9 copy-start.67
  277.3 10.9 copy-start.68
  277.3 10.9 copy-start.73
  288.2 25.7 %copy-start.46 = (f32[512,4,64]{0,2,1:T(8,128)S(1)}, f32[512,4,64]{0,2,1:T(8,128)}, u32[]{:S(2)}) copy-start(f32[512,4,64]{0,2,1:T(8,128)} %custom-call.5) | copy-start | bytes 1572868
  288.2 25.7 %copy-start.53 = (f32[4,512]{1,0:T(4,128)S(1)}, f32[4,512]{1,0:T(4,128)}, u32[]{:S(2)}) copy-start(f32[4,512]{1,0:T(4,128)} %custom-call.4) | copy-start | bytes 24580
  288.2 25.7 %copy-start.65 = (s32[512]{0:T(512)S(1)}, s32[512]{0:T(512)}, u32[]{:S(2)}) copy-start(s32[512]{0:T(512)} %iota_add_fusion.1) | copy-start | bytes 6148
  288.2 25.7 %copy-start.66 = (s32[512]{0:T(512)S(1)}, s32[512]{0:T(512)}, u32[]{:S(2)}) copy-start(s32[512]{0:T(512)} %get-tuple-element.2101) | copy-start | bytes 6148
  288.2 25.7 %copy-start.72 = (s32[3,512]{1,0:T(4,128)S(1)}, s32[3,512]{1,0:T(4,128)}, u32[]{:S(2)}) copy-start(s32[3,512]{1,0:T(4,128)} %slice.324) | copy-start | bytes 18436
  313.9 14.7 %copy-start.52 = (f32[512,4,64]{0,2,1:T(8,128)S(1)}, f32[512,4,64]{0,2,1:T(8,128)}, u32[]{:S(2)}) copy-start(f32[512,4,64]{0,2,1:T(8,128)} %get-tuple-element.486) | copy-start | bytes 1572868
  328.7 56.4 %copy-start.30 = (f32[512,4,64]{0,2,1:T(8,128)}, f32[512,4,64]{0,2,1:T(8,128)S(1)}, u32[]{:S(2)}) copy-start(f32[512,4,64]{0,2,1:T(8,128)S(1)} %broadcast_divide_fusion.2) | copy-start | bytes 1572868
  330.0 55.1 %copy-start.32 = (f32[512,4,64]{0,2,1:T(8,128)}, f32[512,4,64]{0,2,1:T(8,128)S(1)}, u32[]{:S(2)}) copy-start(f32[512,4,64]{0,2,1:T(8,128)S(1)} %broadcast_divide_fusion) | copy-start | bytes 1572868
  520.6 90.8 %copy-start.2 = (f32[512,4,64]{0,2,1:T(8,128)S(1)}, f32[512,4,64]{0,2,1:T(8,128)}, u32[]{:S(2)}) copy-start(f32[512,4,64]{0,2,1:T(8,128)} %custom-call.9) | copy-start | bytes 1572868
  615.9 12.1 copy-start.38
  638.2 12.1 copy-start.38
  656.3 9.6 copy-start.25
  656.3 9.6 copy-start.58
  656.3 9.6 copy-start.60
  656.3 9.6 copy-start.80
  691.9 13.3 copy-start.81
  725.4 13.1 copy-start.90
  725.4 13.1 copy-start.18
  754.9 122.5 %reduce-scatter.12.cloned.1.call-start = ((), (), s32[]{:S(2)}) async-start(), calls=%async_computation.18 | async-start | bytes 2621440 | tf_op jit(solution)/shard_map/reduce_scatter | solution.py:262
  766.7 133.8 %reduce-scatter.14.cloned.1.call-start = ((), (), s32[]{:S(2)}) async-start(), calls=%async_computation.19 | async-start | bytes 5242880 | tf_op jit(solution)/shard_map/reduce_scatter | solution.py:423
  783.5 288.1 %reduce-scatter.8.cloned.1.call-start = ((), (), s32[]{:S(2)}) async-start(), calls=%async_computation.16 | async-start | bytes 9437184 | tf_op jit(solution)/shard_map/reduce_scatter | solution.py:408
  784.7 12.6 copy-start.16
  784.7 12.6 copy-start.91
  811.3 16.9 %copy-start.22 = (bf16[2048,4,64]{0,2,1:T(8,128)(2,1)S(1)}, bf16[2048,4,64]{0,2,1:T(8,128)(2,1)}, u32[]{:S(2)}) copy-start(bf16[2048,4,64]{0,2,1:T(8,128)(2,1)} %copy-done.21) | copy-start | bytes 3145732
  811.3 412.0 %reduce-scatter.6.cloned.1.call-start = ((), (), s32[]{:S(2)}) async-start(), calls=%async_computation.14 | async-start | bytes 9437184 | tf_op jit(solution)/shard_map/reduce_scatter | solution.py:371
  811.3 16.8 %copy-start.42 = (bf16[256,2048]{1,0:T(8,128)(2,1)S(1)}, bf16[256,2048]{1,0:T(8,128)(2,1)}, u32[]{:S(2)}) copy-start(bf16[256,2048]{1,0:T(8,128)(2,1)} %all-gather.12.cloned.1.call-done) | copy-start | bytes 3145732
  843.1 39.7 %copy-start.75 = (f32[32,64]{1,0:T(8,128)S(1)}, f32[32,64]{1,0:T(8,128)}, u32[]{:S(2)}) copy-start(f32[32,64]{1,0:T(8,128)} %get-tuple-element.1402) | copy-start | bytes 24580
  843.1 39.8 %copy-start.74 = (f32[32,64]{1,0:T(8,128)S(1)}, f32[32,64]{1,0:T(8,128)}, u32[]{:S(2)}) copy-start(f32[32,64]{1,0:T(8,128)} %get-tuple-element.1403) | copy-start | bytes 24580
  843.1 30.0 %all-to-all-start.2 = ((bf16[512,3,1,256]{3,1,2,0:T(4,128)(2,1)}), bf16[512,3,1,256]{3,1,2,0:T(4,128)(2,1)S(1)}, u32[]{:S(2)}, u32[]{:S(2)}) async-start(bf16[512,3,1,256]{3,1,2,0:T(4,128)(2,1)} %copy.285), calls=%async_computation.5 | async-start | bytes 2097152 | tf_op jit(solution)/shard_map/all_to_all | solution.py:427
  873.0 42.7 %all-to-all-start.3 = ((bf16[512,4,1,256]{3,1,2,0:T(4,128)(2,1)}), bf16[512,4,1,256]{3,1,2,0:T(4,128)(2,1)}, u32[]{:S(2)}, u32[]{:S(2)}) async-start(bf16[512,4,1,256]{3,1,2,0:T(4,128)(2,1)} %copy.288), calls=%async_computation.7 | async-start | bytes 2097152 | tf_op jit(solution)/shard_map/all_to_all | solution.py:430
  877.3 471.4 %all-reduce.10.cloned.1.call-start = ((), (), s32[]{:S(2)}) async-start(), calls=%async_computation.20 | async-start | bytes 163840
  877.4 7.3 collective-permute-start.1
  903.5 168.1 %copy-start.1 = (bf16[256,2048]{1,0:T(8,128)(2,1)S(1)}, bf16[256,2048]{1,0:T(8,128)(2,1)}, u32[]{:S(2)}) copy-start(bf16[256,2048]{1,0:T(8,128)(2,1)} %param.25) | copy-start | bytes 3145732
  903.5 168.1 %copy-start.71 = (f32[2048]{0:T(1024)S(1)}, f32[2048]{0:T(1024)}, u32[]{:S(2)}) copy-start(f32[2048]{0:T(1024)} %copy-done.70) | copy-start | bytes 24580
  903.6 168.1 %copy-start.77 = (f32[256]{0:T(256)S(1)}, f32[256]{0:T(256)}, u32[]{:S(2)}) copy-start(f32[256]{0:T(256)} %copy-done.76) | copy-start | bytes 3076
  903.6 168.1 %copy-start.79 = (f32[256]{0:T(256)S(1)}, f32[256]{0:T(256)}, u32[]{:S(2)}) copy-start(f32[256]{0:T(256)} %copy-done.78) | copy-start | bytes 3076
  905.9 317.4 %copy-start.17 = (bf16[256,2048]{1,0:T(8,128)(2,1)S(1)}, bf16[256,2048]{1,0:T(8,128)(2,1)}, u32[]{:S(2)}) copy-start(bf16[256,2048]{1,0:T(8,128)(2,1)} %param.37) | copy-start | bytes 3145732
  (64 other events, 191.2 us)
Sparse Core Ops, SparseCore 0:
  37.5 27.5 all-gather.9
  68.5 33.7 all-gather.13
  111.6 130.1 all-gather.7
  243.2 14.9 all-gather.11
  260.1 124.9 all-gather.17
  386.5 32.6 all-gather.15
  755.0 63.6 reduce-scatter.9
  821.9 31.4 reduce-scatter.11
  855.9 44.4 reduce-scatter.13
  904.4 167.2 reduce-scatter.7
  1075.2 148.0 reduce-scatter.5
  1230.3 118.4 all-reduce.9

commit v2 on v1

--- a/solution.py
+++ b/solution.py
@@ -1,8 +1,11 @@
+import functools
 import math
 
 import jax
 import jax.numpy as jnp
 from jax import lax
+from jax.experimental import pallas as pl
+from jax.experimental.pallas import tpu as pltpu
 from jax.sharding import PartitionSpec as P
 
 D = 2048
@@ -83,165 +86,164 @@
     return (seg, rows - first_rows)
 
 
-def attend_forward(query, key_all, value_all, query_seg, query_rows, key_seg, key_rows, width):
-    count = key_all.shape[0] // width
-    rows = query.shape[0]
-    heads = query.shape[1]
-    score_scale = 1.0 / math.sqrt(HEAD_DIM)
-
-    def absorb(carry, item):
-        running_max, denominator, weighted = carry
-        key_piece, value_piece, seg_piece, row_piece = item
-        allowed = (
-            (query_seg[:, None] == seg_piece[None, :]) & (row_piece[None, :] <= query_rows[:, None])
-        )[None]
-        scores = (
-            jnp.einsum("ihd,jhd->hij", query, key_piece, preferred_element_type=jnp.float32)
-            * score_scale
+TRANS_B = (((1,), (1,)), ((), ()))
+
+
+def _allowed(segq_ref, segk_ref, i, j, tq, tk):
+    rows = i * tq + lax.broadcasted_iota(jnp.int32, (tq, tk), 0)
+    cols = j * tk + lax.broadcasted_iota(jnp.int32, (tq, tk), 1)
+    return (segq_ref[...] == segk_ref[...]) & (cols <= rows)
+
+
+def _fwd_kernel(q_ref, k_ref, v_ref, segq_ref, segk_ref, o_ref, lse_ref, m_sc, l_sc, acc_sc, *, tq, tk, scale):
+    i = pl.program_id(1)
+    j = pl.program_id(2)
+
+    @pl.when(j == 0)
+    def _():
+        m_sc[...] = jnp.full_like(m_sc, NEGATIVE)
+        l_sc[...] = jnp.zeros_like(l_sc)
+        acc_sc[...] = jnp.zeros_like(acc_sc)
+
+    @pl.when(j * tk <= i * tq + tq - 1)
+    def _():
+        q = q_ref[0]
+        k = k_ref[0]
+        s = lax.dot_general(q, k, TRANS_B, preferred_element_type=jnp.float32) * scale
+        allowed = _allowed(segq_ref, segk_ref, i, j, tq, tk)
+        s = jnp.where(allowed, s, NEGATIVE)
+        m_prev = m_sc[...]
+        m_new = jnp.maximum(m_prev, jnp.max(s, axis=1, keepdims=True))
+        factor = jnp.exp(m_prev - m_new)
+        p = jnp.where(allowed, jnp.exp(s - m_new), 0.0)
+        l_sc[...] = l_sc[...] * factor + jnp.sum(p, axis=1, keepdims=True)
+        acc_sc[...] = acc_sc[...] * factor + jnp.dot(
+            p.astype(jnp.bfloat16), v_ref[0], preferred_element_type=jnp.float32
         )
-        scores = jnp.where(allowed, scores, NEGATIVE)
-        new_max = jnp.maximum(running_max, jnp.max(scores, axis=2))
-        factor = jnp.exp(running_max - new_max)
-        weights = jnp.where(allowed, jnp.exp(scores - new_max[:, :, None]), 0.0)
-        denominator = denominator * factor + jnp.sum(weights, axis=2)
-        weighted = weighted * factor.T[:, :, None] + jnp.einsum(
-            "hij,jhd->ihd",
-            weights.astype(jnp.bfloat16),
-            value_piece,
-            preferred_element_type=jnp.float32,
-        )
-        return ((new_max, denominator, weighted), None)
-
-    start_carry = (
-        jnp.full((heads, rows), NEGATIVE, jnp.float32),
-        jnp.zeros((heads, rows), jnp.float32),
-        jnp.zeros((rows, heads, HEAD_DIM), jnp.float32),
-    )
-    items = (
-        key_all.reshape(count, width, heads, HEAD_DIM),
-        value_all.reshape(count, width, heads, HEAD_DIM),
-        key_seg.reshape(count, width),
-        key_rows.reshape(count, width),
-    )
-    (running_max, denominator, weighted), _ = lax.scan(absorb, start_carry, items)
-    log_total = running_max + jnp.log(denominator)
-    return (weighted / denominator.T[:, :, None], log_total)
-
-
-def attend_backward(
-    query,
-    d_attended,
-    delta,
-    log_total,
-    key_all,
-    value_all,
-    query_seg,
-    query_rows,
-    key_seg,
-    key_rows,
-    width,
-):
-    count = key_all.shape[0] // width
-    heads = query.shape[1]
-    score_scale = 1.0 / math.sqrt(HEAD_DIM)
-
-    def key_step(d_query, item):
-        key_block, value_block, seg_block, row_block = item
-        allowed = (
-            (query_seg[:, None] == seg_block[None, :]) & (row_block[None, :] <= query_rows[:, None])
-        )[None]
-        scores = (
-            jnp.einsum("ihd,jhd->hij", query, key_block, preferred_element_type=jnp.float32)
-            * score_scale
-        )
-        probs = jnp.where(allowed, jnp.exp(scores - log_total[:, :, None]), 0.0)
-        d_probs = jnp.einsum(
-            "ihd,jhd->hij", d_attended, value_block, preferred_element_type=jnp.float32
-        )
-        d_scores = (probs * (d_probs - delta[:, :, None])).astype(jnp.bfloat16)
-        d_query = (
-            d_query
-            + jnp.einsum("hij,jhd->ihd", d_scores, key_block, preferred_element_type=jnp.float32)
-            * score_scale
-        )
-        d_key = (
-            jnp.einsum("hij,ihd->jhd", d_scores, query, preferred_element_type=jnp.float32)
-            * score_scale
-        )
-        d_value = jnp.einsum(
-            "hij,ihd->jhd",
-            probs.astype(jnp.bfloat16),
-            d_attended,
-            preferred_element_type=jnp.float32,
-        )
-        return (d_query, (d_key, d_value))
-
-    items = (
-        key_all.reshape(count, width, heads, HEAD_DIM),
-        value_all.reshape(count, width, heads, HEAD_DIM),
-        key_seg.reshape(count, width),
-        key_rows.reshape(count, width),
-    )
-    d_query, (key_terms, value_terms) = lax.scan(
-        key_step, jnp.zeros(query.shape, jnp.float32), items
-    )
-    total = key_all.shape[0]
-    return (
-        d_query,
-        key_terms.reshape(total, heads, HEAD_DIM),
-        value_terms.reshape(total, heads, HEAD_DIM),
-    )
-
-
-def causal_forward(query, keys, values, seg, rows, width):
-    count = query.shape[0] // width
-    results = []
-    logs = []
-    for block in range(count):
-        lower = block * width
-        upper = lower + width
-        result, log_total = attend_forward(
-            query[lower:upper],
-            keys[:upper],
-            values[:upper],
-            seg[lower:upper],
-            rows[lower:upper],
-            seg[:upper],
-            rows[:upper],
-            width,
-        )
-        results.append(result)
-        logs.append(log_total)
-    return (jnp.concatenate(results, axis=0), jnp.concatenate(logs, axis=1))
-
-
-def causal_backward(query, d_attended, delta, log_total, keys, values, seg, rows, width):
-    total = query.shape[0]
-    count = total // width
-    query_parts = []
-    key_sum = jnp.zeros(keys.shape, jnp.float32)
-    value_sum = jnp.zeros(values.shape, jnp.float32)
-    for block in range(count):
-        lower = block * width
-        upper = lower + width
-        d_query, key_terms, value_terms = attend_backward(
-            query[lower:upper],
-            d_attended[lower:upper],
-            delta[:, lower:upper],
-            log_total[:, lower:upper],
-            keys[:upper],
-            values[:upper],
-            seg[lower:upper],
-            rows[lower:upper],
-            seg[:upper],
-            rows[:upper],
-            width,
-        )
-        query_parts.append(d_query)
-        padding = ((0, total - upper), (0, 0), (0, 0))
-        key_sum = key_sum + jnp.pad(key_terms, padding)
-        value_sum = value_sum + jnp.pad(value_terms, padding)
-    return (jnp.concatenate(query_parts, axis=0), key_sum, value_sum)
+        m_sc[...] = m_new
+
+    @pl.when(j == pl.num_programs(2) - 1)
+    def _():
+        total = l_sc[...]
+        o_ref[0] = acc_sc[...] / total
+        lse_ref[0] = m_sc[...] + jnp.log(total)
+
+
+def attention_forward(q, k, v, seg, tq=512, tk=512):
+    heads, total, dim = q.shape
+    nq, nk = total // tq, total // tk
+    scale = 1.0 / math.sqrt(dim)
+    segq = seg.reshape(total, 1)
+    segk = seg.reshape(1, total)
+
+    def kv_map(h, i, j):
+        return (h, jnp.minimum(j, (i * tq + tq - 1) // tk), 0)
+
+    def segk_map(h, i, j):
+        return (0, jnp.minimum(j, (i * tq + tq - 1) // tk))
+
+    return pl.pallas_call(
+        functools.partial(_fwd_kernel, tq=tq, tk=tk, scale=scale),
+        out_shape=(
+            jax.ShapeDtypeStruct((heads, total, dim), jnp.float32),
+            jax.ShapeDtypeStruct((heads, total, 1), jnp.float32),
+        ),
+        grid=(heads, nq, nk),
+        in_specs=[
+            pl.BlockSpec((1, tq, dim), lambda h, i, j: (h, i, 0)),
+            pl.BlockSpec((1, tk, dim), kv_map),
+            pl.BlockSpec((1, tk, dim), kv_map),
+            pl.BlockSpec((tq, 1), lambda h, i, j: (i, 0)),
+            pl.BlockSpec((1, tk), segk_map),
+        ],
+        out_specs=[
+            pl.BlockSpec((1, tq, dim), lambda h, i, j: (h, i, 0)),
+            pl.BlockSpec((1, tq, 1), lambda h, i, j: (h, i, 0)),
+        ],
+        scratch_shapes=[
+            pltpu.VMEM((tq, 1), jnp.float32),
+            pltpu.VMEM((tq, 1), jnp.float32),
+            pltpu.VMEM((tq, dim), jnp.float32),
+        ],
+        cost_estimate=pl.CostEstimate(
+            flops=2 * heads * total * total * dim,
+            transcendentals=heads * total * total // 2,
+            bytes_accessed=heads * total * dim * 10,
+        ),
+    )(q, k, v, segq, segk)
+
+
+def _bwd_kernel(q_ref, k_ref, v_ref, do_ref, lse_ref, delta_ref, segq_ref, segk_ref, dq_ref, dk_ref, dv_ref, *, tq, tk, scale):
+    j = pl.program_id(1)
+    i = pl.program_id(2)
+
+    @pl.when((j == 0) & (i == 0))
+    def _():
+        dq_ref[...] = jnp.zeros_like(dq_ref)
+
+    @pl.when(i == 0)
+    def _():
+        dk_ref[...] = jnp.zeros_like(dk_ref)
+        dv_ref[...] = jnp.zeros_like(dv_ref)
+
+    @pl.when(i * tq + tq - 1 >= j * tk)
+    def _():
+        q = q_ref[0]
+        k = k_ref[0]
+        do = do_ref[0]
+        s = lax.dot_general(q, k, TRANS_B, preferred_element_type=jnp.float32) * scale
+        allowed = _allowed(segq_ref, segk_ref, i, j, tq, tk)
+        p = jnp.where(allowed, jnp.exp(s - lse_ref[0]), 0.0)
+        dp = lax.dot_general(do, v_ref[0], TRANS_B, preferred_element_type=jnp.float32)
+        ds = (p * (dp - delta_ref[0])).astype(jnp.bfloat16)
+        dv_ref[0] += lax.dot(p.astype(jnp.bfloat16).T, do, preferred_element_type=jnp.float32)
+        dk_ref[0] += lax.dot(ds.T, q, preferred_element_type=jnp.float32) * scale
+        rows = pl.ds(pl.multiple_of(i * tq, tq), tq)
+        dq_ref[0, rows, :] += lax.dot(ds, k, preferred_element_type=jnp.float32) * scale
+
+
+def attention_backward(q, k, v, do, lse, delta, seg, tq=512, tk=512):
+    heads, total, dim = q.shape
+    nq, nk = total // tq, total // tk
+    scale = 1.0 / math.sqrt(dim)
+    segq = seg.reshape(total, 1)
+    segk = seg.reshape(1, total)
+
+    def q_map(h, j, i):
+        return (h, jnp.maximum(i, (j * tk) // tq), 0)
+
+    def segq_map(h, j, i):
+        return (jnp.maximum(i, (j * tk) // tq), 0)
+
+    return pl.pallas_call(
+        functools.partial(_bwd_kernel, tq=tq, tk=tk, scale=scale),
+        out_shape=(
+            jax.ShapeDtypeStruct((heads, total, dim), jnp.float32),
+            jax.ShapeDtypeStruct((heads, total, dim), jnp.float32),
+            jax.ShapeDtypeStruct((heads, total, dim), jnp.float32),
+        ),
+        grid=(heads, nk, nq),
+        in_specs=[
+            pl.BlockSpec((1, tq, dim), q_map),
+            pl.BlockSpec((1, tk, dim), lambda h, j, i: (h, j, 0)),
+            pl.BlockSpec((1, tk, dim), lambda h, j, i: (h, j, 0)),
+            pl.BlockSpec((1, tq, dim), q_map),
+            pl.BlockSpec((1, tq, 1), q_map),
+            pl.BlockSpec((1, tq, 1), q_map),
+            pl.BlockSpec((tq, 1), segq_map),
+            pl.BlockSpec((1, tk), lambda h, j, i: (0, j)),
+        ],
+        out_specs=[
+            pl.BlockSpec((1, total, dim), lambda h, j, i: (h, 0, 0)),
+            pl.BlockSpec((1, tk, dim), lambda h, j, i: (h, j, 0)),
+            pl.BlockSpec((1, tk, dim), lambda h, j, i: (h, j, 0)),
+        ],
+        cost_estimate=pl.CostEstimate(
+            flops=5 * heads * total * total * dim,
+            transcendentals=heads * total * total // 2,
+            bytes_accessed=heads * total * dim * 24,
+        ),
+    )(q, k, v, do, lse, delta, segq, segk)
 
 
 def block_moves(n_dp, n_ctx):
@@ -321,7 +323,6 @@
     ctx_count = lax.axis_size("ctx")
     count = dp_count * ctx_count
     group = rows_here * ctx_count
-    width = min(512, group)
     head_width = D // ctx_count
     local_heads = HEADS // ctx_count
     unit = FF // (dp_count * ctx_count)
@@ -343,12 +344,15 @@
     out_rows = fetch_out_rows(w_out)
     qkv_cols, fc1_cols, fc2_rows = fetch_heads(w_qkv, w_fc1, w_fc2)
     gain32 = gain_low.astype(jnp.float32)
+    shift32 = shift_low.astype(jnp.float32)
     inputs = tokens.astype(jnp.float32)
-    normed, scaled, hidden32 = norm_parts(inputs, gain32, shift_low.astype(jnp.float32))
-    hidden = hidden32.astype(jnp.bfloat16)
-    hidden_group, dy_group = (
-        lax.all_gather(hidden, "ctx", axis=0, tiled=True),
+    normed, scaled, _ = norm_parts(inputs, gain32, shift32)
+    tokens_group, dy_group = (
+        lax.all_gather(tokens, "ctx", axis=0, tiled=True),
         lax.all_gather(cotangent, "ctx", axis=0, tiled=True),
+    )
+    hidden_group = norm_parts(tokens_group.astype(jnp.float32), gain32, shift32)[2].astype(
+        jnp.bfloat16
     )
     bias_cols = lax.dynamic_slice_in_dim(
         qkv_bias.reshape(3, D), here * head_width, head_width, 1
@@ -362,8 +366,11 @@
         jnp.bfloat16
     )
     values = qkv[:, 2 * head_width :].reshape(shape).astype(jnp.bfloat16)
-    attended32, log_total = causal_forward(query, keys, values, seg, group_rows, width)
-    attended = attended32.reshape(group, head_width).astype(jnp.bfloat16)
+    q_heads = query.transpose(1, 0, 2)
+    k_heads = keys.transpose(1, 0, 2)
+    v_heads = values.transpose(1, 0, 2)
+    attended_heads, log_total = attention_forward(q_heads, k_heads, v_heads, seg)
+    attended = attended_heads.transpose(1, 0, 2).reshape(group, head_width).astype(jnp.bfloat16)
     pre = jnp.dot(hidden_group, fc1_cols, preferred_element_type=jnp.float32) + fc1_bias.astype(
         jnp.float32
     )
@@ -394,10 +401,14 @@
         .astype(jnp.bfloat16)
         .reshape(shape)
     )
-    delta = jnp.sum(d_attended.astype(jnp.float32) * attended32, axis=2).T
-    d_query, d_keys, d_values = causal_backward(
-        query, d_attended, delta, log_total, keys, values, seg, group_rows, width
-    )
+    d_heads = d_attended.transpose(1, 0, 2)
+    delta = jnp.sum(d_heads.astype(jnp.float32) * attended_heads, axis=2, keepdims=True)
+    dq_heads, dk_heads, dv_heads = attention_backward(
+        q_heads, k_heads, v_heads, d_heads, log_total, delta, seg
+    )
+    d_query = dq_heads.transpose(1, 0, 2)
+    d_keys = dk_heads.transpose(1, 0, 2)
+    d_values = dv_heads.transpose(1, 0, 2)
     d_query = rotate_back(d_query, cosine, sine).reshape(group, head_width)
     d_keys = rotate_back(d_keys, cosine, sine).reshape(group, head_width)
     d_qkv = jnp.concatenate([d_query, d_keys, d_values.reshape(group, head_width)], axis=1).astype(
@@ -450,7 +461,13 @@
         ],
         axis=1,
     )
-    owned_small = lax.psum_scatter(small, ("dp", "ctx"), scatter_dimension=0, tiled=True)[0]
+    width_small = small.shape[1]
+    over_dp = lax.psum_scatter(
+        small.reshape(dp_count, ctx_count * width_small), "dp", scatter_dimension=0, tiled=True
+    )
+    owned_small = lax.psum_scatter(
+        over_dp.reshape(ctx_count, width_small), "ctx", scatter_dimension=0, tiled=True
+    )[0]
     cuts = [0, 3 * D // count, D // count, D // count, D // count, FF // count]
     bounds = [sum(cuts[: i + 1]) for i in range(len(cuts))]
     owned_bqkv, owned_bout, owned_gain, owned_shift, owned_bfc1 = [

time: 1380 us -> 1190 us (0.86)
  local copies, waits for them, and re-layouts: 292 us -> 90.5 us
  Pallas kernels: 0 us -> 135 us
  matrix products: 260 us -> 152 us
  waiting for transfers between devices: 626 us -> 553 us
  blocking collectives: 95.5 us -> 147 us
  other arithmetic: 56.9 us -> 74.5 us
    dynamic_update_slice x36 -> x0, local copies, waits for them, and re-layouts: 195 us -> none  [attend_backward(): lax.scan(key_step, jnp.zeros(query.shape, jnp.float32), items)]
    pallas_call x0 -> x2, Pallas kernels: none -> 135 us  [the longest x1 74.1 us: attention_forward(): pl.pallas_call(functools.partial(_fwd_kernel, tq=tq, tk=tk, scale=scale),...]
    dot_general x69 -> x0, matrix products: 107 us -> none  [the longest x10 25.1 us: key_step(): jnp.einsum('ihd,jhd->hij', d_attended, value_block, preferred_element_typ...]
    unnamed x13, waiting for transfers between devices: 118 us -> 27.2 us
    unnamed x1 -> x2, blocking collectives: 39.5 us -> 91 us
    all_gather x1, waiting for transfers between devices: 48.6 us -> 88.9 us  [head_plan(): lax.all_gather(cotangent, 'ctx', axis=0, tiled=True)]
    reshape x11 -> x3, local copies, waits for them, and re-layouts: 22.6 us -> 2.53 us  [the longest x1 1.84 us: head_plan(): d_attended = jnp.einsum('td,cd->tc', dy_group, out_rows, preferred_elemen...]
    all_gather x1, waiting for transfers between devices: 108 us -> 89.6 us  [head_plan(): lax.all_gather(tokens, 'ctx', axis=0, tiled=True)]
  transfers between devices with their start and end apart: 16 -> 16, of which waited for: 8 -> 8; matrix products, arithmetic and copies ran while one was open for 39% -> 21% of each run, Pallas kernels for 0% -> 11%
where the time goes in v2:
time: 1190 us; the launch traced here: 1180 us
  waiting for transfers between devices  553 us (46%)
  matrix products  152 us (13%)
  blocking collectives  147 us (12%)
  Pallas kernels  135 us (11%)
  local copies, waits for them, and re-layouts  90.5 us (8%)
  other arithmetic  74.5 us (6%)
  starting transfers between devices  15.4 us (1%)
  between operations  15.2 us (1%)
    reduce_scatter x1, waiting for transfers between devices, head_plan(): lax.psum_scatter((jnp.einsum('tc,dc->td', d_qkv, qkv_cols, preferred_elem...  155 us
    reduce_scatter x1, waiting for transfers between devices, head_plan(): lax.psum_scatter((jnp.dot(attended, out_rows, preferred_element_type=jnp....  149 us
    unnamed x2, blocking collectives  91 us
    all_gather x1, waiting for transfers between devices, head_plan(): lax.all_gather(tokens, 'ctx', axis=0, tiled=True)  89.6 us
    all_gather x1, waiting for transfers between devices, head_plan(): lax.all_gather(cotangent, 'ctx', axis=0, tiled=True)  88.9 us
    pallas_call x1, Pallas kernels, attention_forward(): pl.pallas_call(functools.partial(_fwd_kernel, tq=tq, tk=tk, scale=scale),...  74.1 us
    pallas_call x1, Pallas kernels, attention_backward(): pl.pallas_call(functools.partial(_bwd_kernel, tq=tq, tk=tk, scale=scale),...  61.2 us
    unnamed x89, local copies, waits for them, and re-layouts  30.9 us
  transfers between devices with their start and end apart: 16, of which 8 were waited for; matrix products, arithmetic and copies ran while one was open for 21% of the time, Pallas kernels for 11%

profile of v2, /device:TPU:0, one launch (start us, length us, event | category | flops | bytes accessed | tf_op | source)
XLA Modules:
  0.0 1183.3 jit_solution(10725746255892656530)
XLA Ops:
  7.2 1.6 convert_element_type.210
  9.2 27.2 %all_to_all.54 = bf16[64,3,8,256]{3,0,1,2:T(8,128)(2,1)S(1)} all-to-all(bf16[64,3,8,256]{3,0,1,2:T(8,128)(2,1)S(1)} %copy.150), channel_id=1, replica_groups=mesh['dp'=4,'ctx'=8] {'ctx'}, dimensions={2} | all-to-all | bytes 1572864 | tf_op jit(solution)/shard_map/all_to_all | solution.py:290
  38.3 29.0 %all_to_all.55 = bf16[64,4,8,256]{3,1,0,2:T(4,128)(2,1)S(1)} all-to-all(bf16[64,4,8,256]{3,1,0,2:T(4,128)(2,1)S(1)} %copy.164), channel_id=1, replica_groups=mesh['dp'=4,'ctx'=8] {'ctx'}, dimensions={2} | all-to-all | bytes 2097152 | tf_op jit(solution)/shard_map/all_to_all | solution.py:291
  73.0 53.9 %all-reduce = bf16[22528]{0:T(1024)(128)(2,1)S(1)} all-reduce(bf16[22528]{0:T(1024)(128)(2,1)S(1)} %dynamic-update-slice), channel_id=2, replica_groups=mesh['dp'=4,'ctx'=8] {'dp','ctx'}, use_global_device_ids=true, to_apply=%add | all-reduce | flops 22528 | bytes 90112
  131.1 4.7 copy.152
  135.8 6.3 copy.166
  142.1 89.6 %all-gather.8.cloned.1.call-done = bf16[2048,2048]{1,0:T(8,128)(2,1)} async-done(((bf16[256,2048]{1,0:T(8,128)(2,1)}), bf16[2048,2048]{1,0:T(8,128)(2,1)}) %all-gather.8.cloned.1.call-update) | async-done | bytes 8388624 | tf_op jit(solution)/shard_map/all_gather | solution.py:351
  231.6 4.7 convert_reduce_fusion
  237.4 2.3 fusion.2
  239.8 3.9 fusion.5
  243.7 6.8 broadcast_add_fusion
  254.8 3.6 copy.179
  258.4 3.7 copy.180
  262.0 3.5 copy.182
  265.5 3.5 copy.183
  269.1 2.6 copy.181
  271.7 2.7 copy.184
  274.4 1.8 copy.161
  276.1 9.8 subtract_convert_fusion.2
  285.9 88.9 %all-gather.18.cloned.1.call-done = bf16[2048,2048]{1,0:T(8,128)(2,1)} async-done(((bf16[256,2048]{1,0:T(8,128)(2,1)}), bf16[2048,2048]{1,0:T(8,128)(2,1)}) %all-gather.18.cloned.1.call-update) | async-done | bytes 8388624 | tf_op jit(solution)/shard_map/all_gather | solution.py:352
  374.8 6.0 convolution_convert_fusion.3
  380.8 1.8 copy.167
  382.6 9.0 maximum_bitcast_fusion
  391.6 74.1 %shard_map.220 = (f32[4,2048,64]{2,1,0:T(8,128)}, f32[4,2048,1]{2,1,0:T(8,128)}) custom-call(bf16[4,2048,64]{2,1,0:T(8,128)(2,1)} %get-tuple-element.60.q_ref, bf16[4,2048,64]{2,1,0:T(8,128)(2,1)} %get-tuple-element.61.k_ref, bf16[4,2048,64]{2,1,0:T(8,128)(2,1)} %bitcast.138, s32[2048,1]{1,0:T(8,128)} %copy.162.segq_ref, s32[1,2048]{1,0:T(1,128)} %bitcast.144), custom_call_target="tpu_custom_call" | custom-call | flops 2147483648 | bytes 5242880 | tf_op jit(solution)/shard_map/pallas_call | solution.py:145
  465.7 6.7 multiply_reduce_fusion
  472.5 2.7 copy.168.delta_ref
  475.1 61.2 %shard_map.221 = (f32[4,2048,64]{2,1,0:T(8,128)}, f32[4,2048,64]{2,1,0:T(8,128)}, f32[4,2048,64]{2,1,0:T(8,128)}) custom-call(bf16[4,2048,64]{2,1,0:T(8,128)(2,1)} %get-tuple-element.60.q_ref, bf16[4,2048,64]{2,1,0:T(8,128)(2,1)} %get-tuple-element.61.k_ref, bf16[4,2048,64]{2,1,0:T(8,128)(2,1)} %bitcast.139, bf16[4,2048,64]{2,1,0:T(8,128)(2,1)} %bitcast.107, ...), custom_call_target="tpu_custom_call" | custom-call | flops 5368709120 | bytes 12582912 | tf_op jit(solution)/shard_map/pallas_call | solution.py:218
  536.4 2.9 slice.179
  539.8 1.9 slice.178
  541.7 4.3 add_convert_fusion.3
  546.0 3.3 pad_maximum_fusion.2
  549.3 2.1 copy.170
  551.4 5.4 pad_maximum_fusion.3
  556.8 2.7 copy.171
  559.5 2.5 convert_bitcast_fusion.1
  562.0 1.6 copy.172
  563.6 14.5 %fusion.34 = f32[2048,1024]{1,0:T(8,128)} fusion(bf16[2048,2048]{1,0:T(8,128)(2,1)} %copy-done.4, bf16[2048,1024]{0,1:T(8,128)(2,1)} %bitcast.124), kind=kOutput, calls=%fused_computation.108 | convolution fusion | flops 8589934592 | bytes 20971520 | tf_op jit(solution)/shard_map/dot_general | solution.py:374
  578.1 19.6 %convert_reduce_fusion.1 = (f32[1024]{0:T(1024)S(1)}, bf16[2048,1024]{1,0:T(8,128)(2,1)S(1)}) fusion(f32[2048,1024]{1,0:T(8,128)} %fusion.34, f32[1024]{0:T(1024)S(1)} %bitcast.146, bf16[2048,2048]{1,0:T(8,128)(2,1)} %all-gather.18.cloned.1.call-done, bf16[1024,2048]{1,0:T(8,128)(2,1)} %all-gather.16.cloned.1.call-done), kind=kOutput, calls=%fused_computation.19 | convolution fusion | flops 8636070912 | bytes 25174016 | tf_op jit(solution)/shard_map/td,fd->tf/dot_general | solution.py:393
  597.7 13.1 %convolution_convert_fusion.1 = bf16[2048,1024]{0,1:T(8,128)(2,1)S(1)} fusion(bf16[2048,2048]{1,0:T(8,128)(2,1)} %copy-done.4, bf16[2048,1024]{1,0:T(8,128)(2,1)S(1)} %get-tuple-element.59), kind=kOutput, calls=%fused_computation.35 | convolution fusion | flops 8592031744 | bytes 16777216 | tf_op jit(solution)/shard_map/td,tf->df/dot_general | solution.py:395
  610.9 10.7 convolution_convert_fusion.2
  621.6 5.9 pad_maximum_fusion
  629.0 1.6 copy.163
  630.6 9.3 fusion.35
  640.0 16.7 %convolution_convert_fusion = bf16[1024,2048]{1,0:T(8,128)(2,1)} fusion(bf16[2048,2048]{1,0:T(8,128)(2,1)} %all-gather.18.cloned.1.call-done, f32[2048,1024]{1,0:T(8,128)} %fusion.34, f32[1024]{0:T(1024)S(1)} %bitcast.147), kind=kOutput, calls=%fused_computation.34 | convolution fusion | flops 8613003264 | bytes 20975616 | tf_op jit(solution)/shard_map/tf,td->fd/dot_general | solution.py:392
  658.2 12.4 %fusion.29 = f32[2048,2048]{1,0:T(8,128)} fusion(bf16[2048,768]{0,1:T(8,128)(2,1)} %bitcast.132, bf16[2048,256]{0,1:T(8,128)(2,1)S(1)} %bitcast.120, bf16[2048,256]{0,1:T(8,128)(2,1)S(1)} %bitcast.116, bf16[2048,256]{0,1:T(8,128)(2,1)S(1)} %bitcast.113), kind=kOutput, calls=%fused_computation.103 | convolution fusion | flops 6451888128 | bytes 23068672 | tf_op jit(solution)/shard_map/tc,dc->td/dot_general | solution.py:421
  670.6 14.1 %add_convert_fusion = bf16[2048,2048]{1,0:T(8,128)(2,1)} fusion(f32[2048,2048]{1,0:T(8,128)} %fusion.29, bf16[2048,1024]{1,0:T(8,128)(2,1)S(1)} %copy-done.36, bf16[2048,1024]{0,1:T(8,128)(2,1)S(1)} %bitcast.125), kind=kOutput, calls=%fused_computation.8 | convolution fusion | flops 8598323200 | bytes 33554432 | tf_op jit(solution)/shard_map/tf,df->td/dot_general | solution.py:422
  684.8 16.7 %fusion.30 = f32[2048,2048]{1,0:T(8,128)} fusion(bf16[1024,2048]{1,0:T(8,128)(2,1)} %all-gather.16.cloned.1.call-done, f32[2048,1024]{1,0:T(8,128)} %fusion.34, f32[1024]{0:T(1024)S(1)} %bitcast.148), kind=kOutput, calls=%fused_computation.104 | convolution fusion | flops 8610906112 | bytes 29364224 | tf_op jit(solution)/shard_map/dot_general | solution.py:381
  701.5 12.1 %add_convert_fusion.1 = bf16[2048,2048]{1,0:T(8,128)(2,1)} fusion(f32[2048,2048]{1,0:T(8,128)} %fusion.30, bf16[2048,256]{0,1:T(8,128)(2,1)S(1)} %bitcast.130, bf16[256,2048]{1,0:T(8,128)(2,1)S(1)} %copy-done.17), kind=kOutput, calls=%fused_computation.9 | convolution fusion | flops 2155872256 | bytes 27262976 | tf_op jit(solution)/shard_map/dot_general | solution.py:380
  716.3 4.6 all-to-all-start.2
  720.9 2.3 slice.159
  723.1 2.4 copy.176
  725.5 21.0 %all-to-all-done.2 = bf16[512,3,1,256]{3,1,2,0:T(4,128)(2,1)} async-done(((bf16[512,3,1,256]{3,1,2,0:T(4,128)(2,1)}), bf16[512,3,1,256]{3,1,2,0:T(4,128)(2,1)}, u32[]{:S(2)}, u32[]{:S(2)}) %all-to-all-start.2) | async-done | bytes 786464 | tf_op jit(solution)/shard_map/all_to_all | solution.py:438
  746.5 4.2 all-to-all-start.3
  752.9 5.4 collective-permute-start.1
  760.1 13.4 %reduce-scatter.14.cloned.1.call-done = bf16[256,2048]{1,0:T(8,128)(2,1)} async-done(((bf16[1024,2048]{1,0:T(8,128)(2,1)}), bf16[256,2048]{1,0:T(8,128)(2,1)}) %reduce-scatter.14.cloned.1.call-update) | async-done | bytes 1048592 | tf_op jit(solution)/shard_map/reduce_scatter | solution.py:434
  773.6 2.8 convert_element_type.250
  780.2 9.1 all-to-all-done.3
  790.6 154.6 %reduce-scatter.8.cloned.1.call-done = bf16[256,2048]{1,0:T(8,128)(2,1)} async-done(((bf16[2048,2048]{1,0:T(8,128)(2,1)}), bf16[256,2048]{1,0:T(8,128)(2,1)}) %reduce-scatter.8.cloned.1.call-update) | async-done | bytes 1048592 | tf_op jit(solution)/shard_map/reduce_scatter | solution.py:419
  945.3 2.3 fusion.27
  947.6 149.4 %reduce-scatter.6.cloned.1.call-done = bf16[256,2048]{1,0:T(8,128)(2,1)} async-done(((bf16[2048,2048]{1,0:T(8,128)(2,1)}), bf16[256,2048]{1,0:T(8,128)(2,1)}) %reduce-scatter.6.cloned.1.call-update) | async-done | bytes 1048592 | tf_op jit(solution)/shard_map/reduce_scatter | solution.py:378
  1097.0 4.5 convert_reduce_fusion.5
  1105.5 25.9 %all-reduce.5.cloned.1.call-done = f32[4,5120]{1,0:T(4,128)} async-done(((f32[4,5120]{1,0:T(4,128)}), f32[4,5120]{1,0:T(4,128)}) %all-reduce.5.cloned.1.call-update) | async-done | bytes 81936
  1132.9 37.1 %all-reduce.2 = f32[8,640]{1,0:T(8,128)S(1)} all-reduce(f32[8,640]{1,0:T(8,128)S(1)} %reshape.294), channel_id=7, replica_groups=mesh['dp'=4,'ctx'=8] {'ctx'}, use_global_device_ids=true, to_apply=%region_19.20.clone | all-reduce | flops 5120 | bytes 40960
  1174.3 1.9 copy.194
  (191 shorter events, 42.5 us)
Async XLA Ops:
  7.2 30.3 %copy-start.15 = (f32[64,8192]{1,0:T(8,128)S(1)}, f32[64,8192]{1,0:T(8,128)}, u32[]{:S(2)}) copy-start(f32[64,8192]{1,0:T(8,128)} %param.19) | copy-start | bytes 6291460
  7.2 123.9 %all-gather.10.cloned.1.call-start = ((), (), s32[]{:S(2)}) async-start(), calls=%async_computation.10 | async-start | bytes 3932160 | tf_op jit(solution)/shard_map/all_gather | solution.py:294
  37.4 98.4 %all-gather.14.cloned.1.call-start = ((), (), s32[]{:S(2)}) async-start(), calls=%async_computation.12 | async-start | bytes 5242880 | tf_op jit(solution)/shard_map/all_gather | solution.py:295
  37.8 31.4 %copy-start.18 = (f32[64,2048]{1,0:T(8,128)S(1)}, f32[64,2048]{1,0:T(8,128)}, u32[]{:S(2)}) copy-start(f32[64,2048]{1,0:T(8,128)} %param.17) | copy-start | bytes 1572868
  38.3 33.1 %copy-start.16 = (f32[256,2048]{1,0:T(8,128)S(1)}, f32[256,2048]{1,0:T(8,128)}, u32[]{:S(2)}) copy-start(f32[256,2048]{1,0:T(8,128)} %param.21) | copy-start | bytes 6291460
  68.4 4.2 copy-start.26
  68.4 4.2 copy-start.28
  68.4 4.2 copy-start.29
  68.4 4.2 copy-start.30
  68.4 4.2 copy-start.31
  68.4 4.3 copy-start.27
  68.5 59.6 %copy-start.32 = (s32[1,3]{1,0:T(1,128)S(1)}, s32[1,3]{1,0:T(1,128)}, u32[]{:S(2)}) copy-start(s32[1,3]{1,0:T(1,128)} %param.14) | copy-start | bytes 40
  68.5 163.1 %all-gather.8.cloned.1.call-start = ((), (), s32[]{:S(2)}) async-start(), calls=%async_computation.9 | async-start | bytes 9437184 | tf_op jit(solution)/shard_map/all_gather | solution.py:351
  69.2 216.7 %all-gather.12.cloned.1.call-start = ((), (), s32[]{:S(2)}) async-start(), calls=%async_computation.11 | async-start | bytes 1310720 | tf_op jit(solution)/shard_map/all_gather | solution.py:258
  69.3 0.7 collective-permute-start
  70.0 0.7 copy-start.19
  70.7 304.1 %all-gather.18.cloned.1.call-start = ((), (), s32[]{:S(2)}) async-start(), calls=%async_computation.15 | async-start | bytes 9437184 | tf_op jit(solution)/shard_map/all_gather | solution.py:352
  71.3 506.7 %all-gather.16.cloned.1.call-start = ((), (), s32[]{:S(2)}) async-start(), calls=%async_computation.13 | async-start | bytes 5242880 | tf_op jit(solution)/shard_map/all_gather | solution.py:296
  72.5 641.1 %reduce-scatter.10.cloned.1.call-start = ((), (), s32[]{:S(2)}) async-start(), calls=%async_computation.17 | async-start | bytes 9175040 | tf_op jit(solution)/shard_map/reduce_scatter | solution.py:431
  127.9 111.9 %copy-start.20 = (f32[2048]{0:T(1024)}, f32[2048]{0:T(1024)S(1)}, u32[]{:S(2)}) copy-start(f32[2048]{0:T(1024)S(1)} %reshape.296) | copy-start | bytes 24580
  128.4 7.4 copy-start.22
  231.6 5.8 copy-start
  239.8 3.9 copy-start.14
  243.6 6.8 copy-start.4
  536.4 3.5 copy-start.2
  536.4 5.4 copy-start.1
  546.0 5.4 copy-start.6
  597.7 13.1 %copy-start.35 = (bf16[2048,1024]{1,0:T(8,128)(2,1)}, bf16[2048,1024]{1,0:T(8,128)(2,1)S(1)}, u32[]{:S(2)}) copy-start(bf16[2048,1024]{1,0:T(8,128)(2,1)S(1)} %get-tuple-element.59) | copy-start | bytes 12582916
  597.7 13.1 %copy-start.7 = (bf16[2048,4,64]{0,2,1:T(8,128)(2,1)S(1)}, bf16[2048,4,64]{0,2,1:T(8,128)(2,1)}, u32[]{:S(2)}) copy-start(bf16[2048,4,64]{0,2,1:T(8,128)(2,1)} %copy.171) | copy-start | bytes 3145732
  597.7 13.1 %copy-start.9 = (bf16[2048,4,64]{0,2,1:T(8,128)(2,1)S(1)}, bf16[2048,4,64]{0,2,1:T(8,128)(2,1)}, u32[]{:S(2)}) copy-start(bf16[2048,4,64]{0,2,1:T(8,128)(2,1)} %copy.172) | copy-start | bytes 3145732
  627.4 1.6 copy-start.5
  627.5 125.4 %reduce-scatter.12.cloned.1.call-start = ((), (), s32[]{:S(2)}) async-start(), calls=%async_computation.18 | async-start | bytes 2621440 | tf_op jit(solution)/shard_map/reduce_scatter | solution.py:264
  639.9 133.6 %reduce-scatter.14.cloned.1.call-start = ((), (), s32[]{:S(2)}) async-start(), calls=%async_computation.19 | async-start | bytes 5242880 | tf_op jit(solution)/shard_map/reduce_scatter | solution.py:434
  656.7 1.2 copy-start.8
  656.7 1.5 copy-start.10
  656.7 288.6 %reduce-scatter.8.cloned.1.call-start = ((), (), s32[]{:S(2)}) async-start(), calls=%async_computation.16 | async-start | bytes 9437184 | tf_op jit(solution)/shard_map/reduce_scatter | solution.py:419
  658.2 12.4 %copy-start.11 = (bf16[2048,4,1,256]{0,3,1,2:T(8,128)(2,1)S(1)}, bf16[2048,4,1,256]{0,3,1,2:T(8,128)(2,1)}, u32[]{:S(2)}) copy-start(bf16[2048,4,1,256]{0,3,1,2:T(8,128)(2,1)} %copy.166) | copy-start | bytes 12582916
  658.2 12.4 %copy-start.36 = (bf16[2048,1024]{1,0:T(8,128)(2,1)S(1)}, bf16[2048,1024]{1,0:T(8,128)(2,1)}, u32[]{:S(2)}) copy-start(bf16[2048,1024]{1,0:T(8,128)(2,1)} %copy-done.35) | copy-start | bytes 12582916
  684.7 16.8 %copy-start.13 = (bf16[2048,4,64]{0,2,1:T(8,128)(2,1)S(1)}, bf16[2048,4,64]{0,2,1:T(8,128)(2,1)}, u32[]{:S(2)}) copy-start(bf16[2048,4,64]{0,2,1:T(8,128)(2,1)} %copy.163) | copy-start | bytes 3145732
  684.7 412.2 %reduce-scatter.6.cloned.1.call-start = ((), (), s32[]{:S(2)}) async-start(), calls=%async_computation.14 | async-start | bytes 9437184 | tf_op jit(solution)/shard_map/reduce_scatter | solution.py:378
  684.8 16.7 %copy-start.17 = (bf16[256,2048]{1,0:T(8,128)(2,1)S(1)}, bf16[256,2048]{1,0:T(8,128)(2,1)}, u32[]{:S(2)}) copy-start(bf16[256,2048]{1,0:T(8,128)(2,1)} %all-gather.12.cloned.1.call-done) | copy-start | bytes 3145732
  716.3 34.6 %copy-start.24 = (f32[32,64]{1,0:T(8,128)S(1)}, f32[32,64]{1,0:T(8,128)}, u32[]{:S(2)}) copy-start(f32[32,64]{1,0:T(8,128)} %get-tuple-element.49) | copy-start | bytes 24580
  716.3 34.7 %copy-start.23 = (f32[32,64]{1,0:T(8,128)S(1)}, f32[32,64]{1,0:T(8,128)}, u32[]{:S(2)}) copy-start(f32[32,64]{1,0:T(8,128)} %get-tuple-element.50) | copy-start | bytes 24580
  716.3 34.8 %copy-start.34 = (u32[32]{0:T(128)S(1)}, u32[32]{0:T(128)}, u32[]{:S(2)}) copy-start(u32[32]{0:T(128)} %constant.54) | copy-start | bytes 388
  716.3 35.3 %copy-start.33 = (u32[32]{0:T(128)S(1)}, u32[32]{0:T(128)}, u32[]{:S(2)}) copy-start(u32[32]{0:T(128)} %constant.58) | copy-start | bytes 388
  716.3 36.0 %copy-start.3 = (bf16[256,2048]{1,0:T(8,128)(2,1)S(1)}, bf16[256,2048]{1,0:T(8,128)(2,1)}, u32[]{:S(2)}) copy-start(bf16[256,2048]{1,0:T(8,128)(2,1)} %param.13) | copy-start | bytes 3145732
  716.3 30.3 %all-to-all-start.2 = ((bf16[512,3,1,256]{3,1,2,0:T(4,128)(2,1)}), bf16[512,3,1,256]{3,1,2,0:T(4,128)(2,1)}, u32[]{:S(2)}, u32[]{:S(2)}) async-start(bf16[512,3,1,256]{3,1,2,0:T(4,128)(2,1)} %copy.173), calls=%async_computation.5 | async-start | bytes 2097152 | tf_op jit(solution)/shard_map/all_to_all | solution.py:438
  746.5 42.7 %all-to-all-start.3 = ((bf16[512,4,1,256]{3,1,2,0:T(4,128)(2,1)}), bf16[512,4,1,256]{3,1,2,0:T(4,128)(2,1)}, u32[]{:S(2)}, u32[]{:S(2)}) async-start(bf16[512,4,1,256]{3,1,2,0:T(4,128)(2,1)} %copy.176), calls=%async_computation.7 | async-start | bytes 2097152 | tf_op jit(solution)/shard_map/all_to_all | solution.py:441
  750.8 380.5 %all-reduce.5.cloned.1.call-start = ((), (), s32[]{:S(2)}) async-start(), calls=%async_computation.20 | async-start | bytes 163840
  752.9 7.2 collective-permute-start.1
  777.9 167.4 %copy-start.21 = (f32[2048]{0:T(1024)S(1)}, f32[2048]{0:T(1024)}, u32[]{:S(2)}) copy-start(f32[2048]{0:T(1024)} %copy-done.20) | copy-start | bytes 24580
  780.2 316.8 %copy-start.12 = (bf16[256,2048]{1,0:T(8,128)(2,1)S(1)}, bf16[256,2048]{1,0:T(8,128)(2,1)}, u32[]{:S(2)}) copy-start(bf16[256,2048]{1,0:T(8,128)(2,1)} %param.25) | copy-start | bytes 3145732
  1172.5 3.7 copy-start.25
Sparse Core Ops, SparseCore 0:
  37.5 27.5 all-gather.9
  68.6 34.2 all-gather.13
  105.0 126.5 all-gather.7
  233.0 14.9 all-gather.11
  249.9 124.8 all-gather.17
  376.8 32.6 all-gather.15
  627.6 64.1 reduce-scatter.9
  695.0 31.4 reduce-scatter.11
  729.0 44.4 reduce-scatter.13
  777.5 167.7 reduce-scatter.7
  948.9 148.0 reduce-scatter.5
  1102.6 28.6 all-reduce.4

commit v3 on v2

--- a/solution.py
+++ b/solution.py
@@ -246,6 +246,185 @@
     )(q, k, v, do, lse, delta, segq, segk)
 
 
+MESH_ID = pl.DeviceIdType.MESH
+
+
+class Ring:
+    def __init__(self, size, a_stride, b_stride):
+        self.size = size
+        self.half = size // 2
+        self.a_stride = a_stride
+        self.b_stride = b_stride
+
+    def position(self, c):
+        a = (c // self.a_stride) % self.half
+        b = (c // self.b_stride) % 2
+        return a + b * (2 * self.half - 1 - 2 * a)
+
+    def device(self, pos):
+        pos = pos % self.size
+        b = pos // self.half
+        a = pos + b * (2 * self.half - 1 - 2 * pos)
+        return a * self.a_stride + b * self.b_stride
+
+
+def ring_of(mesh):
+    size = mesh.shape["ctx"]
+    devices = list(mesh.devices.reshape(-1, size)[0])
+    try:
+        coords = [tuple(d.coords) for d in devices]
+    except AttributeError:
+        coords = None
+    if coords and size % 2 == 0 and size >= 4:
+        for b_stride in range(1, size):
+            for a_stride in range(1, size):
+                ring = Ring(size, a_stride, b_stride)
+                order = [ring.device(p) for p in range(size)]
+                if sorted(order) != list(range(size)):
+                    continue
+                hops = [
+                    sum(abs(x - y) for x, y in zip(coords[order[p]], coords[order[(p + 1) % size]]))
+                    for p in range(size)
+                ]
+                if max(hops) == 1:
+                    return ring
+    return Ring(size, 2, 1) if size % 2 == 0 and size >= 4 else None
+
+
+def _barrier(g, left, right):
+    barrier = pltpu.get_barrier_semaphore()
+    for other in (left, right):
+        pl.semaphore_signal(barrier, 1, device_id=(g, other), device_id_type=MESH_ID)
+    pl.semaphore_wait(barrier, 2)
+
+
+def _gather_kernel(x_ref, y_ref, own_sem, send_sem, recv_sem, *, ring, rows):
+    n = ring.size
+    half = rows // 2
+    g = lax.axis_index("dp")
+    c = lax.axis_index("ctx")
+    pos = ring.position(c)
+    right = ring.device(pos + 1)
+    left = ring.device(pos + n - 1)
+    own = pltpu.make_async_copy(x_ref, y_ref.at[pl.ds(c * rows, rows)], own_sem)
+    own.start()
+    _barrier(g, left, right)
+
+    def link(direction, step, origin, source):
+        offset = origin * rows + direction * half
+        return pltpu.make_async_remote_copy(
+            src_ref=source,
+            dst_ref=y_ref.at[pl.ds(offset, half)],
+            send_sem=send_sem.at[direction, step],
+            recv_sem=recv_sem.at[direction, step],
+            device_id=(g, right if direction == 0 else left),
+            device_id_type=MESH_ID,
+        )
+
+    sent = []
+    for step in range(n - 1):
+        origins = (ring.device(pos - step + n), ring.device(pos + step))
+        for direction in (0, 1):
+            origin = origins[direction]
+            if step == 0:
+                source = x_ref.at[pl.ds(direction * half, half)]
+            else:
+                link(direction, step - 1, origin, None if False else y_ref.at[pl.ds(origin * rows + direction * half, half)]).wait_recv()
+                source = y_ref.at[pl.ds(origin * rows + direction * half, half)]
+            copy = link(direction, step, origin, source)
+            copy.start()
+            sent.append(copy)
+    last = n - 2
+    for direction, origin in ((0, ring.device(pos - last - 1 + n)), (1, ring.device(pos + last + 1))):
+        link(direction, last, origin, y_ref.at[pl.ds(origin * rows + direction * half, half)]).wait_recv()
+    for copy in sent:
+        copy.wait_send()
+    own.wait()
+
+
+def ring_all_gather(x, ring, collective_id):
+    rows, cols = x.shape
+    n = ring.size
+    return pl.pallas_call(
+        functools.partial(_gather_kernel, ring=ring, rows=rows),
+        out_shape=jax.ShapeDtypeStruct((n * rows, cols), x.dtype),
+        in_specs=[pl.BlockSpec(memory_space=pl.ANY)],
+        out_specs=pl.BlockSpec(memory_space=pl.ANY),
+        scratch_shapes=[
+            pltpu.SemaphoreType.DMA(()),
+            pltpu.SemaphoreType.DMA((2, n - 1)),
+            pltpu.SemaphoreType.DMA((2, n - 1)),
+        ],
+        compiler_params=pltpu.CompilerParams(collective_id=collective_id, has_side_effects=True),
+    )(x)
+
+
+def _scatter_kernel(p_ref, out_ref, recv_buf, send_buf, send_sem, recv_sem, *, ring, rows):
+    n = ring.size
+    half = rows // 2
+    g = lax.axis_index("dp")
+    c = lax.axis_index("ctx")
+    pos = ring.position(c)
+    right = ring.device(pos + 1)
+    left = ring.device(pos + n - 1)
+    _barrier(g, left, right)
+
+    def link(direction, step):
+        return pltpu.make_async_remote_copy(
+            src_ref=send_buf.at[direction, step],
+            dst_ref=recv_buf.at[direction, step],
+            send_sem=send_sem.at[direction, step],
+            recv_sem=recv_sem.at[direction, step],
+            device_id=(g, right if direction == 0 else left),
+            device_id_type=MESH_ID,
+        )
+
+    sent = []
+    for step in range(n - 1):
+        targets = (ring.device(pos - 1 - step + 2 * n), ring.device(pos + 1 + step))
+        for direction in (0, 1):
+            start = pl.multiple_of(targets[direction] * rows + direction * half, half)
+            total = p_ref[pl.ds(start, half), :].astype(jnp.float32)
+            if step > 0:
+                link(direction, step - 1).wait_recv()
+                total = total + recv_buf[direction, step - 1].astype(jnp.float32)
+            send_buf[direction, step] = total.astype(send_buf.dtype)
+            copy = link(direction, step)
+            copy.start()
+            sent.append(copy)
+    for direction in (0, 1):
+        link(direction, n - 2).wait_recv()
+        start = pl.multiple_of(c * rows + direction * half, half)
+        out_ref[pl.ds(direction * half, half), :] = (
+            p_ref[pl.ds(start, half), :].astype(jnp.float32)
+            + recv_buf[direction, n - 2].astype(jnp.float32)
+        ).astype(out_ref.dtype)
+    for copy in sent:
+        copy.wait_send()
+
+
+def ring_reduce_scatter(p, ring, collective_id, out_dtype=jnp.float32, wire=jnp.bfloat16):
+    total_rows, cols = p.shape
+    n = ring.size
+    rows = total_rows // n
+    half = rows // 2
+    return pl.pallas_call(
+        functools.partial(_scatter_kernel, ring=ring, rows=rows),
+        out_shape=jax.ShapeDtypeStruct((rows, cols), out_dtype),
+        in_specs=[pl.BlockSpec(memory_space=pltpu.VMEM)],
+        out_specs=pl.BlockSpec(memory_space=pltpu.VMEM),
+        scratch_shapes=[
+            pltpu.VMEM((2, n - 1, half, cols), wire),
+            pltpu.VMEM((2, n - 1, half, cols), wire),
+            pltpu.SemaphoreType.DMA((2, n - 1)),
+            pltpu.SemaphoreType.DMA((2, n - 1)),
+        ],
+        compiler_params=pltpu.CompilerParams(
+            collective_id=collective_id, has_side_effects=True, vmem_limit_bytes=60 * 1024 * 1024
+        ),
+    )(p)
+
+
 def block_moves(n_dp, n_ctx):
     count = n_dp * n_ctx
     return [(f, (f % n_dp) * n_ctx + f // n_dp) for f in range(count)]
@@ -303,6 +482,7 @@
 
 
 def head_plan(
+    ring,
     tokens,
     lengths,
     w_qkv,
@@ -347,10 +527,8 @@
     shift32 = shift_low.astype(jnp.float32)
     inputs = tokens.astype(jnp.float32)
     normed, scaled, _ = norm_parts(inputs, gain32, shift32)
-    tokens_group, dy_group = (
-        lax.all_gather(tokens, "ctx", axis=0, tiled=True),
-        lax.all_gather(cotangent, "ctx", axis=0, tiled=True),
-    )
+    tokens_group = ring_all_gather(tokens, ring, 0)
+    dy_group = ring_all_gather(cotangent, ring, 1)
     hidden_group = norm_parts(tokens_group.astype(jnp.float32), gain32, shift32)[2].astype(
         jnp.bfloat16
     )
@@ -375,15 +553,12 @@
         jnp.float32
     )
     act = gelu_tanh(pre).astype(jnp.bfloat16)
-    branches = lax.psum_scatter(
-        (
-            jnp.dot(attended, out_rows, preferred_element_type=jnp.float32)
-            + jnp.dot(act, fc2_rows, preferred_element_type=jnp.float32)
-        ).astype(jnp.bfloat16),
-        "ctx",
-        scatter_dimension=0,
-        tiled=True,
-    ).astype(jnp.float32)
+    branches = ring_reduce_scatter(
+        jnp.dot(attended, out_rows, preferred_element_type=jnp.float32)
+        + jnp.dot(act, fc2_rows, preferred_element_type=jnp.float32),
+        ring,
+        2,
+    )
     block_out = (
         inputs + branches + out_bias.astype(jnp.float32) + fc2_bias.astype(jnp.float32)
     ).astype(jnp.bfloat16)
@@ -416,15 +591,12 @@
     )
     grad_qkv_part = jnp.einsum("td,tc->dc", hidden_group, d_qkv, preferred_element_type=jnp.float32)
     bias_part = jnp.sum(d_qkv.astype(jnp.float32), axis=0).reshape(3, head_width)
-    d_hidden = lax.psum_scatter(
-        (
-            jnp.einsum("tc,dc->td", d_qkv, qkv_cols, preferred_element_type=jnp.float32)
-            + jnp.einsum("tf,df->td", d_pre, fc1_cols, preferred_element_type=jnp.float32)
-        ).astype(jnp.bfloat16),
-        "ctx",
-        scatter_dimension=0,
-        tiled=True,
-    ).astype(jnp.float32)
+    d_hidden = ring_reduce_scatter(
+        jnp.einsum("tc,dc->td", d_qkv, qkv_cols, preferred_element_type=jnp.float32)
+        + jnp.einsum("tf,df->td", d_pre, fc1_cols, preferred_element_type=jnp.float32),
+        ring,
+        3,
+    )
     grad_gain, grad_shift, d_inputs = norm_back(d_hidden, normed, scaled, gain32)
     grad_tokens = (grad_out32 + d_inputs).astype(jnp.bfloat16)
     weight_parts = jnp.concatenate([grad_qkv_part, grad_fc1_part], axis=1).astype(jnp.bfloat16)
@@ -490,6 +662,7 @@
 
 
 def body(
+    ring,
     tokens,
     lengths,
     w_qkv,
@@ -505,6 +678,7 @@
     cotangent,
 ):
     return head_plan(
+        ring,
         tokens,
         lengths,
         w_qkv,
@@ -551,4 +725,5 @@
         P(("dp", "ctx")),
         P(("dp", "ctx")),
     )
-    return jax.shard_map(body, mesh=mesh, in_specs=in_specs, out_specs=out_specs, check_vma=False)
+    ring = ring_of(mesh)
+    return jax.shard_map(functools.partial(body, ring), mesh=mesh, in_specs=in_specs, out_specs=out_specs, check_vma=False)

time: 1190 us -> 1020 us (0.86)
  waiting for transfers between devices: 553 us -> 30 us
  Pallas kernels: 135 us -> 478 us
  blocking collectives: 147 us -> 168 us
    pallas_call x0 -> x4, Pallas kernels: none -> 342 us  [the longest x2 172 us: ring_all_gather(): pl.pallas_call(functools.partial(_gather_kernel, ring=ring, rows=rows), o...]
    reduce_scatter x2 -> x0, waiting for transfers between devices: 304 us -> none  [the longest x1 155 us: head_plan(): lax.psum_scatter((jnp.einsum('tc,dc->td', d_qkv, qkv_cols, preferred_elem...]
    all_gather x2 -> x0, waiting for transfers between devices: 178 us -> none  [the longest x1 89.6 us: head_plan(): lax.all_gather(tokens, 'ctx', axis=0, tiled=True)]
    unnamed x13 -> x9, waiting for transfers between devices: 27.2 us -> 0.13 us
    reduce_scatter x1, waiting for transfers between devices: 13.4 us -> 0.01 us  [head_plan(): lax.psum_scatter(grad_fc2_part.astype(jnp.bfloat16), 'dp', scatter_dimens...]
    all_to_all x1, blocking collectives: 27.2 us -> 40.3 us  [fetch_heads(): lax.all_to_all(qkv_piece, 'ctx', split_axis=2, concat_axis=0, tiled=True)]
    unnamed x89 -> x85, local copies, waits for them, and re-layouts: 30.9 us -> 30 us
  transfers between devices with their start and end apart: 16 -> 12, of which waited for: 8 -> 1; matrix products, arithmetic and copies ran while one was open for 21% -> 26% of each run, Pallas kernels for 11% -> 47%
where the time goes in v3:
time: 1020 us; the launch traced here: 1010 us
  Pallas kernels  478 us (47%)
  blocking collectives  168 us (16%)
  matrix products  151 us (15%)
  local copies, waits for them, and re-layouts  84.3 us (8%)
  other arithmetic  73 us (7%)
  waiting for transfers between devices  30 us (3%)
  between operations  15.1 us (1%)
    pallas_call x2, Pallas kernels, ring_all_gather(): pl.pallas_call(functools.partial(_gather_kernel, ring=ring, rows=rows), o...  172 us
    pallas_call x2, Pallas kernels, ring_reduce_scatter(): pl.pallas_call(functools.partial(_scatter_kernel, ring=ring, rows=rows),...  171 us
    unnamed x2, blocking collectives  98.9 us
    pallas_call x1, Pallas kernels, attention_forward(): pl.pallas_call(functools.partial(_fwd_kernel, tq=tq, tk=tk, scale=scale),...  74 us
    pallas_call x1, Pallas kernels, attention_backward(): pl.pallas_call(functools.partial(_bwd_kernel, tq=tq, tk=tk, scale=scale),...  61.3 us
    all_to_all x1, blocking collectives, fetch_heads(): lax.all_to_all(qkv_piece, 'ctx', split_axis=2, concat_axis=0, tiled=True)  40.3 us
    unnamed x85, local copies, waits for them, and re-layouts  30 us
    all_to_all x1, waiting for transfers between devices, head_plan(): lax.all_to_all(owned_qkv, 'ctx', split_axis=0, concat_axis=2, tiled=True)  29.8 us
  transfers between devices with their start and end apart: 12, of which 1 were waited for; matrix products, arithmetic and copies ran while one was open for 26% of the time, Pallas kernels for 47%

profile of v3, /device:TPU:0, one launch (start us, length us, event | category | flops | bytes accessed | tf_op | source)
XLA Modules:
  0.0 1008.9 jit_solution(16455498509567082269)
XLA Ops:
  9.8 1.6 convert_element_type.198
  11.8 40.3 %all_to_all.54 = bf16[64,3,8,256]{3,0,1,2:T(8,128)(2,1)S(1)} all-to-all(bf16[64,3,8,256]{3,0,1,2:T(8,128)(2,1)S(1)} %copy.150), channel_id=1, replica_groups=mesh['dp'=4,'ctx'=8] {'ctx'}, dimensions={2} | all-to-all | bytes 1572864 | tf_op jit(solution)/shard_map/all_to_all | solution.py:469
  53.9 28.8 %all_to_all.55 = bf16[64,4,8,256]{3,1,0,2:T(4,128)(2,1)S(1)} all-to-all(bf16[64,4,8,256]{3,1,0,2:T(4,128)(2,1)S(1)} %copy.164), channel_id=1, replica_groups=mesh['dp'=4,'ctx'=8] {'ctx'}, dimensions={2} | all-to-all | bytes 2097152 | tf_op jit(solution)/shard_map/all_to_all | solution.py:470
  85.7 41.9 %all-reduce = bf16[22528]{0:T(1024)(128)(2,1)S(1)} all-reduce(bf16[22528]{0:T(1024)(128)(2,1)S(1)} %dynamic-update-slice), channel_id=2, replica_groups=mesh['dp'=4,'ctx'=8] {'dp','ctx'}, use_global_device_ids=true, to_apply=%add | all-reduce | flops 22528 | bytes 90112
  128.7 83.3 %shard_map.220 = bf16[2048,2048]{1,0:T(8,128)(2,1)} custom-call(bf16[256,2048]{1,0:T(8,128)(2,1)} %x_ref.2), custom_call_target="tpu_custom_call" | custom-call | tf_op jit(solution)/shard_map/pallas_call | solution.py:348
  212.0 4.7 convert_reduce_fusion
  217.7 2.3 fusion.2
  223.2 88.2 %shard_map.223 = bf16[2048,2048]{1,0:T(8,128)(2,1)} custom-call(bf16[256,2048]{1,0:T(8,128)(2,1)} %x_ref.3), custom_call_target="tpu_custom_call" | custom-call | tf_op jit(solution)/shard_map/pallas_call | solution.py:348
  311.5 8.6 fusion.5
  320.1 6.0 convolution_convert_fusion.3
  326.0 1.7 copy.167
  327.8 4.7 copy.152
  332.5 10.2 %broadcast_add_fusion = f32[2048,768]{0,1:T(8,128)S(1)} fusion(f32[768]{0:T(1024)S(1)} %reshape.298, bf16[2048,2048]{1,0:T(8,128)(2,1)} %fusion.5, bf16[2048,768]{0,1:T(8,128)(2,1)} %bitcast.132), kind=kOutput, calls=%fused_computation.38 | convolution fusion | flops 6444023808 | bytes 17828864 | tf_op jit(solution)/shard_map/dot_general | solution.py:538
  347.0 3.5 copy.179
  350.5 3.6 copy.180
  354.2 3.5 copy.182
  357.7 3.5 copy.183
  361.2 2.6 copy.181
  363.8 2.6 copy.184
  366.4 1.8 copy.161
  368.2 7.2 subtract_convert_fusion.2
  375.4 5.2 maximum_bitcast_fusion
  380.6 74.0 %shard_map.221 = (f32[4,2048,64]{2,1,0:T(8,128)}, f32[4,2048,1]{2,1,0:T(8,128)}) custom-call(bf16[4,2048,64]{2,1,0:T(8,128)(2,1)} %get-tuple-element.60.q_ref, bf16[4,2048,64]{2,1,0:T(8,128)(2,1)} %get-tuple-element.61.k_ref, bf16[4,2048,64]{2,1,0:T(8,128)(2,1)} %bitcast.138, s32[2048,1]{1,0:T(8,128)} %copy.162.segq_ref, s32[1,2048]{1,0:T(1,128)} %bitcast.144), custom_call_target="tpu_custom_call" | custom-call | flops 2147483648 | bytes 5242880 | tf_op jit(solution)/shard_map/pallas_call | solution.py:145
  454.5 6.8 multiply_reduce_fusion
  461.3 2.8 copy.168.delta_ref
  464.2 61.3 %shard_map.224 = (f32[4,2048,64]{2,1,0:T(8,128)}, f32[4,2048,64]{2,1,0:T(8,128)}, f32[4,2048,64]{2,1,0:T(8,128)}) custom-call(bf16[4,2048,64]{2,1,0:T(8,128)(2,1)} %get-tuple-element.60.q_ref, bf16[4,2048,64]{2,1,0:T(8,128)(2,1)} %get-tuple-element.61.k_ref, bf16[4,2048,64]{2,1,0:T(8,128)(2,1)} %bitcast.139, bf16[4,2048,64]{2,1,0:T(8,128)(2,1)} %bitcast.107, ...), custom_call_target="tpu_custom_call" | custom-call | flops 5368709120 | bytes 12582912 | tf_op jit(solution)/shard_map/pallas_call | solution.py:218
  525.5 2.9 slice.179
  528.9 1.9 slice.178
  530.8 4.3 add_convert_fusion.1
  535.2 3.2 pad_maximum_fusion.2
  538.3 1.9 copy.170
  540.3 5.8 pad_maximum_fusion.3
  546.1 2.7 copy.171
  548.8 2.5 convert_bitcast_fusion.1
  551.2 1.6 copy.172
  552.9 10.9 %convolution_convert_fusion.2 = bf16[2048,768]{0,1:T(8,128)(2,1)} fusion(bf16[2048,2048]{1,0:T(8,128)(2,1)} %fusion.5, bf16[2048,256]{0,1:T(8,128)(2,1)} %bitcast.120, bf16[2048,256]{0,1:T(8,128)(2,1)} %bitcast.117, bf16[2048,256]{0,1:T(8,128)(2,1)S(1)} %bitcast.114), kind=kOutput, calls=%fused_computation.36 | convolution fusion | flops 6453460992 | bytes 14680064 | tf_op jit(solution)/shard_map/td,tc->dc/dot_general | solution.py:592
  563.7 6.6 copy.166
  570.4 14.5 %fusion.33 = f32[2048,1024]{1,0:T(8,128)} fusion(bf16[2048,2048]{1,0:T(8,128)(2,1)} %fusion.5, bf16[2048,1024]{0,1:T(8,128)(2,1)} %bitcast.126), kind=kOutput, calls=%fused_computation.105 | convolution fusion | flops 8589934592 | bytes 20971520 | tf_op jit(solution)/shard_map/dot_general | solution.py:552
  584.9 19.6 %convert_reduce_fusion.1 = (f32[1024]{0:T(1024)S(1)}, bf16[2048,1024]{1,0:T(8,128)(2,1)S(1)}) fusion(f32[2048,1024]{1,0:T(8,128)} %fusion.33, f32[1024]{0:T(1024)S(1)} %bitcast.146, bf16[2048,2048]{1,0:T(8,128)(2,1)} %shard_map.223, bf16[1024,2048]{1,0:T(8,128)(2,1)} %all-gather.12.cloned.1.call-done), kind=kOutput, calls=%fused_computation.18 | convolution fusion | flops 8636070912 | bytes 25174016 | tf_op jit(solution)/shard_map/td,fd->tf/dot_general | solution.py:568
  604.5 1.9 copy-done.34
  606.4 11.7 %convolution_convert_fusion.1 = bf16[2048,1024]{0,1:T(8,128)(2,1)S(1)} fusion(bf16[2048,2048]{1,0:T(8,128)(2,1)} %fusion.5, bf16[2048,1024]{1,0:T(8,128)(2,1)S(1)} %get-tuple-element.59), kind=kOutput, calls=%fused_computation.35 | convolution fusion | flops 8592031744 | bytes 16777216 | tf_op jit(solution)/shard_map/td,tf->df/dot_general | solution.py:570
  618.1 5.9 pad_maximum_fusion
  625.9 2.1 convert_reduce_fusion.2
  628.2 1.6 copy.163
  629.8 9.2 fusion.34
  639.0 12.0 %fusion.28 = f32[2048,2048]{1,0:T(8,128)} fusion(bf16[2048,768]{0,1:T(8,128)(2,1)} %bitcast.133, bf16[2048,256]{0,1:T(8,128)(2,1)} %bitcast.122, bf16[2048,256]{0,1:T(8,128)(2,1)S(1)} %bitcast.119, bf16[2048,256]{0,1:T(8,128)(2,1)S(1)} %bitcast.116), kind=kOutput, calls=%fused_computation.100 | convolution fusion | flops 6451888128 | bytes 23068672 | tf_op jit(solution)/shard_map/tc,dc->td/dot_general | solution.py:595
  651.1 17.9 %convolution_add_fusion.1.p_ref = f32[2048,2048]{1,0:T(8,128)} fusion(f32[2048,2048]{1,0:T(8,128)} %fusion.28, bf16[2048,1024]{1,0:T(8,128)(2,1)} %copy-done.34, bf16[2048,1024]{0,1:T(8,128)(2,1)} %bitcast.127), kind=kOutput, calls=%fused_computation.20 | convolution fusion | flops 8594128896 | bytes 41943040 | tf_op jit(solution)/shard_map/tf,df->td/dot_general | solution.py:596
  669.0 87.0 %shard_map.225 = f32[256,2048]{1,0:T(8,128)} custom-call(f32[2048,2048]{1,0:T(8,128)} %convolution_add_fusion.1.p_ref), custom_call_target="tpu_custom_call" | custom-call | tf_op jit(solution)/shard_map/pallas_call | solution.py:411
  756.0 13.9 %fusion.29 = f32[2048,2048]{1,0:T(8,128)S(1)} fusion(bf16[1024,2048]{1,0:T(8,128)(2,1)} %all-gather.12.cloned.1.call-done, f32[2048,1024]{1,0:T(8,128)} %fusion.33, f32[1024]{0:T(1024)S(1)} %bitcast.147), kind=kOutput, calls=%fused_computation.101 | convolution fusion | flops 8610906112 | bytes 29364224 | tf_op jit(solution)/shard_map/dot_general | solution.py:558
  769.9 8.3 convolution_add_fusion.p_ref
  778.2 83.7 %shard_map.222 = f32[256,2048]{1,0:T(8,128)} custom-call(f32[2048,2048]{1,0:T(8,128)} %convolution_add_fusion.p_ref), custom_call_target="tpu_custom_call" | custom-call | tf_op jit(solution)/shard_map/pallas_call | solution.py:411
  863.6 4.1 convert_reduce_fusion.4
  868.8 16.7 %convolution_convert_fusion = bf16[1024,2048]{1,0:T(8,128)(2,1)} fusion(bf16[2048,2048]{1,0:T(8,128)(2,1)} %shard_map.223, f32[2048,1024]{1,0:T(8,128)} %fusion.33, f32[1024]{0:T(1024)S(1)} %bitcast.148), kind=kOutput, calls=%fused_computation.34 | convolution fusion | flops 8613003264 | bytes 20975616 | tf_op jit(solution)/shard_map/tf,td->fd/dot_general | solution.py:567
  886.8 1.4 copy.173
  888.2 3.8 all-to-all-start.2
  892.0 1.4 copy.176
  893.4 29.8 %all-to-all-done.2 = bf16[512,3,1,256]{3,1,2,0:T(4,128)(2,1)S(1)} async-done(((bf16[512,3,1,256]{3,1,2,0:T(4,128)(2,1)}), bf16[512,3,1,256]{3,1,2,0:T(4,128)(2,1)S(1)}, u32[]{:S(2)}, u32[]{:S(2)}) %all-to-all-start.2) | async-done | bytes 786464 | tf_op jit(solution)/shard_map/all_to_all | solution.py:610
  923.2 3.6 all-to-all-start.3
  926.8 1.7 collective-permute-start.1
  929.7 1.6 dynamic-slice_reduce_fusion
  931.3 57.0 %all-reduce.2 = f32[8,640]{1,0:T(8,128)S(1)} all-reduce(f32[8,640]{1,0:T(8,128)S(1)} %reshape.294), channel_id=5, replica_groups=mesh['dp'=4,'ctx'=8] {'ctx'}, use_global_device_ids=true, to_apply=%region_17.18.clone | all-reduce | flops 5120 | bytes 40960
  992.0 2.8 convert_element_type.234
  996.0 1.4 reshape.302
  999.0 1.5 reshape.303
  (181 shorter events, 32.5 us)
Async XLA Ops:
  7.2 312.9 %all-gather.8.cloned.1.call-start = ((), (), s32[]{:S(2)}) async-start(), calls=%async_computation.8 | async-start | bytes 1310720 | tf_op jit(solution)/shard_map/all_gather | solution.py:437
  8.3 0.7 collective-permute-start
  9.0 0.7 copy-start.18
  9.7 43.4 %copy-start.14 = (f32[64,8192]{1,0:T(8,128)S(1)}, f32[64,8192]{1,0:T(8,128)}, u32[]{:S(2)}) copy-start(f32[64,8192]{1,0:T(8,128)} %param.19) | copy-start | bytes 6291460
  9.7 318.0 %all-gather.6.cloned.1.call-start = ((), (), s32[]{:S(2)}) async-start(), calls=%async_computation.7 | async-start | bytes 3932160 | tf_op jit(solution)/shard_map/all_gather | solution.py:473
  53.1 510.7 %all-gather.10.cloned.1.call-start = ((), (), s32[]{:S(2)}) async-start(), calls=%async_computation.9 | async-start | bytes 5242880 | tf_op jit(solution)/shard_map/all_gather | solution.py:474
  53.5 30.5 %copy-start.15 = (f32[256,2048]{1,0:T(8,128)S(1)}, f32[256,2048]{1,0:T(8,128)}, u32[]{:S(2)}) copy-start(f32[256,2048]{1,0:T(8,128)} %param.21) | copy-start | bytes 6291460
  82.8 2.5 copy-start.25
  82.8 2.5 copy-start.27
  82.8 2.5 copy-start.28
  82.8 2.5 copy-start.29
  82.8 2.6 copy-start.30
  82.8 2.6 copy-start.26
  84.0 500.9 %all-gather.12.cloned.1.call-start = ((), (), s32[]{:S(2)}) async-start(), calls=%async_computation.10 | async-start | bytes 5242880 | tf_op jit(solution)/shard_map/all_gather | solution.py:475
  85.2 800.3 %reduce-scatter.4.cloned.1.call-start = ((), (), s32[]{:S(2)}) async-start(), calls=%async_computation.11 | async-start | bytes 9175040 | tf_op jit(solution)/shard_map/reduce_scatter | solution.py:603
  127.7 84.2 %copy-start.17 = (bf16[32,704]{1,0:T(8,128)(2,1)}, bf16[32,704]{1,0:T(8,128)(2,1)S(1)}, u32[]{:S(2)}) copy-start(bf16[32,704]{1,0:T(8,128)(2,1)S(1)} %reshape.306) | copy-start | bytes 135172
  128.6 182.9 %copy-start.19 = (f32[2048]{0:T(1024)}, f32[2048]{0:T(1024)S(1)}, u32[]{:S(2)}) copy-start(f32[2048]{0:T(1024)S(1)} %reshape.296) | copy-start | bytes 24580
  212.0 5.8 copy-start
  217.7 2.3 slice-start.1
  217.7 2.5 copy-start.31
  220.5 90.9 %copy-start.21 = (s32[2048]{0:T(1024)}, s32[2048]{0:T(1024)S(1)}, u32[]{:S(2)}) copy-start(s32[2048]{0:T(1024)S(1)} %convert_reduce_fusion.5) | copy-start | bytes 24580
  368.2 7.2 copy-start.8
  368.2 7.2 copy-start.9
  525.5 3.5 copy-start.2
  525.5 5.4 copy-start.1
  535.1 5.1 copy-start.7
  540.3 12.6 %copy-start.11 = (bf16[2048,4,64]{0,2,1:T(8,128)(2,1)}, bf16[2048,4,64]{0,2,1:T(8,128)(2,1)S(1)}, u32[]{:S(2)}) copy-start(bf16[2048,4,64]{0,2,1:T(8,128)(2,1)S(1)} %copy.170) | copy-start | bytes 3145732
  604.5 1.9 copy-start.34
  624.0 0.7 copy-start.23
  624.0 0.8 copy-start.22
  624.0 1.3 copy-start.3
  624.0 4.1 copy-start.6
  624.0 302.7 %reduce-scatter.6.cloned.1.call-start = ((), (), s32[]{:S(2)}) async-start(), calls=%async_computation.12 | async-start | bytes 2621440 | tf_op jit(solution)/shard_map/reduce_scatter | solution.py:443
  629.8 9.2 copy-start.12
  629.8 9.2 copy-start.13
  651.1 278.6 %all-reduce.5.cloned.1.call-start = ((), (), s32[]{:S(2)}) async-start(), calls=%async_computation.14 | async-start | bytes 163840
  756.0 13.9 %copy-start.10 = (bf16[2048,4,64]{0,2,1:T(8,128)(2,1)S(1)}, bf16[2048,4,64]{0,2,1:T(8,128)(2,1)}, u32[]{:S(2)}) copy-start(bf16[2048,4,64]{0,2,1:T(8,128)(2,1)} %copy.163) | copy-start | bytes 3145732
  756.0 13.9 %copy-start.16 = (bf16[256,2048]{1,0:T(8,128)(2,1)S(1)}, bf16[256,2048]{1,0:T(8,128)(2,1)}, u32[]{:S(2)}) copy-start(bf16[256,2048]{1,0:T(8,128)(2,1)} %all-gather.8.cloned.1.call-done) | copy-start | bytes 3145732
  778.2 83.8 %copy-start.4 = (f32[256,2048]{1,0:T(8,128)S(1)}, f32[256,2048]{1,0:T(8,128)}, u32[]{:S(2)}) copy-start(f32[256,2048]{1,0:T(8,128)} %shard_map.225) | copy-start | bytes 6291460
  778.2 83.8 %copy-start.20 = (f32[2048]{0:T(1024)S(1)}, f32[2048]{0:T(1024)}, u32[]{:S(2)}) copy-start(f32[2048]{0:T(1024)} %copy-done.19) | copy-start | bytes 24580
  862.0 1.6 copy-start.5
  868.7 123.2 %reduce-scatter.8.cloned.1.call-start = ((), (), s32[]{:S(2)}) async-start(), calls=%async_computation.13 | async-start | bytes 5242880 | tf_op jit(solution)/shard_map/reduce_scatter | solution.py:606
  885.5 6.5 slice-start
  888.2 40.3 %copy-start.33 = (u32[32]{0:T(128)S(1)}, u32[32]{0:T(128)}, u32[]{:S(2)}) copy-start(u32[32]{0:T(128)} %constant.54) | copy-start | bytes 388
  888.2 40.9 %copy-start.32 = (u32[32]{0:T(128)S(1)}, u32[32]{0:T(128)}, u32[]{:S(2)}) copy-start(u32[32]{0:T(128)} %constant.58) | copy-start | bytes 388
  888.2 35.0 %all-to-all-start.2 = ((bf16[512,3,1,256]{3,1,2,0:T(4,128)(2,1)}), bf16[512,3,1,256]{3,1,2,0:T(4,128)(2,1)S(1)}, u32[]{:S(2)}, u32[]{:S(2)}) async-start(bf16[512,3,1,256]{3,1,2,0:T(4,128)(2,1)} %copy.173), calls=%async_computation.3 | async-start | bytes 2097152 | tf_op jit(solution)/shard_map/all_to_all | solution.py:610
  923.2 74.2 %all-to-all-start.3 = ((bf16[512,4,1,256]{3,1,2,0:T(4,128)(2,1)}), bf16[512,4,1,256]{3,1,2,0:T(4,128)(2,1)S(1)}, u32[]{:S(2)}, u32[]{:S(2)}) async-start(bf16[512,4,1,256]{3,1,2,0:T(4,128)(2,1)} %copy.176), calls=%async_computation.5 | async-start | bytes 2097152 | tf_op jit(solution)/shard_map/all_to_all | solution.py:613
  926.8 65.2 %collective-permute-start.1 = (f32[64,2048]{1,0:T(8,128)}, f32[64,2048]{1,0:T(8,128)S(1)}, u32[]{:S(2)}, u32[]{:S(2)}) collective-permute-start(f32[64,2048]{1,0:T(8,128)} %reduce-scatter.6.cloned.1.call-done), channel_id=1, source_target_pairs={{0,0},{8,1},{16,2},{24,3},{1,4},{9,5},{17,6},{25,7},{2,8},{10,9},{... | collective-permute-start | bytes 1572872 | tf_op jit(solution)/shard_map/ppermute | solution.py:445
  989.5 11.1 %copy-start.24 = (f32[64]{0:T(128)}, f32[64]{0:T(128)S(1)}, u32[]{:S(2)}) copy-start(f32[64]{0:T(128)S(1)} %get-tuple-element.103) | copy-start | bytes 772
Sparse Core Ops, SparseCore 0:
  10.1 34.0 all-gather.7
  53.2 29.7 all-gather.5
  84.5 35.8 all-gather.9
  121.8 34.4 all-gather.11
  624.1 64.5 reduce-scatter.3
  691.9 31.4 reduce-scatter.5
  868.9 31.5 all-reduce.4
  903.1 48.7 reduce-scatter.7

commit v4 on v3

--- a/solution.py
+++ b/solution.py
@@ -425,6 +425,66 @@
     )(p)
 
 
+def _exchange_kernel(x_ref, out_ref, own_sem, send_sem, recv_sem, *, everyone):
+    n = x_ref.shape[0]
+    g = lax.axis_index("dp")
+    c = lax.axis_index("ctx")
+    n_ctx = lax.axis_size("ctx")
+    me = g * n_ctx + c if everyone else c
+
+    def address(member):
+        if everyone:
+            return (member // n_ctx, member % n_ctx)
+        return (g, member)
+
+    own = pltpu.make_async_copy(x_ref.at[me], out_ref.at[me], own_sem)
+    own.start()
+    barrier = pltpu.get_barrier_semaphore()
+    for offset in range(1, n):
+        pl.semaphore_signal(
+            barrier, 1, device_id=address((me + offset) % n), device_id_type=MESH_ID
+        )
+    pl.semaphore_wait(barrier, n - 1)
+
+    def link(offset, source, target):
+        return pltpu.make_async_remote_copy(
+            src_ref=x_ref.at[target],
+            dst_ref=out_ref.at[source],
+            send_sem=send_sem.at[offset],
+            recv_sem=recv_sem.at[offset],
+            device_id=address(target),
+            device_id_type=MESH_ID,
+        )
+
+    sent = []
+    for offset in range(1, n):
+        copy = link(offset, me, (me + offset) % n)
+        copy.start()
+        sent.append(copy)
+    for offset in range(1, n):
+        link(offset, (me + n - offset) % n, me).wait_recv()
+    for copy in sent:
+        copy.wait_send()
+    own.wait()
+
+
+def exchange(x, everyone, collective_id):
+    n = x.shape[0]
+    space = pltpu.VMEM
+    return pl.pallas_call(
+        functools.partial(_exchange_kernel, everyone=everyone),
+        out_shape=jax.ShapeDtypeStruct(x.shape, x.dtype),
+        in_specs=[pl.BlockSpec(memory_space=space)],
+        out_specs=pl.BlockSpec(memory_space=space),
+        scratch_shapes=[
+            pltpu.SemaphoreType.DMA(()),
+            pltpu.SemaphoreType.DMA((n,)),
+            pltpu.SemaphoreType.DMA((n,)),
+        ],
+        compiler_params=pltpu.CompilerParams(collective_id=collective_id, has_side_effects=True),
+    )(x)
+
+
 def block_moves(n_dp, n_ctx):
     count = n_dp * n_ctx
     return [(f, (f % n_dp) * n_ctx + f // n_dp) for f in range(count)]
@@ -445,16 +505,31 @@
     return lax.ppermute(part, ("dp", "ctx"), perm=back)
 
 
+def pack_rows(vector, lanes):
+    size = vector.shape[0]
+    total = -(-size // (16 * lanes)) * 16 * lanes
+    return jnp.pad(vector, (0, total - size)).reshape(-1, lanes)
+
+
 def fetch_small(b_qkv, b_out, b_fc2, ln_gain, ln_shift, b_fc1):
     pieces = (b_qkv, b_out, b_fc2, ln_gain, ln_shift, b_fc1)
-    packed = jnp.concatenate([p.astype(jnp.bfloat16) for p in pieces])
-    table = lax.all_gather(packed, ("dp", "ctx"), axis=0, tiled=False)
+    count = lax.axis_size("dp") * lax.axis_size("ctx")
+    packed = pack_rows(jnp.concatenate([p.astype(jnp.bfloat16) for p in pieces]), 128)
+    table = exchange(jnp.broadcast_to(packed[None], (count,) + packed.shape), True, 4)
+    table = table.reshape(count, -1)
     result = []
     offset = 0
     for p in pieces:
         result.append(table[:, offset : offset + p.shape[0]])
         offset += p.shape[0]
     return result
+
+
+def reduce_small(small):
+    count, width = small.shape
+    packed = jax.vmap(lambda row: pack_rows(row, 128))(small)
+    received = exchange(packed, True, 7)
+    return jnp.sum(received, axis=0).reshape(-1)[:width]
 
 
 def fetch_heads(w_qkv, w_fc1, w_fc2):
@@ -465,19 +540,33 @@
     unit = FF // (dp_count * ctx_count)
     qkv_piece = w_qkv.astype(jnp.bfloat16).reshape(rows_piece, 3, ctx_count, head_width)
     fc1_piece = w_fc1.astype(jnp.bfloat16).reshape(rows_piece, dp_count, ctx_count, unit)
-    qkv_sent, fc1_sent = (
-        lax.all_to_all(qkv_piece, "ctx", split_axis=2, concat_axis=0, tiled=True),
-        lax.all_to_all(fc1_piece, "ctx", split_axis=2, concat_axis=0, tiled=True),
-    )
-    qkv_cols, fc1_cols, fc2_rows = (
-        lax.all_gather(qkv_sent, "dp", axis=0, tiled=True),
-        lax.all_gather(fc1_sent, "dp", axis=0, tiled=True),
+    pieces = jnp.concatenate(
+        [
+            qkv_piece.transpose(2, 0, 1, 3).reshape(ctx_count, rows_piece, 3 * head_width),
+            fc1_piece.transpose(2, 0, 1, 3).reshape(ctx_count, rows_piece, dp_count * unit),
+        ],
+        axis=2,
+    )
+    sent = exchange(pieces, False, 5).reshape(ctx_count * rows_piece, -1)
+    cols, fc2_rows = (
+        lax.all_gather(sent, "dp", axis=0, tiled=True),
         lax.all_gather(w_fc2.astype(jnp.bfloat16), "dp", axis=0, tiled=True),
     )
+    return (cols, fc2_rows)
+
+
+def return_heads(owned_parts):
+    dp_count = lax.axis_size("dp")
+    ctx_count = lax.axis_size("ctx")
+    head_width = D // ctx_count
+    unit = FF // (dp_count * ctx_count)
+    rows_piece = owned_parts.shape[0] // ctx_count
+    got = exchange(owned_parts.reshape(ctx_count, rows_piece, -1), False, 6)
+    qkv = got[:, :, : 3 * head_width].reshape(ctx_count, rows_piece, 3, head_width)
+    fc1 = got[:, :, 3 * head_width :].reshape(ctx_count, rows_piece, dp_count, unit)
     return (
-        qkv_cols.reshape(D, 3 * head_width),
-        fc1_cols.reshape(D, dp_count * unit),
-        fc2_rows,
+        qkv.transpose(1, 2, 0, 3).reshape(rows_piece, 3 * D).astype(jnp.float32),
+        fc1.transpose(1, 2, 0, 3).reshape(rows_piece, FF).astype(jnp.float32),
     )
 
 
@@ -522,7 +611,7 @@
         fc1_table.reshape(dp_count, ctx_count, unit), here, 1, keepdims=False
     ).reshape(dp_count * unit)
     out_rows = fetch_out_rows(w_out)
-    qkv_cols, fc1_cols, fc2_rows = fetch_heads(w_qkv, w_fc1, w_fc2)
+    cols, fc2_rows = fetch_heads(w_qkv, w_fc1, w_fc2)
     gain32 = gain_low.astype(jnp.float32)
     shift32 = shift_low.astype(jnp.float32)
     inputs = tokens.astype(jnp.float32)
@@ -535,9 +624,11 @@
     bias_cols = lax.dynamic_slice_in_dim(
         qkv_bias.reshape(3, D), here * head_width, head_width, 1
     ).reshape(3 * head_width)
-    qkv = jnp.dot(hidden_group, qkv_cols, preferred_element_type=jnp.float32) + bias_cols.astype(
-        jnp.float32
-    )
+    both = jnp.dot(hidden_group, cols, preferred_element_type=jnp.float32) + jnp.concatenate(
+        [bias_cols, fc1_bias]
+    ).astype(jnp.float32)
+    qkv = both[:, : 3 * head_width]
+    pre = both[:, 3 * head_width :]
     shape = (group, local_heads, HEAD_DIM)
     query = rotate(qkv[:, :head_width].reshape(shape), cosine, sine).astype(jnp.bfloat16)
     keys = rotate(qkv[:, head_width : 2 * head_width].reshape(shape), cosine, sine).astype(
@@ -549,9 +640,6 @@
     v_heads = values.transpose(1, 0, 2)
     attended_heads, log_total = attention_forward(q_heads, k_heads, v_heads, seg)
     attended = attended_heads.transpose(1, 0, 2).reshape(group, head_width).astype(jnp.bfloat16)
-    pre = jnp.dot(hidden_group, fc1_cols, preferred_element_type=jnp.float32) + fc1_bias.astype(
-        jnp.float32
-    )
     act = gelu_tanh(pre).astype(jnp.bfloat16)
     branches = ring_reduce_scatter(
         jnp.dot(attended, out_rows, preferred_element_type=jnp.float32)
@@ -567,7 +655,6 @@
     grad_fc2_part = jnp.einsum("tf,td->fd", act, dy_group, preferred_element_type=jnp.float32)
     d_act = jnp.einsum("td,fd->tf", dy_group, fc2_rows, preferred_element_type=jnp.float32)
     d_pre = (d_act * gelu_slope(pre)).astype(jnp.bfloat16)
-    grad_fc1_part = jnp.einsum("td,tf->df", hidden_group, d_pre, preferred_element_type=jnp.float32)
     grad_bfc1_part = jnp.sum(d_pre.astype(jnp.float32), axis=0)
     grad_out_rows = jnp.einsum("tc,td->cd", attended, dy_group, preferred_element_type=jnp.float32)
     owned_w_out = return_out_rows(grad_out_rows)
@@ -589,31 +676,21 @@
     d_qkv = jnp.concatenate([d_query, d_keys, d_values.reshape(group, head_width)], axis=1).astype(
         jnp.bfloat16
     )
-    grad_qkv_part = jnp.einsum("td,tc->dc", hidden_group, d_qkv, preferred_element_type=jnp.float32)
+    d_both = jnp.concatenate([d_qkv, d_pre], axis=1)
     bias_part = jnp.sum(d_qkv.astype(jnp.float32), axis=0).reshape(3, head_width)
     d_hidden = ring_reduce_scatter(
-        jnp.einsum("tc,dc->td", d_qkv, qkv_cols, preferred_element_type=jnp.float32)
-        + jnp.einsum("tf,df->td", d_pre, fc1_cols, preferred_element_type=jnp.float32),
-        ring,
-        3,
+        jnp.einsum("tc,dc->td", d_both, cols, preferred_element_type=jnp.float32), ring, 3
     )
     grad_gain, grad_shift, d_inputs = norm_back(d_hidden, normed, scaled, gain32)
     grad_tokens = (grad_out32 + d_inputs).astype(jnp.bfloat16)
-    weight_parts = jnp.concatenate([grad_qkv_part, grad_fc1_part], axis=1).astype(jnp.bfloat16)
+    weight_parts = jnp.einsum(
+        "td,tc->dc", hidden_group, d_both, preferred_element_type=jnp.float32
+    ).astype(jnp.bfloat16)
     owned_parts = lax.psum_scatter(weight_parts, "dp", scatter_dimension=0, tiled=True)
-    owned_qkv = owned_parts[:, : 3 * head_width].reshape(-1, 3, 1, head_width)
-    owned_fc1 = owned_parts[:, 3 * head_width :].reshape(-1, dp_count, 1, unit)
+    split_qkv, split_fc1 = return_heads(owned_parts)
     owned_fc2 = lax.psum_scatter(
         grad_fc2_part.astype(jnp.bfloat16), "dp", scatter_dimension=0, tiled=True
     ).astype(jnp.float32)
-    split_qkv, split_fc1 = (
-        lax.all_to_all(owned_qkv, "ctx", split_axis=0, concat_axis=2, tiled=True).astype(
-            jnp.float32
-        ),
-        lax.all_to_all(owned_fc1, "ctx", split_axis=0, concat_axis=2, tiled=True).astype(
-            jnp.float32
-        ),
-    )
     full_bqkv = lax.dynamic_update_slice_in_dim(
         jnp.zeros((3, D), jnp.float32), bias_part, here * head_width, 1
     )
@@ -633,13 +710,7 @@
         ],
         axis=1,
     )
-    width_small = small.shape[1]
-    over_dp = lax.psum_scatter(
-        small.reshape(dp_count, ctx_count * width_small), "dp", scatter_dimension=0, tiled=True
-    )
-    owned_small = lax.psum_scatter(
-        over_dp.reshape(ctx_count, width_small), "ctx", scatter_dimension=0, tiled=True
-    )[0]
+    owned_small = reduce_small(small)
     cuts = [0, 3 * D // count, D // count, D // count, D // count, FF // count]
     bounds = [sum(cuts[: i + 1]) for i in range(len(cuts))]
     owned_bqkv, owned_bout, owned_gain, owned_shift, owned_bfc1 = [

time: 1020 us -> 970 us (0.951)
  blocking collectives: 168 us -> 0 us
  Pallas kernels: 478 us -> 645 us
  waiting for transfers between devices: 30 us -> 0.15 us
    pallas_call x0 -> x4, Pallas kernels: none -> 160 us  [exchange(): pl.pallas_call(functools.partial(_exchange_kernel, everyone=everyone), ou...]
    unnamed x2 -> x0, blocking collectives: 98.9 us -> none
    all_to_all x2 -> x0, blocking collectives: 69.2 us -> none  [the longest x1 40.3 us: fetch_heads(): lax.all_to_all(qkv_piece, 'ctx', split_axis=2, concat_axis=0, tiled=True)]
    all_to_all x2 -> x0, waiting for transfers between devices: 29.8 us -> none  [the longest x1 29.8 us: head_plan(): lax.all_to_all(owned_qkv, 'ctx', split_axis=0, concat_axis=2, tiled=True)]
    all_gather x3 -> x0, local copies, waits for them, and re-layouts: 11.5 us -> none  [the longest x1 6.64 us: fetch_heads(): lax.all_gather(fc1_sent, 'dp', axis=0, tiled=True)]
    dot_general x6 -> x3, matrix products: 77.2 us -> 73.8 us  [the longest x1 28.6 us: head_plan(): jnp.einsum('td,tc->dc', hidden_group, d_both, preferred_element_type=jnp....]
    unnamed x85 -> x66, local copies, waits for them, and re-layouts: 30 us -> 30.5 us
  transfers between devices with their start and end apart: 12 -> 8, of which waited for: 1 -> 0; matrix products, arithmetic and copies ran while one was open for 26% -> 28% of each run, Pallas kernels for 47% -> 60%
where the time goes in v4:
time: 970 us; the launch traced here: 955 us
  Pallas kernels  645 us (66%)
  matrix products  146 us (15%)
  local copies, waits for them, and re-layouts  78.7 us (8%)
  other arithmetic  66.8 us (7%)
  between operations  15.1 us (2%)
    pallas_call x2, Pallas kernels, ring_reduce_scatter(): pl.pallas_call(functools.partial(_scatter_kernel, ring=ring, rows=rows),...  175 us
    pallas_call x2, Pallas kernels, ring_all_gather(): pl.pallas_call(functools.partial(_gather_kernel, ring=ring, rows=rows), o...  173 us
    pallas_call x4, Pallas kernels, exchange(): pl.pallas_call(functools.partial(_exchange_kernel, everyone=everyone), ou...  160 us
    pallas_call x1, Pallas kernels, attention_forward(): pl.pallas_call(functools.partial(_fwd_kernel, tq=tq, tk=tk, scale=scale),...  74.4 us
    pallas_call x1, Pallas kernels, attention_backward(): pl.pallas_call(functools.partial(_bwd_kernel, tq=tq, tk=tk, scale=scale),...  62 us
    unnamed x66, local copies, waits for them, and re-layouts  30.5 us
    dot_general x1, matrix products, head_plan(): jnp.einsum('td,tc->dc', hidden_group, d_both, preferred_element_type=jnp....  28.6 us
    dot_general x1, matrix products, head_plan(): jnp.dot(hidden_group, cols, preferred_element_type=jnp.float32)  23.4 us
  transfers between devices with their start and end apart: 8, of which 0 were waited for; matrix products, arithmetic and copies ran while one was open for 28% of the time, Pallas kernels for 60%

profile of v4, /device:TPU:0, one launch (start us, length us, event | category | flops | bytes accessed | tf_op | source)
XLA Modules:
  0.0 955.1 jit_solution(16146281098297507488)
XLA Ops:
  9.8 1.7 convert_element_type.190
  12.9 1.5 convert_element_type.189
  15.9 1.4 pad_maximum_fusion.3.x_ref
  17.3 52.2 %shard_map.222 = bf16[8,64,1792]{2,1,0:T(8,128)(2,1)} custom-call(bf16[8,64,1792]{2,1,0:T(8,128)(2,1)} %pad_maximum_fusion.3.x_ref), custom_call_target="tpu_custom_call" | custom-call | tf_op jit(solution)/shard_map/pallas_call | solution.py:474
  69.6 1.1 convert_element_type.200
  71.9 23.6 %shard_map.221 = bf16[32,16,128]{2,1,0:T(8,128)(2,1)} custom-call(bf16[32,16,128]{2,1,0:T(8,128)(2,1)} %broadcast_in_dim.27.x_ref), custom_call_target="tpu_custom_call" | custom-call | tf_op jit(solution)/shard_map/pallas_call | solution.py:474
  97.4 85.1 %shard_map.220 = bf16[2048,2048]{1,0:T(8,128)(2,1)} custom-call(bf16[256,2048]{1,0:T(8,128)(2,1)} %x_ref.2), custom_call_target="tpu_custom_call" | custom-call | tf_op jit(solution)/shard_map/pallas_call | solution.py:348
  182.5 4.7 convert_reduce_fusion
  188.3 2.3 fusion.2
  192.4 1.4 copy.100.segq_ref
  193.7 87.9 %shard_map.225 = bf16[2048,2048]{1,0:T(8,128)(2,1)} custom-call(bf16[256,2048]{1,0:T(8,128)(2,1)} %x_ref.3), custom_call_target="tpu_custom_call" | custom-call | tf_op jit(solution)/shard_map/pallas_call | solution.py:348
  281.7 6.0 convolution_convert_fusion.2
  287.7 1.8 copy.102
  289.5 23.4 %convolution_add_fusion = f32[2048,1792]{0,1:T(8,128)} fusion(bf16[2048,1792]{1,0:T(8,128)(2,1)} %all-gather.4.cloned.1.call-done, f32[1792]{0:T(1024)S(1)} %maximum_convert_fusion, bf16[2048,2048]{1,0:T(8,128)(2,1)} %shard_map.220, f32[2048]{0:T(1024)S(1)} %reshape.299, f32[2048]{0:T(1024)S(1)} %reshape.298, f32[2048]{0:T(1024)S(1)} %add_rsqrt_fusion, ...), kind=kOutput, calls=%fused_computation.10 | convolution fusion | flops 15061221376 | bytes 30448640 | tf_op jit(solution)/shard_map/dot_general | solution.py:627
  312.9 1.7 slice.195
  314.6 3.9 fusion.34
  320.4 3.6 copy.112
  324.0 3.5 copy.113
  327.6 2.1 slice.196
  329.7 2.3 fusion.35
  331.9 3.5 copy.115
  335.5 3.6 copy.116
  339.1 2.6 copy.114
  341.7 2.6 copy.117
  344.3 1.8 copy.99
  346.1 7.2 subtract_convert_fusion.2
  353.3 5.2 maximum_bitcast_fusion
  358.5 74.4 %shard_map.223 = (f32[4,2048,64]{2,1,0:T(8,128)}, f32[4,2048,1]{2,1,0:T(8,128)}) custom-call(bf16[4,2048,64]{2,1,0:T(8,128)(2,1)} %get-tuple-element.60.q_ref, bf16[4,2048,64]{2,1,0:T(8,128)(2,1)} %get-tuple-element.61.k_ref, bf16[4,2048,64]{2,1,0:T(8,128)(2,1)} %bitcast.117, s32[2048,1]{1,0:T(8,128)} %copy.100.segq_ref, s32[1,2048]{1,0:T(1,128)} %bitcast.131), custom_call_target="tpu_custom_call" | custom-call | flops 2147483648 | bytes 5242880 | tf_op jit(solution)/shard_map/pallas_call | solution.py:145
  432.9 6.7 multiply_reduce_fusion
  439.6 1.9 copy.101
  441.5 7.1 fusion.38
  448.7 2.6 copy.103.delta_ref
  451.3 16.0 %convolution_convert_fusion.1 = bf16[1024,2048]{1,0:T(8,128)(2,1)} fusion(bf16[2048,2048]{1,0:T(8,128)(2,1)} %shard_map.225, f32[2048,1792]{0,1:T(8,128)} %convolution_add_fusion), kind=kOutput, calls=%fused_computation.35 | convolution fusion | flops 8610906112 | bytes 20971520 | tf_op jit(solution)/shard_map/tf,td->fd/dot_general | solution.py:655
  467.4 62.0 %shard_map.226 = (f32[4,2048,64]{2,1,0:T(8,128)}, f32[4,2048,64]{2,1,0:T(8,128)}, f32[4,2048,64]{2,1,0:T(8,128)}) custom-call(bf16[4,2048,64]{2,1,0:T(8,128)(2,1)} %get-tuple-element.60.q_ref, bf16[4,2048,64]{2,1,0:T(8,128)(2,1)} %get-tuple-element.61.k_ref, bf16[4,2048,64]{2,1,0:T(8,128)(2,1)} %bitcast.118, bf16[4,2048,64]{2,1,0:T(8,128)(2,1)} %bitcast.92, ...), custom_call_target="tpu_custom_call" | custom-call | flops 5368709120 | bytes 12582912 | tf_op jit(solution)/shard_map/pallas_call | solution.py:218
  529.3 2.9 slice.194
  532.8 1.9 slice.193
  534.7 4.3 add_convert_fusion.1
  539.0 3.2 pad_maximum_fusion.1
  542.2 2.7 copy.105
  544.9 5.4 pad_maximum_fusion.2
  550.4 2.7 copy.106
  553.0 2.5 convert_bitcast_fusion
  555.5 1.6 copy.107
  557.1 18.4 %convert_reduce_fusion.1 = (f32[1024]{0:T(1024)S(1)}, bf16[2048,1024]{0,1:T(8,128)(2,1)}) fusion(f32[2048,1792]{0,1:T(8,128)} %convolution_add_fusion, bf16[2048,2048]{1,0:T(8,128)(2,1)} %shard_map.225, bf16[1024,2048]{1,0:T(8,128)(2,1)} %all-gather.8.cloned.1.call-done), kind=kOutput, calls=%fused_computation.19 | convolution fusion | flops 8633973760 | bytes 25169920 | tf_op jit(solution)/shard_map/td,fd->tf/dot_general | solution.py:656
  575.5 28.6 %convolution_convert_fusion = bf16[2048,1792]{1,0:T(8,128)(2,1)} fusion(bf16[2048,1024]{0,1:T(8,128)(2,1)} %get-tuple-element.59, bf16[2048,256]{0,1:T(8,128)(2,1)} %bitcast.107, bf16[2048,256]{0,1:T(8,128)(2,1)S(1)} %bitcast.105, bf16[2048,256]{0,1:T(8,128)(2,1)S(1)} %bitcast.101, bf16[2048,2048]{1,0:T(8,128)(2,1)} %shard_map.220, f32[2048]{0:T(1024)S(1)} %reshape.299, ...), kind=kOutput, calls=%fused_computation.21 | convolution fusion | flops 15090581504 | bytes 23101440 | tf_op jit(solution)/shard_map/td,tc->dc/dot_general | solution.py:686
  606.0 1.8 convert_reduce_fusion.2
  607.9 14.8 %fusion.31 = f32[2048,2048]{1,0:T(8,128)S(1)} fusion(bf16[1024,2048]{1,0:T(8,128)(2,1)} %all-gather.8.cloned.1.call-done, f32[2048,1792]{0,1:T(8,128)} %convolution_add_fusion), kind=kOutput, calls=%fused_computation.104 | convolution fusion | flops 8608808960 | bytes 29360128 | tf_op jit(solution)/shard_map/dot_general | solution.py:646
  622.7 10.4 %convolution_add_fusion.1.p_ref = f32[2048,2048]{1,0:T(8,128)} fusion(f32[2048,2048]{1,0:T(8,128)S(1)} %fusion.31, bf16[2048,256]{0,1:T(8,128)(2,1)S(1)} %bitcast.95, bf16[256,2048]{1,0:T(8,128)(2,1)} %all-gather.6.cloned.1.call-done), kind=kOutput, calls=%fused_computation.11 | convolution fusion | flops 2151677952 | bytes 35651584 | tf_op jit(solution)/shard_map/dot_general | solution.py:645
  633.1 84.4 %shard_map.224 = f32[256,2048]{1,0:T(8,128)} custom-call(f32[2048,2048]{1,0:T(8,128)} %convolution_add_fusion.1.p_ref), custom_call_target="tpu_custom_call" | custom-call | tf_op jit(solution)/shard_map/pallas_call | solution.py:411
  717.5 21.9 %fusion.27.p_ref = f32[2048,2048]{1,0:T(8,128)} fusion(bf16[2048,1792]{1,0:T(8,128)(2,1)} %all-gather.4.cloned.1.call-done, bf16[2048,1024]{0,1:T(8,128)(2,1)} %get-tuple-element.59, bf16[2048,256]{0,1:T(8,128)(2,1)} %bitcast.109, bf16[2048,256]{0,1:T(8,128)(2,1)S(1)} %bitcast.106, bf16[2048,256]{0,1:T(8,128)(2,1)S(1)} %bitcast.103), kind=kOutput, calls=%fused_computation.65 | convolution fusion | flops 15061745664 | bytes 31457280 | tf_op jit(solution)/shard_map/tc,dc->td/dot_general | solution.py:682
  739.4 90.9 %shard_map.227 = f32[256,2048]{1,0:T(8,128)} custom-call(f32[2048,2048]{1,0:T(8,128)} %fusion.27.p_ref), custom_call_target="tpu_custom_call" | custom-call | tf_op jit(solution)/shard_map/pallas_call | solution.py:411
  830.3 2.7 fusion.21
  833.1 4.2 convert_reduce_fusion.4
  838.3 16.9 %shard_map.229 = f32[32,16,128]{2,1,0:T(8,128)} custom-call(f32[32,16,128]{2,1,0:T(8,128)} %bitcast.123), custom_call_target="tpu_custom_call" | custom-call | tf_op jit(solution)/shard_map/pallas_call | solution.py:474
  856.3 1.7 collective-permute-start.1
  859.7 2.8 convert_element_type.223
  862.5 67.8 %shard_map.228 = bf16[8,64,1792]{2,1,0:T(8,128)(2,1)} custom-call(bf16[8,64,1792]{2,1,0:T(8,128)(2,1)} %bitcast.120), custom_call_target="tpu_custom_call" | custom-call | tf_op jit(solution)/shard_map/pallas_call | solution.py:474
  930.3 1.5 slice_convert_fusion.5
  931.8 2.4 slice_convert_fusion.6
  934.2 2.0 reshape.305
  936.2 2.8 copy.110
  939.0 2.5 copy.124
  941.5 2.6 reshape.304
  945.0 1.6 copy.122
  (140 shorter events, 21.9 us)
Async XLA Ops:
  7.2 274.5 %all-gather.6.cloned.1.call-start = ((), (), s32[]{:S(2)}) async-start(), calls=%async_computation.4 | async-start | bytes 1310720 | tf_op jit(solution)/shard_map/all_gather | solution.py:497
  8.3 0.7 collective-permute-start
  9.0 0.7 copy-start.13
  9.7 279.7 %all-gather.4.cloned.1.call-start = ((), (), s32[]{:S(2)}) async-start(), calls=%async_computation.3 | async-start | bytes 9175040 | tf_op jit(solution)/shard_map/all_gather | solution.py:552
  17.3 52.3 %copy-start.12 = (f32[256,2048]{1,0:T(8,128)S(1)}, f32[256,2048]{1,0:T(8,128)}, u32[]{:S(2)}) copy-start(f32[256,2048]{1,0:T(8,128)} %param.21) | copy-start | bytes 6291460
  17.3 53.7 %copy-start.18 = (f32[192]{0:T(256)S(1)}, f32[192]{0:T(256)}, u32[]{:S(2)}) copy-start(f32[192]{0:T(256)} %param.16) | copy-start | bytes 2308
  17.3 53.7 %copy-start.20 = (f32[64]{0:T(128)S(1)}, f32[64]{0:T(128)}, u32[]{:S(2)}) copy-start(f32[64]{0:T(128)} %param.18) | copy-start | bytes 772
  17.3 53.7 %copy-start.21 = (f32[64]{0:T(128)S(1)}, f32[64]{0:T(128)}, u32[]{:S(2)}) copy-start(f32[64]{0:T(128)} %param.22) | copy-start | bytes 772
  17.3 53.7 %copy-start.22 = (f32[64]{0:T(128)S(1)}, f32[64]{0:T(128)}, u32[]{:S(2)}) copy-start(f32[64]{0:T(128)} %param.23) | copy-start | bytes 772
  17.3 53.7 %copy-start.23 = (f32[64]{0:T(128)S(1)}, f32[64]{0:T(128)}, u32[]{:S(2)}) copy-start(f32[64]{0:T(128)} %param.24) | copy-start | bytes 772
  17.3 53.7 %copy-start.19 = (f32[256]{0:T(256)S(1)}, f32[256]{0:T(256)}, u32[]{:S(2)}) copy-start(f32[256]{0:T(256)} %param.20) | copy-start | bytes 3076
  69.5 487.6 %all-gather.8.cloned.1.call-start = ((), (), s32[]{:S(2)}) async-start(), calls=%async_computation.5 | async-start | bytes 5242880 | tf_op jit(solution)/shard_map/all_gather | solution.py:553
  70.7 785.5 %reduce-scatter.6.cloned.1.call-start = ((), (), s32[]{:S(2)}) async-start(), calls=%async_computation.7 | async-start | bytes 2621440 | tf_op jit(solution)/shard_map/reduce_scatter | solution.py:503
  182.5 5.8 copy-start
  188.3 2.5 copy-start.24
  191.0 90.6 %copy-start.14 = (s32[2048]{0:T(1024)}, s32[2048]{0:T(1024)S(1)}, u32[]{:S(2)}) copy-start(s32[2048]{0:T(1024)S(1)} %convert_reduce_fusion.5) | copy-start | bytes 24580
  346.1 7.2 copy-start.7
  346.1 7.2 copy-start.8
  448.6 411.1 %reduce-scatter.8.cloned.1.call-start = ((), (), s32[]{:S(2)}) async-start(), calls=%async_computation.8 | async-start | bytes 5242880 | tf_op jit(solution)/shard_map/reduce_scatter | solution.py:691
  467.3 395.2 %reduce-scatter.4.cloned.1.call-start = ((), (), s32[]{:S(2)}) async-start(), calls=%async_computation.6 | async-start | bytes 9175040 | tf_op jit(solution)/shard_map/reduce_scatter | solution.py:689
  529.3 3.5 copy-start.2
  529.3 5.4 copy-start.1
  539.0 5.9 copy-start.6
  557.1 18.4 %copy-start.9 = (bf16[2048,4,64]{0,2,1:T(8,128)(2,1)S(1)}, bf16[2048,4,64]{0,2,1:T(8,128)(2,1)}, u32[]{:S(2)}) copy-start(bf16[2048,4,64]{0,2,1:T(8,128)(2,1)} %copy.105) | copy-start | bytes 3145732
  557.1 18.4 %copy-start.10 = (bf16[2048,4,64]{0,2,1:T(8,128)(2,1)S(1)}, bf16[2048,4,64]{0,2,1:T(8,128)(2,1)}, u32[]{:S(2)}) copy-start(bf16[2048,4,64]{0,2,1:T(8,128)(2,1)} %copy.106) | copy-start | bytes 3145732
  604.1 0.7 copy-start.16
  604.1 0.8 copy-start.15
  604.1 1.2 copy-start.3
  633.1 84.4 %copy-start.11 = (bf16[2048,4,64]{0,2,1:T(8,128)(2,1)S(1)}, bf16[2048,4,64]{0,2,1:T(8,128)(2,1)}, u32[]{:S(2)}) copy-start(bf16[2048,4,64]{0,2,1:T(8,128)(2,1)} %copy.106) | copy-start | bytes 3145732
  739.4 93.7 %copy-start.5 = (f32[256,2048]{1,0:T(8,128)S(1)}, f32[256,2048]{1,0:T(8,128)}, u32[]{:S(2)}) copy-start(f32[256,2048]{1,0:T(8,128)} %shard_map.224) | copy-start | bytes 6291460
  830.3 2.7 copy-start.4
  856.3 3.4 collective-permute-start.1
  859.1 87.5 %copy-start.17 = (f32[64]{0:T(128)}, f32[64]{0:T(128)S(1)}, u32[]{:S(2)}) copy-start(f32[64]{0:T(128)S(1)} %get-tuple-element.103) | copy-start | bytes 772
Sparse Core Ops, SparseCore 0:
  10.1 34.0 all-gather.5
  69.7 65.1 all-gather.3
  137.0 34.5 all-gather.7
  448.7 32.3 reduce-scatter.5
  483.6 44.5 reduce-scatter.7
  604.2 66.1 reduce-scatter.3

commit v5 on v4

--- a/solution.py
+++ b/solution.py
@@ -425,17 +425,19 @@
     )(p)
 
 
-def _exchange_kernel(x_ref, out_ref, own_sem, send_sem, recv_sem, *, everyone):
+def _exchange_kernel(x_ref, out_ref, own_sem, send_sem, recv_sem, *, group):
     n = x_ref.shape[0]
     g = lax.axis_index("dp")
     c = lax.axis_index("ctx")
     n_ctx = lax.axis_size("ctx")
-    me = g * n_ctx + c if everyone else c
+    me = {"all": g * n_ctx + c, "ctx": c, "dp": g}[group]
 
     def address(member):
-        if everyone:
+        if group == "all":
             return (member // n_ctx, member % n_ctx)
-        return (g, member)
+        if group == "ctx":
+            return (g, member)
+        return (member, c)
 
     own = pltpu.make_async_copy(x_ref.at[me], out_ref.at[me], own_sem)
     own.start()
@@ -468,11 +470,11 @@
     own.wait()
 
 
-def exchange(x, everyone, collective_id):
+def exchange(x, group, collective_id):
     n = x.shape[0]
     space = pltpu.VMEM
     return pl.pallas_call(
-        functools.partial(_exchange_kernel, everyone=everyone),
+        functools.partial(_exchange_kernel, group=group),
         out_shape=jax.ShapeDtypeStruct(x.shape, x.dtype),
         in_specs=[pl.BlockSpec(memory_space=space)],
         out_specs=pl.BlockSpec(memory_space=space),
@@ -513,10 +515,12 @@
 
 def fetch_small(b_qkv, b_out, b_fc2, ln_gain, ln_shift, b_fc1):
     pieces = (b_qkv, b_out, b_fc2, ln_gain, ln_shift, b_fc1)
-    count = lax.axis_size("dp") * lax.axis_size("ctx")
+    n_dp = lax.axis_size("dp")
+    n_ctx = lax.axis_size("ctx")
     packed = pack_rows(jnp.concatenate([p.astype(jnp.bfloat16) for p in pieces]), 128)
-    table = exchange(jnp.broadcast_to(packed[None], (count,) + packed.shape), True, 4)
-    table = table.reshape(count, -1)
+    over_dp = exchange(jnp.broadcast_to(packed[None], (n_dp,) + packed.shape), "dp", 4)
+    over_all = exchange(jnp.broadcast_to(over_dp[None], (n_ctx,) + over_dp.shape), "ctx", 8)
+    table = over_all.transpose(1, 0, 2, 3).reshape(n_dp * n_ctx, -1)
     result = []
     offset = 0
     for p in pieces:
@@ -526,10 +530,14 @@
 
 
 def reduce_small(small):
+    n_dp = lax.axis_size("dp")
+    n_ctx = lax.axis_size("ctx")
     count, width = small.shape
     packed = jax.vmap(lambda row: pack_rows(row, 128))(small)
-    received = exchange(packed, True, 7)
-    return jnp.sum(received, axis=0).reshape(-1)[:width]
+    packed = packed.reshape((n_dp, n_ctx) + packed.shape[1:]).transpose(1, 0, 2, 3)
+    over_ctx = jnp.sum(exchange(packed, "ctx", 7), axis=0)
+    over_dp = jnp.sum(exchange(over_ctx, "dp", 9), axis=0)
+    return over_dp.reshape(-1)[:width]
 
 
 def fetch_heads(w_qkv, w_fc1, w_fc2):
@@ -547,7 +555,7 @@
         ],
         axis=2,
     )
-    sent = exchange(pieces, False, 5).reshape(ctx_count * rows_piece, -1)
+    sent = exchange(pieces, "ctx", 5).reshape(ctx_count * rows_piece, -1)
     cols, fc2_rows = (
         lax.all_gather(sent, "dp", axis=0, tiled=True),
         lax.all_gather(w_fc2.astype(jnp.bfloat16), "dp", axis=0, tiled=True),
@@ -561,7 +569,7 @@
     head_width = D // ctx_count
     unit = FF // (dp_count * ctx_count)
     rows_piece = owned_parts.shape[0] // ctx_count
-    got = exchange(owned_parts.reshape(ctx_count, rows_piece, -1), False, 6)
+    got = exchange(owned_parts.reshape(ctx_count, rows_piece, -1), "ctx", 6)
     qkv = got[:, :, : 3 * head_width].reshape(ctx_count, rows_piece, 3, head_width)
     fc1 = got[:, :, 3 * head_width :].reshape(ctx_count, rows_piece, dp_count, unit)
     return (
@@ -617,7 +625,7 @@
     inputs = tokens.astype(jnp.float32)
     normed, scaled, _ = norm_parts(inputs, gain32, shift32)
     tokens_group = ring_all_gather(tokens, ring, 0)
-    dy_group = ring_all_gather(cotangent, ring, 1)
+    dy_group = lax.all_gather(cotangent, "ctx", axis=0, tiled=True)
     hidden_group = norm_parts(tokens_group.astype(jnp.float32), gain32, shift32)[2].astype(
         jnp.bfloat16
     )

time: 970 us -> 926 us (0.955)
  Pallas kernels: 645 us -> 590 us
    pallas_call x2 -> x1, Pallas kernels: 173 us -> 117 us  [ring_all_gather(): pl.pallas_call(functools.partial(_gather_kernel, ring=ring, rows=rows), o...]
    pallas_call x4 -> x6, Pallas kernels: 160 us -> 157 us  [exchange(): pl.pallas_call(functools.partial(_exchange_kernel, group=group), out_shap...]
    unnamed x66 -> x72, local copies, waits for them, and re-layouts: 30.5 us -> 30.1 us
  transfers between devices with their start and end apart: 8 -> 9, of which waited for: 0 -> 0; matrix products, arithmetic and copies ran while one was open for 28% -> 30% of each run, Pallas kernels for 60% -> 53%
where the time goes in v5:
time: 926 us; the launch traced here: 911 us
  Pallas kernels  590 us (64%)
  matrix products  155 us (17%)
  local copies, waits for them, and re-layouts  80.6 us (9%)
  other arithmetic  66.8 us (7%)
  between operations  15.1 us (2%)
    pallas_call x2, Pallas kernels, ring_reduce_scatter(): pl.pallas_call(functools.partial(_scatter_kernel, ring=ring, rows=rows),...  179 us
    pallas_call x6, Pallas kernels, exchange(): pl.pallas_call(functools.partial(_exchange_kernel, group=group), out_shap...  157 us
    pallas_call x1, Pallas kernels, ring_all_gather(): pl.pallas_call(functools.partial(_gather_kernel, ring=ring, rows=rows), o...  117 us
    pallas_call x1, Pallas kernels, attention_forward(): pl.pallas_call(functools.partial(_fwd_kernel, tq=tq, tk=tk, scale=scale),...  74.1 us
    pallas_call x1, Pallas kernels, attention_backward(): pl.pallas_call(functools.partial(_bwd_kernel, tq=tq, tk=tk, scale=scale),...  61.9 us
    unnamed x72, local copies, waits for them, and re-layouts  30.1 us
    dot_general x1, matrix products, head_plan(): jnp.einsum('td,tc->dc', hidden_group, d_both, preferred_element_type=jnp....  28.5 us
    dot_general x1, matrix products, head_plan(): jnp.dot(hidden_group, cols, preferred_element_type=jnp.float32)  23.3 us
  transfers between devices with their start and end apart: 9, of which 0 were waited for; matrix products, arithmetic and copies ran while one was open for 30% of the time, Pallas kernels for 53%

profile of v5, /device:TPU:0, one launch (start us, length us, event | category | flops | bytes accessed | tf_op | source)
XLA Modules:
  0.0 910.5 jit_solution(525860219545464018)
XLA Ops:
  7.2 1.7 convert_element_type.190
  10.4 1.5 convert_element_type.189
  13.4 1.4 pad_maximum_fusion.3.x_ref
  14.8 38.8 %shard_map.223 = bf16[8,64,1792]{2,1,0:T(8,128)(2,1)} custom-call(bf16[8,64,1792]{2,1,0:T(8,128)(2,1)} %pad_maximum_fusion.3.x_ref), custom_call_target="tpu_custom_call" | custom-call | tf_op jit(solution)/shard_map/pallas_call | solution.py:476
  58.2 25.9 %shard_map.221 = bf16[4,16,128]{2,1,0:T(8,128)(2,1)} custom-call(bf16[4,16,128]{2,1,0:T(8,128)(2,1)} %broadcast_in_dim.29.x_ref), custom_call_target="tpu_custom_call" | custom-call | tf_op jit(solution)/shard_map/pallas_call | solution.py:476
  84.1 1.4 broadcast_in_dim.30.x_ref
  85.5 10.4 %shard_map.222 = bf16[8,4,16,128]{3,2,1,0:T(8,128)(2,1)} custom-call(bf16[8,4,16,128]{3,2,1,0:T(8,128)(2,1)} %broadcast_in_dim.30.x_ref), custom_call_target="tpu_custom_call" | custom-call | tf_op jit(solution)/shard_map/pallas_call | solution.py:476
  97.8 117.2 %shard_map.220 = bf16[2048,2048]{1,0:T(8,128)(2,1)} custom-call(bf16[256,2048]{1,0:T(8,128)(2,1)} %x_ref.1), custom_call_target="tpu_custom_call" | custom-call | tf_op jit(solution)/shard_map/pallas_call | solution.py:348
  215.1 5.5 convert_reduce_fusion
  221.9 2.3 fusion.2
  227.3 23.3 %convolution_add_fusion = f32[2048,1792]{0,1:T(8,128)} fusion(bf16[2048,1792]{1,0:T(8,128)(2,1)} %all-gather.5.cloned.1.call-done, f32[1792]{0:T(1024)S(1)} %maximum_convert_fusion, bf16[2048,2048]{1,0:T(8,128)(2,1)} %shard_map.220, f32[2048]{0:T(1024)S(1)} %reshape.300, f32[2048]{0:T(1024)S(1)} %reshape.299, f32[2048]{0:T(1024)S(1)} %add_rsqrt_fusion, ...), kind=kOutput, calls=%fused_computation.10 | convolution fusion | flops 15061221376 | bytes 30448640 | tf_op jit(solution)/shard_map/dot_general | solution.py:635
  250.7 1.7 slice.195
  252.4 3.9 fusion.34
  258.2 3.5 copy.125
  261.8 3.5 copy.126
  265.3 2.2 slice.196
  267.5 2.3 fusion.35
  269.7 3.5 copy.128
  273.2 3.9 copy.129
  277.1 2.6 copy.127
  279.7 2.6 copy.130
  282.4 1.7 copy.110
  284.1 7.2 subtract_convert_fusion.2
  291.3 5.2 maximum_bitcast_fusion
  296.5 74.1 %shard_map.224 = (f32[4,2048,64]{2,1,0:T(8,128)}, f32[4,2048,1]{2,1,0:T(8,128)}) custom-call(bf16[4,2048,64]{2,1,0:T(8,128)(2,1)} %get-tuple-element.60.q_ref, bf16[4,2048,64]{2,1,0:T(8,128)(2,1)} %get-tuple-element.61.k_ref, bf16[4,2048,64]{2,1,0:T(8,128)(2,1)} %bitcast.127, s32[2048,1]{1,0:T(8,128)} %copy.111.segq_ref, s32[1,2048]{1,0:T(1,128)} %bitcast.139), custom_call_target="tpu_custom_call" | custom-call | flops 2147483648 | bytes 5242880 | tf_op jit(solution)/shard_map/pallas_call | solution.py:145
  370.6 6.0 convolution_convert_fusion.2
  376.6 1.8 copy.113
  378.4 6.8 multiply_reduce_fusion
  385.2 1.9 copy.112
  387.1 7.1 fusion.38
  394.2 2.9 copy.114.delta_ref
  397.1 16.5 %convolution_convert_fusion.1 = bf16[1024,2048]{1,0:T(8,128)(2,1)} fusion(bf16[2048,2048]{1,0:T(8,128)(2,1)} %all-gather.11.cloned.1.call-done, f32[2048,1792]{0,1:T(8,128)} %convolution_add_fusion), kind=kOutput, calls=%fused_computation.35 | convolution fusion | flops 8610906112 | bytes 20971520 | tf_op jit(solution)/shard_map/tf,td->fd/dot_general | solution.py:663
  413.7 61.9 %shard_map.226 = (f32[4,2048,64]{2,1,0:T(8,128)}, f32[4,2048,64]{2,1,0:T(8,128)}, f32[4,2048,64]{2,1,0:T(8,128)}) custom-call(bf16[4,2048,64]{2,1,0:T(8,128)(2,1)} %get-tuple-element.60.q_ref, bf16[4,2048,64]{2,1,0:T(8,128)(2,1)} %get-tuple-element.61.k_ref, bf16[4,2048,64]{2,1,0:T(8,128)(2,1)} %bitcast.128, bf16[4,2048,64]{2,1,0:T(8,128)(2,1)} %bitcast.102, ...), custom_call_target="tpu_custom_call" | custom-call | flops 5368709120 | bytes 12582912 | tf_op jit(solution)/shard_map/pallas_call | solution.py:218
  475.6 2.9 slice.194
  479.0 1.9 slice.193
  480.9 4.3 add_convert_fusion.1
  485.2 3.2 pad_maximum_fusion.1
  488.4 2.7 copy.116
  491.2 5.4 pad_maximum_fusion.2
  496.6 2.7 copy.117
  499.3 2.5 convert_bitcast_fusion
  501.7 1.6 copy.118
  503.4 18.3 %convert_reduce_fusion.1 = (f32[1024]{0:T(1024)S(1)}, bf16[2048,1024]{0,1:T(8,128)(2,1)}) fusion(f32[2048,1792]{0,1:T(8,128)} %convolution_add_fusion, bf16[2048,2048]{1,0:T(8,128)(2,1)} %all-gather.11.cloned.1.call-done, bf16[1024,2048]{1,0:T(8,128)(2,1)} %all-gather.9.cloned.1.call-done), kind=kOutput, calls=%fused_computation.19 | convolution fusion | flops 8633973760 | bytes 25169920 | tf_op jit(solution)/shard_map/td,fd->tf/dot_general | solution.py:664
  521.7 28.5 %convolution_convert_fusion = bf16[2048,1792]{1,0:T(8,128)(2,1)} fusion(bf16[2048,1024]{0,1:T(8,128)(2,1)} %get-tuple-element.59, bf16[2048,256]{0,1:T(8,128)(2,1)} %bitcast.117, bf16[2048,256]{0,1:T(8,128)(2,1)S(1)} %bitcast.114, bf16[2048,256]{0,1:T(8,128)(2,1)S(1)} %bitcast.111, bf16[2048,2048]{1,0:T(8,128)(2,1)} %shard_map.220, f32[2048]{0:T(1024)S(1)} %reshape.300, ...), kind=kOutput, calls=%fused_computation.21 | convolution fusion | flops 15090581504 | bytes 23101440 | tf_op jit(solution)/shard_map/td,tc->dc/dot_general | solution.py:694
  552.2 18.3 %fusion.31 = f32[2048,2048]{1,0:T(8,128)} fusion(bf16[1024,2048]{1,0:T(8,128)(2,1)} %all-gather.9.cloned.1.call-done, f32[2048,1792]{0,1:T(8,128)} %convolution_add_fusion), kind=kOutput, calls=%fused_computation.107 | convolution fusion | flops 8608808960 | bytes 29360128 | tf_op jit(solution)/shard_map/dot_general | solution.py:654
  571.1 14.7 %convolution_add_fusion.1.p_ref = f32[2048,2048]{1,0:T(8,128)} fusion(f32[2048,2048]{1,0:T(8,128)} %fusion.31, bf16[2048,256]{0,1:T(8,128)(2,1)S(1)} %bitcast.105, bf16[256,2048]{1,0:T(8,128)(2,1)} %all-gather.7.cloned.1.call-done), kind=kOutput, calls=%fused_computation.11 | convolution fusion | flops 2151677952 | bytes 35651584 | tf_op jit(solution)/shard_map/dot_general | solution.py:653
  585.8 94.9 %shard_map.225 = f32[256,2048]{1,0:T(8,128)} custom-call(f32[2048,2048]{1,0:T(8,128)} %convolution_add_fusion.1.p_ref), custom_call_target="tpu_custom_call" | custom-call | tf_op jit(solution)/shard_map/pallas_call | solution.py:411
  680.8 22.0 %fusion.27.p_ref = f32[2048,2048]{1,0:T(8,128)} fusion(bf16[2048,1792]{1,0:T(8,128)(2,1)} %all-gather.5.cloned.1.call-done, bf16[2048,1024]{0,1:T(8,128)(2,1)} %get-tuple-element.59, bf16[2048,256]{0,1:T(8,128)(2,1)} %bitcast.118, bf16[2048,256]{0,1:T(8,128)(2,1)S(1)} %bitcast.116, bf16[2048,256]{0,1:T(8,128)(2,1)S(1)} %bitcast.113), kind=kOutput, calls=%fused_computation.65 | convolution fusion | flops 15061745664 | bytes 31457280 | tf_op jit(solution)/shard_map/tc,dc->td/dot_general | solution.py:690
  702.7 84.5 %shard_map.227 = f32[256,2048]{1,0:T(8,128)} custom-call(f32[2048,2048]{1,0:T(8,128)} %fusion.27.p_ref), custom_call_target="tpu_custom_call" | custom-call | tf_op jit(solution)/shard_map/pallas_call | solution.py:411
  787.2 2.7 fusion.21
  790.0 4.2 convert_reduce_fusion.4
  795.3 8.6 shard_map.229
  803.9 1.6 reduce_sum.158.x_ref
  805.5 5.1 shard_map.230
  811.4 1.7 collective-permute-start.1
  814.8 2.8 convert_element_type.223
  817.6 68.2 %shard_map.228 = bf16[8,64,1792]{2,1,0:T(8,128)(2,1)} custom-call(bf16[8,64,1792]{2,1,0:T(8,128)(2,1)} %bitcast.130), custom_call_target="tpu_custom_call" | custom-call | tf_op jit(solution)/shard_map/pallas_call | solution.py:476
  885.8 1.5 slice_convert_fusion.5
  887.2 2.4 slice_convert_fusion.6
  889.7 2.0 reshape.306
  891.6 2.8 copy.122
  894.4 2.5 copy.137
  897.0 2.6 reshape.305
  900.5 1.6 copy.135
  (153 shorter events, 24.5 us)
Async XLA Ops:
  7.2 220.2 %all-gather.5.cloned.1.call-start = ((), (), s32[]{:S(2)}) async-start(), calls=%async_computation.3 | async-start | bytes 9175040 | tf_op jit(solution)/shard_map/all_gather | solution.py:560
  13.4 40.3 %copy-start.15 = (f32[64,2048]{1,0:T(8,128)S(1)}, f32[64,2048]{1,0:T(8,128)}, u32[]{:S(2)}) copy-start(f32[64,2048]{1,0:T(8,128)} %param.17) | copy-start | bytes 1572868
  14.8 41.2 %copy-start.14 = (f32[256,2048]{1,0:T(8,128)S(1)}, f32[256,2048]{1,0:T(8,128)}, u32[]{:S(2)}) copy-start(f32[256,2048]{1,0:T(8,128)} %param.21) | copy-start | bytes 6291460
  53.6 3.8 copy-start.21
  53.6 3.8 copy-start.23
  53.6 3.8 copy-start.24
  53.6 3.8 copy-start.25
  53.6 3.8 copy-start.26
  53.6 3.8 copy-start.22
  53.7 316.9 %all-gather.7.cloned.1.call-start = ((), (), s32[]{:S(2)}) async-start(), calls=%async_computation.4 | async-start | bytes 1310720 | tf_op jit(solution)/shard_map/all_gather | solution.py:499
  53.8 0.7 collective-permute-start
  54.5 0.7 copy-start.16
  55.2 315.4 %all-gather.11.cloned.1.call-start = ((), (), s32[]{:S(2)}) async-start(), calls=%async_computation.6 | async-start | bytes 9437184 | tf_op jit(solution)/shard_map/all_gather | solution.py:628
  56.0 447.4 %all-gather.9.cloned.1.call-start = ((), (), s32[]{:S(2)}) async-start(), calls=%async_computation.5 | async-start | bytes 5242880 | tf_op jit(solution)/shard_map/all_gather | solution.py:561
  57.1 754.2 %reduce-scatter.6.cloned.1.call-start = ((), (), s32[]{:S(2)}) async-start(), calls=%async_computation.8 | async-start | bytes 2621440 | tf_op jit(solution)/shard_map/reduce_scatter | solution.py:505
  215.1 6.8 copy-start
  221.9 2.5 copy-start.27
  224.7 26.0 %copy-start.17 = (s32[2048]{0:T(1024)}, s32[2048]{0:T(1024)S(1)}, u32[]{:S(2)}) copy-start(s32[2048]{0:T(1024)S(1)} %convert_reduce_fusion.5) | copy-start | bytes 24580
  284.1 7.2 copy-start.7
  284.1 7.2 copy-start.8
  394.2 420.6 %reduce-scatter.8.cloned.1.call-start = ((), (), s32[]{:S(2)}) async-start(), calls=%async_computation.9 | async-start | bytes 5242880 | tf_op jit(solution)/shard_map/reduce_scatter | solution.py:699
  413.7 403.9 %reduce-scatter.4.cloned.1.call-start = ((), (), s32[]{:S(2)}) async-start(), calls=%async_computation.7 | async-start | bytes 9175040 | tf_op jit(solution)/shard_map/reduce_scatter | solution.py:697
  475.6 3.5 copy-start.2
  475.6 5.4 copy-start.1
  485.2 5.9 copy-start.6
  503.4 18.3 %copy-start.9 = (bf16[2048,4,64]{0,2,1:T(8,128)(2,1)S(1)}, bf16[2048,4,64]{0,2,1:T(8,128)(2,1)}, u32[]{:S(2)}) copy-start(bf16[2048,4,64]{0,2,1:T(8,128)(2,1)} %copy.116) | copy-start | bytes 3145732
  503.4 18.3 %copy-start.10 = (bf16[2048,4,64]{0,2,1:T(8,128)(2,1)S(1)}, bf16[2048,4,64]{0,2,1:T(8,128)(2,1)}, u32[]{:S(2)}) copy-start(bf16[2048,4,64]{0,2,1:T(8,128)(2,1)} %copy.117) | copy-start | bytes 3145732
  550.2 0.7 copy-start.19
  550.2 0.8 copy-start.18
  550.2 1.2 copy-start.3
  552.1 18.3 %copy-start.11 = (bf16[2048,4,64]{0,2,1:T(8,128)(2,1)S(1)}, bf16[2048,4,64]{0,2,1:T(8,128)(2,1)}, u32[]{:S(2)}) copy-start(bf16[2048,4,64]{0,2,1:T(8,128)(2,1)} %copy.117) | copy-start | bytes 3145732
  552.1 18.3 %copy-start.13 = (bf16[2048,4,64]{0,2,1:T(8,128)(2,1)S(1)}, bf16[2048,4,64]{0,2,1:T(8,128)(2,1)}, u32[]{:S(2)}) copy-start(bf16[2048,4,64]{0,2,1:T(8,128)(2,1)} %copy.118) | copy-start | bytes 3145732
  585.8 94.9 %copy-start.12 = (bf16[2048,4,64]{0,2,1:T(8,128)(2,1)S(1)}, bf16[2048,4,64]{0,2,1:T(8,128)(2,1)}, u32[]{:S(2)}) copy-start(bf16[2048,4,64]{0,2,1:T(8,128)(2,1)} %copy.117) | copy-start | bytes 3145732
  702.7 87.2 %copy-start.5 = (f32[256,2048]{1,0:T(8,128)S(1)}, f32[256,2048]{1,0:T(8,128)}, u32[]{:S(2)}) copy-start(f32[256,2048]{1,0:T(8,128)} %shard_map.225) | copy-start | bytes 6291460
  787.2 2.7 copy-start.4
  811.4 3.4 collective-permute-start.1
  814.2 87.9 %copy-start.20 = (f32[64]{0:T(128)}, f32[64]{0:T(128)S(1)}, u32[]{:S(2)}) copy-start(f32[64]{0:T(128)S(1)} %get-tuple-element.103) | copy-start | bytes 772
Sparse Core Ops, SparseCore 0:
  53.8 63.3 all-gather.4
  118.7 16.7 all-gather.6
  137.6 153.2 all-gather.10
  292.9 32.7 all-gather.8
  394.3 30.4 reduce-scatter.5
  427.3 44.4 reduce-scatter.7
  550.4 63.4 reduce-scatter.3

commit v6 on v5

--- a/solution.py
+++ b/solution.py
@@ -649,11 +649,13 @@
     attended_heads, log_total = attention_forward(q_heads, k_heads, v_heads, seg)
     attended = attended_heads.transpose(1, 0, 2).reshape(group, head_width).astype(jnp.bfloat16)
     act = gelu_tanh(pre).astype(jnp.bfloat16)
-    branches = ring_reduce_scatter(
+    partial = (
         jnp.dot(attended, out_rows, preferred_element_type=jnp.float32)
-        + jnp.dot(act, fc2_rows, preferred_element_type=jnp.float32),
-        ring,
-        2,
+        + jnp.dot(act, fc2_rows, preferred_element_type=jnp.float32)
+    ).astype(jnp.bfloat16)
+    partial, q_heads = lax.optimization_barrier((partial, q_heads))
+    branches = lax.psum_scatter(partial, "ctx", scatter_dimension=0, tiled=True).astype(
+        jnp.float32
     )
     block_out = (
         inputs + branches + out_bias.astype(jnp.float32) + fc2_bias.astype(jnp.float32)
@@ -665,6 +667,9 @@
     d_pre = (d_act * gelu_slope(pre)).astype(jnp.bfloat16)
     grad_bfc1_part = jnp.sum(d_pre.astype(jnp.float32), axis=0)
     grad_out_rows = jnp.einsum("tc,td->cd", attended, dy_group, preferred_element_type=jnp.float32)
+    branches, grad_out_rows, grad_fc2_part = lax.optimization_barrier(
+        (branches, grad_out_rows, grad_fc2_part)
+    )
     owned_w_out = return_out_rows(grad_out_rows)
     d_attended = (
         jnp.einsum("td,cd->tc", dy_group, out_rows, preferred_element_type=jnp.float32)

time: 926 us -> 928 us (level); the launches traced: 911 us -> 923 us
  Pallas kernels: 590 us -> 610 us
    pallas_call x6, Pallas kernels: 157 us -> 179 us  [exchange(): pl.pallas_call(functools.partial(_exchange_kernel, group=group), out_shap...]
    unnamed x72 -> x70, local copies, waits for them, and re-layouts: 30.1 us -> 27.5 us
    pallas_call x2 -> x1, Pallas kernels: 179 us -> 178 us  [ring_reduce_scatter(): pl.pallas_call(functools.partial(_scatter_kernel, ring=ring, rows=rows),...]
  transfers between devices with their start and end apart: 9 -> 10, of which waited for: 0 -> 1; matrix products, arithmetic and copies ran while one was open for 30% -> 29% of each run, Pallas kernels for 53% -> 58%
where the time goes in v6:
time: 928 us; the launch traced here: 923 us
  Pallas kernels  610 us (66%)
  matrix products  150 us (16%)
  local copies, waits for them, and re-layouts  73.8 us (8%)
  other arithmetic  64.3 us (7%)
  between operations  15.2 us (2%)
    pallas_call x6, Pallas kernels, exchange(): pl.pallas_call(functools.partial(_exchange_kernel, group=group), out_shap...  179 us
    pallas_call x1, Pallas kernels, ring_reduce_scatter(): pl.pallas_call(functools.partial(_scatter_kernel, ring=ring, rows=rows),...  178 us
    pallas_call x1, Pallas kernels, ring_all_gather(): pl.pallas_call(functools.partial(_gather_kernel, ring=ring, rows=rows), o...  118 us
    pallas_call x1, Pallas kernels, attention_forward(): pl.pallas_call(functools.partial(_fwd_kernel, tq=tq, tk=tk, scale=scale),...  74.2 us
    pallas_call x1, Pallas kernels, attention_backward(): pl.pallas_call(functools.partial(_bwd_kernel, tq=tq, tk=tk, scale=scale),...  61.9 us
    dot_general x1, matrix products, head_plan(): jnp.einsum('td,tc->dc', hidden_group, d_both, preferred_element_type=jnp....  28.6 us
    unnamed x70, local copies, waits for them, and re-layouts  27.5 us
    dot_general x1, matrix products, head_plan(): jnp.dot(hidden_group, cols, preferred_element_type=jnp.float32)  23.3 us
  transfers between devices with their start and end apart: 10, of which 1 were waited for; matrix products, arithmetic and copies ran while one was open for 29% of the time, Pallas kernels for 58%

profile of v6, /device:TPU:0, one launch (start us, length us, event | category | flops | bytes accessed | tf_op | source)
XLA Modules:
  0.0 922.5 jit_solution(11605634495017835449)
XLA Ops:
  7.2 1.5 convert_element_type.195
  10.2 1.7 convert_element_type.196
  13.4 1.4 pad_maximum_fusion.3.x_ref
  14.8 38.8 %shard_map.223 = bf16[8,64,1792]{2,1,0:T(8,128)(2,1)} custom-call(bf16[8,64,1792]{2,1,0:T(8,128)(2,1)} %pad_maximum_fusion.3.x_ref), custom_call_target="tpu_custom_call" | custom-call | tf_op jit(solution)/shard_map/pallas_call | solution.py:476
  58.0 26.1 %shard_map.221 = bf16[4,16,128]{2,1,0:T(8,128)(2,1)} custom-call(bf16[4,16,128]{2,1,0:T(8,128)(2,1)} %broadcast_in_dim.29.x_ref), custom_call_target="tpu_custom_call" | custom-call | tf_op jit(solution)/shard_map/pallas_call | solution.py:476
  84.1 1.4 broadcast_in_dim.30.x_ref
  85.5 10.4 %shard_map.222 = bf16[8,4,16,128]{3,2,1,0:T(8,128)(2,1)} custom-call(bf16[8,4,16,128]{3,2,1,0:T(8,128)(2,1)} %broadcast_in_dim.30.x_ref), custom_call_target="tpu_custom_call" | custom-call | tf_op jit(solution)/shard_map/pallas_call | solution.py:476
  99.6 1.4 copy.111.segq_ref
  100.9 117.5 %shard_map.220 = bf16[2048,2048]{1,0:T(8,128)(2,1)} custom-call(bf16[256,2048]{1,0:T(8,128)(2,1)} %x_ref.1), custom_call_target="tpu_custom_call" | custom-call | tf_op jit(solution)/shard_map/pallas_call | solution.py:348
  218.5 5.4 convert_reduce_fusion
  225.1 2.3 fusion.2
  227.4 23.3 %convolution_add_fusion = f32[2048,1792]{0,1:T(8,128)} fusion(bf16[2048,1792]{1,0:T(8,128)(2,1)} %all-gather.5.cloned.1.call-done, f32[1792]{0:T(1024)S(1)} %maximum_convert_fusion, bf16[2048,2048]{1,0:T(8,128)(2,1)} %shard_map.220, f32[2048]{0:T(1024)S(1)} %reshape.300, f32[2048]{0:T(1024)S(1)} %reshape.299, f32[2048]{0:T(1024)S(1)} %add_rsqrt_fusion, ...), kind=kOutput, calls=%fused_computation.11 | convolution fusion | flops 15061221376 | bytes 30448640 | tf_op jit(solution)/shard_map/dot_general | solution.py:635
  250.7 1.7 slice.195
  252.4 3.9 fusion.35
  258.3 1.9 copy.110
  261.5 2.7 copy.130
  264.2 1.7 copy.127
  265.9 3.0 copy.129
  269.0 2.1 fusion.37
  271.1 3.5 copy.126
  274.7 2.6 copy.128
  277.3 2.6 copy.125
  279.9 7.2 subtract_convert_fusion.2
  287.1 3.2 maximum_bitcast_fusion.q_ref
  290.3 3.2 maximum_bitcast_fusion.1.k_ref
  293.5 74.2 %shard_map.224 = (f32[4,2048,64]{2,1,0:T(8,128)}, f32[4,2048,1]{2,1,0:T(8,128)}) custom-call(bf16[4,2048,64]{2,1,0:T(8,128)(2,1)} %maximum_bitcast_fusion.q_ref, bf16[4,2048,64]{2,1,0:T(8,128)(2,1)} %maximum_bitcast_fusion.1.k_ref, bf16[4,2048,64]{2,1,0:T(8,128)(2,1)} %bitcast.127, s32[2048,1]{1,0:T(8,128)} %copy.111.segq_ref, s32[1,2048]{1,0:T(1,128)} %bitcast.139), custom_call_target="tpu_custom_call" | custom-call | flops 2147483648 | bytes 5242880 | tf_op jit(solution)/shard_map/pallas_call | solution.py:145
  367.7 6.0 convolution_convert_fusion.1
  373.7 1.8 copy.113
  375.5 6.8 multiply_reduce_fusion
  382.3 2.1 copy.112
  384.4 7.0 fusion.39
  391.4 15.6 %fusion.31 = bf16[1024,2048]{1,0:T(8,128)(2,1)} fusion(bf16[2048,2048]{1,0:T(8,128)(2,1)} %all-gather.11.cloned.1.call-done, f32[2048,1792]{0,1:T(8,128)} %convolution_add_fusion), kind=kOutput, calls=%fused_computation.106 | convolution fusion | flops 8608808960 | bytes 20971520 | tf_op jit(solution)/shard_map/tf,td->fd/dot_general | solution.py:665
  407.1 16.8 %fusion.32 = f32[2048,2048]{1,0:T(8,128)} fusion(bf16[1024,2048]{1,0:T(8,128)(2,1)} %all-gather.9.cloned.1.call-done, f32[2048,1792]{0,1:T(8,128)} %convolution_add_fusion), kind=kOutput, calls=%fused_computation.107 | convolution fusion | flops 8608808960 | bytes 29360128 | tf_op jit(solution)/shard_map/dot_general | solution.py:654
  423.9 11.5 %add_convert_fusion = bf16[2048,2048]{1,0:T(8,128)(2,1)} fusion(f32[2048,2048]{1,0:T(8,128)} %fusion.32, bf16[2048,256]{0,1:T(8,128)(2,1)S(1)} %bitcast.124, bf16[256,2048]{1,0:T(8,128)(2,1)S(1)} %copy-done.12), kind=kOutput, calls=%fused_computation.8 | convolution fusion | flops 2155872256 | bytes 27262976 | tf_op jit(solution)/shard_map/dot_general | solution.py:653
  435.4 2.6 copy.114.delta_ref
  438.0 61.9 %shard_map.225 = (f32[4,2048,64]{2,1,0:T(8,128)}, f32[4,2048,64]{2,1,0:T(8,128)}, f32[4,2048,64]{2,1,0:T(8,128)}) custom-call(bf16[4,2048,64]{2,1,0:T(8,128)(2,1)} %maximum_bitcast_fusion.q_ref, bf16[4,2048,64]{2,1,0:T(8,128)(2,1)} %maximum_bitcast_fusion.1.k_ref, bf16[4,2048,64]{2,1,0:T(8,128)(2,1)} %bitcast.128, bf16[4,2048,64]{2,1,0:T(8,128)(2,1)} %bitcast.102, ...), custom_call_target="tpu_custom_call" | custom-call | flops 5368709120 | bytes 12582912 | tf_op jit(solution)/shard_map/pallas_call | solution.py:218
  500.0 2.9 slice.193
  504.7 3.0 add_convert_fusion.2
  507.7 4.8 pad_maximum_fusion.1
  512.5 1.9 copy.116
  514.4 1.6 copy.117
  516.0 2.5 convert_bitcast_fusion
  518.4 1.6 copy.118
  520.1 18.0 %convert_reduce_fusion.1 = (f32[1024]{0:T(1024)S(1)}, bf16[2048,1024]{0,1:T(8,128)(2,1)}) fusion(f32[2048,1792]{0,1:T(8,128)} %convolution_add_fusion, bf16[2048,2048]{1,0:T(8,128)(2,1)} %all-gather.11.cloned.1.call-done, bf16[1024,2048]{1,0:T(8,128)(2,1)} %all-gather.9.cloned.1.call-done), kind=kOutput, calls=%fused_computation.19 | convolution fusion | flops 8633973760 | bytes 25169920 | tf_op jit(solution)/shard_map/td,fd->tf/dot_general | solution.py:666
  538.0 28.6 %convolution_convert_fusion = bf16[2048,1792]{1,0:T(8,128)(2,1)} fusion(bf16[2048,1024]{0,1:T(8,128)(2,1)} %get-tuple-element.67, bf16[2048,256]{0,1:T(8,128)(2,1)S(1)} %bitcast.117, bf16[2048,256]{0,1:T(8,128)(2,1)S(1)} %bitcast.112, bf16[2048,256]{0,1:T(8,128)(2,1)S(1)} %bitcast.109, bf16[2048,2048]{1,0:T(8,128)(2,1)} %shard_map.220, ...), kind=kOutput, calls=%fused_computation.21 | convolution fusion | flops 15090581504 | bytes 23101440 | tf_op jit(solution)/shard_map/td,tc->dc/dot_general | solution.py:699
  568.6 1.6 convert_reduce_fusion.2
  570.2 23.2 %fusion.27.p_ref = f32[2048,2048]{1,0:T(8,128)} fusion(bf16[2048,1792]{1,0:T(8,128)(2,1)} %all-gather.5.cloned.1.call-done, bf16[2048,1024]{0,1:T(8,128)(2,1)} %get-tuple-element.67, bf16[2048,256]{0,1:T(8,128)(2,1)} %bitcast.116, bf16[2048,256]{0,1:T(8,128)(2,1)S(1)} %bitcast.114, bf16[2048,256]{0,1:T(8,128)(2,1)S(1)} %bitcast.111), kind=kOutput, calls=%fused_computation.64 | convolution fusion | flops 15061745664 | bytes 31457280 | tf_op jit(solution)/shard_map/tc,dc->td/dot_general | solution.py:695
  593.5 177.8 %shard_map.226 = f32[256,2048]{1,0:T(8,128)} custom-call(f32[2048,2048]{1,0:T(8,128)} %fusion.27.p_ref), custom_call_target="tpu_custom_call" | custom-call | tf_op jit(solution)/shard_map/pallas_call | solution.py:411
  771.3 2.6 fusion.21
  773.9 1.7 collective-permute-start.1
  776.2 3.0 convert_element_type.231
  779.2 62.9 %shard_map.227 = bf16[8,64,1792]{2,1,0:T(8,128)(2,1)} custom-call(bf16[8,64,1792]{2,1,0:T(8,128)(2,1)} %bitcast.130), custom_call_target="tpu_custom_call" | custom-call | tf_op jit(solution)/shard_map/pallas_call | solution.py:476
  842.1 2.8 slice_convert_fusion.5
  844.9 2.2 reshape.306
  848.3 2.5 copy.137
  852.1 1.9 reshape.305
  854.0 2.7 copy.120
  856.6 1.6 copy.135
  858.3 4.9 reduce-scatter.5.cloned.1.call-done
  863.2 4.4 convert_reduce_fusion.4
  868.5 26.0 %shard_map.228 = f32[8,4,16,128]{3,2,1,0:T(8,128)} custom-call(f32[8,4,16,128]{3,2,1,0:T(8,128)} %copy_bitcast_fusion.3.x_ref), custom_call_target="tpu_custom_call" | custom-call | tf_op jit(solution)/shard_map/pallas_call | solution.py:476
  894.5 1.6 reduce_sum.158.x_ref
  896.1 14.5 %shard_map.229 = f32[4,16,128]{2,1,0:T(8,128)} custom-call(f32[4,16,128]{2,1,0:T(8,128)} %reduce_sum.158.x_ref), custom_call_target="tpu_custom_call" | custom-call | tf_op jit(solution)/shard_map/pallas_call | solution.py:476
  913.5 1.9 copy.153
  (153 shorter events, 26.0 us)
Async XLA Ops:
  7.2 220.3 %all-gather.5.cloned.1.call-start = ((), (), s32[]{:S(2)}) async-start(), calls=%async_computation.4 | async-start | bytes 9175040 | tf_op jit(solution)/shard_map/all_gather | solution.py:560
  13.4 40.3 %copy-start.13 = (f32[64,2048]{1,0:T(8,128)S(1)}, f32[64,2048]{1,0:T(8,128)}, u32[]{:S(2)}) copy-start(f32[64,2048]{1,0:T(8,128)} %param.17) | copy-start | bytes 1572868
  14.8 41.2 %copy-start.9 = (f32[256,2048]{1,0:T(8,128)S(1)}, f32[256,2048]{1,0:T(8,128)}, u32[]{:S(2)}) copy-start(f32[256,2048]{1,0:T(8,128)} %param.21) | copy-start | bytes 6291460
  53.6 3.6 copy-start.20
  53.6 3.6 copy-start.22
  53.6 3.7 copy-start.21
  53.6 3.7 copy-start.23
  53.6 3.7 copy-start.24
  53.6 3.7 copy-start.25
  53.7 44.0 %copy-start.26 = (s32[1,3]{1,0:T(1,128)S(1)}, s32[1,3]{1,0:T(1,128)}, u32[]{:S(2)}) copy-start(s32[1,3]{1,0:T(1,128)} %param.14) | copy-start | bytes 40
  53.7 314.1 %all-gather.7.cloned.1.call-start = ((), (), s32[]{:S(2)}) async-start(), calls=%async_computation.5 | async-start | bytes 1310720 | tf_op jit(solution)/shard_map/all_gather | solution.py:499
  53.8 0.7 collective-permute-start
  54.5 0.7 copy-start.15
  55.2 312.6 %all-gather.11.cloned.1.call-start = ((), (), s32[]{:S(2)}) async-start(), calls=%async_computation.8 | async-start | bytes 9437184 | tf_op jit(solution)/shard_map/all_gather | solution.py:628
  55.9 351.2 %all-gather.9.cloned.1.call-start = ((), (), s32[]{:S(2)}) async-start(), calls=%async_computation.6 | async-start | bytes 5242880 | tf_op jit(solution)/shard_map/all_gather | solution.py:561
  57.1 716.7 %reduce-scatter.9.cloned.1.call-start = ((), (), s32[]{:S(2)}) async-start(), calls=%async_computation.10 | async-start | bytes 2621440 | tf_op jit(solution)/shard_map/reduce_scatter | solution.py:505
  97.9 120.6 %copy-start.16 = (s32[2048]{0:T(1024)}, s32[2048]{0:T(1024)S(1)}, u32[]{:S(2)}) copy-start(s32[2048]{0:T(1024)S(1)} %convert_reduce_fusion.5) | copy-start | bytes 24580
  218.5 6.6 copy-start
  260.2 5.7 copy-start.11
  269.0 5.7 copy-start.10
  279.9 7.2 copy-start.6
  287.1 3.2 copy-start.5
  407.0 369.1 %reduce-scatter.11.cloned.1.call-start = ((), (), s32[]{:S(2)}) async-start(), calls=%async_computation.11 | async-start | bytes 5242880 | tf_op jit(solution)/shard_map/reduce_scatter | solution.py:704
  407.1 16.8 %copy-start.12 = (bf16[256,2048]{1,0:T(8,128)(2,1)S(1)}, bf16[256,2048]{1,0:T(8,128)(2,1)}, u32[]{:S(2)}) copy-start(bf16[256,2048]{1,0:T(8,128)(2,1)} %all-gather.7.cloned.1.call-done) | copy-start | bytes 3145732
  438.0 341.2 %reduce-scatter.7.cloned.1.call-start = ((), (), s32[]{:S(2)}) async-start(), calls=%async_computation.9 | async-start | bytes 9175040 | tf_op jit(solution)/shard_map/reduce_scatter | solution.py:702
  499.9 3.5 copy-start.1
  499.9 4.7 copy-start.2
  520.1 18.0 %copy-start.7 = (bf16[2048,4,64]{0,2,1:T(8,128)(2,1)S(1)}, bf16[2048,4,64]{0,2,1:T(8,128)(2,1)}, u32[]{:S(2)}) copy-start(bf16[2048,4,64]{0,2,1:T(8,128)(2,1)} %copy.117) | copy-start | bytes 3145732
  520.1 18.0 %copy-start.8 = (bf16[2048,4,64]{0,2,1:T(8,128)(2,1)S(1)}, bf16[2048,4,64]{0,2,1:T(8,128)(2,1)}, u32[]{:S(2)}) copy-start(bf16[2048,4,64]{0,2,1:T(8,128)(2,1)} %copy.118) | copy-start | bytes 3145732
  566.7 0.8 copy-start.18
  566.7 0.9 copy-start.17
  566.7 1.2 copy-start.3
  566.7 296.4 %reduce-scatter.5.cloned.1.call-start = ((), (), s32[]{:S(2)}) async-start(), calls=%async_computation.7 | async-start | bytes 9437184 | tf_op jit(solution)/shard_map/reduce_scatter | solution.py:657
  773.9 2.3 collective-permute-start.1
  776.1 66.0 %copy-start.14 = (f32[64,2048]{1,0:T(8,128)}, f32[64,2048]{1,0:T(8,128)S(1)}, u32[]{:S(2)}) copy-start(f32[64,2048]{1,0:T(8,128)S(1)} %collective-permute-done.1) | copy-start | bytes 1572868
  854.0 9.2 copy-start.4
  913.0 2.4 copy-start.19
Sparse Core Ops, SparseCore 0:
  53.8 63.3 all-gather.4
  118.7 16.7 all-gather.6
  137.6 154.8 all-gather.10
  294.4 32.6 all-gather.8
  407.2 29.7 reduce-scatter.8
  439.5 44.4 reduce-scatter.10
  566.8 64.2 reduce-scatter.6
  635.2 227.9 reduce-scatter.4

commit v7 on v5

--- a/solution.py
+++ b/solution.py
@@ -540,7 +540,7 @@
     return over_dp.reshape(-1)[:width]
 
 
-def fetch_heads(w_qkv, w_fc1, w_fc2):
+def fetch_heads(w_qkv, w_fc1, w_fc2, tokens):
     dp_count = lax.axis_size("dp")
     ctx_count = lax.axis_size("ctx")
     rows_piece = w_qkv.shape[0]
@@ -556,11 +556,12 @@
         axis=2,
     )
     sent = exchange(pieces, "ctx", 5).reshape(ctx_count * rows_piece, -1)
+    sent, tokens = lax.optimization_barrier((sent, tokens))
     cols, fc2_rows = (
         lax.all_gather(sent, "dp", axis=0, tiled=True),
         lax.all_gather(w_fc2.astype(jnp.bfloat16), "dp", axis=0, tiled=True),
     )
-    return (cols, fc2_rows)
+    return (cols, fc2_rows, tokens)
 
 
 def return_heads(owned_parts):
@@ -619,13 +620,14 @@
         fc1_table.reshape(dp_count, ctx_count, unit), here, 1, keepdims=False
     ).reshape(dp_count * unit)
     out_rows = fetch_out_rows(w_out)
-    cols, fc2_rows = fetch_heads(w_qkv, w_fc1, w_fc2)
+    cols, fc2_rows, tokens = fetch_heads(w_qkv, w_fc1, w_fc2, tokens)
     gain32 = gain_low.astype(jnp.float32)
     shift32 = shift_low.astype(jnp.float32)
     inputs = tokens.astype(jnp.float32)
     normed, scaled, _ = norm_parts(inputs, gain32, shift32)
     tokens_group = ring_all_gather(tokens, ring, 0)
-    dy_group = lax.all_gather(cotangent, "ctx", axis=0, tiled=True)
+    late_dy, tokens_group = lax.optimization_barrier((cotangent, tokens_group))
+    dy_group = lax.all_gather(late_dy, "ctx", axis=0, tiled=True)
     hidden_group = norm_parts(tokens_group.astype(jnp.float32), gain32, shift32)[2].astype(
         jnp.bfloat16
     )

time: 926 us -> 904 us (0.976)
  Pallas kernels: 590 us -> 569 us
    pallas_call x6, Pallas kernels: 157 us -> 138 us  [exchange(): pl.pallas_call(functools.partial(_exchange_kernel, group=group), out_shap...]
  transfers between devices with their start and end apart: 9 -> 9, of which waited for: 0 -> 0; matrix products, arithmetic and copies ran while one was open for 30% -> 31% of each run, Pallas kernels for 53% -> 52%
where the time goes in v7:
time: 904 us; the launch traced here: 887 us
  Pallas kernels  569 us (63%)
  matrix products  153 us (17%)
  local copies, waits for them, and re-layouts  80.5 us (9%)
  other arithmetic  66.3 us (7%)
  between operations  15.1 us (2%)
    pallas_call x2, Pallas kernels, ring_reduce_scatter(): pl.pallas_call(functools.partial(_scatter_kernel, ring=ring, rows=rows),...  187 us
    pallas_call x6, Pallas kernels, exchange(): pl.pallas_call(functools.partial(_exchange_kernel, group=group), out_shap...  138 us
    pallas_call x1, Pallas kernels, ring_all_gather(): pl.pallas_call(functools.partial(_gather_kernel, ring=ring, rows=rows), o...  109 us
    pallas_call x1, Pallas kernels, attention_forward(): pl.pallas_call(functools.partial(_fwd_kernel, tq=tq, tk=tk, scale=scale),...  74 us
    pallas_call x1, Pallas kernels, attention_backward(): pl.pallas_call(functools.partial(_bwd_kernel, tq=tq, tk=tk, scale=scale),...  61.9 us
    unnamed x72, local copies, waits for them, and re-layouts  30.1 us
    dot_general x1, matrix products, head_plan(): jnp.einsum('td,tc->dc', hidden_group, d_both, preferred_element_type=jnp....  28.6 us
    dot_general x1, matrix products, head_plan(): jnp.dot(hidden_group, cols, preferred_element_type=jnp.float32)  23.4 us
  transfers between devices with their start and end apart: 9, of which 0 were waited for; matrix products, arithmetic and copies ran while one was open for 31% of the time, Pallas kernels for 52%

profile of v7, /device:TPU:0, one launch (start us, length us, event | category | flops | bytes accessed | tf_op | source)
XLA Modules:
  0.0 886.7 jit_solution(18054323229166179609)
XLA Ops:
  7.2 1.7 convert_element_type.177
  10.4 1.5 convert_element_type.176
  13.4 1.4 pad_maximum_fusion.3.x_ref
  14.8 38.6 %shard_map.220 = bf16[8,64,1792]{2,1,0:T(8,128)(2,1)} custom-call(bf16[8,64,1792]{2,1,0:T(8,128)(2,1)} %pad_maximum_fusion.3.x_ref), custom_call_target="tpu_custom_call" | custom-call | tf_op jit(solution)/shard_map/pallas_call | solution.py:476
  55.0 108.6 %shard_map.221 = bf16[2048,2048]{1,0:T(8,128)(2,1)} custom-call(bf16[256,2048]{1,0:T(8,128)(2,1)} %x_ref), custom_call_target="tpu_custom_call" | custom-call | tf_op jit(solution)/shard_map/pallas_call | solution.py:348
  165.8 5.2 shard_map.222
  171.0 1.4 broadcast_in_dim.30.x_ref
  172.4 10.0 %shard_map.223 = bf16[8,4,16,128]{3,2,1,0:T(8,128)(2,1)} custom-call(bf16[8,4,16,128]{3,2,1,0:T(8,128)(2,1)} %broadcast_in_dim.30.x_ref), custom_call_target="tpu_custom_call" | custom-call | tf_op jit(solution)/shard_map/pallas_call | solution.py:476
  184.3 4.7 convert_reduce_fusion
  190.1 2.3 fusion.2
  195.6 23.4 %convolution_add_fusion = f32[2048,1792]{0,1:T(8,128)} fusion(bf16[2048,1792]{1,0:T(8,128)(2,1)} %all-gather.5.cloned.1.call-done, f32[1792]{0:T(1024)S(1)} %maximum_convert_fusion, bf16[2048,2048]{1,0:T(8,128)(2,1)} %shard_map.221, f32[2048]{0:T(1024)S(1)} %reshape.300, f32[2048]{0:T(1024)S(1)} %reshape.299, f32[2048]{0:T(1024)S(1)} %add_rsqrt_fusion, ...), kind=kOutput, calls=%fused_computation.10 | convolution fusion | flops 15061221376 | bytes 30448640 | tf_op jit(solution)/shard_map/dot_general | solution.py:637
  218.9 1.7 slice.195
  220.7 3.9 fusion.34
  226.5 3.7 copy.125
  230.1 3.5 copy.126
  233.7 2.1 slice.196
  235.8 2.3 fusion.35
  238.0 3.5 copy.128
  241.6 3.5 copy.129
  245.0 3.0 copy.127
  248.0 2.6 copy.130
  250.7 1.7 copy.110
  252.4 7.3 subtract_convert_fusion.2
  259.7 5.2 maximum_bitcast_fusion
  264.9 74.0 %shard_map.224 = (f32[4,2048,64]{2,1,0:T(8,128)}, f32[4,2048,1]{2,1,0:T(8,128)}) custom-call(bf16[4,2048,64]{2,1,0:T(8,128)(2,1)} %get-tuple-element.68.q_ref, bf16[4,2048,64]{2,1,0:T(8,128)(2,1)} %get-tuple-element.69.k_ref, bf16[4,2048,64]{2,1,0:T(8,128)(2,1)} %bitcast.127, s32[2048,1]{1,0:T(8,128)} %copy.111.segq_ref, s32[1,2048]{1,0:T(1,128)} %bitcast.139), custom_call_target="tpu_custom_call" | custom-call | flops 2147483648 | bytes 5242880 | tf_op jit(solution)/shard_map/pallas_call | solution.py:145
  338.9 6.0 convolution_convert_fusion.2
  344.9 1.8 copy.113
  346.7 7.0 multiply_reduce_fusion
  353.7 1.9 copy.112
  355.6 7.0 fusion.38
  362.7 2.9 copy.114.delta_ref
  365.6 15.6 %convolution_convert_fusion.1 = bf16[1024,2048]{1,0:T(8,128)(2,1)} fusion(bf16[2048,2048]{1,0:T(8,128)(2,1)} %all-gather.11.cloned.1.call-done, f32[2048,1792]{0,1:T(8,128)} %convolution_add_fusion), kind=kOutput, calls=%fused_computation.35 | convolution fusion | flops 8610906112 | bytes 20971520 | tf_op jit(solution)/shard_map/tf,td->fd/dot_general | solution.py:665
  381.3 61.9 %shard_map.226 = (f32[4,2048,64]{2,1,0:T(8,128)}, f32[4,2048,64]{2,1,0:T(8,128)}, f32[4,2048,64]{2,1,0:T(8,128)}) custom-call(bf16[4,2048,64]{2,1,0:T(8,128)(2,1)} %get-tuple-element.68.q_ref, bf16[4,2048,64]{2,1,0:T(8,128)(2,1)} %get-tuple-element.69.k_ref, bf16[4,2048,64]{2,1,0:T(8,128)(2,1)} %bitcast.128, bf16[4,2048,64]{2,1,0:T(8,128)(2,1)} %bitcast.102, ...), custom_call_target="tpu_custom_call" | custom-call | flops 5368709120 | bytes 12582912 | tf_op jit(solution)/shard_map/pallas_call | solution.py:218
  443.2 3.0 slice.194
  446.7 1.9 slice.193
  448.7 4.3 add_convert_fusion.1
  453.0 3.2 pad_maximum_fusion.1
  456.2 2.7 copy.116
  458.9 5.4 pad_maximum_fusion.2
  464.3 2.7 copy.117
  467.0 2.5 convert_bitcast_fusion
  469.5 1.6 copy.118
  471.1 18.3 %convert_reduce_fusion.1 = (f32[1024]{0:T(1024)S(1)}, bf16[2048,1024]{0,1:T(8,128)(2,1)}) fusion(f32[2048,1792]{0,1:T(8,128)} %convolution_add_fusion, bf16[2048,2048]{1,0:T(8,128)(2,1)} %all-gather.11.cloned.1.call-done, bf16[1024,2048]{1,0:T(8,128)(2,1)} %all-gather.9.cloned.1.call-done), kind=kOutput, calls=%fused_computation.19 | convolution fusion | flops 8633973760 | bytes 25169920 | tf_op jit(solution)/shard_map/td,fd->tf/dot_general | solution.py:666
  489.4 28.6 %convolution_convert_fusion = bf16[2048,1792]{1,0:T(8,128)(2,1)} fusion(bf16[2048,1024]{0,1:T(8,128)(2,1)} %get-tuple-element.67, bf16[2048,256]{0,1:T(8,128)(2,1)} %bitcast.117, bf16[2048,256]{0,1:T(8,128)(2,1)S(1)} %bitcast.114, bf16[2048,256]{0,1:T(8,128)(2,1)S(1)} %bitcast.111, bf16[2048,2048]{1,0:T(8,128)(2,1)} %shard_map.221, f32[2048]{0:T(1024)S(1)} %reshape.300, ...), kind=kOutput, calls=%fused_computation.21 | convolution fusion | flops 15090581504 | bytes 23101440 | tf_op jit(solution)/shard_map/td,tc->dc/dot_general | solution.py:696
  520.0 16.9 %fusion.31 = f32[2048,2048]{1,0:T(8,128)} fusion(bf16[1024,2048]{1,0:T(8,128)(2,1)} %all-gather.9.cloned.1.call-done, f32[2048,1792]{0,1:T(8,128)} %convolution_add_fusion), kind=kOutput, calls=%fused_computation.107 | convolution fusion | flops 8608808960 | bytes 29360128 | tf_op jit(solution)/shard_map/dot_general | solution.py:656
  537.6 15.0 %convolution_add_fusion.1.p_ref = f32[2048,2048]{1,0:T(8,128)} fusion(f32[2048,2048]{1,0:T(8,128)} %fusion.31, bf16[2048,256]{0,1:T(8,128)(2,1)S(1)} %bitcast.105, bf16[256,2048]{1,0:T(8,128)(2,1)} %all-gather.7.cloned.1.call-done), kind=kOutput, calls=%fused_computation.11 | convolution fusion | flops 2151677952 | bytes 35651584 | tf_op jit(solution)/shard_map/dot_general | solution.py:655
  552.6 93.9 %shard_map.225 = f32[256,2048]{1,0:T(8,128)} custom-call(f32[2048,2048]{1,0:T(8,128)} %convolution_add_fusion.1.p_ref), custom_call_target="tpu_custom_call" | custom-call | tf_op jit(solution)/shard_map/pallas_call | solution.py:411
  646.5 22.0 %fusion.27.p_ref = f32[2048,2048]{1,0:T(8,128)} fusion(bf16[2048,1792]{1,0:T(8,128)(2,1)} %all-gather.5.cloned.1.call-done, bf16[2048,1024]{0,1:T(8,128)(2,1)} %get-tuple-element.67, bf16[2048,256]{0,1:T(8,128)(2,1)} %bitcast.118, bf16[2048,256]{0,1:T(8,128)(2,1)S(1)} %bitcast.116, bf16[2048,256]{0,1:T(8,128)(2,1)S(1)} %bitcast.113), kind=kOutput, calls=%fused_computation.65 | convolution fusion | flops 15061745664 | bytes 31457280 | tf_op jit(solution)/shard_map/tc,dc->td/dot_general | solution.py:692
  668.5 92.7 %shard_map.227 = f32[256,2048]{1,0:T(8,128)} custom-call(f32[2048,2048]{1,0:T(8,128)} %fusion.27.p_ref), custom_call_target="tpu_custom_call" | custom-call | tf_op jit(solution)/shard_map/pallas_call | solution.py:411
  761.2 2.7 fusion.21
  763.9 4.2 convert_reduce_fusion.4
  769.2 9.3 %shard_map.229 = f32[8,4,16,128]{3,2,1,0:T(8,128)} custom-call(f32[8,4,16,128]{3,2,1,0:T(8,128)} %copy_bitcast_fusion.3.x_ref), custom_call_target="tpu_custom_call" | custom-call | tf_op jit(solution)/shard_map/pallas_call | solution.py:476
  778.5 1.6 reduce_sum.158.x_ref
  780.1 6.5 shard_map.230
  787.4 1.7 collective-permute-start.1
  790.8 2.8 convert_element_type.223
  793.6 68.3 %shard_map.228 = bf16[8,64,1792]{2,1,0:T(8,128)(2,1)} custom-call(bf16[8,64,1792]{2,1,0:T(8,128)(2,1)} %bitcast.130), custom_call_target="tpu_custom_call" | custom-call | tf_op jit(solution)/shard_map/pallas_call | solution.py:476
  861.9 1.5 slice_convert_fusion.5
  863.4 2.4 slice_convert_fusion.6
  865.8 2.0 reshape.306
  867.8 2.8 copy.122
  870.6 2.5 copy.137
  873.1 2.6 reshape.305
  876.6 1.6 copy.135
  (153 shorter events, 23.5 us)
Async XLA Ops:
  7.2 188.4 %all-gather.5.cloned.1.call-start = ((), (), s32[]{:S(2)}) async-start(), calls=%async_computation.3 | async-start | bytes 9175040 | tf_op jit(solution)/shard_map/all_gather | solution.py:561
  13.4 40.1 %copy-start.15 = (f32[64,2048]{1,0:T(8,128)S(1)}, f32[64,2048]{1,0:T(8,128)}, u32[]{:S(2)}) copy-start(f32[64,2048]{1,0:T(8,128)} %param.17) | copy-start | bytes 1572868
  53.4 285.5 %all-gather.7.cloned.1.call-start = ((), (), s32[]{:S(2)}) async-start(), calls=%async_computation.4 | async-start | bytes 1310720 | tf_op jit(solution)/shard_map/all_gather | solution.py:499
  53.5 0.7 collective-permute-start
  54.2 0.7 copy-start.16
  54.9 108.8 %copy-start.14 = (f32[256,2048]{1,0:T(8,128)S(1)}, f32[256,2048]{1,0:T(8,128)}, u32[]{:S(2)}) copy-start(f32[256,2048]{1,0:T(8,128)} %param.21) | copy-start | bytes 6291460
  54.9 284.0 %all-gather.11.cloned.1.call-start = ((), (), s32[]{:S(2)}) async-start(), calls=%async_computation.6 | async-start | bytes 9437184 | tf_op jit(solution)/shard_map/all_gather | solution.py:630
  163.6 1.4 copy-start.21
  163.6 1.4 copy-start.23
  163.6 1.4 copy-start.24
  163.6 1.4 copy-start.25
  163.6 1.4 copy-start.26
  163.6 1.4 copy-start.22
  163.7 307.4 %all-gather.9.cloned.1.call-start = ((), (), s32[]{:S(2)}) async-start(), calls=%async_computation.5 | async-start | bytes 5242880 | tf_op jit(solution)/shard_map/all_gather | solution.py:562
  164.9 622.5 %reduce-scatter.6.cloned.1.call-start = ((), (), s32[]{:S(2)}) async-start(), calls=%async_computation.8 | async-start | bytes 2621440 | tf_op jit(solution)/shard_map/reduce_scatter | solution.py:505
  184.3 5.8 copy-start
  190.1 2.5 copy-start.27
  192.9 26.1 %copy-start.17 = (s32[2048]{0:T(1024)}, s32[2048]{0:T(1024)S(1)}, u32[]{:S(2)}) copy-start(s32[2048]{0:T(1024)S(1)} %convert_reduce_fusion.5) | copy-start | bytes 24580
  252.4 7.3 copy-start.7
  252.4 7.3 copy-start.8
  362.7 428.1 %reduce-scatter.8.cloned.1.call-start = ((), (), s32[]{:S(2)}) async-start(), calls=%async_computation.9 | async-start | bytes 5242880 | tf_op jit(solution)/shard_map/reduce_scatter | solution.py:701
  381.2 412.4 %reduce-scatter.4.cloned.1.call-start = ((), (), s32[]{:S(2)}) async-start(), calls=%async_computation.7 | async-start | bytes 9175040 | tf_op jit(solution)/shard_map/reduce_scatter | solution.py:699
  443.2 3.5 copy-start.2
  443.2 5.4 copy-start.1
  453.0 5.9 copy-start.6
  471.1 18.3 %copy-start.9 = (bf16[2048,4,64]{0,2,1:T(8,128)(2,1)S(1)}, bf16[2048,4,64]{0,2,1:T(8,128)(2,1)}, u32[]{:S(2)}) copy-start(bf16[2048,4,64]{0,2,1:T(8,128)(2,1)} %copy.116) | copy-start | bytes 3145732
  471.1 18.3 %copy-start.10 = (bf16[2048,4,64]{0,2,1:T(8,128)(2,1)S(1)}, bf16[2048,4,64]{0,2,1:T(8,128)(2,1)}, u32[]{:S(2)}) copy-start(bf16[2048,4,64]{0,2,1:T(8,128)(2,1)} %copy.117) | copy-start | bytes 3145732
  518.0 0.7 copy-start.19
  518.0 0.8 copy-start.18
  518.1 1.2 copy-start.3
  520.0 16.9 %copy-start.11 = (bf16[2048,4,64]{0,2,1:T(8,128)(2,1)S(1)}, bf16[2048,4,64]{0,2,1:T(8,128)(2,1)}, u32[]{:S(2)}) copy-start(bf16[2048,4,64]{0,2,1:T(8,128)(2,1)} %copy.117) | copy-start | bytes 3145732
  520.0 16.9 %copy-start.13 = (bf16[2048,4,64]{0,2,1:T(8,128)(2,1)S(1)}, bf16[2048,4,64]{0,2,1:T(8,128)(2,1)}, u32[]{:S(2)}) copy-start(bf16[2048,4,64]{0,2,1:T(8,128)(2,1)} %copy.118) | copy-start | bytes 3145732
  552.6 93.9 %copy-start.12 = (bf16[2048,4,64]{0,2,1:T(8,128)(2,1)S(1)}, bf16[2048,4,64]{0,2,1:T(8,128)(2,1)}, u32[]{:S(2)}) copy-start(bf16[2048,4,64]{0,2,1:T(8,128)(2,1)} %copy.117) | copy-start | bytes 3145732
  668.5 95.5 %copy-start.5 = (f32[256,2048]{1,0:T(8,128)S(1)}, f32[256,2048]{1,0:T(8,128)}, u32[]{:S(2)}) copy-start(f32[256,2048]{1,0:T(8,128)} %shard_map.225) | copy-start | bytes 6291460
  761.2 2.7 copy-start.4
  787.4 3.4 collective-permute-start.1
  790.2 88.0 %copy-start.20 = (f32[64]{0:T(128)}, f32[64]{0:T(128)S(1)}, u32[]{:S(2)}) copy-start(f32[64]{0:T(128)S(1)} %get-tuple-element.111) | copy-start | bytes 772
Sparse Core Ops, SparseCore 0:
  53.5 63.1 all-gather.4
  118.3 16.7 all-gather.6
  163.8 126.5 all-gather.10
  292.4 32.6 all-gather.8
  362.8 34.0 reduce-scatter.5
  399.5 44.5 reduce-scatter.7
  518.2 67.8 reduce-scatter.3

commit v8 on v7

--- a/solution.py
+++ b/solution.py
@@ -89,10 +89,13 @@
 TRANS_B = (((1,), (1,)), ((), ()))
 
 
-def _allowed(segq_ref, segk_ref, i, j, tq, tk):
+def _allowed(segq_ref, segk_ref, i, j, tq, tk, causal):
+    same = segq_ref[...] == segk_ref[...]
+    if not causal:
+        return same
     rows = i * tq + lax.broadcasted_iota(jnp.int32, (tq, tk), 0)
     cols = j * tk + lax.broadcasted_iota(jnp.int32, (tq, tk), 1)
-    return (segq_ref[...] == segk_ref[...]) & (cols <= rows)
+    return same & (cols <= rows)
 
 
 def _fwd_kernel(q_ref, k_ref, v_ref, segq_ref, segk_ref, o_ref, lse_ref, m_sc, l_sc, acc_sc, *, tq, tk, scale):
@@ -105,22 +108,31 @@
         l_sc[...] = jnp.zeros_like(l_sc)
         acc_sc[...] = jnp.zeros_like(acc_sc)
 
-    @pl.when(j * tk <= i * tq + tq - 1)
-    def _():
+    def absorb(causal):
         q = q_ref[0]
         k = k_ref[0]
         s = lax.dot_general(q, k, TRANS_B, preferred_element_type=jnp.float32) * scale
-        allowed = _allowed(segq_ref, segk_ref, i, j, tq, tk)
-        s = jnp.where(allowed, s, NEGATIVE)
+        s = jnp.where(_allowed(segq_ref, segk_ref, i, j, tq, tk, causal), s, -jnp.inf)
         m_prev = m_sc[...]
         m_new = jnp.maximum(m_prev, jnp.max(s, axis=1, keepdims=True))
         factor = jnp.exp(m_prev - m_new)
-        p = jnp.where(allowed, jnp.exp(s - m_new), 0.0)
+        p = jnp.exp(s - m_new)
         l_sc[...] = l_sc[...] * factor + jnp.sum(p, axis=1, keepdims=True)
         acc_sc[...] = acc_sc[...] * factor + jnp.dot(
             p.astype(jnp.bfloat16), v_ref[0], preferred_element_type=jnp.float32
         )
         m_sc[...] = m_new
+
+    below = (j + 1) * tk <= i * tq
+    near = jnp.logical_and(jnp.logical_not(below), j * tk <= i * tq + tq - 1)
+
+    @pl.when(below)
+    def _():
+        absorb(False)
+
+    @pl.when(near)
+    def _():
+        absorb(True)
 
     @pl.when(j == pl.num_programs(2) - 1)
     def _():
@@ -186,20 +198,30 @@
         dk_ref[...] = jnp.zeros_like(dk_ref)
         dv_ref[...] = jnp.zeros_like(dv_ref)
 
-    @pl.when(i * tq + tq - 1 >= j * tk)
-    def _():
+    def absorb(causal):
         q = q_ref[0]
         k = k_ref[0]
         do = do_ref[0]
         s = lax.dot_general(q, k, TRANS_B, preferred_element_type=jnp.float32) * scale
-        allowed = _allowed(segq_ref, segk_ref, i, j, tq, tk)
-        p = jnp.where(allowed, jnp.exp(s - lse_ref[0]), 0.0)
+        s = jnp.where(_allowed(segq_ref, segk_ref, i, j, tq, tk, causal), s, -jnp.inf)
+        p = jnp.exp(s - lse_ref[0])
         dp = lax.dot_general(do, v_ref[0], TRANS_B, preferred_element_type=jnp.float32)
         ds = (p * (dp - delta_ref[0])).astype(jnp.bfloat16)
         dv_ref[0] += lax.dot(p.astype(jnp.bfloat16).T, do, preferred_element_type=jnp.float32)
         dk_ref[0] += lax.dot(ds.T, q, preferred_element_type=jnp.float32) * scale
         rows = pl.ds(pl.multiple_of(i * tq, tq), tq)
         dq_ref[0, rows, :] += lax.dot(ds, k, preferred_element_type=jnp.float32) * scale
+
+    below = (j + 1) * tk <= i * tq
+    near = jnp.logical_and(jnp.logical_not(below), i * tq + tq - 1 >= j * tk)
+
+    @pl.when(below)
+    def _():
+        absorb(False)
+
+    @pl.when(near)
+    def _():
+        absorb(True)
 
 
 def attention_backward(q, k, v, do, lse, delta, seg, tq=512, tk=512):

time: 904 us -> 898 us (level)
  no operation moved by 1% of the time
where the time goes in v8:
time: 898 us; the launch traced here: 882 us
  Pallas kernels  564 us (63%)
  matrix products  153 us (17%)
  local copies, waits for them, and re-layouts  80.6 us (9%)
  other arithmetic  66.3 us (7%)
  between operations  15.1 us (2%)
    pallas_call x2, Pallas kernels, ring_reduce_scatter(): pl.pallas_call(functools.partial(_scatter_kernel, ring=ring, rows=rows),...  186 us
    pallas_call x6, Pallas kernels, exchange(): pl.pallas_call(functools.partial(_exchange_kernel, group=group), out_shap...  136 us
    pallas_call x1, Pallas kernels, ring_all_gather(): pl.pallas_call(functools.partial(_gather_kernel, ring=ring, rows=rows), o...  109 us
    pallas_call x1, Pallas kernels, attention_forward(): pl.pallas_call(functools.partial(_fwd_kernel, tq=tq, tk=tk, scale=scale),...  72.7 us
    pallas_call x1, Pallas kernels, attention_backward(): pl.pallas_call(functools.partial(_bwd_kernel, tq=tq, tk=tk, scale=scale),...  60.8 us
    unnamed x72, local copies, waits for them, and re-layouts  30.1 us
    dot_general x1, matrix products, head_plan(): jnp.einsum('td,tc->dc', hidden_group, d_both, preferred_element_type=jnp....  28.6 us
    dot_general x1, matrix products, head_plan(): jnp.dot(hidden_group, cols, preferred_element_type=jnp.float32)  23.4 us
  transfers between devices with their start and end apart: 9, of which 0 were waited for; matrix products, arithmetic and copies ran while one was open for 31% of the time, Pallas kernels for 52%

profile of v8, /device:TPU:0, one launch (start us, length us, event | category | flops | bytes accessed | tf_op | source)
XLA Modules:
  0.0 882.0 jit_solution(14267237696725856524)
XLA Ops:
  7.2 1.7 convert_element_type.177
  10.4 1.5 convert_element_type.176
  13.4 1.4 pad_maximum_fusion.3.x_ref
  14.8 38.6 %shard_map.220 = bf16[8,64,1792]{2,1,0:T(8,128)(2,1)} custom-call(bf16[8,64,1792]{2,1,0:T(8,128)(2,1)} %pad_maximum_fusion.3.x_ref), custom_call_target="tpu_custom_call" | custom-call | tf_op jit(solution)/shard_map/pallas_call | solution.py:498
  55.0 108.6 %shard_map.221 = bf16[2048,2048]{1,0:T(8,128)(2,1)} custom-call(bf16[256,2048]{1,0:T(8,128)(2,1)} %x_ref), custom_call_target="tpu_custom_call" | custom-call | tf_op jit(solution)/shard_map/pallas_call | solution.py:370
  165.8 5.2 shard_map.222
  171.0 1.4 broadcast_in_dim.30.x_ref
  172.4 10.0 %shard_map.223 = bf16[8,4,16,128]{3,2,1,0:T(8,128)(2,1)} custom-call(bf16[8,4,16,128]{3,2,1,0:T(8,128)(2,1)} %broadcast_in_dim.30.x_ref), custom_call_target="tpu_custom_call" | custom-call | tf_op jit(solution)/shard_map/pallas_call | solution.py:498
  184.3 4.7 convert_reduce_fusion
  190.1 2.3 fusion.2
  195.6 23.4 %convolution_add_fusion = f32[2048,1792]{0,1:T(8,128)} fusion(bf16[2048,1792]{1,0:T(8,128)(2,1)} %all-gather.5.cloned.1.call-done, f32[1792]{0:T(1024)S(1)} %maximum_convert_fusion, bf16[2048,2048]{1,0:T(8,128)(2,1)} %shard_map.221, f32[2048]{0:T(1024)S(1)} %reshape.300, f32[2048]{0:T(1024)S(1)} %reshape.299, f32[2048]{0:T(1024)S(1)} %add_rsqrt_fusion, ...), kind=kOutput, calls=%fused_computation.10 | convolution fusion | flops 15061221376 | bytes 30448640 | tf_op jit(solution)/shard_map/dot_general | solution.py:659
  218.9 1.7 slice.195
  220.7 3.9 fusion.34
  226.5 3.7 copy.125
  230.1 3.5 copy.126
  233.7 2.1 slice.196
  235.8 2.3 fusion.35
  238.0 3.5 copy.128
  241.6 3.5 copy.129
  245.0 3.0 copy.127
  248.0 2.6 copy.130
  250.7 1.7 copy.110
  252.4 7.3 subtract_convert_fusion.2
  259.7 5.2 maximum_bitcast_fusion
  264.9 72.7 %shard_map.224 = (f32[4,2048,64]{2,1,0:T(8,128)}, f32[4,2048,1]{2,1,0:T(8,128)}) custom-call(bf16[4,2048,64]{2,1,0:T(8,128)(2,1)} %get-tuple-element.68.q_ref, bf16[4,2048,64]{2,1,0:T(8,128)(2,1)} %get-tuple-element.69.k_ref, bf16[4,2048,64]{2,1,0:T(8,128)(2,1)} %bitcast.127, s32[2048,1]{1,0:T(8,128)} %copy.111.segq_ref, s32[1,2048]{1,0:T(1,128)} %bitcast.139), custom_call_target="tpu_custom_call" | custom-call | flops 2147483648 | bytes 5242880 | tf_op jit(solution)/shard_map/pallas_call | solution.py:157
  337.6 6.0 convolution_convert_fusion.2
  343.6 1.8 copy.113
  345.4 7.0 multiply_reduce_fusion
  352.4 2.1 copy.112
  354.4 7.0 fusion.38
  361.5 2.7 copy.114.delta_ref
  364.2 15.6 %convolution_convert_fusion.1 = bf16[1024,2048]{1,0:T(8,128)(2,1)} fusion(bf16[2048,2048]{1,0:T(8,128)(2,1)} %all-gather.11.cloned.1.call-done, f32[2048,1792]{0,1:T(8,128)} %convolution_add_fusion), kind=kOutput, calls=%fused_computation.35 | convolution fusion | flops 8610906112 | bytes 20971520 | tf_op jit(solution)/shard_map/tf,td->fd/dot_general | solution.py:687
  379.9 60.8 %shard_map.226 = (f32[4,2048,64]{2,1,0:T(8,128)}, f32[4,2048,64]{2,1,0:T(8,128)}, f32[4,2048,64]{2,1,0:T(8,128)}) custom-call(bf16[4,2048,64]{2,1,0:T(8,128)(2,1)} %get-tuple-element.68.q_ref, bf16[4,2048,64]{2,1,0:T(8,128)(2,1)} %get-tuple-element.69.k_ref, bf16[4,2048,64]{2,1,0:T(8,128)(2,1)} %bitcast.128, bf16[4,2048,64]{2,1,0:T(8,128)(2,1)} %bitcast.102, ...), custom_call_target="tpu_custom_call" | custom-call | flops 5368709120 | bytes 12582912 | tf_op jit(solution)/shard_map/pallas_call | solution.py:240
  440.7 3.0 slice.194
  444.3 1.9 slice.193
  446.2 4.3 add_convert_fusion.1
  450.5 3.2 pad_maximum_fusion.1
  453.7 2.7 copy.116
  456.4 5.4 pad_maximum_fusion.2
  461.9 2.7 copy.117
  464.5 2.5 convert_bitcast_fusion
  467.0 1.6 copy.118
  468.6 18.3 %convert_reduce_fusion.1 = (f32[1024]{0:T(1024)S(1)}, bf16[2048,1024]{0,1:T(8,128)(2,1)}) fusion(f32[2048,1792]{0,1:T(8,128)} %convolution_add_fusion, bf16[2048,2048]{1,0:T(8,128)(2,1)} %all-gather.11.cloned.1.call-done, bf16[1024,2048]{1,0:T(8,128)(2,1)} %all-gather.9.cloned.1.call-done), kind=kOutput, calls=%fused_computation.19 | convolution fusion | flops 8633973760 | bytes 25169920 | tf_op jit(solution)/shard_map/td,fd->tf/dot_general | solution.py:688
  487.0 28.6 %convolution_convert_fusion = bf16[2048,1792]{1,0:T(8,128)(2,1)} fusion(bf16[2048,1024]{0,1:T(8,128)(2,1)} %get-tuple-element.67, bf16[2048,256]{0,1:T(8,128)(2,1)} %bitcast.117, bf16[2048,256]{0,1:T(8,128)(2,1)S(1)} %bitcast.114, bf16[2048,256]{0,1:T(8,128)(2,1)S(1)} %bitcast.111, bf16[2048,2048]{1,0:T(8,128)(2,1)} %shard_map.221, f32[2048]{0:T(1024)S(1)} %reshape.300, ...), kind=kOutput, calls=%fused_computation.21 | convolution fusion | flops 15090581504 | bytes 23101440 | tf_op jit(solution)/shard_map/td,tc->dc/dot_general | solution.py:718
  517.5 16.9 %fusion.31 = f32[2048,2048]{1,0:T(8,128)} fusion(bf16[1024,2048]{1,0:T(8,128)(2,1)} %all-gather.9.cloned.1.call-done, f32[2048,1792]{0,1:T(8,128)} %convolution_add_fusion), kind=kOutput, calls=%fused_computation.107 | convolution fusion | flops 8608808960 | bytes 29360128 | tf_op jit(solution)/shard_map/dot_general | solution.py:678
  535.1 15.0 %convolution_add_fusion.1.p_ref = f32[2048,2048]{1,0:T(8,128)} fusion(f32[2048,2048]{1,0:T(8,128)} %fusion.31, bf16[2048,256]{0,1:T(8,128)(2,1)S(1)} %bitcast.105, bf16[256,2048]{1,0:T(8,128)(2,1)} %all-gather.7.cloned.1.call-done), kind=kOutput, calls=%fused_computation.11 | convolution fusion | flops 2151677952 | bytes 35651584 | tf_op jit(solution)/shard_map/dot_general | solution.py:677
  550.1 93.4 %shard_map.225 = f32[256,2048]{1,0:T(8,128)} custom-call(f32[2048,2048]{1,0:T(8,128)} %convolution_add_fusion.1.p_ref), custom_call_target="tpu_custom_call" | custom-call | tf_op jit(solution)/shard_map/pallas_call | solution.py:433
  643.6 22.0 %fusion.27.p_ref = f32[2048,2048]{1,0:T(8,128)} fusion(bf16[2048,1792]{1,0:T(8,128)(2,1)} %all-gather.5.cloned.1.call-done, bf16[2048,1024]{0,1:T(8,128)(2,1)} %get-tuple-element.67, bf16[2048,256]{0,1:T(8,128)(2,1)} %bitcast.118, bf16[2048,256]{0,1:T(8,128)(2,1)S(1)} %bitcast.116, bf16[2048,256]{0,1:T(8,128)(2,1)S(1)} %bitcast.113), kind=kOutput, calls=%fused_computation.65 | convolution fusion | flops 15061745664 | bytes 31457280 | tf_op jit(solution)/shard_map/tc,dc->td/dot_general | solution.py:714
  665.5 92.7 %shard_map.227 = f32[256,2048]{1,0:T(8,128)} custom-call(f32[2048,2048]{1,0:T(8,128)} %fusion.27.p_ref), custom_call_target="tpu_custom_call" | custom-call | tf_op jit(solution)/shard_map/pallas_call | solution.py:433
  758.2 2.7 fusion.21
  761.0 4.2 convert_reduce_fusion.4
  766.3 9.7 %shard_map.229 = f32[8,4,16,128]{3,2,1,0:T(8,128)} custom-call(f32[8,4,16,128]{3,2,1,0:T(8,128)} %copy_bitcast_fusion.3.x_ref), custom_call_target="tpu_custom_call" | custom-call | tf_op jit(solution)/shard_map/pallas_call | solution.py:498
  776.0 1.6 reduce_sum.158.x_ref
  777.6 5.1 shard_map.230
  783.5 1.7 collective-permute-start.1
  786.9 2.8 convert_element_type.223
  789.7 67.6 %shard_map.228 = bf16[8,64,1792]{2,1,0:T(8,128)(2,1)} custom-call(bf16[8,64,1792]{2,1,0:T(8,128)(2,1)} %bitcast.130), custom_call_target="tpu_custom_call" | custom-call | tf_op jit(solution)/shard_map/pallas_call | solution.py:498
  857.3 1.5 slice_convert_fusion.5
  858.8 2.4 slice_convert_fusion.6
  861.2 2.0 reshape.306
  863.1 2.8 copy.122
  865.9 2.5 copy.137
  868.5 2.6 reshape.305
  872.0 1.6 copy.135
  (153 shorter events, 23.5 us)
Async XLA Ops:
  7.2 188.4 %all-gather.5.cloned.1.call-start = ((), (), s32[]{:S(2)}) async-start(), calls=%async_computation.3 | async-start | bytes 9175040 | tf_op jit(solution)/shard_map/all_gather | solution.py:583
  13.4 40.1 %copy-start.15 = (f32[64,2048]{1,0:T(8,128)S(1)}, f32[64,2048]{1,0:T(8,128)}, u32[]{:S(2)}) copy-start(f32[64,2048]{1,0:T(8,128)} %param.17) | copy-start | bytes 1572868
  53.4 284.1 %all-gather.7.cloned.1.call-start = ((), (), s32[]{:S(2)}) async-start(), calls=%async_computation.4 | async-start | bytes 1310720 | tf_op jit(solution)/shard_map/all_gather | solution.py:521
  53.5 0.7 collective-permute-start
  54.2 0.7 copy-start.16
  54.9 108.8 %copy-start.14 = (f32[256,2048]{1,0:T(8,128)S(1)}, f32[256,2048]{1,0:T(8,128)}, u32[]{:S(2)}) copy-start(f32[256,2048]{1,0:T(8,128)} %param.21) | copy-start | bytes 6291460
  54.9 282.6 %all-gather.11.cloned.1.call-start = ((), (), s32[]{:S(2)}) async-start(), calls=%async_computation.6 | async-start | bytes 9437184 | tf_op jit(solution)/shard_map/all_gather | solution.py:652
  163.6 1.4 copy-start.21
  163.6 1.4 copy-start.23
  163.6 1.4 copy-start.24
  163.6 1.4 copy-start.25
  163.6 1.4 copy-start.26
  163.6 1.4 copy-start.22
  163.7 304.9 %all-gather.9.cloned.1.call-start = ((), (), s32[]{:S(2)}) async-start(), calls=%async_computation.5 | async-start | bytes 5242880 | tf_op jit(solution)/shard_map/all_gather | solution.py:584
  164.9 618.6 %reduce-scatter.6.cloned.1.call-start = ((), (), s32[]{:S(2)}) async-start(), calls=%async_computation.8 | async-start | bytes 2621440 | tf_op jit(solution)/shard_map/reduce_scatter | solution.py:527
  184.3 5.8 copy-start
  190.1 2.5 copy-start.27
  192.9 26.1 %copy-start.17 = (s32[2048]{0:T(1024)}, s32[2048]{0:T(1024)S(1)}, u32[]{:S(2)}) copy-start(s32[2048]{0:T(1024)S(1)} %convert_reduce_fusion.5) | copy-start | bytes 24580
  252.4 7.3 copy-start.7
  252.4 7.3 copy-start.8
  361.5 425.4 %reduce-scatter.8.cloned.1.call-start = ((), (), s32[]{:S(2)}) async-start(), calls=%async_computation.9 | async-start | bytes 5242880 | tf_op jit(solution)/shard_map/reduce_scatter | solution.py:723
  379.9 409.8 %reduce-scatter.4.cloned.1.call-start = ((), (), s32[]{:S(2)}) async-start(), calls=%async_computation.7 | async-start | bytes 9175040 | tf_op jit(solution)/shard_map/reduce_scatter | solution.py:721
  440.7 3.5 copy-start.2
  440.7 5.5 copy-start.1
  450.5 5.9 copy-start.6
  468.6 18.3 %copy-start.9 = (bf16[2048,4,64]{0,2,1:T(8,128)(2,1)S(1)}, bf16[2048,4,64]{0,2,1:T(8,128)(2,1)}, u32[]{:S(2)}) copy-start(bf16[2048,4,64]{0,2,1:T(8,128)(2,1)} %copy.116) | copy-start | bytes 3145732
  468.6 18.3 %copy-start.10 = (bf16[2048,4,64]{0,2,1:T(8,128)(2,1)S(1)}, bf16[2048,4,64]{0,2,1:T(8,128)(2,1)}, u32[]{:S(2)}) copy-start(bf16[2048,4,64]{0,2,1:T(8,128)(2,1)} %copy.117) | copy-start | bytes 3145732
  515.6 0.7 copy-start.19
  515.6 0.8 copy-start.18
  515.6 1.2 copy-start.3
  517.5 16.9 %copy-start.11 = (bf16[2048,4,64]{0,2,1:T(8,128)(2,1)S(1)}, bf16[2048,4,64]{0,2,1:T(8,128)(2,1)}, u32[]{:S(2)}) copy-start(bf16[2048,4,64]{0,2,1:T(8,128)(2,1)} %copy.117) | copy-start | bytes 3145732
  517.5 16.9 %copy-start.13 = (bf16[2048,4,64]{0,2,1:T(8,128)(2,1)S(1)}, bf16[2048,4,64]{0,2,1:T(8,128)(2,1)}, u32[]{:S(2)}) copy-start(bf16[2048,4,64]{0,2,1:T(8,128)(2,1)} %copy.118) | copy-start | bytes 3145732
  550.1 93.5 %copy-start.12 = (bf16[2048,4,64]{0,2,1:T(8,128)(2,1)S(1)}, bf16[2048,4,64]{0,2,1:T(8,128)(2,1)}, u32[]{:S(2)}) copy-start(bf16[2048,4,64]{0,2,1:T(8,128)(2,1)} %copy.117) | copy-start | bytes 3145732
  665.5 95.4 %copy-start.5 = (f32[256,2048]{1,0:T(8,128)S(1)}, f32[256,2048]{1,0:T(8,128)}, u32[]{:S(2)}) copy-start(f32[256,2048]{1,0:T(8,128)} %shard_map.225) | copy-start | bytes 6291460
  758.2 2.7 copy-start.4
  783.5 3.4 collective-permute-start.1
  786.3 87.3 %copy-start.20 = (f32[64]{0:T(128)}, f32[64]{0:T(128)S(1)}, u32[]{:S(2)}) copy-start(f32[64]{0:T(128)S(1)} %get-tuple-element.111) | copy-start | bytes 772
Sparse Core Ops, SparseCore 0:
  53.5 63.1 all-gather.4
  118.3 16.7 all-gather.6
  163.8 126.5 all-gather.10
  292.4 32.6 all-gather.8
  361.6 34.0 reduce-scatter.5
  398.2 44.5 reduce-scatter.7
  515.7 67.8 reduce-scatter.3

commit v9 on v8

--- a/solution.py
+++ b/solution.py
@@ -713,13 +713,14 @@
     d_hidden = ring_reduce_scatter(
         jnp.einsum("tc,dc->td", d_both, cols, preferred_element_type=jnp.float32), ring, 3
     )
-    grad_gain, grad_shift, d_inputs = norm_back(d_hidden, normed, scaled, gain32)
-    grad_tokens = (grad_out32 + d_inputs).astype(jnp.bfloat16)
     weight_parts = jnp.einsum(
         "td,tc->dc", hidden_group, d_both, preferred_element_type=jnp.float32
     ).astype(jnp.bfloat16)
     owned_parts = lax.psum_scatter(weight_parts, "dp", scatter_dimension=0, tiled=True)
     split_qkv, split_fc1 = return_heads(owned_parts)
+    d_hidden, split_qkv, split_fc1 = lax.optimization_barrier((d_hidden, split_qkv, split_fc1))
+    grad_gain, grad_shift, d_inputs = norm_back(d_hidden, normed, scaled, gain32)
+    grad_tokens = (grad_out32 + d_inputs).astype(jnp.bfloat16)
     owned_fc2 = lax.psum_scatter(
         grad_fc2_part.astype(jnp.bfloat16), "dp", scatter_dimension=0, tiled=True
     ).astype(jnp.float32)

time: 898 us -> 872 us (0.971); the launches traced: 882 us -> 866 us
  Pallas kernels: 564 us -> 547 us
    pallas_call x6, Pallas kernels: 136 us -> 113 us  [exchange(): pl.pallas_call(functools.partial(_exchange_kernel, group=group), out_shap...]
    unnamed x72 -> x82, local copies, waits for them, and re-layouts: 30.1 us -> 31.3 us
  transfers between devices with their start and end apart: 9 -> 9, of which waited for: 0 -> 0; matrix products, arithmetic and copies ran while one was open for 31% -> 30% of each run, Pallas kernels for 52% -> 52%
where the time goes in v9:
time: 872 us; the launch traced here: 866 us
  Pallas kernels  547 us (63%)
  matrix products  152 us (17%)
  local copies, waits for them, and re-layouts  81.1 us (9%)
  other arithmetic  63.4 us (7%)
  between operations  15.2 us (2%)
    pallas_call x2, Pallas kernels, ring_reduce_scatter(): pl.pallas_call(functools.partial(_scatter_kernel, ring=ring, rows=rows),...  192 us
    pallas_call x6, Pallas kernels, exchange(): pl.pallas_call(functools.partial(_exchange_kernel, group=group), out_shap...  113 us
    pallas_call x1, Pallas kernels, ring_all_gather(): pl.pallas_call(functools.partial(_gather_kernel, ring=ring, rows=rows), o...  109 us
    pallas_call x1, Pallas kernels, attention_forward(): pl.pallas_call(functools.partial(_fwd_kernel, tq=tq, tk=tk, scale=scale),...  72.7 us
    pallas_call x1, Pallas kernels, attention_backward(): pl.pallas_call(functools.partial(_bwd_kernel, tq=tq, tk=tk, scale=scale),...  60.8 us
    unnamed x82, local copies, waits for them, and re-layouts  31.3 us
    dot_general x1, matrix products, head_plan(): jnp.einsum('td,tc->dc', hidden_group, d_both, preferred_element_type=jnp....  28.7 us
    dot_general x1, matrix products, head_plan(): jnp.dot(hidden_group, cols, preferred_element_type=jnp.float32)  23.3 us
  transfers between devices with their start and end apart: 9, of which 0 were waited for; matrix products, arithmetic and copies ran while one was open for 30% of the time, Pallas kernels for 52%

profile of v9, /device:TPU:0, one launch (start us, length us, event | category | flops | bytes accessed | tf_op | source)
XLA Modules:
  0.0 865.7 jit_solution(4103269312227042799)
XLA Ops:
  7.2 1.7 convert_element_type.177
  10.4 1.5 convert_element_type.176
  13.4 1.4 pad_maximum_fusion.3.x_ref
  14.8 38.6 %shard_map.220 = bf16[8,64,1792]{2,1,0:T(8,128)(2,1)} custom-call(bf16[8,64,1792]{2,1,0:T(8,128)(2,1)} %pad_maximum_fusion.3.x_ref), custom_call_target="tpu_custom_call" | custom-call | tf_op jit(solution)/shard_map/pallas_call | solution.py:498
  55.0 108.6 %shard_map.221 = bf16[2048,2048]{1,0:T(8,128)(2,1)} custom-call(bf16[256,2048]{1,0:T(8,128)(2,1)} %x_ref), custom_call_target="tpu_custom_call" | custom-call | tf_op jit(solution)/shard_map/pallas_call | solution.py:370
  165.8 5.2 shard_map.222
  171.0 1.4 broadcast_in_dim.30.x_ref
  172.4 10.0 %shard_map.223 = bf16[8,4,16,128]{3,2,1,0:T(8,128)(2,1)} custom-call(bf16[8,4,16,128]{3,2,1,0:T(8,128)(2,1)} %broadcast_in_dim.30.x_ref), custom_call_target="tpu_custom_call" | custom-call | tf_op jit(solution)/shard_map/pallas_call | solution.py:498
  184.3 4.7 convert_reduce_fusion
  190.1 2.3 fusion.2
  195.6 23.3 %convolution_add_fusion = f32[2048,1792]{0,1:T(8,128)} fusion(bf16[2048,1792]{1,0:T(8,128)(2,1)} %all-gather.5.cloned.1.call-done, f32[1792]{0:T(1024)S(1)} %maximum_convert_fusion, bf16[2048,2048]{1,0:T(8,128)(2,1)} %shard_map.221, f32[2048]{0:T(1024)S(1)} %reshape.300, f32[2048]{0:T(1024)S(1)} %reshape.299, f32[2048]{0:T(1024)S(1)} %add_rsqrt_fusion, ...), kind=kOutput, calls=%fused_computation.10 | convolution fusion | flops 15061221376 | bytes 30448640 | tf_op jit(solution)/shard_map/dot_general | solution.py:659
  218.8 1.7 slice.195
  220.6 3.9 fusion.34
  226.4 3.5 copy.125
  229.9 3.5 copy.126
  233.5 2.1 slice.196
  235.6 2.3 fusion.35
  237.8 3.6 copy.128
  241.5 3.6 copy.129
  245.1 3.0 copy.127
  248.1 2.6 copy.130
  250.7 1.8 copy.110
  252.5 7.3 subtract_convert_fusion.2
  259.7 5.2 maximum_bitcast_fusion
  264.9 72.7 %shard_map.224 = (f32[4,2048,64]{2,1,0:T(8,128)}, f32[4,2048,1]{2,1,0:T(8,128)}) custom-call(bf16[4,2048,64]{2,1,0:T(8,128)(2,1)} %get-tuple-element.74.q_ref, bf16[4,2048,64]{2,1,0:T(8,128)(2,1)} %get-tuple-element.75.k_ref, bf16[4,2048,64]{2,1,0:T(8,128)(2,1)} %bitcast.127, s32[2048,1]{1,0:T(8,128)} %copy.111.segq_ref, s32[1,2048]{1,0:T(1,128)} %bitcast.139), custom_call_target="tpu_custom_call" | custom-call | flops 2147483648 | bytes 5242880 | tf_op jit(solution)/shard_map/pallas_call | solution.py:157
  337.6 6.0 convolution_convert_fusion.2
  343.6 1.8 copy.113
  345.3 6.7 multiply_reduce_fusion
  352.1 2.1 copy.112
  354.2 7.4 fusion.38
  361.7 2.7 copy.114.delta_ref
  364.4 15.6 %convolution_convert_fusion.1 = bf16[1024,2048]{1,0:T(8,128)(2,1)} fusion(bf16[2048,2048]{1,0:T(8,128)(2,1)} %all-gather.11.cloned.1.call-done, f32[2048,1792]{0,1:T(8,128)} %convolution_add_fusion), kind=kOutput, calls=%fused_computation.35 | convolution fusion | flops 8610906112 | bytes 20971520 | tf_op jit(solution)/shard_map/tf,td->fd/dot_general | solution.py:687
  380.1 60.8 %shard_map.226 = (f32[4,2048,64]{2,1,0:T(8,128)}, f32[4,2048,64]{2,1,0:T(8,128)}, f32[4,2048,64]{2,1,0:T(8,128)}) custom-call(bf16[4,2048,64]{2,1,0:T(8,128)(2,1)} %get-tuple-element.74.q_ref, bf16[4,2048,64]{2,1,0:T(8,128)(2,1)} %get-tuple-element.75.k_ref, bf16[4,2048,64]{2,1,0:T(8,128)(2,1)} %bitcast.128, bf16[4,2048,64]{2,1,0:T(8,128)(2,1)} %bitcast.102, ...), custom_call_target="tpu_custom_call" | custom-call | flops 5368709120 | bytes 12582912 | tf_op jit(solution)/shard_map/pallas_call | solution.py:240
  440.8 3.0 slice.194
  444.4 1.9 slice.193
  446.3 4.3 add_convert_fusion.1
  450.6 3.2 pad_maximum_fusion.1
  453.8 1.9 copy.116
  455.7 5.4 pad_maximum_fusion.2
  461.2 2.7 copy.117
  463.9 2.5 convert_bitcast_fusion
  466.3 1.6 copy.118
  468.0 18.4 %convert_reduce_fusion.1 = (f32[1024]{0:T(1024)S(1)}, bf16[2048,1024]{0,1:T(8,128)(2,1)}) fusion(f32[2048,1792]{0,1:T(8,128)} %convolution_add_fusion, bf16[2048,2048]{1,0:T(8,128)(2,1)} %all-gather.11.cloned.1.call-done, bf16[1024,2048]{1,0:T(8,128)(2,1)} %all-gather.9.cloned.1.call-done), kind=kOutput, calls=%fused_computation.19 | convolution fusion | flops 8633973760 | bytes 25169920 | tf_op jit(solution)/shard_map/td,fd->tf/dot_general | solution.py:688
  486.4 28.7 %convolution_convert_fusion = bf16[2048,1792]{1,0:T(8,128)(2,1)} fusion(bf16[2048,1024]{0,1:T(8,128)(2,1)} %get-tuple-element.73, bf16[2048,256]{0,1:T(8,128)(2,1)S(1)} %bitcast.117, bf16[2048,256]{0,1:T(8,128)(2,1)S(1)} %bitcast.114, bf16[2048,256]{0,1:T(8,128)(2,1)S(1)} %bitcast.111, bf16[2048,2048]{1,0:T(8,128)(2,1)} %shard_map.221, ...), kind=kOutput, calls=%fused_computation.21 | convolution fusion | flops 15090581504 | bytes 23101440 | tf_op jit(solution)/shard_map/td,tc->dc/dot_general | solution.py:716
  517.0 16.8 %fusion.31 = f32[2048,2048]{1,0:T(8,128)} fusion(bf16[1024,2048]{1,0:T(8,128)(2,1)} %all-gather.9.cloned.1.call-done, f32[2048,1792]{0,1:T(8,128)} %convolution_add_fusion), kind=kOutput, calls=%fused_computation.107 | convolution fusion | flops 8608808960 | bytes 29360128 | tf_op jit(solution)/shard_map/dot_general | solution.py:678
  533.9 21.5 %fusion.27.p_ref = f32[2048,2048]{1,0:T(8,128)} fusion(bf16[2048,1792]{1,0:T(8,128)(2,1)} %all-gather.5.cloned.1.call-done, bf16[2048,1024]{0,1:T(8,128)(2,1)S(1)} %copy-done.32, bf16[2048,256]{0,1:T(8,128)(2,1)S(1)} %bitcast.118, bf16[2048,256]{0,1:T(8,128)(2,1)S(1)} %bitcast.115, bf16[2048,256]{0,1:T(8,128)(2,1)S(1)} %bitcast.112), kind=kOutput, calls=%fused_computation.65 | convolution fusion | flops 15061745664 | bytes 31457280 | tf_op jit(solution)/shard_map/tc,dc->td/dot_general | solution.py:714
  555.4 5.5 collective-permute-start.1
  560.9 14.4 %convolution_add_fusion.1.p_ref = f32[2048,2048]{1,0:T(8,128)} fusion(f32[2048,2048]{1,0:T(8,128)} %fusion.31, bf16[2048,256]{0,1:T(8,128)(2,1)S(1)} %bitcast.105, bf16[256,2048]{1,0:T(8,128)(2,1)} %all-gather.7.cloned.1.call-done), kind=kOutput, calls=%fused_computation.11 | convolution fusion | flops 2151677952 | bytes 35651584 | tf_op jit(solution)/shard_map/dot_general | solution.py:677
  576.2 97.9 %shard_map.227 = f32[256,2048]{1,0:T(8,128)} custom-call(f32[2048,2048]{1,0:T(8,128)} %fusion.27.p_ref), custom_call_target="tpu_custom_call" | custom-call | tf_op jit(solution)/shard_map/pallas_call | solution.py:433
  674.1 94.2 %shard_map.225 = f32[256,2048]{1,0:T(8,128)} custom-call(f32[2048,2048]{1,0:T(8,128)} %convolution_add_fusion.1.p_ref), custom_call_target="tpu_custom_call" | custom-call | tf_op jit(solution)/shard_map/pallas_call | solution.py:433
  768.4 2.8 convert_element_type.223
  771.2 27.4 %shard_map.228 = bf16[8,64,1792]{2,1,0:T(8,128)(2,1)} custom-call(bf16[8,64,1792]{2,1,0:T(8,128)(2,1)} %bitcast.130), custom_call_target="tpu_custom_call" | custom-call | tf_op jit(solution)/shard_map/pallas_call | solution.py:498
  798.6 1.5 slice_convert_fusion.5
  800.0 2.4 slice_convert_fusion.6
  802.5 2.0 reshape.306
  804.4 2.8 copy.121
  807.2 2.5 copy.136
  809.7 2.6 reshape.305
  813.3 1.6 copy.135
  816.0 3.0 convert_reduce_fusion.4
  820.1 19.5 %shard_map.229 = f32[8,4,16,128]{3,2,1,0:T(8,128)} custom-call(f32[8,4,16,128]{3,2,1,0:T(8,128)} %copy_bitcast_fusion.3.x_ref), custom_call_target="tpu_custom_call" | custom-call | tf_op jit(solution)/shard_map/pallas_call | solution.py:498
  839.6 1.6 reduce_sum.158.x_ref
  841.2 12.5 %shard_map.230 = f32[4,16,128]{2,1,0:T(8,128)} custom-call(f32[4,16,128]{2,1,0:T(8,128)} %reduce_sum.158.x_ref), custom_call_target="tpu_custom_call" | custom-call | tf_op jit(solution)/shard_map/pallas_call | solution.py:498
  856.7 1.9 copy.153
  (163 shorter events, 24.1 us)
Async XLA Ops:
  7.2 188.4 %all-gather.5.cloned.1.call-start = ((), (), s32[]{:S(2)}) async-start(), calls=%async_computation.3 | async-start | bytes 9175040 | tf_op jit(solution)/shard_map/all_gather | solution.py:583
  13.4 40.1 %copy-start.19 = (f32[64,2048]{1,0:T(8,128)S(1)}, f32[64,2048]{1,0:T(8,128)}, u32[]{:S(2)}) copy-start(f32[64,2048]{1,0:T(8,128)} %param.17) | copy-start | bytes 1572868
  53.4 284.2 %all-gather.7.cloned.1.call-start = ((), (), s32[]{:S(2)}) async-start(), calls=%async_computation.4 | async-start | bytes 1310720 | tf_op jit(solution)/shard_map/all_gather | solution.py:521
  53.5 0.7 collective-permute-start
  54.2 0.7 copy-start.20
  54.9 108.8 %copy-start.18 = (f32[256,2048]{1,0:T(8,128)S(1)}, f32[256,2048]{1,0:T(8,128)}, u32[]{:S(2)}) copy-start(f32[256,2048]{1,0:T(8,128)} %param.21) | copy-start | bytes 6291460
  54.9 282.6 %all-gather.11.cloned.1.call-start = ((), (), s32[]{:S(2)}) async-start(), calls=%async_computation.6 | async-start | bytes 9437184 | tf_op jit(solution)/shard_map/all_gather | solution.py:652
  163.6 1.4 copy-start.25
  163.6 1.4 copy-start.27
  163.6 1.4 copy-start.28
  163.7 1.4 copy-start.29
  163.7 1.4 copy-start.30
  163.7 1.4 copy-start.26
  163.7 304.2 %all-gather.9.cloned.1.call-start = ((), (), s32[]{:S(2)}) async-start(), calls=%async_computation.5 | async-start | bytes 5242880 | tf_op jit(solution)/shard_map/all_gather | solution.py:584
  164.9 390.5 %reduce-scatter.6.cloned.1.call-start = ((), (), s32[]{:S(2)}) async-start(), calls=%async_computation.8 | async-start | bytes 2621440 | tf_op jit(solution)/shard_map/reduce_scatter | solution.py:527
  184.3 5.8 copy-start
  190.1 2.5 copy-start.31
  192.9 26.0 %copy-start.21 = (s32[2048]{0:T(1024)}, s32[2048]{0:T(1024)S(1)}, u32[]{:S(2)}) copy-start(s32[2048]{0:T(1024)S(1)} %convert_reduce_fusion.5) | copy-start | bytes 24580
  252.5 7.3 copy-start.7
  252.5 7.3 copy-start.8
  354.2 7.4 copy-start.9
  361.6 406.8 %reduce-scatter.8.cloned.1.call-start = ((), (), s32[]{:S(2)}) async-start(), calls=%async_computation.9 | async-start | bytes 5242880 | tf_op jit(solution)/shard_map/reduce_scatter | solution.py:724
  380.0 391.2 %reduce-scatter.4.cloned.1.call-start = ((), (), s32[]{:S(2)}) async-start(), calls=%async_computation.7 | async-start | bytes 9175040 | tf_op jit(solution)/shard_map/reduce_scatter | solution.py:719
  440.8 3.5 copy-start.2
  440.8 5.5 copy-start.1
  450.6 5.1 copy-start.6
  467.9 18.4 %copy-start.11 = (bf16[2048,4,64]{0,2,1:T(8,128)(2,1)S(1)}, bf16[2048,4,64]{0,2,1:T(8,128)(2,1)}, u32[]{:S(2)}) copy-start(bf16[2048,4,64]{0,2,1:T(8,128)(2,1)} %copy.117) | copy-start | bytes 3145732
  467.9 18.4 %copy-start.14 = (bf16[2048,4,64]{0,2,1:T(8,128)(2,1)S(1)}, bf16[2048,4,64]{0,2,1:T(8,128)(2,1)}, u32[]{:S(2)}) copy-start(bf16[2048,4,64]{0,2,1:T(8,128)(2,1)} %copy.118) | copy-start | bytes 3145732
  515.1 0.7 copy-start.23
  515.1 0.8 copy-start.22
  515.1 1.2 copy-start.3
  517.0 16.9 %copy-start.12 = (bf16[2048,4,64]{0,2,1:T(8,128)(2,1)S(1)}, bf16[2048,4,64]{0,2,1:T(8,128)(2,1)}, u32[]{:S(2)}) copy-start(bf16[2048,4,64]{0,2,1:T(8,128)(2,1)} %copy.117) | copy-start | bytes 3145732
  517.0 16.9 %copy-start.15 = (bf16[2048,4,64]{0,2,1:T(8,128)(2,1)S(1)}, bf16[2048,4,64]{0,2,1:T(8,128)(2,1)}, u32[]{:S(2)}) copy-start(bf16[2048,4,64]{0,2,1:T(8,128)(2,1)} %copy.118) | copy-start | bytes 3145732
  517.0 16.9 %copy-start.32 = (bf16[2048,1024]{0,1:T(8,128)(2,1)S(1)}, bf16[2048,1024]{0,1:T(8,128)(2,1)}, u32[]{:S(2)}) copy-start(bf16[2048,1024]{0,1:T(8,128)(2,1)} %get-tuple-element.73) | copy-start | bytes 12582916
  533.9 27.0 %copy-start.10 = (bf16[2048,4,64]{0,2,1:T(8,128)(2,1)S(1)}, bf16[2048,4,64]{0,2,1:T(8,128)(2,1)}, u32[]{:S(2)}) copy-start(bf16[2048,4,64]{0,2,1:T(8,128)(2,1)} %copy-done.9) | copy-start | bytes 3145732
  555.4 19.9 %copy-start.13 = (bf16[2048,4,64]{0,2,1:T(8,128)(2,1)S(1)}, bf16[2048,4,64]{0,2,1:T(8,128)(2,1)}, u32[]{:S(2)}) copy-start(bf16[2048,4,64]{0,2,1:T(8,128)(2,1)} %copy.117) | copy-start | bytes 3145732
  555.4 19.9 %copy-start.16 = (bf16[2048,4,64]{0,2,1:T(8,128)(2,1)S(1)}, bf16[2048,4,64]{0,2,1:T(8,128)(2,1)}, u32[]{:S(2)}) copy-start(bf16[2048,4,64]{0,2,1:T(8,128)(2,1)} %copy.118) | copy-start | bytes 3145732
  555.4 213.0 %collective-permute-start.1 = (f32[64,2048]{1,0:T(8,128)}, f32[64,2048]{1,0:T(8,128)}, u32[]{:S(2)}, u32[]{:S(2)}) collective-permute-start(f32[64,2048]{1,0:T(8,128)} %reduce-scatter.6.cloned.1.call-done), channel_id=1, source_target_pairs={{0,0},{8,1},{16,2},{24,3},{1,4},{9,5},{17,6},{25,7},{2,8},{10,9},{... | collective-permute-start | bytes 1572872 | tf_op jit(solution)/shard_map/ppermute | solution.py:529
  812.4 2.6 copy-start.4
  812.4 3.6 copy-start.5
  812.4 3.6 copy-start.17
  855.1 3.5 copy-start.24
Sparse Core Ops, SparseCore 0:
  53.5 63.1 all-gather.4
  118.3 16.7 all-gather.6
  163.8 126.5 all-gather.10
  292.4 32.7 all-gather.8
  361.7 34.0 reduce-scatter.5
  398.3 44.5 reduce-scatter.7
  515.3 75.3 reduce-scatter.3

commit v10 on v8

--- a/solution.py
+++ b/solution.py
@@ -551,14 +551,10 @@
     return result
 
 
-def reduce_small(small):
-    n_dp = lax.axis_size("dp")
-    n_ctx = lax.axis_size("ctx")
-    count, width = small.shape
-    packed = jax.vmap(lambda row: pack_rows(row, 128))(small)
-    packed = packed.reshape((n_dp, n_ctx) + packed.shape[1:]).transpose(1, 0, 2, 3)
-    over_ctx = jnp.sum(exchange(packed, "ctx", 7), axis=0)
-    over_dp = jnp.sum(exchange(over_ctx, "dp", 9), axis=0)
+def reduce_small(over_ctx):
+    width = over_ctx.shape[1]
+    packed = jax.vmap(lambda row: pack_rows(row, 128))(over_ctx)
+    over_dp = jnp.sum(exchange(packed, "dp", 9), axis=0)
     return over_dp.reshape(-1)[:width]
 
 
@@ -586,18 +582,43 @@
     return (cols, fc2_rows, tokens)
 
 
-def return_heads(owned_parts):
+def split_wide(values):
+    high = values.astype(jnp.bfloat16)
+    low_part = (values - high.astype(jnp.float32)).astype(jnp.bfloat16)
+    return jnp.concatenate([high, low_part], axis=-1)
+
+
+def join_wide(values):
+    half = values.shape[-1] // 2
+    return values[..., :half].astype(jnp.float32) + values[..., half:].astype(jnp.float32)
+
+
+def return_heads(owned_parts, small):
     dp_count = lax.axis_size("dp")
     ctx_count = lax.axis_size("ctx")
     head_width = D // ctx_count
     unit = FF // (dp_count * ctx_count)
     rows_piece = owned_parts.shape[0] // ctx_count
-    got = exchange(owned_parts.reshape(ctx_count, rows_piece, -1), "ctx", 6)
+    width = owned_parts.shape[1]
+    small_width = small.shape[1]
+    small_by_ctx = small.reshape(dp_count, ctx_count, small_width).transpose(1, 0, 2)
+    coded = split_wide(small_by_ctx.reshape(ctx_count, -1))
+    extra = -(-coded.shape[1] // (8 * width)) * 8
+    coded = jnp.pad(coded, ((0, 0), (0, extra * width - coded.shape[1])))
+    payload = jnp.concatenate(
+        [owned_parts.reshape(ctx_count, rows_piece, width), coded.reshape(ctx_count, extra, width)],
+        axis=1,
+    )
+    got = exchange(payload, "ctx", 6)
+    small_got = got[:, rows_piece:, :].reshape(ctx_count, -1)[:, : 2 * dp_count * small_width]
+    over_ctx = jnp.sum(join_wide(small_got), axis=0).reshape(dp_count, small_width)
+    got = got[:, :rows_piece, :]
     qkv = got[:, :, : 3 * head_width].reshape(ctx_count, rows_piece, 3, head_width)
     fc1 = got[:, :, 3 * head_width :].reshape(ctx_count, rows_piece, dp_count, unit)
     return (
         qkv.transpose(1, 2, 0, 3).reshape(rows_piece, 3 * D).astype(jnp.float32),
         fc1.transpose(1, 2, 0, 3).reshape(rows_piece, FF).astype(jnp.float32),
+        over_ctx,
     )
 
 
@@ -715,11 +736,6 @@
     )
     grad_gain, grad_shift, d_inputs = norm_back(d_hidden, normed, scaled, gain32)
     grad_tokens = (grad_out32 + d_inputs).astype(jnp.bfloat16)
-    weight_parts = jnp.einsum(
-        "td,tc->dc", hidden_group, d_both, preferred_element_type=jnp.float32
-    ).astype(jnp.bfloat16)
-    owned_parts = lax.psum_scatter(weight_parts, "dp", scatter_dimension=0, tiled=True)
-    split_qkv, split_fc1 = return_heads(owned_parts)
     owned_fc2 = lax.psum_scatter(
         grad_fc2_part.astype(jnp.bfloat16), "dp", scatter_dimension=0, tiled=True
     ).astype(jnp.float32)
@@ -742,7 +758,12 @@
         ],
         axis=1,
     )
-    owned_small = reduce_small(small)
+    weight_parts = jnp.einsum(
+        "td,tc->dc", hidden_group, d_both, preferred_element_type=jnp.float32
+    ).astype(jnp.bfloat16)
+    owned_parts = lax.psum_scatter(weight_parts, "dp", scatter_dimension=0, tiled=True)
+    split_qkv, split_fc1, over_ctx = return_heads(owned_parts, small)
+    owned_small = reduce_small(over_ctx)
     cuts = [0, 3 * D // count, D // count, D // count, D // count, FF // count]
     bounds = [sum(cuts[: i + 1]) for i in range(len(cuts))]
     owned_bqkv, owned_bout, owned_gain, owned_shift, owned_bfc1 = [

time: 898 us -> 892 us (level)
    pallas_call x6 -> x5, Pallas kernels: 136 us -> 126 us  [exchange(): pl.pallas_call(functools.partial(_exchange_kernel, group=group), out_shap...]
    unnamed x72 -> x76, local copies, waits for them, and re-layouts: 30.1 us -> 31.7 us
  transfers between devices with their start and end apart: 9 -> 9, of which waited for: 0 -> 0; matrix products, arithmetic and copies ran while one was open for 31% -> 30% of each run, Pallas kernels for 52% -> 51%
where the time goes in v10:
time: 892 us; the launch traced here: 876 us
  Pallas kernels  556 us (62%)
  matrix products  153 us (17%)
  local copies, waits for them, and re-layouts  81.5 us (9%)
  other arithmetic  67.7 us (8%)
  between operations  15.2 us (2%)
    pallas_call x2, Pallas kernels, ring_reduce_scatter(): pl.pallas_call(functools.partial(_scatter_kernel, ring=ring, rows=rows),...  188 us
    pallas_call x5, Pallas kernels, exchange(): pl.pallas_call(functools.partial(_exchange_kernel, group=group), out_shap...  126 us
    pallas_call x1, Pallas kernels, ring_all_gather(): pl.pallas_call(functools.partial(_gather_kernel, ring=ring, rows=rows), o...  109 us
    pallas_call x1, Pallas kernels, attention_forward(): pl.pallas_call(functools.partial(_fwd_kernel, tq=tq, tk=tk, scale=scale),...  72.7 us
    pallas_call x1, Pallas kernels, attention_backward(): pl.pallas_call(functools.partial(_bwd_kernel, tq=tq, tk=tk, scale=scale),...  60.7 us
    unnamed x76, local copies, waits for them, and re-layouts  31.7 us
    dot_general x1, matrix products, head_plan(): jnp.einsum('td,tc->dc', hidden_group, d_both, preferred_element_type=jnp....  28.6 us
    dot_general x1, matrix products, head_plan(): jnp.dot(hidden_group, cols, preferred_element_type=jnp.float32)  23.3 us
  transfers between devices with their start and end apart: 9, of which 0 were waited for; matrix products, arithmetic and copies ran while one was open for 30% of the time, Pallas kernels for 51%

profile of v10, /device:TPU:0, one launch (start us, length us, event | category | flops | bytes accessed | tf_op | source)
XLA Modules:
  0.0 875.7 jit_solution(132661351660896607)
XLA Ops:
  7.2 1.7 convert_element_type.194
  10.4 1.5 convert_element_type.193
  13.4 1.4 pad_maximum_fusion.4.x_ref
  14.8 38.6 %shard_map.220 = bf16[8,64,1792]{2,1,0:T(8,128)(2,1)} custom-call(bf16[8,64,1792]{2,1,0:T(8,128)(2,1)} %pad_maximum_fusion.4.x_ref), custom_call_target="tpu_custom_call" | custom-call | tf_op jit(solution)/shard_map/pallas_call | solution.py:498
  55.0 108.6 %shard_map.221 = bf16[2048,2048]{1,0:T(8,128)(2,1)} custom-call(bf16[256,2048]{1,0:T(8,128)(2,1)} %x_ref), custom_call_target="tpu_custom_call" | custom-call | tf_op jit(solution)/shard_map/pallas_call | solution.py:370
  165.8 5.2 shard_map.222
  171.0 1.4 broadcast_in_dim.30.x_ref
  172.4 10.0 %shard_map.223 = bf16[8,4,16,128]{3,2,1,0:T(8,128)(2,1)} custom-call(bf16[8,4,16,128]{3,2,1,0:T(8,128)(2,1)} %broadcast_in_dim.30.x_ref), custom_call_target="tpu_custom_call" | custom-call | tf_op jit(solution)/shard_map/pallas_call | solution.py:498
  184.3 4.7 convert_reduce_fusion
  190.1 2.3 fusion.2
  194.2 1.4 copy.108.segq_ref
  195.6 23.3 %convolution_add_fusion = f32[2048,1792]{0,1:T(8,128)} fusion(bf16[2048,1792]{1,0:T(8,128)(2,1)} %all-gather.5.cloned.1.call-done, f32[1792]{0:T(1024)S(1)} %maximum_convert_fusion, bf16[2048,2048]{1,0:T(8,128)(2,1)} %shard_map.221, f32[2048]{0:T(1024)S(1)} %reshape.312, f32[2048]{0:T(1024)S(1)} %reshape.311, f32[2048]{0:T(1024)S(1)} %add_rsqrt_fusion, ...), kind=kOutput, calls=%fused_computation.10 | convolution fusion | flops 15061221376 | bytes 30448640 | tf_op jit(solution)/shard_map/dot_general | solution.py:680
  218.9 1.7 slice.218
  220.6 3.9 fusion.37
  226.5 3.7 copy.121
  230.1 3.5 copy.122
  233.6 2.1 slice.219
  235.7 2.3 fusion.38
  238.0 3.5 copy.124
  241.5 3.5 copy.125
  245.0 3.0 copy.123
  248.0 2.6 copy.126
  250.6 1.7 copy.107
  252.3 7.3 subtract_convert_fusion.2
  259.6 5.2 maximum_bitcast_fusion
  264.8 72.7 %shard_map.224 = (f32[4,2048,64]{2,1,0:T(8,128)}, f32[4,2048,1]{2,1,0:T(8,128)}) custom-call(bf16[4,2048,64]{2,1,0:T(8,128)(2,1)} %get-tuple-element.70.q_ref, bf16[4,2048,64]{2,1,0:T(8,128)(2,1)} %get-tuple-element.71.k_ref, bf16[4,2048,64]{2,1,0:T(8,128)(2,1)} %bitcast.133, s32[2048,1]{1,0:T(8,128)} %copy.108.segq_ref, s32[1,2048]{1,0:T(1,128)} %bitcast.149), custom_call_target="tpu_custom_call" | custom-call | flops 2147483648 | bytes 5242880 | tf_op jit(solution)/shard_map/pallas_call | solution.py:157
  337.5 6.0 convolution_convert_fusion.2
  343.5 1.8 copy.110
  345.3 7.0 multiply_reduce_fusion
  352.3 2.1 copy.109
  354.4 7.0 fusion.41
  361.5 2.7 copy.111.delta_ref
  364.2 15.6 %convolution_convert_fusion.1 = bf16[1024,2048]{1,0:T(8,128)(2,1)} fusion(bf16[2048,2048]{1,0:T(8,128)(2,1)} %all-gather.11.cloned.1.call-done, f32[2048,1792]{0,1:T(8,128)} %convolution_add_fusion), kind=kOutput, calls=%fused_computation.35 | convolution fusion | flops 8610906112 | bytes 20971520 | tf_op jit(solution)/shard_map/tf,td->fd/dot_general | solution.py:708
  379.9 60.7 %shard_map.226 = (f32[4,2048,64]{2,1,0:T(8,128)}, f32[4,2048,64]{2,1,0:T(8,128)}, f32[4,2048,64]{2,1,0:T(8,128)}) custom-call(bf16[4,2048,64]{2,1,0:T(8,128)(2,1)} %get-tuple-element.70.q_ref, bf16[4,2048,64]{2,1,0:T(8,128)(2,1)} %get-tuple-element.71.k_ref, bf16[4,2048,64]{2,1,0:T(8,128)(2,1)} %bitcast.134, bf16[4,2048,64]{2,1,0:T(8,128)(2,1)} %bitcast.108, ...), custom_call_target="tpu_custom_call" | custom-call | flops 5368709120 | bytes 12582912 | tf_op jit(solution)/shard_map/pallas_call | solution.py:240
  440.6 3.0 slice.217
  444.1 1.9 slice.216
  446.0 4.3 add_convert_fusion.1
  450.3 3.2 pad_maximum_fusion.1
  453.6 2.7 copy.113
  456.3 5.4 pad_maximum_fusion.2
  461.7 2.7 copy.114
  464.4 2.5 convert_bitcast_fusion
  466.8 1.6 copy.115
  468.5 18.3 %convert_reduce_fusion.1 = (f32[1024]{0:T(1024)S(1)}, bf16[2048,1024]{0,1:T(8,128)(2,1)}) fusion(f32[2048,1792]{0,1:T(8,128)} %convolution_add_fusion, bf16[2048,2048]{1,0:T(8,128)(2,1)} %all-gather.11.cloned.1.call-done, bf16[1024,2048]{1,0:T(8,128)(2,1)} %all-gather.9.cloned.1.call-done), kind=kOutput, calls=%fused_computation.19 | convolution fusion | flops 8633973760 | bytes 25169920 | tf_op jit(solution)/shard_map/td,fd->tf/dot_general | solution.py:709
  486.8 28.6 %convolution_convert_fusion = bf16[2048,1792]{1,0:T(8,128)(2,1)} fusion(bf16[2048,1024]{0,1:T(8,128)(2,1)} %get-tuple-element.69, bf16[2048,256]{0,1:T(8,128)(2,1)} %bitcast.123, bf16[2048,256]{0,1:T(8,128)(2,1)S(1)} %bitcast.120, bf16[2048,256]{0,1:T(8,128)(2,1)S(1)} %bitcast.117, bf16[2048,2048]{1,0:T(8,128)(2,1)} %shard_map.221, f32[2048]{0:T(1024)S(1)} %reshape.312, ...), kind=kOutput, calls=%fused_computation.21 | convolution fusion | flops 15090581504 | bytes 23101440 | tf_op jit(solution)/shard_map/td,tc->dc/dot_general | solution.py:761
  517.3 16.9 %fusion.34 = f32[2048,2048]{1,0:T(8,128)} fusion(bf16[1024,2048]{1,0:T(8,128)(2,1)} %all-gather.9.cloned.1.call-done, f32[2048,1792]{0,1:T(8,128)} %convolution_add_fusion), kind=kOutput, calls=%fused_computation.115 | convolution fusion | flops 8608808960 | bytes 29360128 | tf_op jit(solution)/shard_map/dot_general | solution.py:699
  534.9 15.0 %convolution_add_fusion.1.p_ref = f32[2048,2048]{1,0:T(8,128)} fusion(f32[2048,2048]{1,0:T(8,128)} %fusion.34, bf16[2048,256]{0,1:T(8,128)(2,1)S(1)} %bitcast.111, bf16[256,2048]{1,0:T(8,128)(2,1)} %all-gather.7.cloned.1.call-done), kind=kOutput, calls=%fused_computation.11 | convolution fusion | flops 2151677952 | bytes 35651584 | tf_op jit(solution)/shard_map/dot_general | solution.py:698
  549.9 93.9 %shard_map.225 = f32[256,2048]{1,0:T(8,128)} custom-call(f32[2048,2048]{1,0:T(8,128)} %convolution_add_fusion.1.p_ref), custom_call_target="tpu_custom_call" | custom-call | tf_op jit(solution)/shard_map/pallas_call | solution.py:433
  643.8 21.9 %fusion.27.p_ref = f32[2048,2048]{1,0:T(8,128)} fusion(bf16[2048,1792]{1,0:T(8,128)(2,1)} %all-gather.5.cloned.1.call-done, bf16[2048,1024]{0,1:T(8,128)(2,1)} %get-tuple-element.69, bf16[2048,256]{0,1:T(8,128)(2,1)} %bitcast.124, bf16[2048,256]{0,1:T(8,128)(2,1)S(1)} %bitcast.122, bf16[2048,256]{0,1:T(8,128)(2,1)S(1)} %bitcast.119), kind=kOutput, calls=%fused_computation.66 | convolution fusion | flops 15061745664 | bytes 31457280 | tf_op jit(solution)/shard_map/tc,dc->td/dot_general | solution.py:735
  665.7 94.2 %shard_map.227 = f32[256,2048]{1,0:T(8,128)} custom-call(f32[2048,2048]{1,0:T(8,128)} %fusion.27.p_ref), custom_call_target="tpu_custom_call" | custom-call | tf_op jit(solution)/shard_map/pallas_call | solution.py:433
  760.0 2.7 fusion.21
  762.7 4.2 convert_reduce_fusion.4
  767.2 1.7 collective-permute-start.1
  769.0 2.8 convert_element_type.245
  771.8 2.9 pad_maximum_fusion.3.x_ref
  774.8 66.1 %shard_map.228 = bf16[8,72,1792]{2,1,0:T(8,128)(2,1)} custom-call(bf16[8,72,1792]{2,1,0:T(8,128)(2,1)} %pad_maximum_fusion.3.x_ref), custom_call_target="tpu_custom_call" | custom-call | tf_op jit(solution)/shard_map/pallas_call | solution.py:498
  840.8 1.5 slice_convert_fusion.5
  842.3 2.4 slice_convert_fusion.6
  846.4 5.9 shard_map.229
  854.8 2.0 reshape.318
  856.8 2.8 copy.118
  859.6 2.5 copy.135
  862.1 2.6 reshape.317
  865.6 1.6 copy.132
  (159 shorter events, 23.2 us)
Async XLA Ops:
  7.2 188.4 %all-gather.5.cloned.1.call-start = ((), (), s32[]{:S(2)}) async-start(), calls=%async_computation.3 | async-start | bytes 9175040 | tf_op jit(solution)/shard_map/all_gather | solution.py:579
  13.4 40.1 %copy-start.15 = (f32[64,2048]{1,0:T(8,128)S(1)}, f32[64,2048]{1,0:T(8,128)}, u32[]{:S(2)}) copy-start(f32[64,2048]{1,0:T(8,128)} %param.17) | copy-start | bytes 1572868
  53.4 284.1 %all-gather.7.cloned.1.call-start = ((), (), s32[]{:S(2)}) async-start(), calls=%async_computation.4 | async-start | bytes 1310720 | tf_op jit(solution)/shard_map/all_gather | solution.py:521
  53.5 0.7 collective-permute-start
  54.2 0.7 copy-start.16
  54.9 108.8 %copy-start.14 = (f32[256,2048]{1,0:T(8,128)S(1)}, f32[256,2048]{1,0:T(8,128)}, u32[]{:S(2)}) copy-start(f32[256,2048]{1,0:T(8,128)} %param.21) | copy-start | bytes 6291460
  54.9 282.6 %all-gather.11.cloned.1.call-start = ((), (), s32[]{:S(2)}) async-start(), calls=%async_computation.6 | async-start | bytes 9437184 | tf_op jit(solution)/shard_map/all_gather | solution.py:673
  163.6 1.4 copy-start.21
  163.6 1.4 copy-start.23
  163.6 1.4 copy-start.24
  163.6 1.4 copy-start.25
  163.7 1.4 copy-start.26
  163.7 1.4 copy-start.22
  163.7 304.8 %all-gather.9.cloned.1.call-start = ((), (), s32[]{:S(2)}) async-start(), calls=%async_computation.5 | async-start | bytes 5242880 | tf_op jit(solution)/shard_map/all_gather | solution.py:580
  164.9 602.3 %reduce-scatter.6.cloned.1.call-start = ((), (), s32[]{:S(2)}) async-start(), calls=%async_computation.8 | async-start | bytes 2621440 | tf_op jit(solution)/shard_map/reduce_scatter | solution.py:527
  184.3 5.8 copy-start
  190.1 2.5 copy-start.27
  192.9 26.0 %copy-start.17 = (s32[2048]{0:T(1024)}, s32[2048]{0:T(1024)S(1)}, u32[]{:S(2)}) copy-start(s32[2048]{0:T(1024)S(1)} %convert_reduce_fusion.5) | copy-start | bytes 24580
  252.3 7.3 copy-start.7
  252.3 7.3 copy-start.8
  361.4 407.6 %reduce-scatter.8.cloned.1.call-start = ((), (), s32[]{:S(2)}) async-start(), calls=%async_computation.9 | async-start | bytes 5242880 | tf_op jit(solution)/shard_map/reduce_scatter | solution.py:739
  379.8 392.0 %reduce-scatter.4.cloned.1.call-start = ((), (), s32[]{:S(2)}) async-start(), calls=%async_computation.7 | async-start | bytes 9175040 | tf_op jit(solution)/shard_map/reduce_scatter | solution.py:764
  440.6 3.5 copy-start.2
  440.6 5.5 copy-start.1
  450.3 5.9 copy-start.6
  468.5 18.4 %copy-start.9 = (bf16[2048,4,64]{0,2,1:T(8,128)(2,1)S(1)}, bf16[2048,4,64]{0,2,1:T(8,128)(2,1)}, u32[]{:S(2)}) copy-start(bf16[2048,4,64]{0,2,1:T(8,128)(2,1)} %copy.113) | copy-start | bytes 3145732
  468.5 18.4 %copy-start.10 = (bf16[2048,4,64]{0,2,1:T(8,128)(2,1)S(1)}, bf16[2048,4,64]{0,2,1:T(8,128)(2,1)}, u32[]{:S(2)}) copy-start(bf16[2048,4,64]{0,2,1:T(8,128)(2,1)} %copy.114) | copy-start | bytes 3145732
  515.4 0.7 copy-start.19
  515.4 0.8 copy-start.18
  515.4 1.2 copy-start.3
  517.3 16.9 %copy-start.11 = (bf16[2048,4,64]{0,2,1:T(8,128)(2,1)S(1)}, bf16[2048,4,64]{0,2,1:T(8,128)(2,1)}, u32[]{:S(2)}) copy-start(bf16[2048,4,64]{0,2,1:T(8,128)(2,1)} %copy.114) | copy-start | bytes 3145732
  517.3 16.9 %copy-start.13 = (bf16[2048,4,64]{0,2,1:T(8,128)(2,1)S(1)}, bf16[2048,4,64]{0,2,1:T(8,128)(2,1)}, u32[]{:S(2)}) copy-start(bf16[2048,4,64]{0,2,1:T(8,128)(2,1)} %copy.115) | copy-start | bytes 3145732
  549.9 93.9 %copy-start.12 = (bf16[2048,4,64]{0,2,1:T(8,128)(2,1)S(1)}, bf16[2048,4,64]{0,2,1:T(8,128)(2,1)}, u32[]{:S(2)}) copy-start(bf16[2048,4,64]{0,2,1:T(8,128)(2,1)} %copy.114) | copy-start | bytes 3145732
  665.7 97.0 %copy-start.5 = (f32[256,2048]{1,0:T(8,128)S(1)}, f32[256,2048]{1,0:T(8,128)}, u32[]{:S(2)}) copy-start(f32[256,2048]{1,0:T(8,128)} %shard_map.225) | copy-start | bytes 6291460
  759.9 2.7 copy-start.4
  767.2 1.8 collective-permute-start.1
  853.7 13.6 %copy-start.20 = (f32[64]{0:T(128)}, f32[64]{0:T(128)S(1)}, u32[]{:S(2)}) copy-start(f32[64]{0:T(128)S(1)} %get-tuple-element.113) | copy-start | bytes 772
Sparse Core Ops, SparseCore 0:
  53.5 63.1 all-gather.4
  118.3 16.7 all-gather.6
  163.8 126.5 all-gather.10
  292.4 32.6 all-gather.8
  361.6 34.0 reduce-scatter.5
  398.2 44.4 reduce-scatter.7
  515.6 67.9 reduce-scatter.3

commit v11 on v9

--- a/solution.py
+++ b/solution.py
@@ -98,9 +98,10 @@
     return same & (cols <= rows)
 
 
-def _fwd_kernel(q_ref, k_ref, v_ref, segq_ref, segk_ref, o_ref, lse_ref, m_sc, l_sc, acc_sc, *, tq, tk, scale):
-    i = pl.program_id(1)
-    j = pl.program_id(2)
+def _fwd_kernel(qi_ref, kj_ref, q_ref, k_ref, v_ref, segq_ref, segk_ref, o_ref, lse_ref, m_sc, l_sc, acc_sc, *, tq, tk, scale):
+    t = pl.program_id(1)
+    i = qi_ref[t]
+    j = kj_ref[t]
 
     @pl.when(j == 0)
     def _():
@@ -123,77 +124,82 @@
         )
         m_sc[...] = m_new
 
-    below = (j + 1) * tk <= i * tq
-    near = jnp.logical_and(jnp.logical_not(below), j * tk <= i * tq + tq - 1)
-
-    @pl.when(below)
+    @pl.when(j < i)
     def _():
         absorb(False)
 
-    @pl.when(near)
+    @pl.when(j == i)
     def _():
         absorb(True)
-
-    @pl.when(j == pl.num_programs(2) - 1)
-    def _():
         total = l_sc[...]
         o_ref[0] = acc_sc[...] / total
         lse_ref[0] = m_sc[...] + jnp.log(total)
 
 
-def attention_forward(q, k, v, seg, tq=512, tk=512):
+def _schedule(count, queries_outer):
+    if queries_outer:
+        pairs = [(i, j) for i in range(count) for j in range(i + 1)]
+    else:
+        pairs = [(i, j) for j in range(count) for i in range(j, count)]
+    return (
+        jnp.asarray([p[0] for p in pairs], jnp.int32),
+        jnp.asarray([p[1] for p in pairs], jnp.int32),
+    )
+
+
+def attention_forward(q, k, v, seg, block=512):
     heads, total, dim = q.shape
-    nq, nk = total // tq, total // tk
+    count = total // block
     scale = 1.0 / math.sqrt(dim)
     segq = seg.reshape(total, 1)
     segk = seg.reshape(1, total)
-
-    def kv_map(h, i, j):
-        return (h, jnp.minimum(j, (i * tq + tq - 1) // tk), 0)
-
-    def segk_map(h, i, j):
-        return (0, jnp.minimum(j, (i * tq + tq - 1) // tk))
+    qi, kj = _schedule(count, True)
+    steps = qi.shape[0]
 
     return pl.pallas_call(
-        functools.partial(_fwd_kernel, tq=tq, tk=tk, scale=scale),
+        functools.partial(_fwd_kernel, tq=block, tk=block, scale=scale),
         out_shape=(
             jax.ShapeDtypeStruct((heads, total, dim), jnp.float32),
             jax.ShapeDtypeStruct((heads, total, 1), jnp.float32),
         ),
-        grid=(heads, nq, nk),
-        in_specs=[
-            pl.BlockSpec((1, tq, dim), lambda h, i, j: (h, i, 0)),
-            pl.BlockSpec((1, tk, dim), kv_map),
-            pl.BlockSpec((1, tk, dim), kv_map),
-            pl.BlockSpec((tq, 1), lambda h, i, j: (i, 0)),
-            pl.BlockSpec((1, tk), segk_map),
-        ],
-        out_specs=[
-            pl.BlockSpec((1, tq, dim), lambda h, i, j: (h, i, 0)),
-            pl.BlockSpec((1, tq, 1), lambda h, i, j: (h, i, 0)),
-        ],
-        scratch_shapes=[
-            pltpu.VMEM((tq, 1), jnp.float32),
-            pltpu.VMEM((tq, 1), jnp.float32),
-            pltpu.VMEM((tq, dim), jnp.float32),
-        ],
+        grid_spec=pltpu.PrefetchScalarGridSpec(
+            num_scalar_prefetch=2,
+            grid=(heads, steps),
+            in_specs=[
+                pl.BlockSpec((1, block, dim), lambda h, t, qi, kj: (h, qi[t], 0)),
+                pl.BlockSpec((1, block, dim), lambda h, t, qi, kj: (h, kj[t], 0)),
+                pl.BlockSpec((1, block, dim), lambda h, t, qi, kj: (h, kj[t], 0)),
+                pl.BlockSpec((block, 1), lambda h, t, qi, kj: (qi[t], 0)),
+                pl.BlockSpec((1, block), lambda h, t, qi, kj: (0, kj[t])),
+            ],
+            out_specs=[
+                pl.BlockSpec((1, block, dim), lambda h, t, qi, kj: (h, qi[t], 0)),
+                pl.BlockSpec((1, block, 1), lambda h, t, qi, kj: (h, qi[t], 0)),
+            ],
+            scratch_shapes=[
+                pltpu.VMEM((block, 1), jnp.float32),
+                pltpu.VMEM((block, 1), jnp.float32),
+                pltpu.VMEM((block, dim), jnp.float32),
+            ],
+        ),
         cost_estimate=pl.CostEstimate(
             flops=2 * heads * total * total * dim,
             transcendentals=heads * total * total // 2,
             bytes_accessed=heads * total * dim * 10,
         ),
-    )(q, k, v, segq, segk)
-
-
-def _bwd_kernel(q_ref, k_ref, v_ref, do_ref, lse_ref, delta_ref, segq_ref, segk_ref, dq_ref, dk_ref, dv_ref, *, tq, tk, scale):
-    j = pl.program_id(1)
-    i = pl.program_id(2)
-
-    @pl.when((j == 0) & (i == 0))
+    )(qi, kj, q, k, v, segq, segk)
+
+
+def _bwd_kernel(qi_ref, kj_ref, q_ref, k_ref, v_ref, do_ref, lse_ref, delta_ref, segq_ref, segk_ref, dq_ref, dk_ref, dv_ref, *, tq, tk, scale):
+    t = pl.program_id(1)
+    i = qi_ref[t]
+    j = kj_ref[t]
+
+    @pl.when(t == 0)
     def _():
         dq_ref[...] = jnp.zeros_like(dq_ref)
 
-    @pl.when(i == 0)
+    @pl.when(i == j)
     def _():
         dk_ref[...] = jnp.zeros_like(dk_ref)
         dv_ref[...] = jnp.zeros_like(dv_ref)
@@ -212,60 +218,62 @@
         rows = pl.ds(pl.multiple_of(i * tq, tq), tq)
         dq_ref[0, rows, :] += lax.dot(ds, k, preferred_element_type=jnp.float32) * scale
 
-    below = (j + 1) * tk <= i * tq
-    near = jnp.logical_and(jnp.logical_not(below), i * tq + tq - 1 >= j * tk)
-
-    @pl.when(below)
+    @pl.when(j < i)
     def _():
         absorb(False)
 
-    @pl.when(near)
+    @pl.when(j == i)
     def _():
         absorb(True)
 
 
-def attention_backward(q, k, v, do, lse, delta, seg, tq=512, tk=512):
+def attention_backward(q, k, v, do, lse, delta, seg, block=512):
     heads, total, dim = q.shape
-    nq, nk = total // tq, total // tk
+    count = total // block
     scale = 1.0 / math.sqrt(dim)
     segq = seg.reshape(total, 1)
     segk = seg.reshape(1, total)
-
-    def q_map(h, j, i):
-        return (h, jnp.maximum(i, (j * tk) // tq), 0)
-
-    def segq_map(h, j, i):
-        return (jnp.maximum(i, (j * tk) // tq), 0)
+    qi, kj = _schedule(count, False)
+    steps = qi.shape[0]
+
+    def q_map(h, t, qi, kj):
+        return (h, qi[t], 0)
+
+    def k_map(h, t, qi, kj):
+        return (h, kj[t], 0)
 
     return pl.pallas_call(
-        functools.partial(_bwd_kernel, tq=tq, tk=tk, scale=scale),
+        functools.partial(_bwd_kernel, tq=block, tk=block, scale=scale),
         out_shape=(
             jax.ShapeDtypeStruct((heads, total, dim), jnp.float32),
             jax.ShapeDtypeStruct((heads, total, dim), jnp.float32),
             jax.ShapeDtypeStruct((heads, total, dim), jnp.float32),
         ),
-        grid=(heads, nk, nq),
-        in_specs=[
-            pl.BlockSpec((1, tq, dim), q_map),
-            pl.BlockSpec((1, tk, dim), lambda h, j, i: (h, j, 0)),
-            pl.BlockSpec((1, tk, dim), lambda h, j, i: (h, j, 0)),
-            pl.BlockSpec((1, tq, dim), q_map),
-            pl.BlockSpec((1, tq, 1), q_map),
-            pl.BlockSpec((1, tq, 1), q_map),
-            pl.BlockSpec((tq, 1), segq_map),
-            pl.BlockSpec((1, tk), lambda h, j, i: (0, j)),
-        ],
-        out_specs=[
-            pl.BlockSpec((1, total, dim), lambda h, j, i: (h, 0, 0)),
-            pl.BlockSpec((1, tk, dim), lambda h, j, i: (h, j, 0)),
-            pl.BlockSpec((1, tk, dim), lambda h, j, i: (h, j, 0)),
-        ],
+        grid_spec=pltpu.PrefetchScalarGridSpec(
+            num_scalar_prefetch=2,
+            grid=(heads, steps),
+            in_specs=[
+                pl.BlockSpec((1, block, dim), q_map),
+                pl.BlockSpec((1, block, dim), k_map),
+                pl.BlockSpec((1, block, dim), k_map),
+                pl.BlockSpec((1, block, dim), q_map),
+                pl.BlockSpec((1, block, 1), q_map),
+                pl.BlockSpec((1, block, 1), q_map),
+                pl.BlockSpec((block, 1), lambda h, t, qi, kj: (qi[t], 0)),
+                pl.BlockSpec((1, block), lambda h, t, qi, kj: (0, kj[t])),
+            ],
+            out_specs=[
+                pl.BlockSpec((1, total, dim), lambda h, t, qi, kj: (h, 0, 0)),
+                pl.BlockSpec((1, block, dim), k_map),
+                pl.BlockSpec((1, block, dim), k_map),
+            ],
+        ),
         cost_estimate=pl.CostEstimate(
             flops=5 * heads * total * total * dim,
             transcendentals=heads * total * total // 2,
             bytes_accessed=heads * total * dim * 24,
         ),
-    )(q, k, v, do, lse, delta, segq, segk)
+    )(qi, kj, q, k, v, do, lse, delta, segq, segk)
 
 
 MESH_ID = pl.DeviceIdType.MESH

time: 872 us -> 860 us (0.986)
  Pallas kernels: 547 us -> 536 us
    pallas_call x2, Pallas kernels: 133 us -> 123 us  [the longest x1 66.5 us: attention_forward(): pl.pallas_call(functools.partial(_fwd_kernel, tq=block, tk=block, scale=s...]
where the time goes in v11:
time: 860 us; the launch traced here: 854 us
  Pallas kernels  536 us (62%)
  matrix products  152 us (18%)
  local copies, waits for them, and re-layouts  81.1 us (9%)
  other arithmetic  63.4 us (7%)
  between operations  15.2 us (2%)
    pallas_call x2, Pallas kernels, ring_reduce_scatter(): pl.pallas_call(functools.partial(_scatter_kernel, ring=ring, rows=rows),...  194 us
    pallas_call x6, Pallas kernels, exchange(): pl.pallas_call(functools.partial(_exchange_kernel, group=group), out_shap...  111 us
    pallas_call x1, Pallas kernels, ring_all_gather(): pl.pallas_call(functools.partial(_gather_kernel, ring=ring, rows=rows), o...  109 us
    pallas_call x1, Pallas kernels, attention_forward(): pl.pallas_call(functools.partial(_fwd_kernel, tq=block, tk=block, scale=s...  66.5 us
    pallas_call x1, Pallas kernels, attention_backward(): pl.pallas_call(functools.partial(_bwd_kernel, tq=block, tk=block, scale=s...  56.2 us
    unnamed x82, local copies, waits for them, and re-layouts  31.3 us
    dot_general x1, matrix products, head_plan(): jnp.einsum('td,tc->dc', hidden_group, d_both, preferred_element_type=jnp....  28.7 us
    dot_general x1, matrix products, head_plan(): jnp.dot(hidden_group, cols, preferred_element_type=jnp.float32)  23.3 us
  transfers between devices with their start and end apart: 9, of which 0 were waited for; matrix products, arithmetic and copies ran while one was open for 30% of the time, Pallas kernels for 52%

profile of v11, /device:TPU:0, one launch (start us, length us, event | category | flops | bytes accessed | tf_op | source)
XLA Modules:
  0.0 854.4 jit_solution(3800528320191678872)
XLA Ops:
  7.2 1.7 convert_element_type.177
  10.4 1.5 convert_element_type.176
  13.4 1.4 pad_maximum_fusion.3.x_ref
  14.8 38.6 %shard_map.256 = bf16[8,64,1792]{2,1,0:T(8,128)(2,1)} custom-call(bf16[8,64,1792]{2,1,0:T(8,128)(2,1)} %pad_maximum_fusion.3.x_ref), custom_call_target="tpu_custom_call" | custom-call | tf_op jit(solution)/shard_map/pallas_call | solution.py:506
  55.0 108.6 %shard_map.257 = bf16[2048,2048]{1,0:T(8,128)(2,1)} custom-call(bf16[256,2048]{1,0:T(8,128)(2,1)} %x_ref), custom_call_target="tpu_custom_call" | custom-call | tf_op jit(solution)/shard_map/pallas_call | solution.py:378
  165.8 5.2 shard_map.258
  171.0 1.4 broadcast_in_dim.30.x_ref
  172.4 10.0 %shard_map.259 = bf16[8,4,16,128]{3,2,1,0:T(8,128)(2,1)} custom-call(bf16[8,4,16,128]{3,2,1,0:T(8,128)(2,1)} %broadcast_in_dim.30.x_ref), custom_call_target="tpu_custom_call" | custom-call | tf_op jit(solution)/shard_map/pallas_call | solution.py:506
  184.3 4.7 convert_reduce_fusion
  190.1 2.3 fusion.2
  195.6 23.3 %convolution_add_fusion = f32[2048,1792]{0,1:T(8,128)} fusion(bf16[2048,1792]{1,0:T(8,128)(2,1)} %all-gather.5.cloned.1.call-done, f32[1792]{0:T(1024)S(1)} %maximum_convert_fusion, bf16[2048,2048]{1,0:T(8,128)(2,1)} %shard_map.257, f32[2048]{0:T(1024)S(1)} %reshape.300, f32[2048]{0:T(1024)S(1)} %reshape.299, f32[2048]{0:T(1024)S(1)} %add_rsqrt_fusion, ...), kind=kOutput, calls=%fused_computation.10 | convolution fusion | flops 15061221376 | bytes 30448640 | tf_op jit(solution)/shard_map/dot_general | solution.py:667
  218.8 1.7 slice.195
  220.6 3.9 fusion.34
  226.4 3.5 copy.129
  229.9 3.5 copy.130
  233.5 2.1 slice.196
  235.6 2.3 fusion.35
  237.8 3.6 copy.132
  241.5 3.6 copy.133
  245.1 3.0 copy.131
  248.1 2.6 copy.134
  250.7 1.8 copy.114
  252.5 7.3 subtract_convert_fusion.2
  259.7 5.2 maximum_bitcast_fusion
  264.9 66.5 %shard_map.260 = (f32[4,2048,64]{2,1,0:T(8,128)}, f32[4,2048,1]{2,1,0:T(8,128)}) custom-call(s32[10]{0:T(128)} %constant.58.clone.qi_ref, s32[10]{0:T(128)} %constant.59.clone.kj_ref, bf16[4,2048,64]{2,1,0:T(8,128)(2,1)} %get-tuple-element.74.q_ref, bf16[4,2048,64]{2,1,0:T(8,128)(2,1)} %get-tuple-element.75.k_ref, bf16[4,2048,64]{2,1,0:T(8,128)(2,1)} %bitcast.127, ...), custom_call_target="tpu_custom_call" | custom-call | flops 2147483648 | bytes 5242880 | tf_op jit(solution)/shard_map/pallas_call | solution.py:159
  331.4 6.0 convolution_convert_fusion.2
  337.4 1.8 copy.117
  339.2 6.7 multiply_reduce_fusion
  345.9 2.1 copy.116
  348.0 7.4 fusion.38
  355.5 2.7 copy.118.delta_ref
  358.3 15.6 %convolution_convert_fusion.1 = bf16[1024,2048]{1,0:T(8,128)(2,1)} fusion(bf16[2048,2048]{1,0:T(8,128)(2,1)} %all-gather.11.cloned.1.call-done, f32[2048,1792]{0,1:T(8,128)} %convolution_add_fusion), kind=kOutput, calls=%fused_computation.35 | convolution fusion | flops 8610906112 | bytes 20971520 | tf_op jit(solution)/shard_map/tf,td->fd/dot_general | solution.py:695
  373.9 56.2 %shard_map.262 = (f32[4,2048,64]{2,1,0:T(8,128)}, f32[4,2048,64]{2,1,0:T(8,128)}, f32[4,2048,64]{2,1,0:T(8,128)}) custom-call(s32[10]{0:T(128)} %constant.60.clone.qi_ref, s32[10]{0:T(128)} %constant.61.clone.kj_ref, bf16[4,2048,64]{2,1,0:T(8,128)(2,1)} %get-tuple-element.74.q_ref, bf16[4,2048,64]{2,1,0:T(8,128)(2,1)} %get-tuple-element.75.k_ref, ...), custom_call_target="tpu_custom_call" | custom-call | flops 5368709120 | bytes 12582912 | tf_op jit(solution)/shard_map/pallas_call | solution.py:245
  430.1 3.0 slice.194
  433.7 1.9 slice.193
  435.6 4.3 add_convert_fusion.1
  439.9 3.2 pad_maximum_fusion.1
  443.1 1.9 copy.120
  445.1 5.4 pad_maximum_fusion.2
  450.5 2.7 copy.121
  453.2 2.5 convert_bitcast_fusion
  455.6 1.6 copy.122
  457.3 18.4 %convert_reduce_fusion.1 = (f32[1024]{0:T(1024)S(1)}, bf16[2048,1024]{0,1:T(8,128)(2,1)}) fusion(f32[2048,1792]{0,1:T(8,128)} %convolution_add_fusion, bf16[2048,2048]{1,0:T(8,128)(2,1)} %all-gather.11.cloned.1.call-done, bf16[1024,2048]{1,0:T(8,128)(2,1)} %all-gather.9.cloned.1.call-done), kind=kOutput, calls=%fused_computation.19 | convolution fusion | flops 8633973760 | bytes 25169920 | tf_op jit(solution)/shard_map/td,fd->tf/dot_general | solution.py:696
  475.7 28.7 %convolution_convert_fusion = bf16[2048,1792]{1,0:T(8,128)(2,1)} fusion(bf16[2048,1024]{0,1:T(8,128)(2,1)} %get-tuple-element.73, bf16[2048,256]{0,1:T(8,128)(2,1)S(1)} %bitcast.117, bf16[2048,256]{0,1:T(8,128)(2,1)S(1)} %bitcast.114, bf16[2048,256]{0,1:T(8,128)(2,1)S(1)} %bitcast.111, bf16[2048,2048]{1,0:T(8,128)(2,1)} %shard_map.257, ...), kind=kOutput, calls=%fused_computation.21 | convolution fusion | flops 15090581504 | bytes 23101440 | tf_op jit(solution)/shard_map/td,tc->dc/dot_general | solution.py:724
  506.3 16.8 %fusion.31 = f32[2048,2048]{1,0:T(8,128)} fusion(bf16[1024,2048]{1,0:T(8,128)(2,1)} %all-gather.9.cloned.1.call-done, f32[2048,1792]{0,1:T(8,128)} %convolution_add_fusion), kind=kOutput, calls=%fused_computation.107 | convolution fusion | flops 8608808960 | bytes 29360128 | tf_op jit(solution)/shard_map/dot_general | solution.py:686
  523.2 21.5 %fusion.27.p_ref = f32[2048,2048]{1,0:T(8,128)} fusion(bf16[2048,1792]{1,0:T(8,128)(2,1)} %all-gather.5.cloned.1.call-done, bf16[2048,1024]{0,1:T(8,128)(2,1)S(1)} %copy-done.32, bf16[2048,256]{0,1:T(8,128)(2,1)S(1)} %bitcast.118, bf16[2048,256]{0,1:T(8,128)(2,1)S(1)} %bitcast.115, bf16[2048,256]{0,1:T(8,128)(2,1)S(1)} %bitcast.112), kind=kOutput, calls=%fused_computation.65 | convolution fusion | flops 15061745664 | bytes 31457280 | tf_op jit(solution)/shard_map/tc,dc->td/dot_general | solution.py:722
  544.7 5.5 collective-permute-start.1
  550.2 14.4 %convolution_add_fusion.1.p_ref = f32[2048,2048]{1,0:T(8,128)} fusion(f32[2048,2048]{1,0:T(8,128)} %fusion.31, bf16[2048,256]{0,1:T(8,128)(2,1)S(1)} %bitcast.105, bf16[256,2048]{1,0:T(8,128)(2,1)} %all-gather.7.cloned.1.call-done), kind=kOutput, calls=%fused_computation.11 | convolution fusion | flops 2151677952 | bytes 35651584 | tf_op jit(solution)/shard_map/dot_general | solution.py:685
  565.5 98.3 %shard_map.263 = f32[256,2048]{1,0:T(8,128)} custom-call(f32[2048,2048]{1,0:T(8,128)} %fusion.27.p_ref), custom_call_target="tpu_custom_call" | custom-call | tf_op jit(solution)/shard_map/pallas_call | solution.py:441
  663.8 95.5 %shard_map.261 = f32[256,2048]{1,0:T(8,128)} custom-call(f32[2048,2048]{1,0:T(8,128)} %convolution_add_fusion.1.p_ref), custom_call_target="tpu_custom_call" | custom-call | tf_op jit(solution)/shard_map/pallas_call | solution.py:441
  759.4 2.8 convert_element_type.223
  762.2 25.9 %shard_map.264 = bf16[8,64,1792]{2,1,0:T(8,128)(2,1)} custom-call(bf16[8,64,1792]{2,1,0:T(8,128)(2,1)} %bitcast.130), custom_call_target="tpu_custom_call" | custom-call | tf_op jit(solution)/shard_map/pallas_call | solution.py:506
  788.1 1.5 slice_convert_fusion.5
  789.6 2.4 slice_convert_fusion.6
  792.0 2.0 reshape.306
  794.0 2.8 copy.125
  796.8 2.5 copy.140
  799.3 2.6 reshape.305
  802.9 1.6 copy.139
  805.6 3.0 convert_reduce_fusion.4
  809.7 19.8 %shard_map.265 = f32[8,4,16,128]{3,2,1,0:T(8,128)} custom-call(f32[8,4,16,128]{3,2,1,0:T(8,128)} %copy_bitcast_fusion.3.x_ref), custom_call_target="tpu_custom_call" | custom-call | tf_op jit(solution)/shard_map/pallas_call | solution.py:506
  829.5 1.6 reduce_sum.158.x_ref
  831.1 11.4 %shard_map.266 = f32[4,16,128]{2,1,0:T(8,128)} custom-call(f32[4,16,128]{2,1,0:T(8,128)} %reduce_sum.158.x_ref), custom_call_target="tpu_custom_call" | custom-call | tf_op jit(solution)/shard_map/pallas_call | solution.py:506
  845.5 1.9 copy.157
  (163 shorter events, 24.0 us)
Async XLA Ops:
  7.2 188.4 %all-gather.5.cloned.1.call-start = ((), (), s32[]{:S(2)}) async-start(), calls=%async_computation.3 | async-start | bytes 9175040 | tf_op jit(solution)/shard_map/all_gather | solution.py:591
  13.4 40.1 %copy-start.19 = (f32[64,2048]{1,0:T(8,128)S(1)}, f32[64,2048]{1,0:T(8,128)}, u32[]{:S(2)}) copy-start(f32[64,2048]{1,0:T(8,128)} %param.21) | copy-start | bytes 1572868
  53.4 278.0 %all-gather.7.cloned.1.call-start = ((), (), s32[]{:S(2)}) async-start(), calls=%async_computation.4 | async-start | bytes 1310720 | tf_op jit(solution)/shard_map/all_gather | solution.py:529
  53.5 0.7 collective-permute-start
  54.2 0.7 copy-start.20
  54.9 108.8 %copy-start.18 = (f32[256,2048]{1,0:T(8,128)S(1)}, f32[256,2048]{1,0:T(8,128)}, u32[]{:S(2)}) copy-start(f32[256,2048]{1,0:T(8,128)} %param.25) | copy-start | bytes 6291460
  54.9 276.5 %all-gather.11.cloned.1.call-start = ((), (), s32[]{:S(2)}) async-start(), calls=%async_computation.6 | async-start | bytes 9437184 | tf_op jit(solution)/shard_map/all_gather | solution.py:660
  163.6 1.4 copy-start.25
  163.6 1.4 copy-start.27
  163.6 1.4 copy-start.28
  163.7 1.4 copy-start.29
  163.7 1.4 copy-start.30
  163.7 1.4 copy-start.26
  163.7 293.5 %all-gather.9.cloned.1.call-start = ((), (), s32[]{:S(2)}) async-start(), calls=%async_computation.5 | async-start | bytes 5242880 | tf_op jit(solution)/shard_map/all_gather | solution.py:592
  164.9 379.8 %reduce-scatter.6.cloned.1.call-start = ((), (), s32[]{:S(2)}) async-start(), calls=%async_computation.8 | async-start | bytes 2621440 | tf_op jit(solution)/shard_map/reduce_scatter | solution.py:535
  184.3 5.8 copy-start
  190.1 2.5 copy-start.31
  192.9 26.0 %copy-start.21 = (s32[2048]{0:T(1024)}, s32[2048]{0:T(1024)S(1)}, u32[]{:S(2)}) copy-start(s32[2048]{0:T(1024)S(1)} %convert_reduce_fusion.5) | copy-start | bytes 24580
  252.5 7.3 copy-start.7
  252.5 7.3 copy-start.8
  348.0 7.4 copy-start.9
  355.5 403.9 %reduce-scatter.8.cloned.1.call-start = ((), (), s32[]{:S(2)}) async-start(), calls=%async_computation.9 | async-start | bytes 5242880 | tf_op jit(solution)/shard_map/reduce_scatter | solution.py:732
  373.9 388.4 %reduce-scatter.4.cloned.1.call-start = ((), (), s32[]{:S(2)}) async-start(), calls=%async_computation.7 | async-start | bytes 9175040 | tf_op jit(solution)/shard_map/reduce_scatter | solution.py:727
  430.1 3.5 copy-start.2
  430.1 5.5 copy-start.1
  439.9 5.1 copy-start.6
  457.3 18.4 %copy-start.11 = (bf16[2048,4,64]{0,2,1:T(8,128)(2,1)S(1)}, bf16[2048,4,64]{0,2,1:T(8,128)(2,1)}, u32[]{:S(2)}) copy-start(bf16[2048,4,64]{0,2,1:T(8,128)(2,1)} %copy.121) | copy-start | bytes 3145732
  457.3 18.4 %copy-start.14 = (bf16[2048,4,64]{0,2,1:T(8,128)(2,1)S(1)}, bf16[2048,4,64]{0,2,1:T(8,128)(2,1)}, u32[]{:S(2)}) copy-start(bf16[2048,4,64]{0,2,1:T(8,128)(2,1)} %copy.122) | copy-start | bytes 3145732
  504.4 0.7 copy-start.23
  504.4 0.8 copy-start.22
  504.4 1.2 copy-start.3
  506.3 16.9 %copy-start.12 = (bf16[2048,4,64]{0,2,1:T(8,128)(2,1)S(1)}, bf16[2048,4,64]{0,2,1:T(8,128)(2,1)}, u32[]{:S(2)}) copy-start(bf16[2048,4,64]{0,2,1:T(8,128)(2,1)} %copy.121) | copy-start | bytes 3145732
  506.3 16.9 %copy-start.15 = (bf16[2048,4,64]{0,2,1:T(8,128)(2,1)S(1)}, bf16[2048,4,64]{0,2,1:T(8,128)(2,1)}, u32[]{:S(2)}) copy-start(bf16[2048,4,64]{0,2,1:T(8,128)(2,1)} %copy.122) | copy-start | bytes 3145732
  506.3 16.9 %copy-start.32 = (bf16[2048,1024]{0,1:T(8,128)(2,1)S(1)}, bf16[2048,1024]{0,1:T(8,128)(2,1)}, u32[]{:S(2)}) copy-start(bf16[2048,1024]{0,1:T(8,128)(2,1)} %get-tuple-element.73) | copy-start | bytes 12582916
  523.2 27.0 %copy-start.10 = (bf16[2048,4,64]{0,2,1:T(8,128)(2,1)S(1)}, bf16[2048,4,64]{0,2,1:T(8,128)(2,1)}, u32[]{:S(2)}) copy-start(bf16[2048,4,64]{0,2,1:T(8,128)(2,1)} %copy-done.9) | copy-start | bytes 3145732
  544.7 19.9 %copy-start.13 = (bf16[2048,4,64]{0,2,1:T(8,128)(2,1)S(1)}, bf16[2048,4,64]{0,2,1:T(8,128)(2,1)}, u32[]{:S(2)}) copy-start(bf16[2048,4,64]{0,2,1:T(8,128)(2,1)} %copy.121) | copy-start | bytes 3145732
  544.7 19.9 %copy-start.16 = (bf16[2048,4,64]{0,2,1:T(8,128)(2,1)S(1)}, bf16[2048,4,64]{0,2,1:T(8,128)(2,1)}, u32[]{:S(2)}) copy-start(bf16[2048,4,64]{0,2,1:T(8,128)(2,1)} %copy.122) | copy-start | bytes 3145732
  544.7 214.7 %collective-permute-start.1 = (f32[64,2048]{1,0:T(8,128)}, f32[64,2048]{1,0:T(8,128)}, u32[]{:S(2)}, u32[]{:S(2)}) collective-permute-start(f32[64,2048]{1,0:T(8,128)} %reduce-scatter.6.cloned.1.call-done), channel_id=1, source_target_pairs={{0,0},{8,1},{16,2},{24,3},{1,4},{9,5},{17,6},{25,7},{2,8},{10,9},{... | collective-permute-start | bytes 1572872 | tf_op jit(solution)/shard_map/ppermute | solution.py:537
  801.9 2.6 copy-start.4
  801.9 3.6 copy-start.5
  801.9 3.6 copy-start.17
  843.8 3.5 copy-start.24
Sparse Core Ops, SparseCore 0:
  53.5 63.1 all-gather.4
  118.3 16.7 all-gather.6
  163.8 126.5 all-gather.10
  292.4 32.6 all-gather.8
  355.6 33.8 reduce-scatter.5
  392.0 44.5 reduce-scatter.7
  504.6 75.2 reduce-scatter.3

commit v12 on v11

--- a/solution.py
+++ b/solution.py
@@ -389,9 +389,10 @@
     )(x)
 
 
-def _scatter_kernel(p_ref, out_ref, recv_buf, send_buf, send_sem, recv_sem, *, ring, rows):
+def _scatter_kernel(p_ref, out_ref, recv_buf, send_buf, send_sem, recv_sem, *, ring, rows, parts):
     n = ring.size
     half = rows // 2
+    piece = half // parts
     g = lax.axis_index("dp")
     c = lax.axis_index("ctx")
     pos = ring.position(c)
@@ -399,12 +400,13 @@
     left = ring.device(pos + n - 1)
     _barrier(g, left, right)
 
-    def link(direction, step):
+    def link(direction, step, part):
+        window = pl.ds(part * piece, piece)
         return pltpu.make_async_remote_copy(
-            src_ref=send_buf.at[direction, step],
-            dst_ref=recv_buf.at[direction, step],
-            send_sem=send_sem.at[direction, step],
-            recv_sem=recv_sem.at[direction, step],
+            src_ref=send_buf.at[direction, step, window],
+            dst_ref=recv_buf.at[direction, step, window],
+            send_sem=send_sem.at[direction, step, part],
+            recv_sem=recv_sem.at[direction, step, part],
             device_id=(g, right if direction == 0 else left),
             device_id_type=MESH_ID,
         )
@@ -412,42 +414,48 @@
     sent = []
     for step in range(n - 1):
         targets = (ring.device(pos - 1 - step + 2 * n), ring.device(pos + 1 + step))
+        for part in range(parts):
+            for direction in (0, 1):
+                start = pl.multiple_of(
+                    targets[direction] * rows + direction * half + part * piece, piece
+                )
+                window = pl.ds(part * piece, piece)
+                total = p_ref[pl.ds(start, piece), :].astype(jnp.float32)
+                if step > 0:
+                    link(direction, step - 1, part).wait_recv()
+                    total = total + recv_buf[direction, step - 1, window].astype(jnp.float32)
+                send_buf[direction, step, window] = total.astype(send_buf.dtype)
+                copy = link(direction, step, part)
+                copy.start()
+                sent.append(copy)
+    for part in range(parts):
         for direction in (0, 1):
-            start = pl.multiple_of(targets[direction] * rows + direction * half, half)
-            total = p_ref[pl.ds(start, half), :].astype(jnp.float32)
-            if step > 0:
-                link(direction, step - 1).wait_recv()
-                total = total + recv_buf[direction, step - 1].astype(jnp.float32)
-            send_buf[direction, step] = total.astype(send_buf.dtype)
-            copy = link(direction, step)
-            copy.start()
-            sent.append(copy)
-    for direction in (0, 1):
-        link(direction, n - 2).wait_recv()
-        start = pl.multiple_of(c * rows + direction * half, half)
-        out_ref[pl.ds(direction * half, half), :] = (
-            p_ref[pl.ds(start, half), :].astype(jnp.float32)
-            + recv_buf[direction, n - 2].astype(jnp.float32)
-        ).astype(out_ref.dtype)
+            link(direction, n - 2, part).wait_recv()
+            start = pl.multiple_of(c * rows + direction * half + part * piece, piece)
+            window = pl.ds(part * piece, piece)
+            out_ref[pl.ds(direction * half + part * piece, piece), :] = (
+                p_ref[pl.ds(start, piece), :].astype(jnp.float32)
+                + recv_buf[direction, n - 2, window].astype(jnp.float32)
+            ).astype(out_ref.dtype)
     for copy in sent:
         copy.wait_send()
 
 
-def ring_reduce_scatter(p, ring, collective_id, out_dtype=jnp.float32, wire=jnp.bfloat16):
+def ring_reduce_scatter(p, ring, collective_id, out_dtype=jnp.float32, wire=jnp.bfloat16, parts=2):
     total_rows, cols = p.shape
     n = ring.size
     rows = total_rows // n
     half = rows // 2
     return pl.pallas_call(
-        functools.partial(_scatter_kernel, ring=ring, rows=rows),
+        functools.partial(_scatter_kernel, ring=ring, rows=rows, parts=parts),
         out_shape=jax.ShapeDtypeStruct((rows, cols), out_dtype),
         in_specs=[pl.BlockSpec(memory_space=pltpu.VMEM)],
         out_specs=pl.BlockSpec(memory_space=pltpu.VMEM),
         scratch_shapes=[
             pltpu.VMEM((2, n - 1, half, cols), wire),
             pltpu.VMEM((2, n - 1, half, cols), wire),
-            pltpu.SemaphoreType.DMA((2, n - 1)),
-            pltpu.SemaphoreType.DMA((2, n - 1)),
+            pltpu.SemaphoreType.DMA((2, n - 1, parts)),
+            pltpu.SemaphoreType.DMA((2, n - 1, parts)),
         ],
         compiler_params=pltpu.CompilerParams(
             collective_id=collective_id, has_side_effects=True, vmem_limit_bytes=60 * 1024 * 1024

time: 860 us -> 858 us (level)
  transfers between devices with their start and end apart: 9 -> 9, of which waited for: 0 -> 0; matrix products, arithmetic and copies ran while one was open for 30% -> 30% of each run, Pallas kernels for 52% -> 51%
where the time goes in v12:
time: 858 us; the launch traced here: 852 us
  Pallas kernels  534 us (62%)
  matrix products  152 us (18%)
  local copies, waits for them, and re-layouts  81.1 us (9%)
  other arithmetic  63.4 us (7%)
  between operations  15.2 us (2%)
    pallas_call x2, Pallas kernels, ring_reduce_scatter(): pl.pallas_call(functools.partial(_scatter_kernel, ring=ring, rows=rows, p...  187 us
    pallas_call x6, Pallas kernels, exchange(): pl.pallas_call(functools.partial(_exchange_kernel, group=group), out_shap...  116 us
    pallas_call x1, Pallas kernels, ring_all_gather(): pl.pallas_call(functools.partial(_gather_kernel, ring=ring, rows=rows), o...  109 us
    pallas_call x1, Pallas kernels, attention_forward(): pl.pallas_call(functools.partial(_fwd_kernel, tq=block, tk=block, scale=s...  66.5 us
    pallas_call x1, Pallas kernels, attention_backward(): pl.pallas_call(functools.partial(_bwd_kernel, tq=block, tk=block, scale=s...  56.2 us
    unnamed x82, local copies, waits for them, and re-layouts  31.3 us
    dot_general x1, matrix products, head_plan(): jnp.einsum('td,tc->dc', hidden_group, d_both, preferred_element_type=jnp....  28.7 us
    dot_general x1, matrix products, head_plan(): jnp.dot(hidden_group, cols, preferred_element_type=jnp.float32)  23.3 us
  transfers between devices with their start and end apart: 9, of which 0 were waited for; matrix products, arithmetic and copies ran while one was open for 30% of the time, Pallas kernels for 51%

profile of v12, /device:TPU:0, one launch (start us, length us, event | category | flops | bytes accessed | tf_op | source)
XLA Modules:
  0.0 852.5 jit_solution(10096347364759067252)
XLA Ops:
  7.2 1.7 convert_element_type.177
  10.4 1.5 convert_element_type.176
  13.4 1.4 pad_maximum_fusion.3.x_ref
  14.8 38.6 %shard_map.256 = bf16[8,64,1792]{2,1,0:T(8,128)(2,1)} custom-call(bf16[8,64,1792]{2,1,0:T(8,128)(2,1)} %pad_maximum_fusion.3.x_ref), custom_call_target="tpu_custom_call" | custom-call | tf_op jit(solution)/shard_map/pallas_call | solution.py:514
  55.0 108.6 %shard_map.257 = bf16[2048,2048]{1,0:T(8,128)(2,1)} custom-call(bf16[256,2048]{1,0:T(8,128)(2,1)} %x_ref), custom_call_target="tpu_custom_call" | custom-call | tf_op jit(solution)/shard_map/pallas_call | solution.py:378
  165.8 5.2 shard_map.258
  171.0 1.4 broadcast_in_dim.30.x_ref
  172.4 10.0 %shard_map.259 = bf16[8,4,16,128]{3,2,1,0:T(8,128)(2,1)} custom-call(bf16[8,4,16,128]{3,2,1,0:T(8,128)(2,1)} %broadcast_in_dim.30.x_ref), custom_call_target="tpu_custom_call" | custom-call | tf_op jit(solution)/shard_map/pallas_call | solution.py:514
  184.3 4.7 convert_reduce_fusion
  190.1 2.3 fusion.2
  195.6 23.3 %convolution_add_fusion = f32[2048,1792]{0,1:T(8,128)} fusion(bf16[2048,1792]{1,0:T(8,128)(2,1)} %all-gather.5.cloned.1.call-done, f32[1792]{0:T(1024)S(1)} %maximum_convert_fusion, bf16[2048,2048]{1,0:T(8,128)(2,1)} %shard_map.257, f32[2048]{0:T(1024)S(1)} %reshape.300, f32[2048]{0:T(1024)S(1)} %reshape.299, f32[2048]{0:T(1024)S(1)} %add_rsqrt_fusion, ...), kind=kOutput, calls=%fused_computation.10 | convolution fusion | flops 15061221376 | bytes 30448640 | tf_op jit(solution)/shard_map/dot_general | solution.py:675
  218.8 1.7 slice.195
  220.6 3.9 fusion.34
  226.4 3.5 copy.129
  229.9 3.5 copy.130
  233.5 2.1 slice.196
  235.6 2.3 fusion.35
  237.8 3.6 copy.132
  241.5 3.6 copy.133
  245.1 3.0 copy.131
  248.1 2.6 copy.134
  250.7 1.8 copy.114
  252.5 7.3 subtract_convert_fusion.2
  259.7 5.2 maximum_bitcast_fusion
  264.9 66.5 %shard_map.260 = (f32[4,2048,64]{2,1,0:T(8,128)}, f32[4,2048,1]{2,1,0:T(8,128)}) custom-call(s32[10]{0:T(128)} %constant.58.clone.qi_ref, s32[10]{0:T(128)} %constant.59.clone.kj_ref, bf16[4,2048,64]{2,1,0:T(8,128)(2,1)} %get-tuple-element.74.q_ref, bf16[4,2048,64]{2,1,0:T(8,128)(2,1)} %get-tuple-element.75.k_ref, bf16[4,2048,64]{2,1,0:T(8,128)(2,1)} %bitcast.127, ...), custom_call_target="tpu_custom_call" | custom-call | flops 2147483648 | bytes 5242880 | tf_op jit(solution)/shard_map/pallas_call | solution.py:159
  331.4 6.0 convolution_convert_fusion.2
  337.4 1.8 copy.117
  339.2 6.7 multiply_reduce_fusion
  345.9 2.1 copy.116
  348.0 7.4 fusion.38
  355.5 2.7 copy.118.delta_ref
  358.3 15.6 %convolution_convert_fusion.1 = bf16[1024,2048]{1,0:T(8,128)(2,1)} fusion(bf16[2048,2048]{1,0:T(8,128)(2,1)} %all-gather.11.cloned.1.call-done, f32[2048,1792]{0,1:T(8,128)} %convolution_add_fusion), kind=kOutput, calls=%fused_computation.35 | convolution fusion | flops 8610906112 | bytes 20971520 | tf_op jit(solution)/shard_map/tf,td->fd/dot_general | solution.py:703
  373.9 56.2 %shard_map.262 = (f32[4,2048,64]{2,1,0:T(8,128)}, f32[4,2048,64]{2,1,0:T(8,128)}, f32[4,2048,64]{2,1,0:T(8,128)}) custom-call(s32[10]{0:T(128)} %constant.60.clone.qi_ref, s32[10]{0:T(128)} %constant.61.clone.kj_ref, bf16[4,2048,64]{2,1,0:T(8,128)(2,1)} %get-tuple-element.74.q_ref, bf16[4,2048,64]{2,1,0:T(8,128)(2,1)} %get-tuple-element.75.k_ref, ...), custom_call_target="tpu_custom_call" | custom-call | flops 5368709120 | bytes 12582912 | tf_op jit(solution)/shard_map/pallas_call | solution.py:245
  430.1 3.0 slice.194
  433.7 1.9 slice.193
  435.6 4.3 add_convert_fusion.1
  439.9 3.2 pad_maximum_fusion.1
  443.1 1.9 copy.120
  445.1 5.4 pad_maximum_fusion.2
  450.5 2.7 copy.121
  453.2 2.5 convert_bitcast_fusion
  455.6 1.6 copy.122
  457.3 18.4 %convert_reduce_fusion.1 = (f32[1024]{0:T(1024)S(1)}, bf16[2048,1024]{0,1:T(8,128)(2,1)}) fusion(f32[2048,1792]{0,1:T(8,128)} %convolution_add_fusion, bf16[2048,2048]{1,0:T(8,128)(2,1)} %all-gather.11.cloned.1.call-done, bf16[1024,2048]{1,0:T(8,128)(2,1)} %all-gather.9.cloned.1.call-done), kind=kOutput, calls=%fused_computation.19 | convolution fusion | flops 8633973760 | bytes 25169920 | tf_op jit(solution)/shard_map/td,fd->tf/dot_general | solution.py:704
  475.7 28.7 %convolution_convert_fusion = bf16[2048,1792]{1,0:T(8,128)(2,1)} fusion(bf16[2048,1024]{0,1:T(8,128)(2,1)} %get-tuple-element.73, bf16[2048,256]{0,1:T(8,128)(2,1)S(1)} %bitcast.117, bf16[2048,256]{0,1:T(8,128)(2,1)S(1)} %bitcast.114, bf16[2048,256]{0,1:T(8,128)(2,1)S(1)} %bitcast.111, bf16[2048,2048]{1,0:T(8,128)(2,1)} %shard_map.257, ...), kind=kOutput, calls=%fused_computation.21 | convolution fusion | flops 15090581504 | bytes 23101440 | tf_op jit(solution)/shard_map/td,tc->dc/dot_general | solution.py:732
  506.3 16.8 %fusion.31 = f32[2048,2048]{1,0:T(8,128)} fusion(bf16[1024,2048]{1,0:T(8,128)(2,1)} %all-gather.9.cloned.1.call-done, f32[2048,1792]{0,1:T(8,128)} %convolution_add_fusion), kind=kOutput, calls=%fused_computation.107 | convolution fusion | flops 8608808960 | bytes 29360128 | tf_op jit(solution)/shard_map/dot_general | solution.py:694
  523.2 21.5 %fusion.27.p_ref = f32[2048,2048]{1,0:T(8,128)} fusion(bf16[2048,1792]{1,0:T(8,128)(2,1)} %all-gather.5.cloned.1.call-done, bf16[2048,1024]{0,1:T(8,128)(2,1)S(1)} %copy-done.32, bf16[2048,256]{0,1:T(8,128)(2,1)S(1)} %bitcast.118, bf16[2048,256]{0,1:T(8,128)(2,1)S(1)} %bitcast.115, bf16[2048,256]{0,1:T(8,128)(2,1)S(1)} %bitcast.112), kind=kOutput, calls=%fused_computation.65 | convolution fusion | flops 15061745664 | bytes 31457280 | tf_op jit(solution)/shard_map/tc,dc->td/dot_general | solution.py:730
  544.7 5.5 collective-permute-start.1
  550.2 14.4 %convolution_add_fusion.1.p_ref = f32[2048,2048]{1,0:T(8,128)} fusion(f32[2048,2048]{1,0:T(8,128)} %fusion.31, bf16[2048,256]{0,1:T(8,128)(2,1)S(1)} %bitcast.105, bf16[256,2048]{1,0:T(8,128)(2,1)} %all-gather.7.cloned.1.call-done), kind=kOutput, calls=%fused_computation.11 | convolution fusion | flops 2151677952 | bytes 35651584 | tf_op jit(solution)/shard_map/dot_general | solution.py:693
  565.5 98.5 %shard_map.263 = f32[256,2048]{1,0:T(8,128)} custom-call(f32[2048,2048]{1,0:T(8,128)} %fusion.27.p_ref), custom_call_target="tpu_custom_call" | custom-call | tf_op jit(solution)/shard_map/pallas_call | solution.py:449
  664.0 88.3 %shard_map.261 = f32[256,2048]{1,0:T(8,128)} custom-call(f32[2048,2048]{1,0:T(8,128)} %convolution_add_fusion.1.p_ref), custom_call_target="tpu_custom_call" | custom-call | tf_op jit(solution)/shard_map/pallas_call | solution.py:449
  752.4 2.8 convert_element_type.223
  755.2 32.7 %shard_map.264 = bf16[8,64,1792]{2,1,0:T(8,128)(2,1)} custom-call(bf16[8,64,1792]{2,1,0:T(8,128)(2,1)} %bitcast.130), custom_call_target="tpu_custom_call" | custom-call | tf_op jit(solution)/shard_map/pallas_call | solution.py:514
  787.9 1.5 slice_convert_fusion.5
  789.4 2.4 slice_convert_fusion.6
  791.8 2.0 reshape.306
  793.8 2.8 copy.125
  796.6 2.5 copy.140
  799.1 2.6 reshape.305
  802.6 1.6 copy.139
  805.4 3.0 convert_reduce_fusion.4
  809.4 19.7 %shard_map.265 = f32[8,4,16,128]{3,2,1,0:T(8,128)} custom-call(f32[8,4,16,128]{3,2,1,0:T(8,128)} %copy_bitcast_fusion.3.x_ref), custom_call_target="tpu_custom_call" | custom-call | tf_op jit(solution)/shard_map/pallas_call | solution.py:514
  829.1 1.6 reduce_sum.158.x_ref
  830.7 9.8 %shard_map.266 = f32[4,16,128]{2,1,0:T(8,128)} custom-call(f32[4,16,128]{2,1,0:T(8,128)} %reduce_sum.158.x_ref), custom_call_target="tpu_custom_call" | custom-call | tf_op jit(solution)/shard_map/pallas_call | solution.py:514
  843.5 1.9 copy.157
  (163 shorter events, 24.0 us)
Async XLA Ops:
  7.2 188.4 %all-gather.5.cloned.1.call-start = ((), (), s32[]{:S(2)}) async-start(), calls=%async_computation.3 | async-start | bytes 9175040 | tf_op jit(solution)/shard_map/all_gather | solution.py:599
  13.4 40.1 %copy-start.19 = (f32[64,2048]{1,0:T(8,128)S(1)}, f32[64,2048]{1,0:T(8,128)}, u32[]{:S(2)}) copy-start(f32[64,2048]{1,0:T(8,128)} %param.21) | copy-start | bytes 1572868
  53.4 278.0 %all-gather.7.cloned.1.call-start = ((), (), s32[]{:S(2)}) async-start(), calls=%async_computation.4 | async-start | bytes 1310720 | tf_op jit(solution)/shard_map/all_gather | solution.py:537
  53.5 0.7 collective-permute-start
  54.2 0.7 copy-start.20
  54.9 108.8 %copy-start.18 = (f32[256,2048]{1,0:T(8,128)S(1)}, f32[256,2048]{1,0:T(8,128)}, u32[]{:S(2)}) copy-start(f32[256,2048]{1,0:T(8,128)} %param.25) | copy-start | bytes 6291460
  54.9 276.5 %all-gather.11.cloned.1.call-start = ((), (), s32[]{:S(2)}) async-start(), calls=%async_computation.6 | async-start | bytes 9437184 | tf_op jit(solution)/shard_map/all_gather | solution.py:668
  163.6 1.4 copy-start.25
  163.6 1.4 copy-start.27
  163.6 1.4 copy-start.28
  163.7 1.4 copy-start.29
  163.7 1.4 copy-start.30
  163.7 1.4 copy-start.26
  163.7 293.5 %all-gather.9.cloned.1.call-start = ((), (), s32[]{:S(2)}) async-start(), calls=%async_computation.5 | async-start | bytes 5242880 | tf_op jit(solution)/shard_map/all_gather | solution.py:600
  164.9 379.8 %reduce-scatter.6.cloned.1.call-start = ((), (), s32[]{:S(2)}) async-start(), calls=%async_computation.8 | async-start | bytes 2621440 | tf_op jit(solution)/shard_map/reduce_scatter | solution.py:543
  184.3 5.8 copy-start
  190.1 2.5 copy-start.31
  192.9 26.0 %copy-start.21 = (s32[2048]{0:T(1024)}, s32[2048]{0:T(1024)S(1)}, u32[]{:S(2)}) copy-start(s32[2048]{0:T(1024)S(1)} %convert_reduce_fusion.5) | copy-start | bytes 24580
  252.5 7.3 copy-start.7
  252.5 7.3 copy-start.8
  348.0 7.4 copy-start.9
  355.5 396.9 %reduce-scatter.8.cloned.1.call-start = ((), (), s32[]{:S(2)}) async-start(), calls=%async_computation.9 | async-start | bytes 5242880 | tf_op jit(solution)/shard_map/reduce_scatter | solution.py:740
  373.9 381.4 %reduce-scatter.4.cloned.1.call-start = ((), (), s32[]{:S(2)}) async-start(), calls=%async_computation.7 | async-start | bytes 9175040 | tf_op jit(solution)/shard_map/reduce_scatter | solution.py:735
  430.1 3.5 copy-start.2
  430.1 5.5 copy-start.1
  439.9 5.1 copy-start.6
  457.3 18.4 %copy-start.11 = (bf16[2048,4,64]{0,2,1:T(8,128)(2,1)S(1)}, bf16[2048,4,64]{0,2,1:T(8,128)(2,1)}, u32[]{:S(2)}) copy-start(bf16[2048,4,64]{0,2,1:T(8,128)(2,1)} %copy.121) | copy-start | bytes 3145732
  457.3 18.4 %copy-start.14 = (bf16[2048,4,64]{0,2,1:T(8,128)(2,1)S(1)}, bf16[2048,4,64]{0,2,1:T(8,128)(2,1)}, u32[]{:S(2)}) copy-start(bf16[2048,4,64]{0,2,1:T(8,128)(2,1)} %copy.122) | copy-start | bytes 3145732
  504.4 0.7 copy-start.23
  504.4 0.8 copy-start.22
  504.4 1.2 copy-start.3
  506.3 16.9 %copy-start.12 = (bf16[2048,4,64]{0,2,1:T(8,128)(2,1)S(1)}, bf16[2048,4,64]{0,2,1:T(8,128)(2,1)}, u32[]{:S(2)}) copy-start(bf16[2048,4,64]{0,2,1:T(8,128)(2,1)} %copy.121) | copy-start | bytes 3145732
  506.3 16.9 %copy-start.15 = (bf16[2048,4,64]{0,2,1:T(8,128)(2,1)S(1)}, bf16[2048,4,64]{0,2,1:T(8,128)(2,1)}, u32[]{:S(2)}) copy-start(bf16[2048,4,64]{0,2,1:T(8,128)(2,1)} %copy.122) | copy-start | bytes 3145732
  506.3 16.9 %copy-start.32 = (bf16[2048,1024]{0,1:T(8,128)(2,1)S(1)}, bf16[2048,1024]{0,1:T(8,128)(2,1)}, u32[]{:S(2)}) copy-start(bf16[2048,1024]{0,1:T(8,128)(2,1)} %get-tuple-element.73) | copy-start | bytes 12582916
  523.2 27.0 %copy-start.10 = (bf16[2048,4,64]{0,2,1:T(8,128)(2,1)S(1)}, bf16[2048,4,64]{0,2,1:T(8,128)(2,1)}, u32[]{:S(2)}) copy-start(bf16[2048,4,64]{0,2,1:T(8,128)(2,1)} %copy-done.9) | copy-start | bytes 3145732
  544.7 19.9 %copy-start.13 = (bf16[2048,4,64]{0,2,1:T(8,128)(2,1)S(1)}, bf16[2048,4,64]{0,2,1:T(8,128)(2,1)}, u32[]{:S(2)}) copy-start(bf16[2048,4,64]{0,2,1:T(8,128)(2,1)} %copy.121) | copy-start | bytes 3145732
  544.7 19.9 %copy-start.16 = (bf16[2048,4,64]{0,2,1:T(8,128)(2,1)S(1)}, bf16[2048,4,64]{0,2,1:T(8,128)(2,1)}, u32[]{:S(2)}) copy-start(bf16[2048,4,64]{0,2,1:T(8,128)(2,1)} %copy.122) | copy-start | bytes 3145732
  544.7 207.7 %collective-permute-start.1 = (f32[64,2048]{1,0:T(8,128)}, f32[64,2048]{1,0:T(8,128)}, u32[]{:S(2)}, u32[]{:S(2)}) collective-permute-start(f32[64,2048]{1,0:T(8,128)} %reduce-scatter.6.cloned.1.call-done), channel_id=1, source_target_pairs={{0,0},{8,1},{16,2},{24,3},{1,4},{9,5},{17,6},{25,7},{2,8},{10,9},{... | collective-permute-start | bytes 1572872 | tf_op jit(solution)/shard_map/ppermute | solution.py:545
  801.7 2.6 copy-start.4
  801.7 3.6 copy-start.5
  801.7 3.6 copy-start.17
  841.9 3.5 copy-start.24
Sparse Core Ops, SparseCore 0:
  53.5 63.1 all-gather.4
  118.3 16.7 all-gather.6
  163.8 126.5 all-gather.10
  292.4 32.6 all-gather.8
  355.6 33.8 reduce-scatter.5
  392.0 44.5 reduce-scatter.7
  504.6 75.2 reduce-scatter.3

commit v13 on v12

--- a/solution.py
+++ b/solution.py
@@ -98,15 +98,15 @@
     return same & (cols <= rows)
 
 
-def _fwd_kernel(qi_ref, kj_ref, q_ref, k_ref, v_ref, segq_ref, segk_ref, o_ref, lse_ref, m_sc, l_sc, acc_sc, *, tq, tk, scale):
+def _fwd_kernel(qi_ref, kj_ref, q_ref, k_ref, v_ref, segq_ref, segk_ref, o_ref, lse_ref, m_sc, acc_sc, *, tq, tk, scale):
     t = pl.program_id(1)
     i = qi_ref[t]
     j = kj_ref[t]
+    dim = o_ref.shape[2]
 
     @pl.when(j == 0)
     def _():
         m_sc[...] = jnp.full_like(m_sc, NEGATIVE)
-        l_sc[...] = jnp.zeros_like(l_sc)
         acc_sc[...] = jnp.zeros_like(acc_sc)
 
     def absorb(causal):
@@ -118,7 +118,6 @@
         m_new = jnp.maximum(m_prev, jnp.max(s, axis=1, keepdims=True))
         factor = jnp.exp(m_prev - m_new)
         p = jnp.exp(s - m_new)
-        l_sc[...] = l_sc[...] * factor + jnp.sum(p, axis=1, keepdims=True)
         acc_sc[...] = acc_sc[...] * factor + jnp.dot(
             p.astype(jnp.bfloat16), v_ref[0], preferred_element_type=jnp.float32
         )
@@ -131,8 +130,9 @@
     @pl.when(j == i)
     def _():
         absorb(True)
-        total = l_sc[...]
-        o_ref[0] = acc_sc[...] / total
+        acc = acc_sc[...]
+        total = acc[:, dim : dim + 1]
+        o_ref[0] = acc[:, :dim] / total
         lse_ref[0] = m_sc[...] + jnp.log(total)
 
 
@@ -155,6 +155,11 @@
     segk = seg.reshape(1, total)
     qi, kj = _schedule(count, True)
     steps = qi.shape[0]
+    lanes = 2 * dim
+    v_ext = jnp.concatenate(
+        [v, jnp.ones((heads, total, 1), v.dtype), jnp.zeros((heads, total, lanes - dim - 1), v.dtype)],
+        axis=2,
+    )
 
     return pl.pallas_call(
         functools.partial(_fwd_kernel, tq=block, tk=block, scale=scale),
@@ -168,7 +173,7 @@
             in_specs=[
                 pl.BlockSpec((1, block, dim), lambda h, t, qi, kj: (h, qi[t], 0)),
                 pl.BlockSpec((1, block, dim), lambda h, t, qi, kj: (h, kj[t], 0)),
-                pl.BlockSpec((1, block, dim), lambda h, t, qi, kj: (h, kj[t], 0)),
+                pl.BlockSpec((1, block, lanes), lambda h, t, qi, kj: (h, kj[t], 0)),
                 pl.BlockSpec((block, 1), lambda h, t, qi, kj: (qi[t], 0)),
                 pl.BlockSpec((1, block), lambda h, t, qi, kj: (0, kj[t])),
             ],
@@ -178,8 +183,7 @@
             ],
             scratch_shapes=[
                 pltpu.VMEM((block, 1), jnp.float32),
-                pltpu.VMEM((block, 1), jnp.float32),
-                pltpu.VMEM((block, dim), jnp.float32),
+                pltpu.VMEM((block, lanes), jnp.float32),
             ],
         ),
         cost_estimate=pl.CostEstimate(
@@ -187,7 +191,7 @@
             transcendentals=heads * total * total // 2,
             bytes_accessed=heads * total * dim * 10,
         ),
-    )(qi, kj, q, k, v, segq, segk)
+    )(qi, kj, q, k, v_ext, segq, segk)
 
 
 def _bwd_kernel(qi_ref, kj_ref, q_ref, k_ref, v_ref, do_ref, lse_ref, delta_ref, segq_ref, segk_ref, dq_ref, dk_ref, dv_ref, *, tq, tk, scale):

time: 858 us -> 842 us (0.981)
  Pallas kernels: 534 us -> 515 us
    pallas_call x1, Pallas kernels: 66.5 us -> 48 us  [attention_forward(): pl.pallas_call(functools.partial(_fwd_kernel, tq=block, tk=block, scale=s...]
    unnamed x82 -> x84, local copies, waits for them, and re-layouts: 31.3 us -> 31.3 us
  transfers between devices with their start and end apart: 9 -> 9, of which waited for: 0 -> 0; matrix products, arithmetic and copies ran while one was open for 30% -> 31% of each run, Pallas kernels for 51% -> 50%
where the time goes in v13:
time: 842 us; the launch traced here: 836 us
  Pallas kernels  515 us (61%)
  matrix products  152 us (18%)
  local copies, waits for them, and re-layouts  81.3 us (10%)
  other arithmetic  65.5 us (8%)
  between operations  15.2 us (2%)
    pallas_call x2, Pallas kernels, ring_reduce_scatter(): pl.pallas_call(functools.partial(_scatter_kernel, ring=ring, rows=rows, p...  186 us
    pallas_call x6, Pallas kernels, exchange(): pl.pallas_call(functools.partial(_exchange_kernel, group=group), out_shap...  116 us
    pallas_call x1, Pallas kernels, ring_all_gather(): pl.pallas_call(functools.partial(_gather_kernel, ring=ring, rows=rows), o...  109 us
    pallas_call x1, Pallas kernels, attention_backward(): pl.pallas_call(functools.partial(_bwd_kernel, tq=block, tk=block, scale=s...  56.3 us
    pallas_call x1, Pallas kernels, attention_forward(): pl.pallas_call(functools.partial(_fwd_kernel, tq=block, tk=block, scale=s...  48 us
    unnamed x84, local copies, waits for them, and re-layouts  31.3 us
    dot_general x1, matrix products, head_plan(): jnp.einsum('td,tc->dc', hidden_group, d_both, preferred_element_type=jnp....  28.7 us
    dot_general x1, matrix products, head_plan(): jnp.dot(hidden_group, cols, preferred_element_type=jnp.float32)  23.2 us
  transfers between devices with their start and end apart: 9, of which 0 were waited for; matrix products, arithmetic and copies ran while one was open for 31% of the time, Pallas kernels for 50%

profile of v13, /device:TPU:0, one launch (start us, length us, event | category | flops | bytes accessed | tf_op | source)
XLA Modules:
  0.0 836.1 jit_solution(5719140751304889126)
XLA Ops:
  7.2 1.7 convert_element_type.177
  10.4 1.5 convert_element_type.176
  14.8 38.6 %shard_map.256 = bf16[8,64,1792]{2,1,0:T(8,128)(2,1)} custom-call(bf16[8,64,1792]{2,1,0:T(8,128)(2,1)} %pad_maximum_fusion.3.x_ref), custom_call_target="tpu_custom_call" | custom-call | tf_op jit(solution)/shard_map/pallas_call | solution.py:518
  55.0 108.6 %shard_map.257 = bf16[2048,2048]{1,0:T(8,128)(2,1)} custom-call(bf16[256,2048]{1,0:T(8,128)(2,1)} %x_ref), custom_call_target="tpu_custom_call" | custom-call | tf_op jit(solution)/shard_map/pallas_call | solution.py:382
  166.0 5.0 shard_map.258
  171.0 1.4 broadcast_in_dim.34.x_ref
  172.4 10.0 %shard_map.259 = bf16[8,4,16,128]{3,2,1,0:T(8,128)(2,1)} custom-call(bf16[8,4,16,128]{3,2,1,0:T(8,128)(2,1)} %broadcast_in_dim.34.x_ref), custom_call_target="tpu_custom_call" | custom-call | tf_op jit(solution)/shard_map/pallas_call | solution.py:518
  184.3 4.7 convert_reduce_fusion
  190.2 2.3 fusion.2
  195.8 23.2 %convolution_add_fusion = f32[2048,1792]{0,1:T(8,128)} fusion(bf16[2048,1792]{1,0:T(8,128)(2,1)} %all-gather.5.cloned.1.call-done, f32[1792]{0:T(1024)S(1)} %maximum_convert_fusion, bf16[2048,2048]{1,0:T(8,128)(2,1)} %shard_map.257, f32[2048]{0:T(1024)S(1)} %reshape.300, f32[2048]{0:T(1024)S(1)} %reshape.299, f32[2048]{0:T(1024)S(1)} %add_rsqrt_fusion, ...), kind=kOutput, calls=%fused_computation.10 | convolution fusion | flops 15061221376 | bytes 30448640 | tf_op jit(solution)/shard_map/dot_general | solution.py:679
  219.0 1.7 slice.195
  220.7 3.9 fusion.34
  226.5 3.5 copy.129
  230.1 3.5 copy.130
  233.6 2.1 slice.196
  235.7 2.3 fusion.35
  238.0 3.7 copy.132
  241.6 3.6 copy.133
  245.2 3.0 copy.131
  248.2 2.6 copy.134
  250.8 1.8 copy.114
  252.6 7.3 subtract_convert_fusion.2
  259.9 5.2 maximum_bitcast_fusion
  265.1 2.0 maximum_maximum_fusion.v_ref
  267.1 48.0 %shard_map.260 = (f32[4,2048,64]{2,1,0:T(8,128)}, f32[4,2048,1]{2,1,0:T(8,128)}) custom-call(s32[10]{0:T(128)} %constant.61.clone.qi_ref, s32[10]{0:T(128)} %constant.62.clone.kj_ref, bf16[4,2048,64]{2,1,0:T(8,128)(2,1)} %get-tuple-element.74.q_ref, bf16[4,2048,64]{2,1,0:T(8,128)(2,1)} %get-tuple-element.75.k_ref, ...), custom_call_target="tpu_custom_call" | custom-call | flops 2147483648 | bytes 5242880 | tf_op jit(solution)/shard_map/pallas_call | solution.py:164
  315.1 6.0 convolution_convert_fusion.2
  321.2 1.8 copy.117
  323.0 6.8 multiply_reduce_fusion
  329.7 2.1 copy.116
  331.8 7.4 fusion.38
  339.3 2.8 copy.118.delta_ref
  342.1 15.6 %convolution_convert_fusion.1 = bf16[1024,2048]{1,0:T(8,128)(2,1)} fusion(bf16[2048,2048]{1,0:T(8,128)(2,1)} %all-gather.11.cloned.1.call-done, f32[2048,1792]{0,1:T(8,128)} %convolution_add_fusion), kind=kOutput, calls=%fused_computation.35 | convolution fusion | flops 8610906112 | bytes 20971520 | tf_op jit(solution)/shard_map/tf,td->fd/dot_general | solution.py:707
  357.7 56.3 %shard_map.262 = (f32[4,2048,64]{2,1,0:T(8,128)}, f32[4,2048,64]{2,1,0:T(8,128)}, f32[4,2048,64]{2,1,0:T(8,128)}) custom-call(s32[10]{0:T(128)} %constant.63.clone.qi_ref, s32[10]{0:T(128)} %constant.64.clone.kj_ref, bf16[4,2048,64]{2,1,0:T(8,128)(2,1)} %get-tuple-element.74.q_ref, bf16[4,2048,64]{2,1,0:T(8,128)(2,1)} %get-tuple-element.75.k_ref, ...), custom_call_target="tpu_custom_call" | custom-call | flops 5368709120 | bytes 12582912 | tf_op jit(solution)/shard_map/pallas_call | solution.py:249
  414.0 3.0 slice.194
  417.5 1.9 slice.193
  419.5 4.3 add_convert_fusion.1
  423.8 3.2 pad_maximum_fusion.1
  427.0 1.9 copy.120
  428.9 5.4 pad_maximum_fusion.2
  434.4 2.7 copy.121
  437.0 2.5 convert_bitcast_fusion
  439.5 1.6 copy.122
  441.1 18.4 %convert_reduce_fusion.1 = (f32[1024]{0:T(1024)S(1)}, bf16[2048,1024]{0,1:T(8,128)(2,1)}) fusion(f32[2048,1792]{0,1:T(8,128)} %convolution_add_fusion, bf16[2048,2048]{1,0:T(8,128)(2,1)} %all-gather.11.cloned.1.call-done, bf16[1024,2048]{1,0:T(8,128)(2,1)} %all-gather.9.cloned.1.call-done), kind=kOutput, calls=%fused_computation.19 | convolution fusion | flops 8633973760 | bytes 25169920 | tf_op jit(solution)/shard_map/td,fd->tf/dot_general | solution.py:708
  459.5 28.7 %convolution_convert_fusion = bf16[2048,1792]{1,0:T(8,128)(2,1)} fusion(bf16[2048,1024]{0,1:T(8,128)(2,1)} %get-tuple-element.73, bf16[2048,256]{0,1:T(8,128)(2,1)S(1)} %bitcast.120, bf16[2048,256]{0,1:T(8,128)(2,1)S(1)} %bitcast.117, bf16[2048,256]{0,1:T(8,128)(2,1)S(1)} %bitcast.114, bf16[2048,2048]{1,0:T(8,128)(2,1)} %shard_map.257, ...), kind=kOutput, calls=%fused_computation.21 | convolution fusion | flops 15090581504 | bytes 23101440 | tf_op jit(solution)/shard_map/td,tc->dc/dot_general | solution.py:736
  490.2 16.8 %fusion.31 = f32[2048,2048]{1,0:T(8,128)} fusion(bf16[1024,2048]{1,0:T(8,128)(2,1)} %all-gather.9.cloned.1.call-done, f32[2048,1792]{0,1:T(8,128)} %convolution_add_fusion), kind=kOutput, calls=%fused_computation.108 | convolution fusion | flops 8608808960 | bytes 29360128 | tf_op jit(solution)/shard_map/dot_general | solution.py:698
  507.0 21.4 %fusion.27.p_ref = f32[2048,2048]{1,0:T(8,128)} fusion(bf16[2048,1792]{1,0:T(8,128)(2,1)} %all-gather.5.cloned.1.call-done, bf16[2048,1024]{0,1:T(8,128)(2,1)S(1)} %copy-done.33, bf16[2048,256]{0,1:T(8,128)(2,1)S(1)} %bitcast.121, bf16[2048,256]{0,1:T(8,128)(2,1)S(1)} %bitcast.118, bf16[2048,256]{0,1:T(8,128)(2,1)S(1)} %bitcast.115), kind=kOutput, calls=%fused_computation.66 | convolution fusion | flops 15061745664 | bytes 31457280 | tf_op jit(solution)/shard_map/tc,dc->td/dot_general | solution.py:734
  528.4 5.5 collective-permute-start.1
  533.9 14.4 %convolution_add_fusion.1.p_ref = f32[2048,2048]{1,0:T(8,128)} fusion(f32[2048,2048]{1,0:T(8,128)} %fusion.31, bf16[2048,256]{0,1:T(8,128)(2,1)S(1)} %bitcast.108, bf16[256,2048]{1,0:T(8,128)(2,1)} %all-gather.7.cloned.1.call-done), kind=kOutput, calls=%fused_computation.11 | convolution fusion | flops 2151677952 | bytes 35651584 | tf_op jit(solution)/shard_map/dot_general | solution.py:697
  549.2 98.5 %shard_map.263 = f32[256,2048]{1,0:T(8,128)} custom-call(f32[2048,2048]{1,0:T(8,128)} %fusion.27.p_ref), custom_call_target="tpu_custom_call" | custom-call | tf_op jit(solution)/shard_map/pallas_call | solution.py:453
  647.7 87.9 %shard_map.261 = f32[256,2048]{1,0:T(8,128)} custom-call(f32[2048,2048]{1,0:T(8,128)} %convolution_add_fusion.1.p_ref), custom_call_target="tpu_custom_call" | custom-call | tf_op jit(solution)/shard_map/pallas_call | solution.py:453
  735.8 2.8 convert_element_type.223
  738.5 32.3 %shard_map.264 = bf16[8,64,1792]{2,1,0:T(8,128)(2,1)} custom-call(bf16[8,64,1792]{2,1,0:T(8,128)(2,1)} %bitcast.131), custom_call_target="tpu_custom_call" | custom-call | tf_op jit(solution)/shard_map/pallas_call | solution.py:518
  770.8 1.5 slice_convert_fusion.5
  772.3 2.4 slice_convert_fusion.6
  774.7 2.0 reshape.306
  776.7 2.8 copy.125
  779.5 2.5 copy.140
  782.0 2.6 reshape.305
  785.6 1.6 copy.139
  788.3 3.0 convert_reduce_fusion.4
  792.4 19.7 %shard_map.265 = f32[8,4,16,128]{3,2,1,0:T(8,128)} custom-call(f32[8,4,16,128]{3,2,1,0:T(8,128)} %copy_bitcast_fusion.3.x_ref), custom_call_target="tpu_custom_call" | custom-call | tf_op jit(solution)/shard_map/pallas_call | solution.py:518
  812.1 1.6 reduce_sum.158.x_ref
  813.7 10.5 %shard_map.266 = f32[4,16,128]{2,1,0:T(8,128)} custom-call(f32[4,16,128]{2,1,0:T(8,128)} %reduce_sum.158.x_ref), custom_call_target="tpu_custom_call" | custom-call | tf_op jit(solution)/shard_map/pallas_call | solution.py:518
  827.2 1.9 copy.157
  (169 shorter events, 25.7 us)
Async XLA Ops:
  7.2 188.6 %all-gather.5.cloned.1.call-start = ((), (), s32[]{:S(2)}) async-start(), calls=%async_computation.3 | async-start | bytes 9175040 | tf_op jit(solution)/shard_map/all_gather | solution.py:603
  13.4 40.1 %copy-start.20 = (f32[64,2048]{1,0:T(8,128)S(1)}, f32[64,2048]{1,0:T(8,128)}, u32[]{:S(2)}) copy-start(f32[64,2048]{1,0:T(8,128)} %param.21) | copy-start | bytes 1572868
  53.4 261.7 %all-gather.7.cloned.1.call-start = ((), (), s32[]{:S(2)}) async-start(), calls=%async_computation.4 | async-start | bytes 1310720 | tf_op jit(solution)/shard_map/all_gather | solution.py:541
  53.5 0.7 collective-permute-start
  54.2 0.7 copy-start.21
  54.9 108.8 %copy-start.19 = (f32[256,2048]{1,0:T(8,128)S(1)}, f32[256,2048]{1,0:T(8,128)}, u32[]{:S(2)}) copy-start(f32[256,2048]{1,0:T(8,128)} %param.25) | copy-start | bytes 6291460
  54.9 260.2 %all-gather.11.cloned.1.call-start = ((), (), s32[]{:S(2)}) async-start(), calls=%async_computation.6 | async-start | bytes 9437184 | tf_op jit(solution)/shard_map/all_gather | solution.py:672
  163.6 1.5 copy-start.26
  163.6 1.5 copy-start.28
  163.6 1.5 copy-start.29
  163.7 1.6 copy-start.30
  163.7 1.6 copy-start.31
  163.7 1.6 copy-start.27
  163.7 277.4 %all-gather.9.cloned.1.call-start = ((), (), s32[]{:S(2)}) async-start(), calls=%async_computation.5 | async-start | bytes 5242880 | tf_op jit(solution)/shard_map/all_gather | solution.py:604
  164.9 363.5 %reduce-scatter.6.cloned.1.call-start = ((), (), s32[]{:S(2)}) async-start(), calls=%async_computation.8 | async-start | bytes 2621440 | tf_op jit(solution)/shard_map/reduce_scatter | solution.py:547
  184.3 5.8 copy-start
  190.2 2.5 copy-start.32
  192.9 26.1 %copy-start.22 = (s32[2048]{0:T(1024)}, s32[2048]{0:T(1024)S(1)}, u32[]{:S(2)}) copy-start(s32[2048]{0:T(1024)S(1)} %convert_reduce_fusion.5) | copy-start | bytes 24580
  252.6 7.3 copy-start.8
  252.6 7.3 copy-start.9
  259.9 5.2 copy-start.5
  331.8 7.4 copy-start.10
  339.3 396.4 %reduce-scatter.8.cloned.1.call-start = ((), (), s32[]{:S(2)}) async-start(), calls=%async_computation.9 | async-start | bytes 5242880 | tf_op jit(solution)/shard_map/reduce_scatter | solution.py:744
  357.7 380.8 %reduce-scatter.4.cloned.1.call-start = ((), (), s32[]{:S(2)}) async-start(), calls=%async_computation.7 | async-start | bytes 9175040 | tf_op jit(solution)/shard_map/reduce_scatter | solution.py:739
  414.0 3.5 copy-start.2
  414.0 5.5 copy-start.1
  423.7 5.2 copy-start.7
  441.1 18.4 %copy-start.12 = (bf16[2048,4,64]{0,2,1:T(8,128)(2,1)S(1)}, bf16[2048,4,64]{0,2,1:T(8,128)(2,1)}, u32[]{:S(2)}) copy-start(bf16[2048,4,64]{0,2,1:T(8,128)(2,1)} %copy.121) | copy-start | bytes 3145732
  441.1 18.4 %copy-start.15 = (bf16[2048,4,64]{0,2,1:T(8,128)(2,1)S(1)}, bf16[2048,4,64]{0,2,1:T(8,128)(2,1)}, u32[]{:S(2)}) copy-start(bf16[2048,4,64]{0,2,1:T(8,128)(2,1)} %copy.122) | copy-start | bytes 3145732
  488.2 0.7 copy-start.24
  488.3 0.8 copy-start.23
  488.3 1.2 copy-start.3
  490.2 16.9 %copy-start.13 = (bf16[2048,4,64]{0,2,1:T(8,128)(2,1)S(1)}, bf16[2048,4,64]{0,2,1:T(8,128)(2,1)}, u32[]{:S(2)}) copy-start(bf16[2048,4,64]{0,2,1:T(8,128)(2,1)} %copy.121) | copy-start | bytes 3145732
  490.2 16.9 %copy-start.16 = (bf16[2048,4,64]{0,2,1:T(8,128)(2,1)S(1)}, bf16[2048,4,64]{0,2,1:T(8,128)(2,1)}, u32[]{:S(2)}) copy-start(bf16[2048,4,64]{0,2,1:T(8,128)(2,1)} %copy.122) | copy-start | bytes 3145732
  490.2 16.8 %copy-start.33 = (bf16[2048,1024]{0,1:T(8,128)(2,1)S(1)}, bf16[2048,1024]{0,1:T(8,128)(2,1)}, u32[]{:S(2)}) copy-start(bf16[2048,1024]{0,1:T(8,128)(2,1)} %get-tuple-element.73) | copy-start | bytes 12582916
  507.0 26.9 %copy-start.11 = (bf16[2048,4,64]{0,2,1:T(8,128)(2,1)S(1)}, bf16[2048,4,64]{0,2,1:T(8,128)(2,1)}, u32[]{:S(2)}) copy-start(bf16[2048,4,64]{0,2,1:T(8,128)(2,1)} %copy-done.10) | copy-start | bytes 3145732
  528.4 19.9 %copy-start.14 = (bf16[2048,4,64]{0,2,1:T(8,128)(2,1)S(1)}, bf16[2048,4,64]{0,2,1:T(8,128)(2,1)}, u32[]{:S(2)}) copy-start(bf16[2048,4,64]{0,2,1:T(8,128)(2,1)} %copy.121) | copy-start | bytes 3145732
  528.4 19.9 %copy-start.17 = (bf16[2048,4,64]{0,2,1:T(8,128)(2,1)S(1)}, bf16[2048,4,64]{0,2,1:T(8,128)(2,1)}, u32[]{:S(2)}) copy-start(bf16[2048,4,64]{0,2,1:T(8,128)(2,1)} %copy.122) | copy-start | bytes 3145732
  528.4 207.3 %collective-permute-start.1 = (f32[64,2048]{1,0:T(8,128)}, f32[64,2048]{1,0:T(8,128)}, u32[]{:S(2)}, u32[]{:S(2)}) collective-permute-start(f32[64,2048]{1,0:T(8,128)} %reduce-scatter.6.cloned.1.call-done), channel_id=1, source_target_pairs={{0,0},{8,1},{16,2},{24,3},{1,4},{9,5},{17,6},{25,7},{2,8},{10,9},{... | collective-permute-start | bytes 1572872 | tf_op jit(solution)/shard_map/ppermute | solution.py:549
  784.6 2.6 copy-start.4
  784.7 3.6 copy-start.6
  784.7 3.6 copy-start.18
  825.6 3.5 copy-start.25
Sparse Core Ops, SparseCore 0:
  53.5 63.1 all-gather.4
  118.3 16.7 all-gather.6
  163.8 126.5 all-gather.10
  292.4 32.6 all-gather.8
  339.4 33.9 reduce-scatter.5
  375.9 44.4 reduce-scatter.7
  488.4 75.2 reduce-scatter.3

commit v14 on v13

--- a/solution.py
+++ b/solution.py
@@ -194,7 +194,7 @@
     )(qi, kj, q, k, v_ext, segq, segk)
 
 
-def _bwd_kernel(qi_ref, kj_ref, q_ref, k_ref, v_ref, do_ref, lse_ref, delta_ref, segq_ref, segk_ref, dq_ref, dk_ref, dv_ref, *, tq, tk, scale):
+def _bwd_kernel(qi_ref, kj_ref, q_ref, k_ref, v_ref, do_ref, lse_ref, delta_ref, segq_ref, segk_ref, dq_ref, dk_ref, dv_ref, dk_sc, dv_sc, *, tq, tk, scale, count):
     t = pl.program_id(1)
     i = qi_ref[t]
     j = kj_ref[t]
@@ -205,8 +205,8 @@
 
     @pl.when(i == j)
     def _():
-        dk_ref[...] = jnp.zeros_like(dk_ref)
-        dv_ref[...] = jnp.zeros_like(dv_ref)
+        dk_sc[...] = jnp.zeros_like(dk_sc)
+        dv_sc[...] = jnp.zeros_like(dv_sc)
 
     def absorb(causal):
         q = q_ref[0]
@@ -217,8 +217,8 @@
         p = jnp.exp(s - lse_ref[0])
         dp = lax.dot_general(do, v_ref[0], TRANS_B, preferred_element_type=jnp.float32)
         ds = (p * (dp - delta_ref[0])).astype(jnp.bfloat16)
-        dv_ref[0] += lax.dot(p.astype(jnp.bfloat16).T, do, preferred_element_type=jnp.float32)
-        dk_ref[0] += lax.dot(ds.T, q, preferred_element_type=jnp.float32) * scale
+        dv_sc[...] += jnp.dot(do.T, p.astype(jnp.bfloat16), preferred_element_type=jnp.float32)
+        dk_sc[...] += jnp.dot(q.T, ds, preferred_element_type=jnp.float32)
         rows = pl.ds(pl.multiple_of(i * tq, tq), tq)
         dq_ref[0, rows, :] += lax.dot(ds, k, preferred_element_type=jnp.float32) * scale
 
@@ -229,6 +229,11 @@
     @pl.when(j == i)
     def _():
         absorb(True)
+
+    @pl.when(i == count - 1)
+    def _():
+        dk_ref[0] = dk_sc[...].T * scale
+        dv_ref[0] = dv_sc[...].T
 
 
 def attention_backward(q, k, v, do, lse, delta, seg, block=512):
@@ -247,7 +252,7 @@
         return (h, kj[t], 0)
 
     return pl.pallas_call(
-        functools.partial(_bwd_kernel, tq=block, tk=block, scale=scale),
+        functools.partial(_bwd_kernel, tq=block, tk=block, scale=scale, count=count),
         out_shape=(
             jax.ShapeDtypeStruct((heads, total, dim), jnp.float32),
             jax.ShapeDtypeStruct((heads, total, dim), jnp.float32),
@@ -270,6 +275,10 @@
                 pl.BlockSpec((1, total, dim), lambda h, t, qi, kj: (h, 0, 0)),
                 pl.BlockSpec((1, block, dim), k_map),
                 pl.BlockSpec((1, block, dim), k_map),
+            ],
+            scratch_shapes=[
+                pltpu.VMEM((dim, block), jnp.float32),
+                pltpu.VMEM((dim, block), jnp.float32),
             ],
         ),
         cost_estimate=pl.CostEstimate(

time: 842 us -> 839 us (level)
  transfers between devices with their start and end apart: 9 -> 9, of which waited for: 0 -> 0; matrix products, arithmetic and copies ran while one was open for 31% -> 31% of each run, Pallas kernels for 50% -> 49%
where the time goes in v14:
time: 839 us; the launch traced here: 833 us
  Pallas kernels  513 us (61%)
  matrix products  152 us (18%)
  local copies, waits for them, and re-layouts  81.2 us (10%)
  other arithmetic  65.5 us (8%)
  between operations  15.2 us (2%)
    pallas_call x2, Pallas kernels, ring_reduce_scatter(): pl.pallas_call(functools.partial(_scatter_kernel, ring=ring, rows=rows, p...  187 us
    pallas_call x6, Pallas kernels, exchange(): pl.pallas_call(functools.partial(_exchange_kernel, group=group), out_shap...  115 us
    pallas_call x1, Pallas kernels, ring_all_gather(): pl.pallas_call(functools.partial(_gather_kernel, ring=ring, rows=rows), o...  109 us
    pallas_call x1, Pallas kernels, attention_backward(): pl.pallas_call(functools.partial(_bwd_kernel, tq=block, tk=block, scale=s...  53.9 us
    pallas_call x1, Pallas kernels, attention_forward(): pl.pallas_call(functools.partial(_fwd_kernel, tq=block, tk=block, scale=s...  48 us
    unnamed x84, local copies, waits for them, and re-layouts  31.3 us
    dot_general x1, matrix products, head_plan(): jnp.einsum('td,tc->dc', hidden_group, d_both, preferred_element_type=jnp....  28.7 us
    dot_general x1, matrix products, head_plan(): jnp.dot(hidden_group, cols, preferred_element_type=jnp.float32)  23.2 us
  transfers between devices with their start and end apart: 9, of which 0 were waited for; matrix products, arithmetic and copies ran while one was open for 31% of the time, Pallas kernels for 49%

profile of v14, /device:TPU:0, one launch (start us, length us, event | category | flops | bytes accessed | tf_op | source)
XLA Modules:
  0.0 833.5 jit_solution(5561995477121891264)
XLA Ops:
  7.2 1.7 convert_element_type.177
  10.4 1.5 convert_element_type.176
  14.8 38.6 %shard_map.256 = bf16[8,64,1792]{2,1,0:T(8,128)(2,1)} custom-call(bf16[8,64,1792]{2,1,0:T(8,128)(2,1)} %pad_maximum_fusion.3.x_ref), custom_call_target="tpu_custom_call" | custom-call | tf_op jit(solution)/shard_map/pallas_call | solution.py:527
  55.0 108.6 %shard_map.257 = bf16[2048,2048]{1,0:T(8,128)(2,1)} custom-call(bf16[256,2048]{1,0:T(8,128)(2,1)} %x_ref), custom_call_target="tpu_custom_call" | custom-call | tf_op jit(solution)/shard_map/pallas_call | solution.py:391
  166.0 5.0 shard_map.258
  171.0 1.4 broadcast_in_dim.34.x_ref
  172.4 10.0 %shard_map.259 = bf16[8,4,16,128]{3,2,1,0:T(8,128)(2,1)} custom-call(bf16[8,4,16,128]{3,2,1,0:T(8,128)(2,1)} %broadcast_in_dim.34.x_ref), custom_call_target="tpu_custom_call" | custom-call | tf_op jit(solution)/shard_map/pallas_call | solution.py:527
  184.3 4.7 convert_reduce_fusion
  190.2 2.3 fusion.2
  195.8 23.2 %convolution_add_fusion = f32[2048,1792]{0,1:T(8,128)} fusion(bf16[2048,1792]{1,0:T(8,128)(2,1)} %all-gather.5.cloned.1.call-done, f32[1792]{0:T(1024)S(1)} %maximum_convert_fusion, bf16[2048,2048]{1,0:T(8,128)(2,1)} %shard_map.257, f32[2048]{0:T(1024)S(1)} %reshape.300, f32[2048]{0:T(1024)S(1)} %reshape.299, f32[2048]{0:T(1024)S(1)} %add_rsqrt_fusion, ...), kind=kOutput, calls=%fused_computation.10 | convolution fusion | flops 15061221376 | bytes 30448640 | tf_op jit(solution)/shard_map/dot_general | solution.py:688
  219.0 1.7 slice.195
  220.7 3.9 fusion.34
  226.5 3.5 copy.129
  230.1 3.5 copy.130
  233.6 2.1 slice.196
  235.7 2.3 fusion.35
  238.0 3.7 copy.132
  241.6 3.6 copy.133
  245.2 3.0 copy.131
  248.2 2.6 copy.134
  250.8 1.8 copy.114
  252.6 7.3 subtract_convert_fusion.2
  259.9 5.2 maximum_bitcast_fusion
  265.1 2.0 maximum_maximum_fusion.v_ref
  267.1 48.0 %shard_map.260 = (f32[4,2048,64]{2,1,0:T(8,128)}, f32[4,2048,1]{2,1,0:T(8,128)}) custom-call(s32[10]{0:T(128)} %constant.61.clone.qi_ref, s32[10]{0:T(128)} %constant.62.clone.kj_ref, bf16[4,2048,64]{2,1,0:T(8,128)(2,1)} %get-tuple-element.74.q_ref, bf16[4,2048,64]{2,1,0:T(8,128)(2,1)} %get-tuple-element.75.k_ref, ...), custom_call_target="tpu_custom_call" | custom-call | flops 2147483648 | bytes 5242880 | tf_op jit(solution)/shard_map/pallas_call | solution.py:164
  315.1 6.0 convolution_convert_fusion.2
  321.2 1.8 copy.117
  323.0 6.8 multiply_reduce_fusion
  329.7 2.1 copy.116
  331.8 7.4 fusion.38
  339.3 2.8 copy.118.delta_ref
  342.1 15.6 %convolution_convert_fusion.1 = bf16[1024,2048]{1,0:T(8,128)(2,1)} fusion(bf16[2048,2048]{1,0:T(8,128)(2,1)} %all-gather.11.cloned.1.call-done, f32[2048,1792]{0,1:T(8,128)} %convolution_add_fusion), kind=kOutput, calls=%fused_computation.35 | convolution fusion | flops 8610906112 | bytes 20971520 | tf_op jit(solution)/shard_map/tf,td->fd/dot_general | solution.py:716
  357.7 53.9 %shard_map.262 = (f32[4,2048,64]{2,1,0:T(8,128)}, f32[4,2048,64]{2,1,0:T(8,128)}, f32[4,2048,64]{2,1,0:T(8,128)}) custom-call(s32[10]{0:T(128)} %constant.63.clone.qi_ref, s32[10]{0:T(128)} %constant.64.clone.kj_ref, bf16[4,2048,64]{2,1,0:T(8,128)(2,1)} %get-tuple-element.74.q_ref, bf16[4,2048,64]{2,1,0:T(8,128)(2,1)} %get-tuple-element.75.k_ref, ...), custom_call_target="tpu_custom_call" | custom-call | flops 5368709120 | bytes 12582912 | tf_op jit(solution)/shard_map/pallas_call | solution.py:254
  411.6 2.9 slice.194
  415.1 1.9 slice.193
  417.0 4.3 add_convert_fusion.1
  421.3 3.2 pad_maximum_fusion.1
  424.5 1.9 copy.120
  426.4 5.4 pad_maximum_fusion.2
  431.9 2.7 copy.121
  434.6 2.5 convert_bitcast_fusion
  437.0 1.6 copy.122
  438.6 18.4 %convert_reduce_fusion.1 = (f32[1024]{0:T(1024)S(1)}, bf16[2048,1024]{0,1:T(8,128)(2,1)}) fusion(f32[2048,1792]{0,1:T(8,128)} %convolution_add_fusion, bf16[2048,2048]{1,0:T(8,128)(2,1)} %all-gather.11.cloned.1.call-done, bf16[1024,2048]{1,0:T(8,128)(2,1)} %all-gather.9.cloned.1.call-done), kind=kOutput, calls=%fused_computation.19 | convolution fusion | flops 8633973760 | bytes 25169920 | tf_op jit(solution)/shard_map/td,fd->tf/dot_general | solution.py:717
  457.0 28.7 %convolution_convert_fusion = bf16[2048,1792]{1,0:T(8,128)(2,1)} fusion(bf16[2048,1024]{0,1:T(8,128)(2,1)} %get-tuple-element.73, bf16[2048,256]{0,1:T(8,128)(2,1)S(1)} %bitcast.120, bf16[2048,256]{0,1:T(8,128)(2,1)S(1)} %bitcast.117, bf16[2048,256]{0,1:T(8,128)(2,1)S(1)} %bitcast.114, bf16[2048,2048]{1,0:T(8,128)(2,1)} %shard_map.257, ...), kind=kOutput, calls=%fused_computation.21 | convolution fusion | flops 15090581504 | bytes 23101440 | tf_op jit(solution)/shard_map/td,tc->dc/dot_general | solution.py:745
  487.7 16.8 %fusion.31 = f32[2048,2048]{1,0:T(8,128)} fusion(bf16[1024,2048]{1,0:T(8,128)(2,1)} %all-gather.9.cloned.1.call-done, f32[2048,1792]{0,1:T(8,128)} %convolution_add_fusion), kind=kOutput, calls=%fused_computation.108 | convolution fusion | flops 8608808960 | bytes 29360128 | tf_op jit(solution)/shard_map/dot_general | solution.py:707
  504.6 21.4 %fusion.27.p_ref = f32[2048,2048]{1,0:T(8,128)} fusion(bf16[2048,1792]{1,0:T(8,128)(2,1)} %all-gather.5.cloned.1.call-done, bf16[2048,1024]{0,1:T(8,128)(2,1)S(1)} %copy-done.33, bf16[2048,256]{0,1:T(8,128)(2,1)S(1)} %bitcast.121, bf16[2048,256]{0,1:T(8,128)(2,1)S(1)} %bitcast.118, bf16[2048,256]{0,1:T(8,128)(2,1)S(1)} %bitcast.115), kind=kOutput, calls=%fused_computation.66 | convolution fusion | flops 15061745664 | bytes 31457280 | tf_op jit(solution)/shard_map/tc,dc->td/dot_general | solution.py:743
  525.9 5.5 collective-permute-start.1
  531.4 14.4 %convolution_add_fusion.1.p_ref = f32[2048,2048]{1,0:T(8,128)} fusion(f32[2048,2048]{1,0:T(8,128)} %fusion.31, bf16[2048,256]{0,1:T(8,128)(2,1)S(1)} %bitcast.108, bf16[256,2048]{1,0:T(8,128)(2,1)} %all-gather.7.cloned.1.call-done), kind=kOutput, calls=%fused_computation.11 | convolution fusion | flops 2151677952 | bytes 35651584 | tf_op jit(solution)/shard_map/dot_general | solution.py:706
  546.7 98.6 %shard_map.263 = f32[256,2048]{1,0:T(8,128)} custom-call(f32[2048,2048]{1,0:T(8,128)} %fusion.27.p_ref), custom_call_target="tpu_custom_call" | custom-call | tf_op jit(solution)/shard_map/pallas_call | solution.py:462
  645.4 88.3 %shard_map.261 = f32[256,2048]{1,0:T(8,128)} custom-call(f32[2048,2048]{1,0:T(8,128)} %convolution_add_fusion.1.p_ref), custom_call_target="tpu_custom_call" | custom-call | tf_op jit(solution)/shard_map/pallas_call | solution.py:462
  733.8 2.8 convert_element_type.223
  736.6 32.7 %shard_map.264 = bf16[8,64,1792]{2,1,0:T(8,128)(2,1)} custom-call(bf16[8,64,1792]{2,1,0:T(8,128)(2,1)} %bitcast.131), custom_call_target="tpu_custom_call" | custom-call | tf_op jit(solution)/shard_map/pallas_call | solution.py:527
  769.4 1.5 slice_convert_fusion.5
  770.8 2.4 slice_convert_fusion.6
  773.2 2.0 reshape.306
  775.2 2.8 copy.125
  778.0 2.5 copy.140
  780.5 2.6 reshape.305
  784.1 1.6 copy.139
  786.8 3.0 convert_reduce_fusion.4
  790.9 19.7 %shard_map.265 = f32[8,4,16,128]{3,2,1,0:T(8,128)} custom-call(f32[8,4,16,128]{3,2,1,0:T(8,128)} %copy_bitcast_fusion.3.x_ref), custom_call_target="tpu_custom_call" | custom-call | tf_op jit(solution)/shard_map/pallas_call | solution.py:527
  810.6 1.6 reduce_sum.158.x_ref
  812.2 9.3 %shard_map.266 = f32[4,16,128]{2,1,0:T(8,128)} custom-call(f32[4,16,128]{2,1,0:T(8,128)} %reduce_sum.158.x_ref), custom_call_target="tpu_custom_call" | custom-call | tf_op jit(solution)/shard_map/pallas_call | solution.py:527
  824.5 1.9 copy.157
  (169 shorter events, 25.7 us)
Async XLA Ops:
  7.2 188.6 %all-gather.5.cloned.1.call-start = ((), (), s32[]{:S(2)}) async-start(), calls=%async_computation.3 | async-start | bytes 9175040 | tf_op jit(solution)/shard_map/all_gather | solution.py:612
  13.4 40.1 %copy-start.20 = (f32[64,2048]{1,0:T(8,128)S(1)}, f32[64,2048]{1,0:T(8,128)}, u32[]{:S(2)}) copy-start(f32[64,2048]{1,0:T(8,128)} %param.21) | copy-start | bytes 1572868
  53.4 261.7 %all-gather.7.cloned.1.call-start = ((), (), s32[]{:S(2)}) async-start(), calls=%async_computation.4 | async-start | bytes 1310720 | tf_op jit(solution)/shard_map/all_gather | solution.py:550
  53.5 0.7 collective-permute-start
  54.2 0.7 copy-start.21
  54.9 108.8 %copy-start.19 = (f32[256,2048]{1,0:T(8,128)S(1)}, f32[256,2048]{1,0:T(8,128)}, u32[]{:S(2)}) copy-start(f32[256,2048]{1,0:T(8,128)} %param.25) | copy-start | bytes 6291460
  54.9 260.2 %all-gather.11.cloned.1.call-start = ((), (), s32[]{:S(2)}) async-start(), calls=%async_computation.6 | async-start | bytes 9437184 | tf_op jit(solution)/shard_map/all_gather | solution.py:681
  163.6 1.5 copy-start.26
  163.6 1.5 copy-start.28
  163.6 1.5 copy-start.29
  163.7 1.6 copy-start.30
  163.7 1.6 copy-start.31
  163.7 1.6 copy-start.27
  163.7 274.9 %all-gather.9.cloned.1.call-start = ((), (), s32[]{:S(2)}) async-start(), calls=%async_computation.5 | async-start | bytes 5242880 | tf_op jit(solution)/shard_map/all_gather | solution.py:613
  164.9 361.0 %reduce-scatter.6.cloned.1.call-start = ((), (), s32[]{:S(2)}) async-start(), calls=%async_computation.8 | async-start | bytes 2621440 | tf_op jit(solution)/shard_map/reduce_scatter | solution.py:556
  184.3 5.8 copy-start
  190.2 2.5 copy-start.32
  192.9 26.1 %copy-start.22 = (s32[2048]{0:T(1024)}, s32[2048]{0:T(1024)S(1)}, u32[]{:S(2)}) copy-start(s32[2048]{0:T(1024)S(1)} %convert_reduce_fusion.5) | copy-start | bytes 24580
  252.6 7.3 copy-start.8
  252.6 7.3 copy-start.9
  259.9 5.2 copy-start.5
  331.8 7.4 copy-start.10
  339.3 394.5 %reduce-scatter.8.cloned.1.call-start = ((), (), s32[]{:S(2)}) async-start(), calls=%async_computation.9 | async-start | bytes 5242880 | tf_op jit(solution)/shard_map/reduce_scatter | solution.py:753
  357.7 378.9 %reduce-scatter.4.cloned.1.call-start = ((), (), s32[]{:S(2)}) async-start(), calls=%async_computation.7 | async-start | bytes 9175040 | tf_op jit(solution)/shard_map/reduce_scatter | solution.py:748
  411.6 3.5 copy-start.2
  411.6 5.4 copy-start.1
  421.3 5.2 copy-start.7
  438.6 18.4 %copy-start.12 = (bf16[2048,4,64]{0,2,1:T(8,128)(2,1)S(1)}, bf16[2048,4,64]{0,2,1:T(8,128)(2,1)}, u32[]{:S(2)}) copy-start(bf16[2048,4,64]{0,2,1:T(8,128)(2,1)} %copy.121) | copy-start | bytes 3145732
  438.6 18.4 %copy-start.15 = (bf16[2048,4,64]{0,2,1:T(8,128)(2,1)S(1)}, bf16[2048,4,64]{0,2,1:T(8,128)(2,1)}, u32[]{:S(2)}) copy-start(bf16[2048,4,64]{0,2,1:T(8,128)(2,1)} %copy.122) | copy-start | bytes 3145732
  485.8 0.7 copy-start.24
  485.8 0.8 copy-start.23
  485.8 1.2 copy-start.3
  487.7 16.8 %copy-start.13 = (bf16[2048,4,64]{0,2,1:T(8,128)(2,1)S(1)}, bf16[2048,4,64]{0,2,1:T(8,128)(2,1)}, u32[]{:S(2)}) copy-start(bf16[2048,4,64]{0,2,1:T(8,128)(2,1)} %copy.121) | copy-start | bytes 3145732
  487.7 16.8 %copy-start.16 = (bf16[2048,4,64]{0,2,1:T(8,128)(2,1)S(1)}, bf16[2048,4,64]{0,2,1:T(8,128)(2,1)}, u32[]{:S(2)}) copy-start(bf16[2048,4,64]{0,2,1:T(8,128)(2,1)} %copy.122) | copy-start | bytes 3145732
  487.7 16.8 %copy-start.33 = (bf16[2048,1024]{0,1:T(8,128)(2,1)S(1)}, bf16[2048,1024]{0,1:T(8,128)(2,1)}, u32[]{:S(2)}) copy-start(bf16[2048,1024]{0,1:T(8,128)(2,1)} %get-tuple-element.73) | copy-start | bytes 12582916
  504.5 26.9 %copy-start.11 = (bf16[2048,4,64]{0,2,1:T(8,128)(2,1)S(1)}, bf16[2048,4,64]{0,2,1:T(8,128)(2,1)}, u32[]{:S(2)}) copy-start(bf16[2048,4,64]{0,2,1:T(8,128)(2,1)} %copy-done.10) | copy-start | bytes 3145732
  525.9 19.9 %copy-start.14 = (bf16[2048,4,64]{0,2,1:T(8,128)(2,1)S(1)}, bf16[2048,4,64]{0,2,1:T(8,128)(2,1)}, u32[]{:S(2)}) copy-start(bf16[2048,4,64]{0,2,1:T(8,128)(2,1)} %copy.121) | copy-start | bytes 3145732
  525.9 19.9 %copy-start.17 = (bf16[2048,4,64]{0,2,1:T(8,128)(2,1)S(1)}, bf16[2048,4,64]{0,2,1:T(8,128)(2,1)}, u32[]{:S(2)}) copy-start(bf16[2048,4,64]{0,2,1:T(8,128)(2,1)} %copy.122) | copy-start | bytes 3145732
  525.9 207.9 %collective-permute-start.1 = (f32[64,2048]{1,0:T(8,128)}, f32[64,2048]{1,0:T(8,128)}, u32[]{:S(2)}, u32[]{:S(2)}) collective-permute-start(f32[64,2048]{1,0:T(8,128)} %reduce-scatter.6.cloned.1.call-done), channel_id=1, source_target_pairs={{0,0},{8,1},{16,2},{24,3},{1,4},{9,5},{17,6},{25,7},{2,8},{10,9},{... | collective-permute-start | bytes 1572872 | tf_op jit(solution)/shard_map/ppermute | solution.py:558
  783.2 2.6 copy-start.4
  783.2 3.6 copy-start.6
  783.2 3.6 copy-start.18
  822.9 3.5 copy-start.25
Sparse Core Ops, SparseCore 0:
  53.5 63.1 all-gather.4
  118.3 16.7 all-gather.6
  163.8 126.5 all-gather.10
  292.4 32.6 all-gather.8
  339.4 33.9 reduce-scatter.5
  375.9 44.4 reduce-scatter.7
  485.9 75.3 reduce-scatter.3

commit v15 on v14

--- a/solution.py
+++ b/solution.py
@@ -685,25 +685,29 @@
     bias_cols = lax.dynamic_slice_in_dim(
         qkv_bias.reshape(3, D), here * head_width, head_width, 1
     ).reshape(3 * head_width)
-    both = jnp.dot(hidden_group, cols, preferred_element_type=jnp.float32) + jnp.concatenate(
-        [bias_cols, fc1_bias]
-    ).astype(jnp.float32)
-    qkv = both[:, : 3 * head_width]
-    pre = both[:, 3 * head_width :]
-    shape = (group, local_heads, HEAD_DIM)
-    query = rotate(qkv[:, :head_width].reshape(shape), cosine, sine).astype(jnp.bfloat16)
-    keys = rotate(qkv[:, head_width : 2 * head_width].reshape(shape), cosine, sine).astype(
+    qkv_width = 3 * head_width
+    head_count = 3 * local_heads
+    qkv_weights = cols[:, :qkv_width].reshape(D, head_count, HEAD_DIM)
+    fc1_weights = cols[:, qkv_width:]
+    qkv_heads = jnp.einsum(
+        "td,dhe->hte", hidden_group, qkv_weights, preferred_element_type=jnp.float32
+    ) + bias_cols.astype(jnp.float32).reshape(head_count, 1, HEAD_DIM)
+    pre = jnp.dot(hidden_group, fc1_weights, preferred_element_type=jnp.float32) + fc1_bias.astype(
+        jnp.float32
+    )
+    cos_heads = cosine.reshape(1, group, -1)
+    sin_heads = sine.reshape(1, group, -1)
+    q_heads = rotate(qkv_heads[:local_heads], cos_heads, sin_heads).astype(jnp.bfloat16)
+    k_heads = rotate(qkv_heads[local_heads : 2 * local_heads], cos_heads, sin_heads).astype(
         jnp.bfloat16
     )
-    values = qkv[:, 2 * head_width :].reshape(shape).astype(jnp.bfloat16)
-    q_heads = query.transpose(1, 0, 2)
-    k_heads = keys.transpose(1, 0, 2)
-    v_heads = values.transpose(1, 0, 2)
+    v_heads = qkv_heads[2 * local_heads :].astype(jnp.bfloat16)
     attended_heads, log_total = attention_forward(q_heads, k_heads, v_heads, seg)
-    attended = attended_heads.transpose(1, 0, 2).reshape(group, head_width).astype(jnp.bfloat16)
+    attended_low = attended_heads.astype(jnp.bfloat16)
+    out_heads = out_rows.reshape(local_heads, HEAD_DIM, D)
     act = gelu_tanh(pre).astype(jnp.bfloat16)
     branches = ring_reduce_scatter(
-        jnp.dot(attended, out_rows, preferred_element_type=jnp.float32)
+        jnp.einsum("hte,hed->td", attended_low, out_heads, preferred_element_type=jnp.float32)
         + jnp.dot(act, fc2_rows, preferred_element_type=jnp.float32),
         ring,
         2,
@@ -717,33 +721,38 @@
     d_act = jnp.einsum("td,fd->tf", dy_group, fc2_rows, preferred_element_type=jnp.float32)
     d_pre = (d_act * gelu_slope(pre)).astype(jnp.bfloat16)
     grad_bfc1_part = jnp.sum(d_pre.astype(jnp.float32), axis=0)
-    grad_out_rows = jnp.einsum("tc,td->cd", attended, dy_group, preferred_element_type=jnp.float32)
+    grad_out_rows = jnp.einsum(
+        "hte,td->hed", attended_low, dy_group, preferred_element_type=jnp.float32
+    ).reshape(head_width, D)
     owned_w_out = return_out_rows(grad_out_rows)
-    d_attended = (
-        jnp.einsum("td,cd->tc", dy_group, out_rows, preferred_element_type=jnp.float32)
-        .astype(jnp.bfloat16)
-        .reshape(shape)
-    )
-    d_heads = d_attended.transpose(1, 0, 2)
+    d_heads = jnp.einsum(
+        "td,hed->hte", dy_group, out_heads, preferred_element_type=jnp.float32
+    ).astype(jnp.bfloat16)
     delta = jnp.sum(d_heads.astype(jnp.float32) * attended_heads, axis=2, keepdims=True)
     dq_heads, dk_heads, dv_heads = attention_backward(
         q_heads, k_heads, v_heads, d_heads, log_total, delta, seg
     )
-    d_query = dq_heads.transpose(1, 0, 2)
-    d_keys = dk_heads.transpose(1, 0, 2)
-    d_values = dv_heads.transpose(1, 0, 2)
-    d_query = rotate_back(d_query, cosine, sine).reshape(group, head_width)
-    d_keys = rotate_back(d_keys, cosine, sine).reshape(group, head_width)
-    d_qkv = jnp.concatenate([d_query, d_keys, d_values.reshape(group, head_width)], axis=1).astype(
-        jnp.bfloat16
-    )
-    d_both = jnp.concatenate([d_qkv, d_pre], axis=1)
-    bias_part = jnp.sum(d_qkv.astype(jnp.float32), axis=0).reshape(3, head_width)
-    d_hidden = ring_reduce_scatter(
-        jnp.einsum("tc,dc->td", d_both, cols, preferred_element_type=jnp.float32), ring, 3
-    )
-    weight_parts = jnp.einsum(
-        "td,tc->dc", hidden_group, d_both, preferred_element_type=jnp.float32
+    d_qkv_heads = jnp.concatenate(
+        [
+            rotate_back(dq_heads, cos_heads, sin_heads),
+            rotate_back(dk_heads, cos_heads, sin_heads),
+            dv_heads,
+        ],
+        axis=0,
+    ).astype(jnp.bfloat16)
+    bias_part = jnp.sum(d_qkv_heads.astype(jnp.float32), axis=1).reshape(3, head_width)
+    d_hidden_part = jnp.einsum(
+        "hte,dhe->td", d_qkv_heads, qkv_weights, preferred_element_type=jnp.float32
+    ) + jnp.einsum("tf,df->td", d_pre, fc1_weights, preferred_element_type=jnp.float32)
+    d_hidden = ring_reduce_scatter(d_hidden_part, ring, 3)
+    weight_parts = jnp.concatenate(
+        [
+            jnp.einsum(
+                "td,hte->dhe", hidden_group, d_qkv_heads, preferred_element_type=jnp.float32
+            ).reshape(D, qkv_width),
+            jnp.einsum("td,tf->df", hidden_group, d_pre, preferred_element_type=jnp.float32),
+        ],
+        axis=1,
     ).astype(jnp.bfloat16)
     owned_parts = lax.psum_scatter(weight_parts, "dp", scatter_dimension=0, tiled=True)
     split_qkv, split_fc1 = return_heads(owned_parts)

time: 839 us -> 848 us (1.011)
  local copies, waits for them, and re-layouts: 81.2 us -> 57.9 us
  other arithmetic: 65.5 us -> 83.2 us
  matrix products: 152 us -> 165 us
    unnamed x84 -> x79, local copies, waits for them, and re-layouts: 31.3 us -> 13.5 us
    reduce_sum x1, other arithmetic: 0.76 us -> 12.5 us  [head_plan(): jnp.sum(d_qkv_heads.astype(jnp.float32), axis=1).reshape(3, head_width)]
    unnamed x0 -> x1, matrix products: none -> 9.04 us
    convert_element_type x1 -> x3, other arithmetic: 0.01 us -> 8.61 us  [the longest x1 8.59 us: head_plan(): norm_parts(tokens_group.astype(jnp.float32), gain32, shift32)[2]]
    dot_general x6 -> x8, matrix products: 101 us -> 105 us  [the longest x1 16.6 us: head_plan(): jnp.einsum('td,dhe->hte', hidden_group, qkv_weights, preferred_element_ty...]
where the time goes in v15:
time: 848 us; the launch traced here: 843 us
  Pallas kernels  519 us (61%)
  matrix products  165 us (19%)
  other arithmetic  83.2 us (10%)
  local copies, waits for them, and re-layouts  57.9 us (7%)
  between operations  15.2 us (2%)
    pallas_call x2, Pallas kernels, ring_reduce_scatter(): pl.pallas_call(functools.partial(_scatter_kernel, ring=ring, rows=rows, p...  192 us
    pallas_call x6, Pallas kernels, exchange(): pl.pallas_call(functools.partial(_exchange_kernel, group=group), out_shap...  117 us
    pallas_call x1, Pallas kernels, ring_all_gather(): pl.pallas_call(functools.partial(_gather_kernel, ring=ring, rows=rows), o...  109 us
    pallas_call x1, Pallas kernels, attention_backward(): pl.pallas_call(functools.partial(_bwd_kernel, tq=block, tk=block, scale=s...  53.4 us
    pallas_call x1, Pallas kernels, attention_forward(): pl.pallas_call(functools.partial(_fwd_kernel, tq=block, tk=block, scale=s...  48.1 us
    dot_general x1, matrix products, head_plan(): jnp.einsum('td,fd->tf', dy_group, fc2_rows, preferred_element_type=jnp.fl...  19.7 us
  transfers between devices with their start and end apart: 9, of which 0 were waited for; matrix products, arithmetic and copies ran while one was open for 31% of the time, Pallas kernels for 49%

profile of v15, /device:TPU:0, one launch (start us, length us, event | category | flops | bytes accessed | tf_op | source)
XLA Modules:
  0.0 842.7 jit_solution(16735646925034007761)
XLA Ops:
  7.2 1.7 convert_element_type.181
  10.4 1.5 convert_element_type.180
  13.4 1.4 pad_maximum_fusion.4.x_ref
  14.8 38.6 %shard_map.256 = bf16[8,64,1792]{2,1,0:T(8,128)(2,1)} custom-call(bf16[8,64,1792]{2,1,0:T(8,128)(2,1)} %pad_maximum_fusion.4.x_ref), custom_call_target="tpu_custom_call" | custom-call | tf_op jit(solution)/shard_map/pallas_call | solution.py:527
  55.0 108.6 %shard_map.257 = bf16[2048,2048]{1,0:T(8,128)(2,1)} custom-call(bf16[256,2048]{1,0:T(8,128)(2,1)} %x_ref), custom_call_target="tpu_custom_call" | custom-call | tf_op jit(solution)/shard_map/pallas_call | solution.py:391
  163.8 1.1 convert_element_type.204
  166.0 5.0 shard_map.258
  171.0 1.4 broadcast_in_dim.34.x_ref
  172.4 10.0 %shard_map.259 = bf16[8,4,16,128]{3,2,1,0:T(8,128)(2,1)} custom-call(bf16[8,4,16,128]{3,2,1,0:T(8,128)(2,1)} %broadcast_in_dim.34.x_ref), custom_call_target="tpu_custom_call" | custom-call | tf_op jit(solution)/shard_map/pallas_call | solution.py:527
  184.1 4.7 convert_reduce_fusion
  190.0 2.3 fusion.2
  193.6 1.3 copy.96
  194.9 1.3 copy.97
  196.4 1.3 copy.98.segq_ref
  197.7 8.6 %fusion.5 = bf16[2048,2048]{1,0:T(8,128)(2,1)} fusion(bf16[2048,2048]{1,0:T(8,128)(2,1)} %shard_map.257, f32[2048]{0:T(1024)S(1)} %reshape.292, f32[2048]{0:T(1024)S(1)} %reshape.291, f32[2048]{0:T(1024)S(1)} %add_rsqrt_fusion, f32[2048]{0:T(1024)S(1)} %broadcast_multiply_fusion), kind=kLoop, calls=%fused_computation.7 | loop fusion | flops 25165824 | bytes 16809984 | tf_op jit(solution)/shard_map/convert_element_type | solution.py:682
  206.3 1.9 slice-done.2
  208.2 3.0 copy.93
  211.2 16.6 %fusion.48 = (bf16[12,2048,64]{2,1,0:T(8,128)(2,1)S(1)}, f32[12,2048,64]{2,1,0:T(8,128)S(1)}) fusion(f32[12,64]{1,0:T(8,128)S(1)} %reshape.293, bf16[2048,12,64]{0,2,1:T(8,128)(2,1)} %bitcast.124, bf16[2048,2048]{1,0:T(8,128)(2,1)} %fusion.5), kind=kOutput, calls=%fused_computation.114 | convolution fusion | flops 6445596672 | bytes 20974592 | tf_op jit(solution)/shard_map/td,dhe->hte/dot_general | solution.py:692
  227.9 1.2 fusion.46
  229.2 1.4 copy-done.6
  231.4 5.1 subtract_convert_fusion.2
  236.4 7.0 pad_maximum_fusion.2
  243.4 2.0 maximum_maximum_fusion.v_ref
  245.4 48.1 %shard_map.260 = (f32[4,2048,64]{2,1,0:T(8,128)}, f32[4,2048,1]{2,1,0:T(8,128)}) custom-call(s32[10]{0:T(128)} %constant.61.clone.qi_ref, s32[10]{0:T(128)} %constant.62.clone.kj_ref, bf16[4,2048,64]{2,1,0:T(8,128)(2,1)} %get-tuple-element.70.q_ref, bf16[4,2048,64]{2,1,0:T(8,128)(2,1)} %get-tuple-element.71.k_ref, ...), custom_call_target="tpu_custom_call" | custom-call | flops 2147483648 | bytes 5242880 | tf_op jit(solution)/shard_map/pallas_call | solution.py:164
  293.5 14.6 %fusion.23 = f32[2048,1024]{1,0:T(8,128)} fusion(bf16[2048,2048]{1,0:T(8,128)(2,1)} %fusion.5, bf16[2048,1792]{1,0:T(8,128)(2,1)} %all-gather.5.cloned.1.call-done), kind=kOutput, calls=%fused_computation.46 | convolution fusion | flops 8589934592 | bytes 20971520 | tf_op jit(solution)/shard_map/dot_general | solution.py:695
  308.1 6.0 fusion.25
  314.1 1.9 copy.100
  316.0 8.4 fusion.13
  324.5 4.0 multiply_reduce_fusion
  328.5 2.6 copy.101.delta_ref
  331.2 53.4 %shard_map.262 = (f32[4,2048,64]{2,1,0:T(8,128)}, f32[4,2048,64]{2,1,0:T(8,128)}, f32[4,2048,64]{2,1,0:T(8,128)}) custom-call(s32[10]{0:T(128)} %constant.63.clone.qi_ref, s32[10]{0:T(128)} %constant.64.clone.kj_ref, bf16[4,2048,64]{2,1,0:T(8,128)(2,1)} %get-tuple-element.70.q_ref, bf16[4,2048,64]{2,1,0:T(8,128)(2,1)} %get-tuple-element.71.k_ref, ...), custom_call_target="tpu_custom_call" | custom-call | flops 5368709120 | bytes 12582912 | tf_op jit(solution)/shard_map/pallas_call | solution.py:254
  384.6 3.9 convert.74
  388.5 1.9 slice.188
  390.5 2.0 slice.189
  392.4 4.9 add_convert_fusion.1
  397.4 14.0 %convolution_convert_fusion = bf16[1024,2048]{1,0:T(8,128)(2,1)} fusion(bf16[2048,2048]{1,0:T(8,128)(2,1)S(1)} %bitcast.108, f32[2048,1024]{1,0:T(8,128)} %fusion.23, f32[1024]{0:T(1024)S(1)} %bitcast.140), kind=kOutput, calls=%fused_computation.42 | convolution fusion | flops 8613003264 | bytes 20975616 | tf_op jit(solution)/shard_map/tf,td->fd/dot_general | solution.py:720
  411.5 1.5 copy-done.8
  413.0 12.5 %convert_reduce_fusion.1 = (f32[12,64]{1,0:T(8,128)}, bf16[12,2048,64]{2,1,0:T(8,128)(2,1)}) fusion(bf16[4,2048,64]{2,1,0:T(8,128)(2,1)S(1)} %copy-done.8, bf16[4,2048,32]{2,1,0:T(8,128)(2,1)} %slice.188, bf16[4,2048,16]{2,1,0:T(8,128)(2,1)} %get-tuple-element.52, bf16[4,2048,16]{2,1,0:T(8,128)(2,1)} %get-tuple-element.53, bf16[4,2048,32]{2,1,0:T(8,128)(2,1)} %slice.189, ...), kind=kLoop, calls=%fused_computation.10 | loop fusion | flops 25165056 | bytes 6294528 | tf_op jit(solution)/shard_map/reduce_sum | solution.py:743
  425.5 5.2 copy.104
  430.7 9.0 %fusion.49 = f32[2048,768]{0,1:S(1)} fusion(bf16[2048,768]{0,1:T(8,128)(2,1)S(1)} %bitcast.127, bf16[2048,2048]{1,0:T(8,128)(2,1)} %fusion.5), kind=kOutput, calls=%fused_computation.115 | convolution fusion | flops 6442450944 | bytes 17825792
  440.2 19.7 %convert_reduce_fusion.2 = (f32[1024]{0:T(1024)S(1)}, bf16[2048,1024]{1,0:T(8,128)(2,1)S(1)}) fusion(f32[2048,1024]{1,0:T(8,128)} %fusion.23, f32[1024]{0:T(1024)S(1)} %bitcast.141, bf16[2048,2048]{1,0:T(8,128)(2,1)} %all-gather.11.cloned.1.call-done, bf16[1024,2048]{1,0:T(8,128)(2,1)} %all-gather.9.cloned.1.call-done), kind=kOutput, calls=%fused_computation.27 | convolution fusion | flops 8636070912 | bytes 25174016 | tf_op jit(solution)/shard_map/td,fd->tf/dot_general | solution.py:721
  460.0 14.6 %convolution_convert_fusion.1 = bf16[2048,1024]{0,1:T(8,128)(2,1)} fusion(bf16[2048,2048]{1,0:T(8,128)(2,1)} %fusion.5, bf16[2048,1024]{1,0:T(8,128)(2,1)S(1)} %get-tuple-element.69), kind=kOutput, calls=%fused_computation.43 | convolution fusion | flops 8592031744 | bytes 16777216 | tf_op jit(solution)/shard_map/td,tf->df/dot_general | solution.py:753
  474.5 6.4 pad_maximum_fusion
  482.8 16.7 %fusion.45 = f32[2048,2048]{1,0:T(8,128)} fusion(bf16[1024,2048]{1,0:T(8,128)(2,1)} %all-gather.9.cloned.1.call-done, f32[2048,1024]{1,0:T(8,128)} %fusion.23, f32[1024]{0:T(1024)S(1)} %bitcast.142), kind=kOutput, calls=%fused_computation.111 | convolution fusion | flops 8610906112 | bytes 29364224 | tf_op jit(solution)/shard_map/dot_general | solution.py:711
  499.6 14.0 %bitcast_add_fusion.1.p_ref = f32[2048,2048]{1,0:T(8,128)} fusion(f32[2048,2048]{1,0:T(8,128)} %fusion.45, bf16[4,64,2048]{2,1,0:T(8,128)(2,1)S(1)} %bitcast.131, f32[4,2048,64]{2,1,0:T(8,128)S(1)} %copy-done.1), kind=kOutput, calls=%fused_computation.9 | convolution fusion | flops 2152202240 | bytes 36700160 | tf_op jit(solution)/shard_map/hte,hed->td/dot_general | solution.py:710
  513.5 91.0 %shard_map.261 = f32[256,2048]{1,0:T(8,128)} custom-call(f32[2048,2048]{1,0:T(8,128)} %bitcast_add_fusion.1.p_ref), custom_call_target="tpu_custom_call" | custom-call | tf_op jit(solution)/shard_map/pallas_call | solution.py:462
  604.5 15.5 %fusion.21 = f32[2048,2048]{1,0:T(8,128)} fusion(bf16[2048,1024]{1,0:T(8,128)(2,1)} %copy-done.32, bf16[2048,1792]{1,0:T(8,128)(2,1)} %all-gather.5.cloned.1.call-done), kind=kOutput, calls=%fused_computation.44 | convolution fusion | flops 8589934592 | bytes 25165824 | tf_op jit(solution)/shard_map/tf,df->td/dot_general | solution.py:746
  620.1 1.7 collective-permute-start.1
  621.8 15.4 %bitcast_add_fusion.p_ref = f32[2048,2048]{1,0:T(8,128)} fusion(f32[2048,2048]{1,0:T(8,128)} %fusion.21, bf16[12,2048,64]{2,1,0:T(8,128)(2,1)} %get-tuple-element.41, bf16[2048,12,64]{0,2,1:T(8,128)(2,1)} %bitcast.125), kind=kOutput, calls=%fused_computation.8 | convolution fusion | flops 6446645248 | bytes 39845888 | tf_op jit(solution)/shard_map/hte,dhe->td/dot_general | solution.py:744
  637.2 100.5 %shard_map.263 = f32[256,2048]{1,0:T(8,128)} custom-call(f32[2048,2048]{1,0:T(8,128)} %bitcast_add_fusion.p_ref), custom_call_target="tpu_custom_call" | custom-call | tf_op jit(solution)/shard_map/pallas_call | solution.py:462
  738.0 3.0 convert_element_type.227
  741.0 4.0 copy.105
  745.0 33.3 %shard_map.264 = bf16[8,64,1792]{2,1,0:T(8,128)(2,1)} custom-call(bf16[8,64,1792]{2,1,0:T(8,128)(2,1)} %bitcast.116), custom_call_target="tpu_custom_call" | custom-call | tf_op jit(solution)/shard_map/pallas_call | solution.py:527
  778.3 1.5 slice_convert_fusion.2
  779.8 2.4 slice_convert_fusion.3
  782.2 2.0 reshape.300
  784.2 2.8 copy.107
  787.0 2.5 copy.118
  789.5 2.6 reshape.299
  793.1 1.6 copy.117
  795.8 3.0 convert_reduce_fusion.4
  799.9 22.0 %shard_map.265 = f32[8,4,16,128]{3,2,1,0:T(8,128)} custom-call(f32[8,4,16,128]{3,2,1,0:T(8,128)} %copy_bitcast_fusion.3.x_ref), custom_call_target="tpu_custom_call" | custom-call | tf_op jit(solution)/shard_map/pallas_call | solution.py:527
  821.9 1.6 reduce_sum.158.x_ref
  823.5 8.4 shard_map.266
  (164 shorter events, 20.4 us)
Async XLA Ops:
  7.2 199.1 %all-gather.5.cloned.1.call-start = ((), (), s32[]{:S(2)}) async-start(), calls=%async_computation.3 | async-start | bytes 9175040 | tf_op jit(solution)/shard_map/all_gather | solution.py:612
  13.4 40.1 %copy-start.14 = (f32[64,2048]{1,0:T(8,128)S(1)}, f32[64,2048]{1,0:T(8,128)}, u32[]{:S(2)}) copy-start(f32[64,2048]{1,0:T(8,128)} %param.21) | copy-start | bytes 1572868
  53.4 254.7 %all-gather.7.cloned.1.call-start = ((), (), s32[]{:S(2)}) async-start(), calls=%async_computation.4 | async-start | bytes 1310720 | tf_op jit(solution)/shard_map/all_gather | solution.py:550
  53.5 0.7 collective-permute-start
  54.2 0.7 copy-start.17
  55.0 108.8 %copy-start.12 = (f32[256,2048]{1,0:T(8,128)S(1)}, f32[256,2048]{1,0:T(8,128)}, u32[]{:S(2)}) copy-start(f32[256,2048]{1,0:T(8,128)} %param.25) | copy-start | bytes 6291460
  55.0 253.1 %all-gather.11.cloned.1.call-start = ((), (), s32[]{:S(2)}) async-start(), calls=%async_computation.6 | async-start | bytes 9437184 | tf_op jit(solution)/shard_map/all_gather | solution.py:681
  163.6 1.5 copy-start.25
  163.7 1.5 copy-start.27
  163.7 1.5 copy-start.28
  163.7 1.6 copy-start.29
  163.7 1.6 copy-start.30
  163.7 1.6 copy-start.26
  163.7 276.5 %all-gather.9.cloned.1.call-start = ((), (), s32[]{:S(2)}) async-start(), calls=%async_computation.5 | async-start | bytes 5242880 | tf_op jit(solution)/shard_map/all_gather | solution.py:613
  164.9 455.1 %reduce-scatter.6.cloned.1.call-start = ((), (), s32[]{:S(2)}) async-start(), calls=%async_computation.8 | async-start | bytes 2621440 | tf_op jit(solution)/shard_map/reduce_scatter | solution.py:556
  184.1 5.8 copy-start
  190.0 2.7 copy-start.31
  192.4 13.9 %copy-start.18 = (f32[2048]{0:T(1024)}, f32[2048]{0:T(1024)S(1)}, u32[]{:S(2)}) copy-start(f32[2048]{0:T(1024)S(1)} %reshape.291) | copy-start | bytes 24580
  192.9 13.4 %copy-start.20 = (s32[2048]{0:T(1024)}, s32[2048]{0:T(1024)S(1)}, u32[]{:S(2)}) copy-start(s32[2048]{0:T(1024)S(1)} %convert_reduce_fusion.5) | copy-start | bytes 24580
  206.3 1.9 slice-start.2
  229.0 1.6 copy-start.6
  229.1 2.3 copy-start.7
  229.2 14.2 %copy-start.9 = (bf16[4,2048,64]{2,1,0:T(8,128)(2,1)}, bf16[4,2048,64]{2,1,0:T(8,128)(2,1)S(1)}, u32[]{:S(2)}) copy-start(bf16[4,2048,64]{2,1,0:T(8,128)(2,1)S(1)} %slice.148.v_ref) | copy-start | bytes 3145732
  324.4 413.6 %reduce-scatter.8.cloned.1.call-start = ((), (), s32[]{:S(2)}) async-start(), calls=%async_computation.9 | async-start | bytes 5242880 | tf_op jit(solution)/shard_map/reduce_scatter | solution.py:762
  384.6 3.9 copy-start.3
  384.6 5.9 copy-start.2
  390.5 6.9 slice-start
  392.4 4.9 slice-start.1
  411.4 1.6 copy-start.8
  411.4 329.6 %reduce-scatter.4.cloned.1.call-start = ((), (), s32[]{:S(2)}) async-start(), calls=%async_computation.7 | async-start | bytes 9175040 | tf_op jit(solution)/shard_map/reduce_scatter | solution.py:757
  460.0 14.6 %copy-start.32 = (bf16[2048,1024]{1,0:T(8,128)(2,1)}, bf16[2048,1024]{1,0:T(8,128)(2,1)S(1)}, u32[]{:S(2)}) copy-start(bf16[2048,1024]{1,0:T(8,128)(2,1)S(1)} %get-tuple-element.69) | copy-start | bytes 12582916
  480.9 0.7 copy-start.22
  480.9 0.8 copy-start.21
  480.9 1.3 copy-start.4
  482.8 16.7 %copy-start.1 = (f32[4,2048,64]{2,1,0:T(8,128)S(1)}, f32[4,2048,64]{2,1,0:T(8,128)}, u32[]{:S(2)}) copy-start(f32[4,2048,64]{2,1,0:T(8,128)} %get-tuple-element.27) | copy-start | bytes 6291460
  482.8 16.7 %copy-start.13 = (bf16[256,2048]{1,0:T(8,128)(2,1)S(1)}, bf16[256,2048]{1,0:T(8,128)(2,1)}, u32[]{:S(2)}) copy-start(bf16[256,2048]{1,0:T(8,128)(2,1)} %all-gather.7.cloned.1.call-done) | copy-start | bytes 3145732
  620.1 117.9 %collective-permute-start.1 = (f32[64,2048]{1,0:T(8,128)}, f32[64,2048]{1,0:T(8,128)S(1)}, u32[]{:S(2)}, u32[]{:S(2)}) collective-permute-start(f32[64,2048]{1,0:T(8,128)} %reduce-scatter.6.cloned.1.call-done), channel_id=1, source_target_pairs={{0,0},{8,1},{16,2},{24,3},{1,4},{9,5},{17,6},{25,7},{2,8},{10,9},{... | collective-permute-start | bytes 1572872 | tf_op jit(solution)/shard_map/ppermute | solution.py:558
  637.2 100.5 %copy-start.23 = (f32[12,64]{1,0:T(8,128)S(1)}, f32[12,64]{1,0:T(8,128)}, u32[]{:S(2)}) copy-start(f32[12,64]{1,0:T(8,128)} %get-tuple-element.40) | copy-start | bytes 9220
  738.0 7.0 copy-start.15
  792.1 2.6 copy-start.5
  792.1 2.6 copy-start.19
  792.1 3.6 copy-start.10
  792.1 3.6 copy-start.11
  795.8 39.0 %copy-start.16 = (f32[64,2048]{1,0:T(8,128)S(1)}, f32[64,2048]{1,0:T(8,128)}, u32[]{:S(2)}) copy-start(f32[64,2048]{1,0:T(8,128)} %copy-done.15) | copy-start | bytes 1572868
  833.2 2.4 copy-start.24
Sparse Core Ops, SparseCore 0:
  53.6 63.1 all-gather.4
  118.9 16.7 all-gather.6
  163.9 126.5 all-gather.10
  292.5 32.6 all-gather.8
  327.5 31.4 reduce-scatter.5
  411.5 47.4 reduce-scatter.7
  481.1 68.2 reduce-scatter.3

commit v16 on v15

--- a/solution.py
+++ b/solution.py
@@ -732,27 +732,18 @@
     dq_heads, dk_heads, dv_heads = attention_backward(
         q_heads, k_heads, v_heads, d_heads, log_total, delta, seg
     )
-    d_qkv_heads = jnp.concatenate(
-        [
-            rotate_back(dq_heads, cos_heads, sin_heads),
-            rotate_back(dk_heads, cos_heads, sin_heads),
-            dv_heads,
-        ],
-        axis=0,
-    ).astype(jnp.bfloat16)
-    bias_part = jnp.sum(d_qkv_heads.astype(jnp.float32), axis=1).reshape(3, head_width)
-    d_hidden_part = jnp.einsum(
-        "hte,dhe->td", d_qkv_heads, qkv_weights, preferred_element_type=jnp.float32
-    ) + jnp.einsum("tf,df->td", d_pre, fc1_weights, preferred_element_type=jnp.float32)
-    d_hidden = ring_reduce_scatter(d_hidden_part, ring, 3)
-    weight_parts = jnp.concatenate(
-        [
-            jnp.einsum(
-                "td,hte->dhe", hidden_group, d_qkv_heads, preferred_element_type=jnp.float32
-            ).reshape(D, qkv_width),
-            jnp.einsum("td,tf->df", hidden_group, d_pre, preferred_element_type=jnp.float32),
-        ],
-        axis=1,
+    shape = (group, local_heads, HEAD_DIM)
+    d_query = rotate_back(dq_heads.transpose(1, 0, 2), cosine, sine).reshape(group, head_width)
+    d_keys = rotate_back(dk_heads.transpose(1, 0, 2), cosine, sine).reshape(group, head_width)
+    d_values = dv_heads.transpose(1, 0, 2).reshape(group, head_width)
+    d_qkv = jnp.concatenate([d_query, d_keys, d_values], axis=1).astype(jnp.bfloat16)
+    d_both = jnp.concatenate([d_qkv, d_pre], axis=1)
+    bias_part = jnp.sum(d_qkv.astype(jnp.float32), axis=0).reshape(3, head_width)
+    d_hidden = ring_reduce_scatter(
+        jnp.einsum("tc,dc->td", d_both, cols, preferred_element_type=jnp.float32), ring, 3
+    )
+    weight_parts = jnp.einsum(
+        "td,tc->dc", hidden_group, d_both, preferred_element_type=jnp.float32
     ).astype(jnp.bfloat16)
     owned_parts = lax.psum_scatter(weight_parts, "dp", scatter_dimension=0, tiled=True)
     split_qkv, split_fc1 = return_heads(owned_parts)

time: 848 us -> 841 us (level)
  other arithmetic: 83.2 us -> 69.2 us
    pallas_call x6, Pallas kernels: 117 us -> 146 us  [exchange(): pl.pallas_call(functools.partial(_exchange_kernel, group=group), out_shap...]
    pallas_call x1, Pallas kernels: 109 us -> 95 us  [ring_all_gather(): pl.pallas_call(functools.partial(_gather_kernel, ring=ring, rows=rows), o...]
    pallas_call x2, Pallas kernels: 192 us -> 179 us  [ring_reduce_scatter(): pl.pallas_call(functools.partial(_scatter_kernel, ring=ring, rows=rows, p...]
    reduce_sum x1, other arithmetic: 12.5 us -> 0.56 us  [head_plan(): jnp.sum(d_qkv.astype(jnp.float32), axis=0).reshape(3, head_width)]
    unnamed x1 -> x0, matrix products: 9.04 us -> none
    convert_element_type x1 -> x0, other arithmetic: 8.59 us -> none  [head_plan(): norm_parts(tokens_group.astype(jnp.float32), gain32, shift32)[2]]
    dot_general x3 -> x2, matrix products: 45.5 us -> 50.9 us  [the longest x1 28.6 us: head_plan(): jnp.einsum('td,tc->dc', hidden_group, d_both, preferred_element_type=jnp....]
  transfers between devices with their start and end apart: 9 -> 9, of which waited for: 0 -> 0; matrix products, arithmetic and copies ran while one was open for 31% -> 30% of each run, Pallas kernels for 49% -> 50%
where the time goes in v16:
time: 841 us; the launch traced here: 835 us
  Pallas kernels  522 us (62%)
  matrix products  167 us (20%)
  other arithmetic  69.2 us (8%)
  local copies, waits for them, and re-layouts  55.6 us (7%)
  between operations  15.2 us (2%)
    pallas_call x2, Pallas kernels, ring_reduce_scatter(): pl.pallas_call(functools.partial(_scatter_kernel, ring=ring, rows=rows, p...  179 us
    pallas_call x6, Pallas kernels, exchange(): pl.pallas_call(functools.partial(_exchange_kernel, group=group), out_shap...  146 us
    pallas_call x1, Pallas kernels, ring_all_gather(): pl.pallas_call(functools.partial(_gather_kernel, ring=ring, rows=rows), o...  95 us
    pallas_call x1, Pallas kernels, attention_backward(): pl.pallas_call(functools.partial(_bwd_kernel, tq=block, tk=block, scale=s...  53.7 us
    pallas_call x1, Pallas kernels, attention_forward(): pl.pallas_call(functools.partial(_fwd_kernel, tq=block, tk=block, scale=s...  48.1 us
    dot_general x1, matrix products, head_plan(): jnp.einsum('td,tc->dc', hidden_group, d_both, preferred_element_type=jnp....  28.6 us
    dot_general x1, matrix products, head_plan(): jnp.einsum('tc,dc->td', d_both, cols, preferred_element_type=jnp.float32)  22.3 us
    dot_general x1, matrix products, head_plan(): jnp.einsum('td,fd->tf', dy_group, fc2_rows, preferred_element_type=jnp.fl...  21.1 us
  transfers between devices with their start and end apart: 9, of which 0 were waited for; matrix products, arithmetic and copies ran while one was open for 30% of the time, Pallas kernels for 50%

profile of v16, /device:TPU:0, one launch (start us, length us, event | category | flops | bytes accessed | tf_op | source)
XLA Modules:
  0.0 835.3 jit_solution(17508212297259222266)
XLA Ops:
  7.2 1.7 convert_element_type.183
  10.4 1.5 convert_element_type.182
  13.4 1.4 pad_maximum_fusion.5.x_ref
  14.7 38.6 %shard_map.256 = bf16[8,64,1792]{2,1,0:T(8,128)(2,1)} custom-call(bf16[8,64,1792]{2,1,0:T(8,128)(2,1)} %pad_maximum_fusion.5.x_ref), custom_call_target="tpu_custom_call" | custom-call | tf_op jit(solution)/shard_map/pallas_call | solution.py:527
  53.5 95.0 %shard_map.257 = bf16[2048,2048]{1,0:T(8,128)(2,1)} custom-call(bf16[256,2048]{1,0:T(8,128)(2,1)} %x_ref), custom_call_target="tpu_custom_call" | custom-call | tf_op jit(solution)/shard_map/pallas_call | solution.py:391
  150.1 1.1 convert_element_type.206
  152.3 19.1 %shard_map.258 = bf16[4,16,128]{2,1,0:T(8,128)(2,1)} custom-call(bf16[4,16,128]{2,1,0:T(8,128)(2,1)} %broadcast_in_dim.33.x_ref), custom_call_target="tpu_custom_call" | custom-call | tf_op jit(solution)/shard_map/pallas_call | solution.py:527
  171.4 1.4 broadcast_in_dim.34.x_ref
  172.8 25.8 %shard_map.259 = bf16[8,4,16,128]{3,2,1,0:T(8,128)(2,1)} custom-call(bf16[8,4,16,128]{3,2,1,0:T(8,128)(2,1)} %broadcast_in_dim.34.x_ref), custom_call_target="tpu_custom_call" | custom-call | tf_op jit(solution)/shard_map/pallas_call | solution.py:527
  200.4 4.7 convert_reduce_fusion
  205.1 1.1 copy-done
  206.1 2.3 fusion.2
  209.4 1.3 copy.102.segq_ref
  210.7 5.5 multiply_cosine_fusion
  216.2 1.9 slice-done
  218.1 3.0 copy.99
  221.1 17.3 %fusion.52 = (bf16[12,2048,64]{2,1,0:T(8,128)(2,1)S(1)}, f32[12,2048,64]{2,1,0:T(8,128)S(1)}) fusion(f32[12,64]{1,0:T(8,128)S(1)} %reshape.350, bf16[2048,12,64]{0,2,1:T(8,128)(2,1)} %bitcast.122, f32[2048]{0:T(1024)S(1)} %reshape.349, f32[2048]{0:T(1024)S(1)} %reshape.348, f32[2048]{0:T(1024)S(1)} %add_rsqrt_fusion, f32[2048]{0:T(1024)S(1)} %broadcast_multiply_fusion, ...), kind=kOutput, calls=%fused_computation.116 | convolution fusion | flops 6470762496 | bytes 21007360 | tf_op jit(solution)/shard_map/td,dhe->hte/dot_general | solution.py:692
  238.6 1.2 fusion.50
  240.8 4.8 subtract_convert_fusion.2
  245.7 7.0 pad_maximum_fusion.1
  252.7 2.0 maximum_maximum_fusion.v_ref
  254.7 48.1 %shard_map.260 = (f32[4,2048,64]{2,1,0:T(8,128)}, f32[4,2048,1]{2,1,0:T(8,128)}) custom-call(s32[10]{0:T(128)} %constant.61.clone.qi_ref, s32[10]{0:T(128)} %constant.62.clone.kj_ref, bf16[4,2048,64]{2,1,0:T(8,128)(2,1)} %get-tuple-element.68.q_ref, bf16[4,2048,64]{2,1,0:T(8,128)(2,1)} %get-tuple-element.69.k_ref, ...), custom_call_target="tpu_custom_call" | custom-call | flops 2147483648 | bytes 5242880 | tf_op jit(solution)/shard_map/pallas_call | solution.py:164
  302.8 9.1 %fusion.13 = f32[4,64,2048]{2,1,0:T(8,128)} fusion(bf16[2048,2048]{1,0:T(8,128)(2,1)} %all-gather.11.cloned.1.call-done, f32[4,2048,64]{2,1,0:T(8,128)} %get-tuple-element.27), kind=kOutput, calls=%fused_computation.19 | convolution fusion | flops 2148007936 | bytes 12582912 | tf_op jit(solution)/shard_map/hte,td->hed/dot_general | solution.py:724
  312.0 15.0 %fusion.21 = f32[2048,1024]{1,0:T(8,128)} fusion(bf16[2048,1792]{1,0:T(8,128)(2,1)} %all-gather.5.cloned.1.call-done, bf16[2048,2048]{1,0:T(8,128)(2,1)} %shard_map.257, f32[2048]{0:T(1024)S(1)} %reshape.349, f32[2048]{0:T(1024)S(1)} %reshape.348, f32[2048]{0:T(1024)S(1)} %add_rsqrt_fusion, f32[2048]{0:T(1024)S(1)} %broadcast_multiply_fusion), kind=kOutput, calls=%fused_computation.32 | convolution fusion | flops 8615100416 | bytes 21004288 | tf_op jit(solution)/shard_map/dot_general | solution.py:695
  326.9 6.0 fusion.23
  333.0 1.8 copy.104
  334.7 16.5 %convolution_convert_fusion.1 = bf16[1024,2048]{1,0:T(8,128)(2,1)} fusion(bf16[2048,2048]{1,0:T(8,128)(2,1)} %all-gather.11.cloned.1.call-done, f32[2048,1024]{1,0:T(8,128)} %fusion.21, f32[1024]{0:T(1024)S(1)} %bitcast.137), kind=kOutput, calls=%fused_computation.43 | convolution fusion | flops 8613003264 | bytes 20975616 | tf_op jit(solution)/shard_map/tf,td->fd/dot_general | solution.py:720
  351.3 4.4 multiply_reduce_fusion
  355.7 2.8 copy.105.delta_ref
  358.5 53.7 %shard_map.262 = (f32[4,2048,64]{2,1,0:T(8,128)}, f32[4,2048,64]{2,1,0:T(8,128)}, f32[4,2048,64]{2,1,0:T(8,128)}) custom-call(s32[10]{0:T(128)} %constant.63.clone.qi_ref, s32[10]{0:T(128)} %constant.64.clone.kj_ref, bf16[4,2048,64]{2,1,0:T(8,128)(2,1)} %get-tuple-element.68.q_ref, bf16[4,2048,64]{2,1,0:T(8,128)(2,1)} %get-tuple-element.69.k_ref, ...), custom_call_target="tpu_custom_call" | custom-call | flops 5368709120 | bytes 12582912 | tf_op jit(solution)/shard_map/pallas_call | solution.py:254
  412.2 2.9 slice.191
  415.8 1.9 slice.190
  417.7 4.3 add_convert_fusion.1
  422.0 3.2 pad_maximum_fusion.3
  425.2 1.9 copy.107
  427.1 6.1 pad_maximum_fusion.4
  433.2 1.9 copy.108
  435.1 3.8 convert_bitcast_fusion
  438.9 1.9 copy.109
  440.8 1.3 copy.110
  442.1 1.3 copy.111
  443.4 1.3 copy.112
  444.7 21.1 %convert_reduce_fusion.1 = (f32[1024]{0:T(1024)S(1)}, bf16[2048,1024]{1,0:T(8,128)(2,1)}) fusion(f32[2048,1024]{1,0:T(8,128)} %fusion.21, f32[1024]{0:T(1024)S(1)} %bitcast.138, bf16[2048,2048]{1,0:T(8,128)(2,1)} %all-gather.11.cloned.1.call-done, bf16[1024,2048]{1,0:T(8,128)(2,1)} %all-gather.9.cloned.1.call-done), kind=kOutput, calls=%fused_computation.25 | convolution fusion | flops 8636070912 | bytes 25174016 | tf_op jit(solution)/shard_map/td,fd->tf/dot_general | solution.py:721
  465.8 28.6 %convolution_convert_fusion = bf16[2048,1792]{1,0:T(8,128)(2,1)} fusion(bf16[2048,1024]{1,0:T(8,128)(2,1)} %get-tuple-element.67, bf16[2048,256]{1,0:T(8,128)(2,1)} %copy.112, bf16[2048,256]{1,0:T(8,128)(2,1)} %copy.111, bf16[2048,256]{1,0:T(8,128)(2,1)} %copy.110, bf16[2048,2048]{1,0:T(8,128)(2,1)} %shard_map.257, f32[2048]{0:T(1024)S(1)} %reshape.349, ...), kind=kOutput, calls=%fused_computation.27 | convolution fusion | flops 15090581504 | bytes 23101440 | tf_op jit(solution)/shard_map/td,tc->dc/dot_general | solution.py:745
  496.3 16.9 %fusion.46 = f32[2048,2048]{1,0:T(8,128)} fusion(bf16[1024,2048]{1,0:T(8,128)(2,1)} %all-gather.9.cloned.1.call-done, f32[2048,1024]{1,0:T(8,128)} %fusion.21, f32[1024]{0:T(1024)S(1)} %bitcast.139), kind=kOutput, calls=%fused_computation.113 | convolution fusion | flops 8610906112 | bytes 29364224 | tf_op jit(solution)/shard_map/dot_general | solution.py:711
  513.2 14.2 %bitcast_add_fusion.p_ref = f32[2048,2048]{1,0:T(8,128)} fusion(f32[2048,2048]{1,0:T(8,128)} %fusion.46, bf16[4,64,2048]{2,1,0:T(8,128)(2,1)S(1)} %bitcast.128, f32[4,2048,64]{2,1,0:T(8,128)S(1)} %copy-done.1), kind=kOutput, calls=%fused_computation.8 | convolution fusion | flops 2152202240 | bytes 36700160 | tf_op jit(solution)/shard_map/hte,hed->td/dot_general | solution.py:710
  527.4 88.8 %shard_map.261 = f32[256,2048]{1,0:T(8,128)} custom-call(f32[2048,2048]{1,0:T(8,128)} %bitcast_add_fusion.p_ref), custom_call_target="tpu_custom_call" | custom-call | tf_op jit(solution)/shard_map/pallas_call | solution.py:462
  616.2 5.5 collective-permute-start.1
  621.8 22.3 %fusion.40.p_ref = f32[2048,2048]{1,0:T(8,128)} fusion(bf16[2048,1792]{1,0:T(8,128)(2,1)} %all-gather.5.cloned.1.call-done, bf16[2048,1024]{1,0:T(8,128)(2,1)} %get-tuple-element.67, bf16[2048,256]{1,0:T(8,128)(2,1)} %copy.112, bf16[2048,256]{1,0:T(8,128)(2,1)} %copy.111, bf16[2048,256]{1,0:T(8,128)(2,1)} %copy.110), kind=kOutput, calls=%fused_computation.74 | convolution fusion | flops 15061745664 | bytes 31457280 | tf_op jit(solution)/shard_map/tc,dc->td/dot_general | solution.py:743
  644.8 89.9 %shard_map.263 = f32[256,2048]{1,0:T(8,128)} custom-call(f32[2048,2048]{1,0:T(8,128)} %fusion.40.p_ref), custom_call_target="tpu_custom_call" | custom-call | tf_op jit(solution)/shard_map/pallas_call | solution.py:462
  734.8 2.8 convert_element_type.230
  737.6 34.5 %shard_map.264 = bf16[8,64,1792]{2,1,0:T(8,128)(2,1)} custom-call(bf16[8,64,1792]{2,1,0:T(8,128)(2,1)} %bitcast.125), custom_call_target="tpu_custom_call" | custom-call | tf_op jit(solution)/shard_map/pallas_call | solution.py:527
  772.1 1.5 slice_convert_fusion.2
  773.6 2.4 slice_convert_fusion.3
  776.0 2.0 reshape.357
  778.0 2.8 copy.114
  780.8 2.5 copy.124
  783.3 2.6 reshape.356
  786.8 1.6 copy.123
  789.6 3.0 convert_reduce_fusion.4
  793.6 20.5 %shard_map.265 = f32[8,4,16,128]{3,2,1,0:T(8,128)} custom-call(f32[8,4,16,128]{3,2,1,0:T(8,128)} %copy_bitcast_fusion.3.x_ref), custom_call_target="tpu_custom_call" | custom-call | tf_op jit(solution)/shard_map/pallas_call | solution.py:527
  814.2 1.6 reduce_sum.158.x_ref
  815.8 7.6 shard_map.266
  826.3 1.9 copy.141
  (148 shorter events, 18.9 us)
Async XLA Ops:
  7.2 209.0 %all-gather.5.cloned.1.call-start = ((), (), s32[]{:S(2)}) async-start(), calls=%async_computation.3 | async-start | bytes 9175040 | tf_op jit(solution)/shard_map/all_gather | solution.py:612
  53.4 95.2 %copy-start.15 = (f32[64,2048]{1,0:T(8,128)S(1)}, f32[64,2048]{1,0:T(8,128)}, u32[]{:S(2)}) copy-start(f32[64,2048]{1,0:T(8,128)} %param.21) | copy-start | bytes 1572868
  53.4 96.7 %copy-start.13 = (f32[256,2048]{1,0:T(8,128)S(1)}, f32[256,2048]{1,0:T(8,128)}, u32[]{:S(2)}) copy-start(f32[256,2048]{1,0:T(8,128)} %param.25) | copy-start | bytes 6291460
  53.4 249.4 %all-gather.11.cloned.1.call-start = ((), (), s32[]{:S(2)}) async-start(), calls=%async_computation.6 | async-start | bytes 9437184 | tf_op jit(solution)/shard_map/all_gather | solution.py:681
  148.4 3.0 copy-start.21
  148.5 3.1 copy-start.23
  148.5 3.1 copy-start.24
  148.5 3.1 copy-start.25
  148.5 3.1 copy-start.26
  148.5 3.1 copy-start.22
  148.5 178.4 %all-gather.7.cloned.1.call-start = ((), (), s32[]{:S(2)}) async-start(), calls=%async_computation.4 | async-start | bytes 1310720 | tf_op jit(solution)/shard_map/all_gather | solution.py:550
  148.6 0.7 collective-permute-start
  149.3 0.7 copy-start.16
  150.1 294.6 %all-gather.9.cloned.1.call-start = ((), (), s32[]{:S(2)}) async-start(), calls=%async_computation.5 | async-start | bytes 5242880 | tf_op jit(solution)/shard_map/all_gather | solution.py:613
  151.3 465.0 %reduce-scatter.6.cloned.1.call-start = ((), (), s32[]{:S(2)}) async-start(), calls=%async_computation.8 | async-start | bytes 2621440 | tf_op jit(solution)/shard_map/reduce_scatter | solution.py:556
  200.4 5.8 copy-start
  206.1 2.7 copy-start.27
  209.1 7.2 copy-start.17
  216.2 1.9 slice-start
  238.5 14.2 %copy-start.10 = (bf16[4,2048,64]{2,1,0:T(8,128)(2,1)}, bf16[4,2048,64]{2,1,0:T(8,128)(2,1)S(1)}, u32[]{:S(2)}) copy-start(bf16[4,2048,64]{2,1,0:T(8,128)(2,1)S(1)} %slice.148.v_ref) | copy-start | bytes 3145732
  238.5 2.0 copy-start.8
  238.6 2.3 copy-start.9
  311.9 422.9 %reduce-scatter.8.cloned.1.call-start = ((), (), s32[]{:S(2)}) async-start(), calls=%async_computation.9 | async-start | bytes 5242880 | tf_op jit(solution)/shard_map/reduce_scatter | solution.py:753
  351.2 386.3 %reduce-scatter.4.cloned.1.call-start = ((), (), s32[]{:S(2)}) async-start(), calls=%async_computation.7 | async-start | bytes 9175040 | tf_op jit(solution)/shard_map/reduce_scatter | solution.py:748
  412.2 3.5 copy-start.3
  412.2 5.5 copy-start.2
  440.8 25.1 %copy-start.6 = (bf16[2048,4,64]{0,2,1:T(8,128)(2,1)}, bf16[2048,4,64]{0,2,1:T(8,128)(2,1)S(1)}, u32[]{:S(2)}) copy-start(bf16[2048,4,64]{0,2,1:T(8,128)(2,1)S(1)} %copy.109) | copy-start | bytes 3145732
  494.4 0.7 copy-start.19
  494.4 0.8 copy-start.18
  494.4 1.3 copy-start.4
  496.3 16.9 %copy-start.1 = (f32[4,2048,64]{2,1,0:T(8,128)S(1)}, f32[4,2048,64]{2,1,0:T(8,128)}, u32[]{:S(2)}) copy-start(f32[4,2048,64]{2,1,0:T(8,128)} %get-tuple-element.27) | copy-start | bytes 6291460
  496.3 16.9 %copy-start.14 = (bf16[256,2048]{1,0:T(8,128)(2,1)S(1)}, bf16[256,2048]{1,0:T(8,128)(2,1)}, u32[]{:S(2)}) copy-start(bf16[256,2048]{1,0:T(8,128)(2,1)} %all-gather.7.cloned.1.call-done) | copy-start | bytes 3145732
  616.2 27.8 %copy-start.7 = (bf16[2048,4,64]{0,2,1:T(8,128)(2,1)S(1)}, bf16[2048,4,64]{0,2,1:T(8,128)(2,1)}, u32[]{:S(2)}) copy-start(bf16[2048,4,64]{0,2,1:T(8,128)(2,1)} %copy-done.6) | copy-start | bytes 3145732
  616.2 118.5 %collective-permute-start.1 = (f32[64,2048]{1,0:T(8,128)}, f32[64,2048]{1,0:T(8,128)}, u32[]{:S(2)}, u32[]{:S(2)}) collective-permute-start(f32[64,2048]{1,0:T(8,128)} %reduce-scatter.6.cloned.1.call-done), channel_id=1, source_target_pairs={{0,0},{8,1},{16,2},{24,3},{1,4},{9,5},{17,6},{25,7},{2,8},{10,9},{... | collective-permute-start | bytes 1572872 | tf_op jit(solution)/shard_map/ppermute | solution.py:558
  785.9 2.6 copy-start.5
  785.9 3.6 copy-start.11
  785.9 3.6 copy-start.12
  824.7 3.5 copy-start.20
Sparse Core Ops, SparseCore 0:
  53.5 63.1 all-gather.4
  148.7 131.4 all-gather.10
  282.3 14.9 all-gather.6
  299.3 34.4 all-gather.8
  336.2 31.4 reduce-scatter.5
  370.2 44.5 reduce-scatter.7
  494.5 67.3 reduce-scatter.3

commit v17 on v14

--- a/solution.py
+++ b/solution.py
@@ -115,7 +115,11 @@
         s = lax.dot_general(q, k, TRANS_B, preferred_element_type=jnp.float32) * scale
         s = jnp.where(_allowed(segq_ref, segk_ref, i, j, tq, tk, causal), s, -jnp.inf)
         m_prev = m_sc[...]
-        m_new = jnp.maximum(m_prev, jnp.max(s, axis=1, keepdims=True))
+        lanes = s.shape[1]
+        folded = s[:, :128]
+        for start in range(128, lanes, 128):
+            folded = jnp.maximum(folded, s[:, start : start + 128])
+        m_new = jnp.maximum(m_prev, jnp.max(folded, axis=1, keepdims=True))
         factor = jnp.exp(m_prev - m_new)
         p = jnp.exp(s - m_new)
         acc_sc[...] = acc_sc[...] * factor + jnp.dot(

time: 839 us -> 839 us (level)
  transfers between devices with their start and end apart: 9 -> 9, of which waited for: 0 -> 0; matrix products, arithmetic and copies ran while one was open for 31% -> 31% of each run, Pallas kernels for 49% -> 50%
where the time goes in v17:
time: 839 us; the launch traced here: 833 us
  Pallas kernels  513 us (61%)
  matrix products  152 us (18%)
  local copies, waits for them, and re-layouts  81.2 us (10%)
  other arithmetic  65.5 us (8%)
  between operations  15.2 us (2%)
    pallas_call x2, Pallas kernels, ring_reduce_scatter(): pl.pallas_call(functools.partial(_scatter_kernel, ring=ring, rows=rows, p...  187 us
    pallas_call x6, Pallas kernels, exchange(): pl.pallas_call(functools.partial(_exchange_kernel, group=group), out_shap...  115 us
    pallas_call x1, Pallas kernels, ring_all_gather(): pl.pallas_call(functools.partial(_gather_kernel, ring=ring, rows=rows), o...  109 us
    pallas_call x1, Pallas kernels, attention_backward(): pl.pallas_call(functools.partial(_bwd_kernel, tq=block, tk=block, scale=s...  53.9 us
    pallas_call x1, Pallas kernels, attention_forward(): pl.pallas_call(functools.partial(_fwd_kernel, tq=block, tk=block, scale=s...  48.1 us
    unnamed x84, local copies, waits for them, and re-layouts  31.3 us
    dot_general x1, matrix products, head_plan(): jnp.einsum('td,tc->dc', hidden_group, d_both, preferred_element_type=jnp....  28.7 us
    dot_general x1, matrix products, head_plan(): jnp.dot(hidden_group, cols, preferred_element_type=jnp.float32)  23.2 us
  transfers between devices with their start and end apart: 9, of which 0 were waited for; matrix products, arithmetic and copies ran while one was open for 31% of the time, Pallas kernels for 50%

profile of v17, /device:TPU:0, one launch (start us, length us, event | category | flops | bytes accessed | tf_op | source)
XLA Modules:
  0.0 833.4 jit_solution(11207436705645688573)
XLA Ops:
  7.2 1.7 convert_element_type.177
  10.4 1.5 convert_element_type.176
  14.8 38.6 %shard_map.256 = bf16[8,64,1792]{2,1,0:T(8,128)(2,1)} custom-call(bf16[8,64,1792]{2,1,0:T(8,128)(2,1)} %pad_maximum_fusion.3.x_ref), custom_call_target="tpu_custom_call" | custom-call | tf_op jit(solution)/shard_map/pallas_call | solution.py:531
  55.0 108.6 %shard_map.257 = bf16[2048,2048]{1,0:T(8,128)(2,1)} custom-call(bf16[256,2048]{1,0:T(8,128)(2,1)} %x_ref), custom_call_target="tpu_custom_call" | custom-call | tf_op jit(solution)/shard_map/pallas_call | solution.py:395
  166.0 5.0 shard_map.258
  171.0 1.4 broadcast_in_dim.34.x_ref
  172.4 10.0 %shard_map.259 = bf16[8,4,16,128]{3,2,1,0:T(8,128)(2,1)} custom-call(bf16[8,4,16,128]{3,2,1,0:T(8,128)(2,1)} %broadcast_in_dim.34.x_ref), custom_call_target="tpu_custom_call" | custom-call | tf_op jit(solution)/shard_map/pallas_call | solution.py:531
  184.3 4.7 convert_reduce_fusion
  190.2 2.3 fusion.2
  195.8 23.2 %convolution_add_fusion = f32[2048,1792]{0,1:T(8,128)} fusion(bf16[2048,1792]{1,0:T(8,128)(2,1)} %all-gather.5.cloned.1.call-done, f32[1792]{0:T(1024)S(1)} %maximum_convert_fusion, bf16[2048,2048]{1,0:T(8,128)(2,1)} %shard_map.257, f32[2048]{0:T(1024)S(1)} %reshape.300, f32[2048]{0:T(1024)S(1)} %reshape.299, f32[2048]{0:T(1024)S(1)} %add_rsqrt_fusion, ...), kind=kOutput, calls=%fused_computation.10 | convolution fusion | flops 15061221376 | bytes 30448640 | tf_op jit(solution)/shard_map/dot_general | solution.py:692
  219.0 1.7 slice.195
  220.7 3.9 fusion.34
  226.5 3.5 copy.129
  230.1 3.5 copy.130
  233.6 2.1 slice.196
  235.7 2.3 fusion.35
  238.0 3.7 copy.132
  241.6 3.6 copy.133
  245.2 3.0 copy.131
  248.2 2.6 copy.134
  250.8 1.8 copy.114
  252.6 7.3 subtract_convert_fusion.2
  259.9 5.2 maximum_bitcast_fusion
  265.1 2.0 maximum_maximum_fusion.v_ref
  267.1 48.1 %shard_map.260 = (f32[4,2048,64]{2,1,0:T(8,128)}, f32[4,2048,1]{2,1,0:T(8,128)}) custom-call(s32[10]{0:T(128)} %constant.61.clone.qi_ref, s32[10]{0:T(128)} %constant.62.clone.kj_ref, bf16[4,2048,64]{2,1,0:T(8,128)(2,1)} %get-tuple-element.74.q_ref, bf16[4,2048,64]{2,1,0:T(8,128)(2,1)} %get-tuple-element.75.k_ref, ...), custom_call_target="tpu_custom_call" | custom-call | flops 2147483648 | bytes 5242880 | tf_op jit(solution)/shard_map/pallas_call | solution.py:168
  315.2 6.0 convolution_convert_fusion.2
  321.2 1.8 copy.117
  323.0 6.8 multiply_reduce_fusion
  329.8 2.1 copy.116
  331.9 7.4 fusion.38
  339.4 2.8 copy.118.delta_ref
  342.2 15.6 %convolution_convert_fusion.1 = bf16[1024,2048]{1,0:T(8,128)(2,1)} fusion(bf16[2048,2048]{1,0:T(8,128)(2,1)} %all-gather.11.cloned.1.call-done, f32[2048,1792]{0,1:T(8,128)} %convolution_add_fusion), kind=kOutput, calls=%fused_computation.35 | convolution fusion | flops 8610906112 | bytes 20971520 | tf_op jit(solution)/shard_map/tf,td->fd/dot_general | solution.py:720
  357.8 53.9 %shard_map.262 = (f32[4,2048,64]{2,1,0:T(8,128)}, f32[4,2048,64]{2,1,0:T(8,128)}, f32[4,2048,64]{2,1,0:T(8,128)}) custom-call(s32[10]{0:T(128)} %constant.63.clone.qi_ref, s32[10]{0:T(128)} %constant.64.clone.kj_ref, bf16[4,2048,64]{2,1,0:T(8,128)(2,1)} %get-tuple-element.74.q_ref, bf16[4,2048,64]{2,1,0:T(8,128)(2,1)} %get-tuple-element.75.k_ref, ...), custom_call_target="tpu_custom_call" | custom-call | flops 5368709120 | bytes 12582912 | tf_op jit(solution)/shard_map/pallas_call | solution.py:258
  411.7 2.9 slice.194
  415.1 1.9 slice.193
  417.0 4.3 add_convert_fusion.1
  421.3 3.2 pad_maximum_fusion.1
  424.6 1.9 copy.120
  426.5 5.4 pad_maximum_fusion.2
  431.9 2.7 copy.121
  434.6 2.5 convert_bitcast_fusion
  437.1 1.6 copy.122
  438.7 18.4 %convert_reduce_fusion.1 = (f32[1024]{0:T(1024)S(1)}, bf16[2048,1024]{0,1:T(8,128)(2,1)}) fusion(f32[2048,1792]{0,1:T(8,128)} %convolution_add_fusion, bf16[2048,2048]{1,0:T(8,128)(2,1)} %all-gather.11.cloned.1.call-done, bf16[1024,2048]{1,0:T(8,128)(2,1)} %all-gather.9.cloned.1.call-done), kind=kOutput, calls=%fused_computation.19 | convolution fusion | flops 8633973760 | bytes 25169920 | tf_op jit(solution)/shard_map/td,fd->tf/dot_general | solution.py:721
  457.1 28.7 %convolution_convert_fusion = bf16[2048,1792]{1,0:T(8,128)(2,1)} fusion(bf16[2048,1024]{0,1:T(8,128)(2,1)} %get-tuple-element.73, bf16[2048,256]{0,1:T(8,128)(2,1)S(1)} %bitcast.120, bf16[2048,256]{0,1:T(8,128)(2,1)S(1)} %bitcast.117, bf16[2048,256]{0,1:T(8,128)(2,1)S(1)} %bitcast.114, bf16[2048,2048]{1,0:T(8,128)(2,1)} %shard_map.257, ...), kind=kOutput, calls=%fused_computation.21 | convolution fusion | flops 15090581504 | bytes 23101440 | tf_op jit(solution)/shard_map/td,tc->dc/dot_general | solution.py:749
  487.8 16.8 %fusion.31 = f32[2048,2048]{1,0:T(8,128)} fusion(bf16[1024,2048]{1,0:T(8,128)(2,1)} %all-gather.9.cloned.1.call-done, f32[2048,1792]{0,1:T(8,128)} %convolution_add_fusion), kind=kOutput, calls=%fused_computation.108 | convolution fusion | flops 8608808960 | bytes 29360128 | tf_op jit(solution)/shard_map/dot_general | solution.py:711
  504.6 21.4 %fusion.27.p_ref = f32[2048,2048]{1,0:T(8,128)} fusion(bf16[2048,1792]{1,0:T(8,128)(2,1)} %all-gather.5.cloned.1.call-done, bf16[2048,1024]{0,1:T(8,128)(2,1)S(1)} %copy-done.33, bf16[2048,256]{0,1:T(8,128)(2,1)S(1)} %bitcast.121, bf16[2048,256]{0,1:T(8,128)(2,1)S(1)} %bitcast.118, bf16[2048,256]{0,1:T(8,128)(2,1)S(1)} %bitcast.115), kind=kOutput, calls=%fused_computation.66 | convolution fusion | flops 15061745664 | bytes 31457280 | tf_op jit(solution)/shard_map/tc,dc->td/dot_general | solution.py:747
  526.0 5.5 collective-permute-start.1
  531.5 14.4 %convolution_add_fusion.1.p_ref = f32[2048,2048]{1,0:T(8,128)} fusion(f32[2048,2048]{1,0:T(8,128)} %fusion.31, bf16[2048,256]{0,1:T(8,128)(2,1)S(1)} %bitcast.108, bf16[256,2048]{1,0:T(8,128)(2,1)} %all-gather.7.cloned.1.call-done), kind=kOutput, calls=%fused_computation.11 | convolution fusion | flops 2151677952 | bytes 35651584 | tf_op jit(solution)/shard_map/dot_general | solution.py:710
  546.8 98.6 %shard_map.263 = f32[256,2048]{1,0:T(8,128)} custom-call(f32[2048,2048]{1,0:T(8,128)} %fusion.27.p_ref), custom_call_target="tpu_custom_call" | custom-call | tf_op jit(solution)/shard_map/pallas_call | solution.py:466
  645.4 88.4 %shard_map.261 = f32[256,2048]{1,0:T(8,128)} custom-call(f32[2048,2048]{1,0:T(8,128)} %convolution_add_fusion.1.p_ref), custom_call_target="tpu_custom_call" | custom-call | tf_op jit(solution)/shard_map/pallas_call | solution.py:466
  733.9 2.8 convert_element_type.223
  736.7 32.8 %shard_map.264 = bf16[8,64,1792]{2,1,0:T(8,128)(2,1)} custom-call(bf16[8,64,1792]{2,1,0:T(8,128)(2,1)} %bitcast.131), custom_call_target="tpu_custom_call" | custom-call | tf_op jit(solution)/shard_map/pallas_call | solution.py:531
  769.5 1.5 slice_convert_fusion.5
  770.9 2.4 slice_convert_fusion.6
  773.3 2.0 reshape.306
  775.3 2.8 copy.125
  778.1 2.5 copy.140
  780.6 2.6 reshape.305
  784.2 1.6 copy.139
  786.9 3.0 convert_reduce_fusion.4
  791.0 19.7 %shard_map.265 = f32[8,4,16,128]{3,2,1,0:T(8,128)} custom-call(f32[8,4,16,128]{3,2,1,0:T(8,128)} %copy_bitcast_fusion.3.x_ref), custom_call_target="tpu_custom_call" | custom-call | tf_op jit(solution)/shard_map/pallas_call | solution.py:531
  810.7 1.6 reduce_sum.158.x_ref
  812.3 9.2 %shard_map.266 = f32[4,16,128]{2,1,0:T(8,128)} custom-call(f32[4,16,128]{2,1,0:T(8,128)} %reduce_sum.158.x_ref), custom_call_target="tpu_custom_call" | custom-call | tf_op jit(solution)/shard_map/pallas_call | solution.py:531
  824.5 1.9 copy.157
  (169 shorter events, 25.7 us)
Async XLA Ops:
  7.2 188.6 %all-gather.5.cloned.1.call-start = ((), (), s32[]{:S(2)}) async-start(), calls=%async_computation.3 | async-start | bytes 9175040 | tf_op jit(solution)/shard_map/all_gather | solution.py:616
  13.4 40.1 %copy-start.20 = (f32[64,2048]{1,0:T(8,128)S(1)}, f32[64,2048]{1,0:T(8,128)}, u32[]{:S(2)}) copy-start(f32[64,2048]{1,0:T(8,128)} %param.21) | copy-start | bytes 1572868
  53.4 261.8 %all-gather.7.cloned.1.call-start = ((), (), s32[]{:S(2)}) async-start(), calls=%async_computation.4 | async-start | bytes 1310720 | tf_op jit(solution)/shard_map/all_gather | solution.py:554
  53.5 0.7 collective-permute-start
  54.2 0.7 copy-start.21
  54.9 108.8 %copy-start.19 = (f32[256,2048]{1,0:T(8,128)S(1)}, f32[256,2048]{1,0:T(8,128)}, u32[]{:S(2)}) copy-start(f32[256,2048]{1,0:T(8,128)} %param.25) | copy-start | bytes 6291460
  54.9 260.2 %all-gather.11.cloned.1.call-start = ((), (), s32[]{:S(2)}) async-start(), calls=%async_computation.6 | async-start | bytes 9437184 | tf_op jit(solution)/shard_map/all_gather | solution.py:685
  163.6 1.5 copy-start.26
  163.6 1.5 copy-start.28
  163.6 1.5 copy-start.29
  163.7 1.6 copy-start.30
  163.7 1.6 copy-start.31
  163.7 1.6 copy-start.27
  163.7 275.0 %all-gather.9.cloned.1.call-start = ((), (), s32[]{:S(2)}) async-start(), calls=%async_computation.5 | async-start | bytes 5242880 | tf_op jit(solution)/shard_map/all_gather | solution.py:617
  164.9 361.1 %reduce-scatter.6.cloned.1.call-start = ((), (), s32[]{:S(2)}) async-start(), calls=%async_computation.8 | async-start | bytes 2621440 | tf_op jit(solution)/shard_map/reduce_scatter | solution.py:560
  184.3 5.8 copy-start
  190.2 2.5 copy-start.32
  192.9 26.1 %copy-start.22 = (s32[2048]{0:T(1024)}, s32[2048]{0:T(1024)S(1)}, u32[]{:S(2)}) copy-start(s32[2048]{0:T(1024)S(1)} %convert_reduce_fusion.5) | copy-start | bytes 24580
  252.6 7.3 copy-start.8
  252.6 7.3 copy-start.9
  259.9 5.2 copy-start.5
  331.9 7.4 copy-start.10
  339.3 394.5 %reduce-scatter.8.cloned.1.call-start = ((), (), s32[]{:S(2)}) async-start(), calls=%async_computation.9 | async-start | bytes 5242880 | tf_op jit(solution)/shard_map/reduce_scatter | solution.py:757
  357.8 378.9 %reduce-scatter.4.cloned.1.call-start = ((), (), s32[]{:S(2)}) async-start(), calls=%async_computation.7 | async-start | bytes 9175040 | tf_op jit(solution)/shard_map/reduce_scatter | solution.py:752
  411.7 3.5 copy-start.2
  411.7 5.4 copy-start.1
  421.3 5.2 copy-start.7
  438.7 18.4 %copy-start.12 = (bf16[2048,4,64]{0,2,1:T(8,128)(2,1)S(1)}, bf16[2048,4,64]{0,2,1:T(8,128)(2,1)}, u32[]{:S(2)}) copy-start(bf16[2048,4,64]{0,2,1:T(8,128)(2,1)} %copy.121) | copy-start | bytes 3145732
  438.7 18.4 %copy-start.15 = (bf16[2048,4,64]{0,2,1:T(8,128)(2,1)S(1)}, bf16[2048,4,64]{0,2,1:T(8,128)(2,1)}, u32[]{:S(2)}) copy-start(bf16[2048,4,64]{0,2,1:T(8,128)(2,1)} %copy.122) | copy-start | bytes 3145732
  485.8 0.7 copy-start.24
  485.8 0.8 copy-start.23
  485.8 1.2 copy-start.3
  487.7 16.9 %copy-start.13 = (bf16[2048,4,64]{0,2,1:T(8,128)(2,1)S(1)}, bf16[2048,4,64]{0,2,1:T(8,128)(2,1)}, u32[]{:S(2)}) copy-start(bf16[2048,4,64]{0,2,1:T(8,128)(2,1)} %copy.121) | copy-start | bytes 3145732
  487.7 16.9 %copy-start.16 = (bf16[2048,4,64]{0,2,1:T(8,128)(2,1)S(1)}, bf16[2048,4,64]{0,2,1:T(8,128)(2,1)}, u32[]{:S(2)}) copy-start(bf16[2048,4,64]{0,2,1:T(8,128)(2,1)} %copy.122) | copy-start | bytes 3145732
  487.8 16.8 %copy-start.33 = (bf16[2048,1024]{0,1:T(8,128)(2,1)S(1)}, bf16[2048,1024]{0,1:T(8,128)(2,1)}, u32[]{:S(2)}) copy-start(bf16[2048,1024]{0,1:T(8,128)(2,1)} %get-tuple-element.73) | copy-start | bytes 12582916
  504.6 26.9 %copy-start.11 = (bf16[2048,4,64]{0,2,1:T(8,128)(2,1)S(1)}, bf16[2048,4,64]{0,2,1:T(8,128)(2,1)}, u32[]{:S(2)}) copy-start(bf16[2048,4,64]{0,2,1:T(8,128)(2,1)} %copy-done.10) | copy-start | bytes 3145732
  526.0 19.9 %copy-start.14 = (bf16[2048,4,64]{0,2,1:T(8,128)(2,1)S(1)}, bf16[2048,4,64]{0,2,1:T(8,128)(2,1)}, u32[]{:S(2)}) copy-start(bf16[2048,4,64]{0,2,1:T(8,128)(2,1)} %copy.121) | copy-start | bytes 3145732
  526.0 19.9 %copy-start.17 = (bf16[2048,4,64]{0,2,1:T(8,128)(2,1)S(1)}, bf16[2048,4,64]{0,2,1:T(8,128)(2,1)}, u32[]{:S(2)}) copy-start(bf16[2048,4,64]{0,2,1:T(8,128)(2,1)} %copy.122) | copy-start | bytes 3145732
  526.0 207.9 %collective-permute-start.1 = (f32[64,2048]{1,0:T(8,128)}, f32[64,2048]{1,0:T(8,128)}, u32[]{:S(2)}, u32[]{:S(2)}) collective-permute-start(f32[64,2048]{1,0:T(8,128)} %reduce-scatter.6.cloned.1.call-done), channel_id=1, source_target_pairs={{0,0},{8,1},{16,2},{24,3},{1,4},{9,5},{17,6},{25,7},{2,8},{10,9},{... | collective-permute-start | bytes 1572872 | tf_op jit(solution)/shard_map/ppermute | solution.py:562
  783.2 2.6 copy-start.4
  783.3 3.6 copy-start.6
  783.3 3.6 copy-start.18
  822.8 3.5 copy-start.25
Sparse Core Ops, SparseCore 0:
  53.5 63.1 all-gather.4
  118.3 16.7 all-gather.6
  163.8 126.5 all-gather.10
  292.4 32.6 all-gather.8
  339.5 33.9 reduce-scatter.5
  376.0 44.5 reduce-scatter.7
  486.0 75.3 reduce-scatter.3

commit v18 on v17

--- a/solution.py
+++ b/solution.py
@@ -458,7 +458,7 @@
         copy.wait_send()
 
 
-def ring_reduce_scatter(p, ring, collective_id, out_dtype=jnp.float32, wire=jnp.bfloat16, parts=2):
+def ring_reduce_scatter(p, ring, collective_id, out_dtype=jnp.float32, wire=jnp.bfloat16, parts=4):
     total_rows, cols = p.shape
     n = ring.size
     rows = total_rows // n

time: 839 us -> 841 us (level)
  no operation moved by 1% of the time
where the time goes in v18:
time: 841 us; the launch traced here: 835 us
  Pallas kernels  514 us (61%)
  matrix products  152 us (18%)
  local copies, waits for them, and re-layouts  81.2 us (10%)
  other arithmetic  65.5 us (8%)
  between operations  15.2 us (2%)
    pallas_call x2, Pallas kernels, ring_reduce_scatter(): pl.pallas_call(functools.partial(_scatter_kernel, ring=ring, rows=rows, p...  188 us
    pallas_call x6, Pallas kernels, exchange(): pl.pallas_call(functools.partial(_exchange_kernel, group=group), out_shap...  116 us
    pallas_call x1, Pallas kernels, ring_all_gather(): pl.pallas_call(functools.partial(_gather_kernel, ring=ring, rows=rows), o...  109 us
    pallas_call x1, Pallas kernels, attention_backward(): pl.pallas_call(functools.partial(_bwd_kernel, tq=block, tk=block, scale=s...  53.8 us
    pallas_call x1, Pallas kernels, attention_forward(): pl.pallas_call(functools.partial(_fwd_kernel, tq=block, tk=block, scale=s...  48.1 us
    unnamed x84, local copies, waits for them, and re-layouts  31.3 us
    dot_general x1, matrix products, head_plan(): jnp.einsum('td,tc->dc', hidden_group, d_both, preferred_element_type=jnp....  28.7 us
    dot_general x1, matrix products, head_plan(): jnp.dot(hidden_group, cols, preferred_element_type=jnp.float32)  23.2 us
  transfers between devices with their start and end apart: 9, of which 0 were waited for; matrix products, arithmetic and copies ran while one was open for 31% of the time, Pallas kernels for 50%

profile of v18, /device:TPU:0, one launch (start us, length us, event | category | flops | bytes accessed | tf_op | source)
XLA Modules:
  0.0 834.7 jit_solution(11287587004728317925)
XLA Ops:
  7.2 1.7 convert_element_type.177
  10.4 1.5 convert_element_type.176
  14.8 38.6 %shard_map.256 = bf16[8,64,1792]{2,1,0:T(8,128)(2,1)} custom-call(bf16[8,64,1792]{2,1,0:T(8,128)(2,1)} %pad_maximum_fusion.3.x_ref), custom_call_target="tpu_custom_call" | custom-call | tf_op jit(solution)/shard_map/pallas_call | solution.py:531
  55.0 108.6 %shard_map.257 = bf16[2048,2048]{1,0:T(8,128)(2,1)} custom-call(bf16[256,2048]{1,0:T(8,128)(2,1)} %x_ref), custom_call_target="tpu_custom_call" | custom-call | tf_op jit(solution)/shard_map/pallas_call | solution.py:395
  166.0 5.0 shard_map.258
  171.0 1.4 broadcast_in_dim.34.x_ref
  172.4 10.0 %shard_map.259 = bf16[8,4,16,128]{3,2,1,0:T(8,128)(2,1)} custom-call(bf16[8,4,16,128]{3,2,1,0:T(8,128)(2,1)} %broadcast_in_dim.34.x_ref), custom_call_target="tpu_custom_call" | custom-call | tf_op jit(solution)/shard_map/pallas_call | solution.py:531
  184.3 4.7 convert_reduce_fusion
  190.2 2.3 fusion.2
  195.8 23.2 %convolution_add_fusion = f32[2048,1792]{0,1:T(8,128)} fusion(bf16[2048,1792]{1,0:T(8,128)(2,1)} %all-gather.5.cloned.1.call-done, f32[1792]{0:T(1024)S(1)} %maximum_convert_fusion, bf16[2048,2048]{1,0:T(8,128)(2,1)} %shard_map.257, f32[2048]{0:T(1024)S(1)} %reshape.300, f32[2048]{0:T(1024)S(1)} %reshape.299, f32[2048]{0:T(1024)S(1)} %add_rsqrt_fusion, ...), kind=kOutput, calls=%fused_computation.10 | convolution fusion | flops 15061221376 | bytes 30448640 | tf_op jit(solution)/shard_map/dot_general | solution.py:692
  219.0 1.7 slice.195
  220.7 3.9 fusion.34
  226.6 3.5 copy.129
  230.1 3.5 copy.130
  233.6 2.1 slice.196
  235.7 2.3 fusion.35
  238.0 3.7 copy.132
  241.7 3.6 copy.133
  245.2 3.0 copy.131
  248.2 2.6 copy.134
  250.8 1.8 copy.114
  252.6 7.3 subtract_convert_fusion.2
  259.9 5.2 maximum_bitcast_fusion
  265.1 2.0 maximum_maximum_fusion.v_ref
  267.1 48.1 %shard_map.260 = (f32[4,2048,64]{2,1,0:T(8,128)}, f32[4,2048,1]{2,1,0:T(8,128)}) custom-call(s32[10]{0:T(128)} %constant.61.clone.qi_ref, s32[10]{0:T(128)} %constant.62.clone.kj_ref, bf16[4,2048,64]{2,1,0:T(8,128)(2,1)} %get-tuple-element.74.q_ref, bf16[4,2048,64]{2,1,0:T(8,128)(2,1)} %get-tuple-element.75.k_ref, ...), custom_call_target="tpu_custom_call" | custom-call | flops 2147483648 | bytes 5242880 | tf_op jit(solution)/shard_map/pallas_call | solution.py:168
  315.2 6.0 convolution_convert_fusion.2
  321.3 1.8 copy.117
  323.0 6.8 multiply_reduce_fusion
  329.8 2.1 copy.116
  331.9 7.4 fusion.38
  339.4 2.8 copy.118.delta_ref
  342.2 15.6 %convolution_convert_fusion.1 = bf16[1024,2048]{1,0:T(8,128)(2,1)} fusion(bf16[2048,2048]{1,0:T(8,128)(2,1)} %all-gather.11.cloned.1.call-done, f32[2048,1792]{0,1:T(8,128)} %convolution_add_fusion), kind=kOutput, calls=%fused_computation.35 | convolution fusion | flops 8610906112 | bytes 20971520 | tf_op jit(solution)/shard_map/tf,td->fd/dot_general | solution.py:720
  357.8 53.8 %shard_map.262 = (f32[4,2048,64]{2,1,0:T(8,128)}, f32[4,2048,64]{2,1,0:T(8,128)}, f32[4,2048,64]{2,1,0:T(8,128)}) custom-call(s32[10]{0:T(128)} %constant.63.clone.qi_ref, s32[10]{0:T(128)} %constant.64.clone.kj_ref, bf16[4,2048,64]{2,1,0:T(8,128)(2,1)} %get-tuple-element.74.q_ref, bf16[4,2048,64]{2,1,0:T(8,128)(2,1)} %get-tuple-element.75.k_ref, ...), custom_call_target="tpu_custom_call" | custom-call | flops 5368709120 | bytes 12582912 | tf_op jit(solution)/shard_map/pallas_call | solution.py:258
  411.7 2.9 slice.194
  415.1 1.9 slice.193
  417.1 4.3 add_convert_fusion.1
  421.3 3.2 pad_maximum_fusion.1
  424.6 1.9 copy.120
  426.5 5.4 pad_maximum_fusion.2
  431.9 2.7 copy.121
  434.6 2.5 convert_bitcast_fusion
  437.1 1.6 copy.122
  438.7 18.4 %convert_reduce_fusion.1 = (f32[1024]{0:T(1024)S(1)}, bf16[2048,1024]{0,1:T(8,128)(2,1)}) fusion(f32[2048,1792]{0,1:T(8,128)} %convolution_add_fusion, bf16[2048,2048]{1,0:T(8,128)(2,1)} %all-gather.11.cloned.1.call-done, bf16[1024,2048]{1,0:T(8,128)(2,1)} %all-gather.9.cloned.1.call-done), kind=kOutput, calls=%fused_computation.19 | convolution fusion | flops 8633973760 | bytes 25169920 | tf_op jit(solution)/shard_map/td,fd->tf/dot_general | solution.py:721
  457.1 28.7 %convolution_convert_fusion = bf16[2048,1792]{1,0:T(8,128)(2,1)} fusion(bf16[2048,1024]{0,1:T(8,128)(2,1)} %get-tuple-element.73, bf16[2048,256]{0,1:T(8,128)(2,1)S(1)} %bitcast.120, bf16[2048,256]{0,1:T(8,128)(2,1)S(1)} %bitcast.117, bf16[2048,256]{0,1:T(8,128)(2,1)S(1)} %bitcast.114, bf16[2048,2048]{1,0:T(8,128)(2,1)} %shard_map.257, ...), kind=kOutput, calls=%fused_computation.21 | convolution fusion | flops 15090581504 | bytes 23101440 | tf_op jit(solution)/shard_map/td,tc->dc/dot_general | solution.py:749
  487.8 16.8 %fusion.31 = f32[2048,2048]{1,0:T(8,128)} fusion(bf16[1024,2048]{1,0:T(8,128)(2,1)} %all-gather.9.cloned.1.call-done, f32[2048,1792]{0,1:T(8,128)} %convolution_add_fusion), kind=kOutput, calls=%fused_computation.108 | convolution fusion | flops 8608808960 | bytes 29360128 | tf_op jit(solution)/shard_map/dot_general | solution.py:711
  504.6 21.4 %fusion.27.p_ref = f32[2048,2048]{1,0:T(8,128)} fusion(bf16[2048,1792]{1,0:T(8,128)(2,1)} %all-gather.5.cloned.1.call-done, bf16[2048,1024]{0,1:T(8,128)(2,1)S(1)} %copy-done.33, bf16[2048,256]{0,1:T(8,128)(2,1)S(1)} %bitcast.121, bf16[2048,256]{0,1:T(8,128)(2,1)S(1)} %bitcast.118, bf16[2048,256]{0,1:T(8,128)(2,1)S(1)} %bitcast.115), kind=kOutput, calls=%fused_computation.66 | convolution fusion | flops 15061745664 | bytes 31457280 | tf_op jit(solution)/shard_map/tc,dc->td/dot_general | solution.py:747
  526.0 5.5 collective-permute-start.1
  531.5 14.4 %convolution_add_fusion.1.p_ref = f32[2048,2048]{1,0:T(8,128)} fusion(f32[2048,2048]{1,0:T(8,128)} %fusion.31, bf16[2048,256]{0,1:T(8,128)(2,1)S(1)} %bitcast.108, bf16[256,2048]{1,0:T(8,128)(2,1)} %all-gather.7.cloned.1.call-done), kind=kOutput, calls=%fused_computation.11 | convolution fusion | flops 2151677952 | bytes 35651584 | tf_op jit(solution)/shard_map/dot_general | solution.py:710
  546.8 99.1 %shard_map.263 = f32[256,2048]{1,0:T(8,128)} custom-call(f32[2048,2048]{1,0:T(8,128)} %fusion.27.p_ref), custom_call_target="tpu_custom_call" | custom-call | tf_op jit(solution)/shard_map/pallas_call | solution.py:466
  646.0 88.9 %shard_map.261 = f32[256,2048]{1,0:T(8,128)} custom-call(f32[2048,2048]{1,0:T(8,128)} %convolution_add_fusion.1.p_ref), custom_call_target="tpu_custom_call" | custom-call | tf_op jit(solution)/shard_map/pallas_call | solution.py:466
  734.9 2.8 convert_element_type.223
  737.7 33.0 %shard_map.264 = bf16[8,64,1792]{2,1,0:T(8,128)(2,1)} custom-call(bf16[8,64,1792]{2,1,0:T(8,128)(2,1)} %bitcast.131), custom_call_target="tpu_custom_call" | custom-call | tf_op jit(solution)/shard_map/pallas_call | solution.py:531
  770.7 1.5 slice_convert_fusion.5
  772.2 2.4 slice_convert_fusion.6
  774.6 2.0 reshape.306
  776.6 2.8 copy.125
  779.4 2.5 copy.140
  781.9 2.6 reshape.305
  785.5 1.6 copy.139
  788.2 3.0 convert_reduce_fusion.4
  792.3 19.7 %shard_map.265 = f32[8,4,16,128]{3,2,1,0:T(8,128)} custom-call(f32[8,4,16,128]{3,2,1,0:T(8,128)} %copy_bitcast_fusion.3.x_ref), custom_call_target="tpu_custom_call" | custom-call | tf_op jit(solution)/shard_map/pallas_call | solution.py:531
  812.0 1.6 reduce_sum.158.x_ref
  813.6 9.2 %shard_map.266 = f32[4,16,128]{2,1,0:T(8,128)} custom-call(f32[4,16,128]{2,1,0:T(8,128)} %reduce_sum.158.x_ref), custom_call_target="tpu_custom_call" | custom-call | tf_op jit(solution)/shard_map/pallas_call | solution.py:531
  825.7 1.9 copy.157
  (169 shorter events, 25.7 us)
Async XLA Ops:
  7.2 188.6 %all-gather.5.cloned.1.call-start = ((), (), s32[]{:S(2)}) async-start(), calls=%async_computation.3 | async-start | bytes 9175040 | tf_op jit(solution)/shard_map/all_gather | solution.py:616
  13.4 40.1 %copy-start.20 = (f32[64,2048]{1,0:T(8,128)S(1)}, f32[64,2048]{1,0:T(8,128)}, u32[]{:S(2)}) copy-start(f32[64,2048]{1,0:T(8,128)} %param.21) | copy-start | bytes 1572868
  53.4 261.8 %all-gather.7.cloned.1.call-start = ((), (), s32[]{:S(2)}) async-start(), calls=%async_computation.4 | async-start | bytes 1310720 | tf_op jit(solution)/shard_map/all_gather | solution.py:554
  53.5 0.7 collective-permute-start
  54.2 0.7 copy-start.21
  54.9 108.8 %copy-start.19 = (f32[256,2048]{1,0:T(8,128)S(1)}, f32[256,2048]{1,0:T(8,128)}, u32[]{:S(2)}) copy-start(f32[256,2048]{1,0:T(8,128)} %param.25) | copy-start | bytes 6291460
  54.9 260.3 %all-gather.11.cloned.1.call-start = ((), (), s32[]{:S(2)}) async-start(), calls=%async_computation.6 | async-start | bytes 9437184 | tf_op jit(solution)/shard_map/all_gather | solution.py:685
  163.6 1.5 copy-start.26
  163.6 1.5 copy-start.28
  163.6 1.5 copy-start.29
  163.7 1.6 copy-start.30
  163.7 1.6 copy-start.31
  163.7 1.6 copy-start.27
  163.7 275.0 %all-gather.9.cloned.1.call-start = ((), (), s32[]{:S(2)}) async-start(), calls=%async_computation.5 | async-start | bytes 5242880 | tf_op jit(solution)/shard_map/all_gather | solution.py:617
  164.9 361.1 %reduce-scatter.6.cloned.1.call-start = ((), (), s32[]{:S(2)}) async-start(), calls=%async_computation.8 | async-start | bytes 2621440 | tf_op jit(solution)/shard_map/reduce_scatter | solution.py:560
  184.3 5.8 copy-start
  190.2 2.5 copy-start.32
  192.9 26.1 %copy-start.22 = (s32[2048]{0:T(1024)}, s32[2048]{0:T(1024)S(1)}, u32[]{:S(2)}) copy-start(s32[2048]{0:T(1024)S(1)} %convert_reduce_fusion.5) | copy-start | bytes 24580
  252.6 7.3 copy-start.8
  252.6 7.3 copy-start.9
  259.9 5.2 copy-start.5
  331.9 7.4 copy-start.10
  339.4 395.5 %reduce-scatter.8.cloned.1.call-start = ((), (), s32[]{:S(2)}) async-start(), calls=%async_computation.9 | async-start | bytes 5242880 | tf_op jit(solution)/shard_map/reduce_scatter | solution.py:757
  357.8 379.9 %reduce-scatter.4.cloned.1.call-start = ((), (), s32[]{:S(2)}) async-start(), calls=%async_computation.7 | async-start | bytes 9175040 | tf_op jit(solution)/shard_map/reduce_scatter | solution.py:752
  411.7 3.5 copy-start.2
  411.7 5.4 copy-start.1
  421.3 5.2 copy-start.7
  438.7 18.4 %copy-start.12 = (bf16[2048,4,64]{0,2,1:T(8,128)(2,1)S(1)}, bf16[2048,4,64]{0,2,1:T(8,128)(2,1)}, u32[]{:S(2)}) copy-start(bf16[2048,4,64]{0,2,1:T(8,128)(2,1)} %copy.121) | copy-start | bytes 3145732
  438.7 18.4 %copy-start.15 = (bf16[2048,4,64]{0,2,1:T(8,128)(2,1)S(1)}, bf16[2048,4,64]{0,2,1:T(8,128)(2,1)}, u32[]{:S(2)}) copy-start(bf16[2048,4,64]{0,2,1:T(8,128)(2,1)} %copy.122) | copy-start | bytes 3145732
  485.8 0.7 copy-start.24
  485.8 0.8 copy-start.23
  485.8 1.2 copy-start.3
  487.7 16.9 %copy-start.13 = (bf16[2048,4,64]{0,2,1:T(8,128)(2,1)S(1)}, bf16[2048,4,64]{0,2,1:T(8,128)(2,1)}, u32[]{:S(2)}) copy-start(bf16[2048,4,64]{0,2,1:T(8,128)(2,1)} %copy.121) | copy-start | bytes 3145732
  487.8 16.9 %copy-start.16 = (bf16[2048,4,64]{0,2,1:T(8,128)(2,1)S(1)}, bf16[2048,4,64]{0,2,1:T(8,128)(2,1)}, u32[]{:S(2)}) copy-start(bf16[2048,4,64]{0,2,1:T(8,128)(2,1)} %copy.122) | copy-start | bytes 3145732
  487.8 16.8 %copy-start.33 = (bf16[2048,1024]{0,1:T(8,128)(2,1)S(1)}, bf16[2048,1024]{0,1:T(8,128)(2,1)}, u32[]{:S(2)}) copy-start(bf16[2048,1024]{0,1:T(8,128)(2,1)} %get-tuple-element.73) | copy-start | bytes 12582916
  504.6 26.9 %copy-start.11 = (bf16[2048,4,64]{0,2,1:T(8,128)(2,1)S(1)}, bf16[2048,4,64]{0,2,1:T(8,128)(2,1)}, u32[]{:S(2)}) copy-start(bf16[2048,4,64]{0,2,1:T(8,128)(2,1)} %copy-done.10) | copy-start | bytes 3145732
  526.0 19.9 %copy-start.14 = (bf16[2048,4,64]{0,2,1:T(8,128)(2,1)S(1)}, bf16[2048,4,64]{0,2,1:T(8,128)(2,1)}, u32[]{:S(2)}) copy-start(bf16[2048,4,64]{0,2,1:T(8,128)(2,1)} %copy.121) | copy-start | bytes 3145732
  526.0 19.9 %copy-start.17 = (bf16[2048,4,64]{0,2,1:T(8,128)(2,1)S(1)}, bf16[2048,4,64]{0,2,1:T(8,128)(2,1)}, u32[]{:S(2)}) copy-start(bf16[2048,4,64]{0,2,1:T(8,128)(2,1)} %copy.122) | copy-start | bytes 3145732
  526.0 208.9 %collective-permute-start.1 = (f32[64,2048]{1,0:T(8,128)}, f32[64,2048]{1,0:T(8,128)}, u32[]{:S(2)}, u32[]{:S(2)}) collective-permute-start(f32[64,2048]{1,0:T(8,128)} %reduce-scatter.6.cloned.1.call-done), channel_id=1, source_target_pairs={{0,0},{8,1},{16,2},{24,3},{1,4},{9,5},{17,6},{25,7},{2,8},{10,9},{... | collective-permute-start | bytes 1572872 | tf_op jit(solution)/shard_map/ppermute | solution.py:562
  784.5 2.6 copy-start.4
  784.5 3.6 copy-start.6
  784.6 3.6 copy-start.18
  824.1 3.5 copy-start.25
Sparse Core Ops, SparseCore 0:
  53.5 63.1 all-gather.4
  118.3 16.7 all-gather.6
  163.8 126.5 all-gather.10
  292.4 32.6 all-gather.8
  339.5 33.8 reduce-scatter.5
  376.0 44.5 reduce-scatter.7
  486.0 75.2 reduce-scatter.3

commit v19 on v17

--- a/solution.py
+++ b/solution.py
@@ -218,9 +218,10 @@
         do = do_ref[0]
         s = lax.dot_general(q, k, TRANS_B, preferred_element_type=jnp.float32) * scale
         s = jnp.where(_allowed(segq_ref, segk_ref, i, j, tq, tk, causal), s, -jnp.inf)
-        p = jnp.exp(s - lse_ref[0])
+        spread = tk // lse_ref.shape[2]
+        p = jnp.exp(s - jnp.concatenate([lse_ref[0]] * spread, axis=1))
         dp = lax.dot_general(do, v_ref[0], TRANS_B, preferred_element_type=jnp.float32)
-        ds = (p * (dp - delta_ref[0])).astype(jnp.bfloat16)
+        ds = (p * (dp - jnp.concatenate([delta_ref[0]] * spread, axis=1))).astype(jnp.bfloat16)
         dv_sc[...] += jnp.dot(do.T, p.astype(jnp.bfloat16), preferred_element_type=jnp.float32)
         dk_sc[...] += jnp.dot(q.T, ds, preferred_element_type=jnp.float32)
         rows = pl.ds(pl.multiple_of(i * tq, tq), tq)
@@ -247,6 +248,8 @@
     segq = seg.reshape(total, 1)
     segk = seg.reshape(1, total)
     qi, kj = _schedule(count, False)
+    lse = jnp.broadcast_to(lse, (heads, total, 128))
+    delta = jnp.broadcast_to(delta, (heads, total, 128))
     steps = qi.shape[0]
 
     def q_map(h, t, qi, kj):
@@ -270,8 +273,8 @@
                 pl.BlockSpec((1, block, dim), k_map),
                 pl.BlockSpec((1, block, dim), k_map),
                 pl.BlockSpec((1, block, dim), q_map),
-                pl.BlockSpec((1, block, 1), q_map),
-                pl.BlockSpec((1, block, 1), q_map),
+                pl.BlockSpec((1, block, 128), q_map),
+                pl.BlockSpec((1, block, 128), q_map),
                 pl.BlockSpec((block, 1), lambda h, t, qi, kj: (qi[t], 0)),
                 pl.BlockSpec((1, block), lambda h, t, qi, kj: (0, kj[t])),
             ],

time: 839 us -> 845 us (level)
  transfers between devices with their start and end apart: 9 -> 9, of which waited for: 0 -> 0; matrix products, arithmetic and copies ran while one was open for 31% -> 32% of each run, Pallas kernels for 50% -> 49%
where the time goes in v19:
time: 845 us; the launch traced here: 839 us
  Pallas kernels  513 us (61%)
  matrix products  152 us (18%)
  local copies, waits for them, and re-layouts  83.8 us (10%)
  other arithmetic  68.9 us (8%)
  between operations  15.2 us (2%)
    pallas_call x2, Pallas kernels, ring_reduce_scatter(): pl.pallas_call(functools.partial(_scatter_kernel, ring=ring, rows=rows, p...  186 us
    pallas_call x6, Pallas kernels, exchange(): pl.pallas_call(functools.partial(_exchange_kernel, group=group), out_shap...  116 us
    pallas_call x1, Pallas kernels, ring_all_gather(): pl.pallas_call(functools.partial(_gather_kernel, ring=ring, rows=rows), o...  109 us
    pallas_call x1, Pallas kernels, attention_backward(): pl.pallas_call(functools.partial(_bwd_kernel, tq=block, tk=block, scale=s...  53.6 us
    pallas_call x1, Pallas kernels, attention_forward(): pl.pallas_call(functools.partial(_fwd_kernel, tq=block, tk=block, scale=s...  48.1 us
    unnamed x84, local copies, waits for them, and re-layouts  31.4 us
    dot_general x1, matrix products, head_plan(): jnp.einsum('td,tc->dc', hidden_group, d_both, preferred_element_type=jnp....  28.7 us
    dot_general x1, matrix products, head_plan(): jnp.dot(hidden_group, cols, preferred_element_type=jnp.float32)  23.3 us
  transfers between devices with their start and end apart: 9, of which 0 were waited for; matrix products, arithmetic and copies ran while one was open for 32% of the time, Pallas kernels for 49%

profile of v19, /device:TPU:0, one launch (start us, length us, event | category | flops | bytes accessed | tf_op | source)
XLA Modules:
  0.0 839.4 jit_solution(8546406333161346306)
XLA Ops:
  7.2 1.7 convert_element_type.177
  10.4 1.5 convert_element_type.176
  14.8 38.6 %shard_map.256 = bf16[8,64,1792]{2,1,0:T(8,128)(2,1)} custom-call(bf16[8,64,1792]{2,1,0:T(8,128)(2,1)} %pad_maximum_fusion.3.x_ref), custom_call_target="tpu_custom_call" | custom-call | tf_op jit(solution)/shard_map/pallas_call | solution.py:534
  55.0 108.6 %shard_map.257 = bf16[2048,2048]{1,0:T(8,128)(2,1)} custom-call(bf16[256,2048]{1,0:T(8,128)(2,1)} %x_ref), custom_call_target="tpu_custom_call" | custom-call | tf_op jit(solution)/shard_map/pallas_call | solution.py:398
  166.0 5.0 shard_map.258
  172.4 10.1 %shard_map.259 = bf16[8,4,16,128]{3,2,1,0:T(8,128)(2,1)} custom-call(bf16[8,4,16,128]{3,2,1,0:T(8,128)(2,1)} %broadcast_in_dim.38.x_ref), custom_call_target="tpu_custom_call" | custom-call | tf_op jit(solution)/shard_map/pallas_call | solution.py:534
  184.4 4.7 convert_reduce_fusion
  190.2 2.3 fusion.2
  195.8 23.3 %convolution_add_fusion = f32[2048,1792]{0,1:T(8,128)} fusion(bf16[2048,1792]{1,0:T(8,128)(2,1)} %all-gather.5.cloned.1.call-done, f32[1792]{0:T(1024)S(1)} %maximum_convert_fusion, bf16[2048,2048]{1,0:T(8,128)(2,1)} %shard_map.257, f32[2048]{0:T(1024)S(1)} %reshape.301, f32[2048]{0:T(1024)S(1)} %reshape.300, f32[2048]{0:T(1024)S(1)} %add_rsqrt_fusion, ...), kind=kOutput, calls=%fused_computation.10 | convolution fusion | flops 15061221376 | bytes 30448640 | tf_op jit(solution)/shard_map/dot_general | solution.py:695
  219.1 1.7 slice.195
  220.8 3.9 fusion.34
  226.6 3.5 copy.125
  230.2 3.5 copy.126
  233.7 2.1 slice.196
  235.8 2.3 fusion.35
  238.1 3.6 copy.128
  241.7 3.6 copy.129
  245.3 3.0 copy.127
  248.3 2.6 copy.130
  250.9 1.8 copy.111
  252.7 7.3 subtract_convert_fusion.2
  260.0 5.2 maximum_bitcast_fusion
  265.1 2.0 maximum_maximum_fusion.v_ref
  267.2 48.1 %shard_map.260 = (f32[4,2048,64]{2,1,0:T(8,128)}, f32[4,2048,1]{2,1,0:T(8,128)}) custom-call(s32[10]{0:T(128)} %constant.61.clone.qi_ref, s32[10]{0:T(128)} %constant.62.clone.kj_ref, bf16[4,2048,64]{2,1,0:T(8,128)(2,1)} %get-tuple-element.74.q_ref, bf16[4,2048,64]{2,1,0:T(8,128)(2,1)} %get-tuple-element.75.k_ref, ...), custom_call_target="tpu_custom_call" | custom-call | flops 2147483648 | bytes 5242880 | tf_op jit(solution)/shard_map/pallas_call | solution.py:168
  315.3 6.0 convolution_convert_fusion.2
  321.3 1.8 copy.114
  323.1 6.8 multiply_reduce_fusion
  329.9 1.9 copy.113
  331.8 7.4 fusion.38
  339.3 3.3 reduce
  342.6 15.7 %convolution_convert_fusion.1 = bf16[1024,2048]{1,0:T(8,128)(2,1)} fusion(bf16[2048,2048]{1,0:T(8,128)(2,1)} %all-gather.11.cloned.1.call-done, f32[2048,1792]{0,1:T(8,128)} %convolution_add_fusion), kind=kOutput, calls=%fused_computation.35 | convolution fusion | flops 8610906112 | bytes 20971520 | tf_op jit(solution)/shard_map/tf,td->fd/dot_general | solution.py:723
  358.4 2.9 broadcast_in_dim.86.delta_ref
  361.3 2.6 broadcast_in_dim.46.lse_ref
  363.9 53.6 %shard_map.262 = (f32[4,2048,64]{2,1,0:T(8,128)}, f32[4,2048,64]{2,1,0:T(8,128)}, f32[4,2048,64]{2,1,0:T(8,128)}) custom-call(s32[10]{0:T(128)} %constant.63.clone.qi_ref, s32[10]{0:T(128)} %constant.64.clone.kj_ref, bf16[4,2048,64]{2,1,0:T(8,128)(2,1)} %get-tuple-element.74.q_ref, bf16[4,2048,64]{2,1,0:T(8,128)(2,1)} %get-tuple-element.75.k_ref, ...), custom_call_target="tpu_custom_call" | custom-call | flops 5368709120 | bytes 12582912 | tf_op jit(solution)/shard_map/pallas_call | solution.py:261
  417.5 2.9 slice.194
  421.0 1.9 slice.193
  422.9 4.3 add_convert_fusion.1
  427.3 3.2 pad_maximum_fusion.1
  430.5 1.9 copy.116
  432.4 5.4 pad_maximum_fusion.2
  437.9 2.7 copy.117
  440.5 2.5 convert_bitcast_fusion
  443.0 1.6 copy.118
  444.6 18.4 %convert_reduce_fusion.1 = (f32[1024]{0:T(1024)S(1)}, bf16[2048,1024]{0,1:T(8,128)(2,1)}) fusion(f32[2048,1792]{0,1:T(8,128)} %convolution_add_fusion, bf16[2048,2048]{1,0:T(8,128)(2,1)} %all-gather.11.cloned.1.call-done, bf16[1024,2048]{1,0:T(8,128)(2,1)} %all-gather.9.cloned.1.call-done), kind=kOutput, calls=%fused_computation.19 | convolution fusion | flops 8633973760 | bytes 25169920 | tf_op jit(solution)/shard_map/td,fd->tf/dot_general | solution.py:724
  463.0 28.7 %convolution_convert_fusion = bf16[2048,1792]{1,0:T(8,128)(2,1)} fusion(bf16[2048,1024]{0,1:T(8,128)(2,1)} %get-tuple-element.73, bf16[2048,256]{0,1:T(8,128)(2,1)S(1)} %bitcast.119, bf16[2048,256]{0,1:T(8,128)(2,1)S(1)} %bitcast.116, bf16[2048,256]{0,1:T(8,128)(2,1)S(1)} %bitcast.113, bf16[2048,2048]{1,0:T(8,128)(2,1)} %shard_map.257, ...), kind=kOutput, calls=%fused_computation.21 | convolution fusion | flops 15090581504 | bytes 23101440 | tf_op jit(solution)/shard_map/td,tc->dc/dot_general | solution.py:752
  493.6 16.8 %fusion.31 = f32[2048,2048]{1,0:T(8,128)} fusion(bf16[1024,2048]{1,0:T(8,128)(2,1)} %all-gather.9.cloned.1.call-done, f32[2048,1792]{0,1:T(8,128)} %convolution_add_fusion), kind=kOutput, calls=%fused_computation.108 | convolution fusion | flops 8608808960 | bytes 29360128 | tf_op jit(solution)/shard_map/dot_general | solution.py:714
  510.5 21.5 %fusion.27.p_ref = f32[2048,2048]{1,0:T(8,128)} fusion(bf16[2048,1792]{1,0:T(8,128)(2,1)} %all-gather.5.cloned.1.call-done, bf16[2048,1024]{0,1:T(8,128)(2,1)S(1)} %copy-done.33, bf16[2048,256]{0,1:T(8,128)(2,1)S(1)} %bitcast.120, bf16[2048,256]{0,1:T(8,128)(2,1)S(1)} %bitcast.117, bf16[2048,256]{0,1:T(8,128)(2,1)S(1)} %bitcast.114), kind=kOutput, calls=%fused_computation.66 | convolution fusion | flops 15061745664 | bytes 31457280 | tf_op jit(solution)/shard_map/tc,dc->td/dot_general | solution.py:750
  532.0 5.5 collective-permute-start.1
  537.5 14.4 %convolution_add_fusion.1.p_ref = f32[2048,2048]{1,0:T(8,128)} fusion(f32[2048,2048]{1,0:T(8,128)} %fusion.31, bf16[2048,256]{0,1:T(8,128)(2,1)S(1)} %bitcast.107, bf16[256,2048]{1,0:T(8,128)(2,1)} %all-gather.7.cloned.1.call-done), kind=kOutput, calls=%fused_computation.11 | convolution fusion | flops 2151677952 | bytes 35651584 | tf_op jit(solution)/shard_map/dot_general | solution.py:713
  552.8 98.5 %shard_map.263 = f32[256,2048]{1,0:T(8,128)} custom-call(f32[2048,2048]{1,0:T(8,128)} %fusion.27.p_ref), custom_call_target="tpu_custom_call" | custom-call | tf_op jit(solution)/shard_map/pallas_call | solution.py:469
  651.2 88.0 %shard_map.261 = f32[256,2048]{1,0:T(8,128)} custom-call(f32[2048,2048]{1,0:T(8,128)} %convolution_add_fusion.1.p_ref), custom_call_target="tpu_custom_call" | custom-call | tf_op jit(solution)/shard_map/pallas_call | solution.py:469
  739.4 2.8 convert_element_type.223
  742.2 32.4 %shard_map.264 = bf16[8,64,1792]{2,1,0:T(8,128)(2,1)} custom-call(bf16[8,64,1792]{2,1,0:T(8,128)(2,1)} %bitcast.130), custom_call_target="tpu_custom_call" | custom-call | tf_op jit(solution)/shard_map/pallas_call | solution.py:534
  776.1 2.4 slice_convert_fusion.6
  778.5 2.0 reshape.307
  780.5 2.8 copy.121
  783.3 2.5 copy.136
  785.8 2.6 reshape.306
  789.4 1.6 copy.135
  792.1 3.0 convert_reduce_fusion.4
  796.2 19.7 %shard_map.265 = f32[8,4,16,128]{3,2,1,0:T(8,128)} custom-call(f32[8,4,16,128]{3,2,1,0:T(8,128)} %copy_bitcast_fusion.3.x_ref), custom_call_target="tpu_custom_call" | custom-call | tf_op jit(solution)/shard_map/pallas_call | solution.py:534
  815.9 1.6 reduce_sum.158.x_ref
  817.4 10.0 %shard_map.266 = f32[4,16,128]{2,1,0:T(8,128)} custom-call(f32[4,16,128]{2,1,0:T(8,128)} %reduce_sum.158.x_ref), custom_call_target="tpu_custom_call" | custom-call | tf_op jit(solution)/shard_map/pallas_call | solution.py:534
  830.4 1.9 copy.153
  (171 shorter events, 28.6 us)
Async XLA Ops:
  7.2 188.6 %all-gather.5.cloned.1.call-start = ((), (), s32[]{:S(2)}) async-start(), calls=%async_computation.3 | async-start | bytes 9175040 | tf_op jit(solution)/shard_map/all_gather | solution.py:619
  13.4 40.0 %copy-start.20 = (f32[64,2048]{1,0:T(8,128)S(1)}, f32[64,2048]{1,0:T(8,128)}, u32[]{:S(2)}) copy-start(f32[64,2048]{1,0:T(8,128)} %param.21) | copy-start | bytes 1572868
  53.4 261.9 %all-gather.7.cloned.1.call-start = ((), (), s32[]{:S(2)}) async-start(), calls=%async_computation.4 | async-start | bytes 1310720 | tf_op jit(solution)/shard_map/all_gather | solution.py:557
  53.5 0.7 collective-permute-start
  54.2 0.7 copy-start.21
  54.9 108.8 %copy-start.19 = (f32[256,2048]{1,0:T(8,128)S(1)}, f32[256,2048]{1,0:T(8,128)}, u32[]{:S(2)}) copy-start(f32[256,2048]{1,0:T(8,128)} %param.25) | copy-start | bytes 6291460
  54.9 260.4 %all-gather.11.cloned.1.call-start = ((), (), s32[]{:S(2)}) async-start(), calls=%async_computation.6 | async-start | bytes 9437184 | tf_op jit(solution)/shard_map/all_gather | solution.py:688
  163.6 1.5 copy-start.26
  163.6 1.5 copy-start.28
  163.6 1.5 copy-start.29
  163.6 1.6 copy-start.30
  163.6 1.6 copy-start.31
  163.7 1.6 copy-start.27
  163.7 280.9 %all-gather.9.cloned.1.call-start = ((), (), s32[]{:S(2)}) async-start(), calls=%async_computation.5 | async-start | bytes 5242880 | tf_op jit(solution)/shard_map/all_gather | solution.py:620
  164.9 367.1 %reduce-scatter.6.cloned.1.call-start = ((), (), s32[]{:S(2)}) async-start(), calls=%async_computation.8 | async-start | bytes 2621440 | tf_op jit(solution)/shard_map/reduce_scatter | solution.py:563
  184.4 5.8 copy-start
  190.2 2.5 copy-start.32
  193.0 26.1 %copy-start.22 = (s32[2048]{0:T(1024)}, s32[2048]{0:T(1024)S(1)}, u32[]{:S(2)}) copy-start(s32[2048]{0:T(1024)S(1)} %convert_reduce_fusion.5) | copy-start | bytes 24580
  252.7 7.3 copy-start.8
  252.7 7.3 copy-start.9
  260.0 5.2 copy-start.5
  331.8 7.4 copy-start.10
  339.2 400.1 %reduce-scatter.8.cloned.1.call-start = ((), (), s32[]{:S(2)}) async-start(), calls=%async_computation.9 | async-start | bytes 5242880 | tf_op jit(solution)/shard_map/reduce_scatter | solution.py:760
  358.4 383.8 %reduce-scatter.4.cloned.1.call-start = ((), (), s32[]{:S(2)}) async-start(), calls=%async_computation.7 | async-start | bytes 9175040 | tf_op jit(solution)/shard_map/reduce_scatter | solution.py:755
  417.5 3.5 copy-start.2
  417.5 5.5 copy-start.1
  427.3 5.1 copy-start.7
  444.6 18.4 %copy-start.12 = (bf16[2048,4,64]{0,2,1:T(8,128)(2,1)S(1)}, bf16[2048,4,64]{0,2,1:T(8,128)(2,1)}, u32[]{:S(2)}) copy-start(bf16[2048,4,64]{0,2,1:T(8,128)(2,1)} %copy.117) | copy-start | bytes 3145732
  444.6 18.4 %copy-start.15 = (bf16[2048,4,64]{0,2,1:T(8,128)(2,1)S(1)}, bf16[2048,4,64]{0,2,1:T(8,128)(2,1)}, u32[]{:S(2)}) copy-start(bf16[2048,4,64]{0,2,1:T(8,128)(2,1)} %copy.118) | copy-start | bytes 3145732
  491.7 0.7 copy-start.24
  491.7 0.8 copy-start.23
  491.7 1.2 copy-start.3
  493.6 16.9 %copy-start.13 = (bf16[2048,4,64]{0,2,1:T(8,128)(2,1)S(1)}, bf16[2048,4,64]{0,2,1:T(8,128)(2,1)}, u32[]{:S(2)}) copy-start(bf16[2048,4,64]{0,2,1:T(8,128)(2,1)} %copy.117) | copy-start | bytes 3145732
  493.6 16.9 %copy-start.16 = (bf16[2048,4,64]{0,2,1:T(8,128)(2,1)S(1)}, bf16[2048,4,64]{0,2,1:T(8,128)(2,1)}, u32[]{:S(2)}) copy-start(bf16[2048,4,64]{0,2,1:T(8,128)(2,1)} %copy.118) | copy-start | bytes 3145732
  493.6 16.8 %copy-start.33 = (bf16[2048,1024]{0,1:T(8,128)(2,1)S(1)}, bf16[2048,1024]{0,1:T(8,128)(2,1)}, u32[]{:S(2)}) copy-start(bf16[2048,1024]{0,1:T(8,128)(2,1)} %get-tuple-element.73) | copy-start | bytes 12582916
  510.5 27.0 %copy-start.11 = (bf16[2048,4,64]{0,2,1:T(8,128)(2,1)S(1)}, bf16[2048,4,64]{0,2,1:T(8,128)(2,1)}, u32[]{:S(2)}) copy-start(bf16[2048,4,64]{0,2,1:T(8,128)(2,1)} %copy-done.10) | copy-start | bytes 3145732
  532.0 19.9 %copy-start.14 = (bf16[2048,4,64]{0,2,1:T(8,128)(2,1)S(1)}, bf16[2048,4,64]{0,2,1:T(8,128)(2,1)}, u32[]{:S(2)}) copy-start(bf16[2048,4,64]{0,2,1:T(8,128)(2,1)} %copy.117) | copy-start | bytes 3145732
  532.0 19.9 %copy-start.17 = (bf16[2048,4,64]{0,2,1:T(8,128)(2,1)S(1)}, bf16[2048,4,64]{0,2,1:T(8,128)(2,1)}, u32[]{:S(2)}) copy-start(bf16[2048,4,64]{0,2,1:T(8,128)(2,1)} %copy.118) | copy-start | bytes 3145732
  532.0 207.4 %collective-permute-start.1 = (f32[64,2048]{1,0:T(8,128)}, f32[64,2048]{1,0:T(8,128)}, u32[]{:S(2)}, u32[]{:S(2)}) collective-permute-start(f32[64,2048]{1,0:T(8,128)} %reduce-scatter.6.cloned.1.call-done), channel_id=1, source_target_pairs={{0,0},{8,1},{16,2},{24,3},{1,4},{9,5},{17,6},{25,7},{2,8},{10,9},{... | collective-permute-start | bytes 1572872 | tf_op jit(solution)/shard_map/ppermute | solution.py:565
  788.4 2.6 copy-start.4
  788.4 3.6 copy-start.6
  788.4 3.6 copy-start.18
  828.8 3.5 copy-start.25
Sparse Core Ops, SparseCore 0:
  53.5 63.1 all-gather.4
  118.3 16.7 all-gather.6
  163.8 126.5 all-gather.10
  292.4 32.6 all-gather.8
  339.4 33.7 reduce-scatter.5
  375.7 44.4 reduce-scatter.7
  491.9 74.9 reduce-scatter.3

commit v20 on v17

--- a/solution.py
+++ b/solution.py
@@ -568,19 +568,21 @@
     return jnp.pad(vector, (0, total - size)).reshape(-1, lanes)
 
 
-def fetch_small(b_qkv, b_out, b_fc2, ln_gain, ln_shift, b_fc1):
+def pack_small(b_qkv, b_out, b_fc2, ln_gain, ln_shift, b_fc1):
     pieces = (b_qkv, b_out, b_fc2, ln_gain, ln_shift, b_fc1)
+    return pack_rows(jnp.concatenate([p.astype(jnp.bfloat16) for p in pieces]), 128)
+
+
+def fetch_small(over_ctx, sizes):
     n_dp = lax.axis_size("dp")
     n_ctx = lax.axis_size("ctx")
-    packed = pack_rows(jnp.concatenate([p.astype(jnp.bfloat16) for p in pieces]), 128)
-    over_dp = exchange(jnp.broadcast_to(packed[None], (n_dp,) + packed.shape), "dp", 4)
-    over_all = exchange(jnp.broadcast_to(over_dp[None], (n_ctx,) + over_dp.shape), "ctx", 8)
-    table = over_all.transpose(1, 0, 2, 3).reshape(n_dp * n_ctx, -1)
+    over_all = exchange(jnp.broadcast_to(over_ctx[None], (n_dp,) + over_ctx.shape), "dp", 4)
+    table = over_all.reshape(n_dp * n_ctx, -1)
     result = []
     offset = 0
-    for p in pieces:
-        result.append(table[:, offset : offset + p.shape[0]])
-        offset += p.shape[0]
+    for size in sizes:
+        result.append(table[:, offset : offset + size])
+        offset += size
     return result
 
 
@@ -595,7 +597,7 @@
     return over_dp.reshape(-1)[:width]
 
 
-def fetch_heads(w_qkv, w_fc1, w_fc2, tokens):
+def fetch_heads(w_qkv, w_fc1, w_fc2, tokens, packed):
     dp_count = lax.axis_size("dp")
     ctx_count = lax.axis_size("ctx")
     rows_piece = w_qkv.shape[0]
@@ -610,13 +612,23 @@
         ],
         axis=2,
     )
-    sent = exchange(pieces, "ctx", 5).reshape(ctx_count * rows_piece, -1)
+    width = pieces.shape[2]
+    flat = packed.reshape(-1)
+    extra = -(-flat.shape[0] // (8 * width)) * 8
+    flat = jnp.pad(flat, (0, extra * width - flat.shape[0])).reshape(extra, width)
+    payload = jnp.concatenate(
+        [pieces, jnp.broadcast_to(flat[None], (ctx_count, extra, width))], axis=1
+    )
+    got = exchange(payload, "ctx", 5)
+    small = got[:, rows_piece:, :].reshape(ctx_count, -1)[:, : packed.size]
+    small = small.reshape((ctx_count,) + packed.shape)
+    sent = got[:, :rows_piece, :].reshape(ctx_count * rows_piece, -1)
     sent, tokens = lax.optimization_barrier((sent, tokens))
     cols, fc2_rows = (
         lax.all_gather(sent, "dp", axis=0, tiled=True),
         lax.all_gather(w_fc2.astype(jnp.bfloat16), "dp", axis=0, tiled=True),
     )
-    return (cols, fc2_rows, tokens)
+    return (cols, fc2_rows, tokens, small)
 
 
 def return_heads(owned_parts):
@@ -663,8 +675,10 @@
     group_rows = jnp.arange(group, dtype=jnp.int32)
     seg, positions = segment_info(lengths[0], group_rows)
     cosine, sine = rotary_tables(positions)
+    packed = pack_small(b_qkv, b_out, b_fc2, ln_gain, ln_shift, b_fc1)
+    cols, fc2_rows, tokens, small_ctx = fetch_heads(w_qkv, w_fc1, w_fc2, tokens, packed)
     qkv_bias, out_bias, fc2_bias, gain_low, shift_low, fc1_table = fetch_small(
-        b_qkv, b_out, b_fc2, ln_gain, ln_shift, b_fc1
+        small_ctx, [p.shape[0] for p in (b_qkv, b_out, b_fc2, ln_gain, ln_shift, b_fc1)]
     )
     qkv_bias = qkv_bias.reshape(3 * D)
     out_bias = out_bias.reshape(D)
@@ -675,7 +689,6 @@
         fc1_table.reshape(dp_count, ctx_count, unit), here, 1, keepdims=False
     ).reshape(dp_count * unit)
     out_rows = fetch_out_rows(w_out)
-    cols, fc2_rows, tokens = fetch_heads(w_qkv, w_fc1, w_fc2, tokens)
     gain32 = gain_low.astype(jnp.float32)
     shift32 = shift_low.astype(jnp.float32)
     inputs = tokens.astype(jnp.float32)

time: 839 us -> 839 us (level)
    pallas_call x6 -> x5, Pallas kernels: 115 us -> 107 us  [exchange(): pl.pallas_call(functools.partial(_exchange_kernel, group=group), out_shap...]
    unnamed x84 -> x87, local copies, waits for them, and re-layouts: 31.3 us -> 32.2 us
  transfers between devices with their start and end apart: 9 -> 9, of which waited for: 0 -> 0; matrix products, arithmetic and copies ran while one was open for 31% -> 31% of each run, Pallas kernels for 50% -> 49%
where the time goes in v20:
time: 839 us; the launch traced here: 833 us
  Pallas kernels  507 us (60%)
  matrix products  155 us (18%)
  local copies, waits for them, and re-layouts  83.7 us (10%)
  other arithmetic  65.6 us (8%)
  between operations  15.2 us (2%)
    pallas_call x2, Pallas kernels, ring_reduce_scatter(): pl.pallas_call(functools.partial(_scatter_kernel, ring=ring, rows=rows, p...  188 us
    pallas_call x1, Pallas kernels, ring_all_gather(): pl.pallas_call(functools.partial(_gather_kernel, ring=ring, rows=rows), o...  111 us
    pallas_call x5, Pallas kernels, exchange(): pl.pallas_call(functools.partial(_exchange_kernel, group=group), out_shap...  107 us
    pallas_call x1, Pallas kernels, attention_backward(): pl.pallas_call(functools.partial(_bwd_kernel, tq=block, tk=block, scale=s...  53.5 us
    pallas_call x1, Pallas kernels, attention_forward(): pl.pallas_call(functools.partial(_fwd_kernel, tq=block, tk=block, scale=s...  48.1 us
    unnamed x87, local copies, waits for them, and re-layouts  32.2 us
    dot_general x1, matrix products, head_plan(): jnp.einsum('td,tc->dc', hidden_group, d_both, preferred_element_type=jnp....  28.6 us
    dot_general x1, matrix products, head_plan(): jnp.dot(hidden_group, cols, preferred_element_type=jnp.float32)  23.3 us
  transfers between devices with their start and end apart: 9, of which 0 were waited for; matrix products, arithmetic and copies ran while one was open for 31% of the time, Pallas kernels for 49%

profile of v20, /device:TPU:0, one launch (start us, length us, event | category | flops | bytes accessed | tf_op | source)
XLA Modules:
  0.0 833.2 jit_solution(16426461595642773630)
XLA Ops:
  7.2 1.7 convert_element_type.179
  10.4 1.5 convert_element_type.178
  13.8 1.5 pad_maximum_fusion.3.x_ref
  15.3 42.6 %shard_map.256 = bf16[8,72,1792]{2,1,0:T(8,128)(2,1)} custom-call(bf16[8,72,1792]{2,1,0:T(8,128)(2,1)} %pad_maximum_fusion.3.x_ref), custom_call_target="tpu_custom_call" | custom-call | tf_op jit(solution)/shard_map/pallas_call | solution.py:531
  57.8 2.9 slice.115
  62.3 110.7 %shard_map.257 = bf16[2048,2048]{1,0:T(8,128)(2,1)} custom-call(bf16[256,2048]{1,0:T(8,128)(2,1)} %x_ref), custom_call_target="tpu_custom_call" | custom-call | tf_op jit(solution)/shard_map/pallas_call | solution.py:395
  176.2 5.7 shard_map.258
  183.8 4.7 convert_reduce_fusion
  189.6 2.3 fusion.2
  195.2 23.3 %convolution_add_fusion = f32[2048,1792]{0,1:T(8,128)} fusion(bf16[2048,1792]{1,0:T(8,128)(2,1)} %all-gather.5.cloned.1.call-done, f32[1792]{0:T(1024)S(1)} %maximum_convert_fusion, bf16[2048,2048]{1,0:T(8,128)(2,1)} %shard_map.257, f32[2048]{0:T(1024)S(1)} %reshape.304, f32[2048]{0:T(1024)S(1)} %reshape.303, f32[2048]{0:T(1024)S(1)} %add_rsqrt_fusion, ...), kind=kOutput, calls=%fused_computation.10 | convolution fusion | flops 15061221376 | bytes 30448640 | tf_op jit(solution)/shard_map/dot_general | solution.py:705
  218.5 1.7 slice.210
  220.3 3.9 fusion.34
  226.1 3.6 copy.120
  229.7 3.5 copy.121
  233.2 2.1 slice.211
  235.3 2.3 fusion.35
  237.6 3.5 copy.123
  241.1 3.6 copy.124
  244.7 2.6 copy.122
  247.3 3.0 copy.125
  250.3 1.8 copy.106
  252.1 7.2 subtract_convert_fusion.2
  259.3 5.2 maximum_bitcast_fusion
  264.4 2.0 maximum_maximum_fusion.v_ref
  266.5 48.1 %shard_map.259 = (f32[4,2048,64]{2,1,0:T(8,128)}, f32[4,2048,1]{2,1,0:T(8,128)}) custom-call(s32[10]{0:T(128)} %constant.61.clone.qi_ref, s32[10]{0:T(128)} %constant.62.clone.kj_ref, bf16[4,2048,64]{2,1,0:T(8,128)(2,1)} %get-tuple-element.74.q_ref, bf16[4,2048,64]{2,1,0:T(8,128)(2,1)} %get-tuple-element.75.k_ref, ...), custom_call_target="tpu_custom_call" | custom-call | flops 2147483648 | bytes 5242880 | tf_op jit(solution)/shard_map/pallas_call | solution.py:168
  314.6 6.0 convolution_convert_fusion.2
  320.6 1.8 copy.109
  322.4 6.9 multiply_reduce_fusion
  329.3 2.1 copy.108
  331.4 7.4 fusion.38
  338.9 2.7 copy.110.delta_ref
  341.6 16.5 %convolution_convert_fusion.1 = bf16[1024,2048]{1,0:T(8,128)(2,1)} fusion(bf16[2048,2048]{1,0:T(8,128)(2,1)} %all-gather.11.cloned.1.call-done, f32[2048,1792]{0,1:T(8,128)} %convolution_add_fusion), kind=kOutput, calls=%fused_computation.35 | convolution fusion | flops 8610906112 | bytes 20971520 | tf_op jit(solution)/shard_map/tf,td->fd/dot_general | solution.py:733
  358.2 53.5 %shard_map.261 = (f32[4,2048,64]{2,1,0:T(8,128)}, f32[4,2048,64]{2,1,0:T(8,128)}, f32[4,2048,64]{2,1,0:T(8,128)}) custom-call(s32[10]{0:T(128)} %constant.63.clone.qi_ref, s32[10]{0:T(128)} %constant.64.clone.kj_ref, bf16[4,2048,64]{2,1,0:T(8,128)(2,1)} %get-tuple-element.74.q_ref, bf16[4,2048,64]{2,1,0:T(8,128)(2,1)} %get-tuple-element.75.k_ref, ...), custom_call_target="tpu_custom_call" | custom-call | flops 5368709120 | bytes 12582912 | tf_op jit(solution)/shard_map/pallas_call | solution.py:258
  411.7 2.9 slice.209
  415.1 1.9 slice.208
  417.1 4.3 add_convert_fusion.1
  421.4 3.2 pad_maximum_fusion.1
  424.6 1.9 copy.112
  426.5 5.4 pad_maximum_fusion.2
  431.9 2.7 copy.113
  434.6 2.5 convert_bitcast_fusion
  437.1 1.6 copy.114
  438.7 18.4 %convert_reduce_fusion.1 = (f32[1024]{0:T(1024)S(1)}, bf16[2048,1024]{0,1:T(8,128)(2,1)}) fusion(f32[2048,1792]{0,1:T(8,128)} %convolution_add_fusion, bf16[2048,2048]{1,0:T(8,128)(2,1)} %all-gather.11.cloned.1.call-done, bf16[1024,2048]{1,0:T(8,128)(2,1)} %all-gather.9.cloned.1.call-done), kind=kOutput, calls=%fused_computation.19 | convolution fusion | flops 8633973760 | bytes 25169920 | tf_op jit(solution)/shard_map/td,fd->tf/dot_general | solution.py:734
  457.1 28.6 %convolution_convert_fusion = bf16[2048,1792]{1,0:T(8,128)(2,1)} fusion(bf16[2048,1024]{0,1:T(8,128)(2,1)} %get-tuple-element.73, bf16[2048,256]{0,1:T(8,128)(2,1)S(1)} %bitcast.122, bf16[2048,256]{0,1:T(8,128)(2,1)S(1)} %bitcast.119, bf16[2048,256]{0,1:T(8,128)(2,1)S(1)} %bitcast.116, bf16[2048,2048]{1,0:T(8,128)(2,1)} %shard_map.257, ...), kind=kOutput, calls=%fused_computation.21 | convolution fusion | flops 15090581504 | bytes 23101440 | tf_op jit(solution)/shard_map/td,tc->dc/dot_general | solution.py:762
  487.7 18.1 %fusion.31 = f32[2048,2048]{1,0:T(8,128)} fusion(bf16[1024,2048]{1,0:T(8,128)(2,1)} %all-gather.9.cloned.1.call-done, f32[2048,1792]{0,1:T(8,128)} %convolution_add_fusion), kind=kOutput, calls=%fused_computation.109 | convolution fusion | flops 8608808960 | bytes 29360128 | tf_op jit(solution)/shard_map/dot_general | solution.py:724
  505.8 22.4 %fusion.27.p_ref = f32[2048,2048]{1,0:T(8,128)} fusion(bf16[2048,1792]{1,0:T(8,128)(2,1)} %all-gather.5.cloned.1.call-done, bf16[2048,1024]{0,1:T(8,128)(2,1)S(1)} %copy-done.33, bf16[2048,256]{0,1:T(8,128)(2,1)S(1)} %bitcast.123, bf16[2048,256]{0,1:T(8,128)(2,1)S(1)} %bitcast.120, bf16[2048,256]{0,1:T(8,128)(2,1)S(1)} %bitcast.117), kind=kOutput, calls=%fused_computation.66 | convolution fusion | flops 15061745664 | bytes 31457280 | tf_op jit(solution)/shard_map/tc,dc->td/dot_general | solution.py:760
  528.2 5.5 collective-permute-start.1
  533.7 14.3 %convolution_add_fusion.1.p_ref = f32[2048,2048]{1,0:T(8,128)} fusion(f32[2048,2048]{1,0:T(8,128)} %fusion.31, bf16[2048,256]{0,1:T(8,128)(2,1)S(1)} %bitcast.110, bf16[256,2048]{1,0:T(8,128)(2,1)} %all-gather.7.cloned.1.call-done), kind=kOutput, calls=%fused_computation.11 | convolution fusion | flops 2151677952 | bytes 35651584 | tf_op jit(solution)/shard_map/dot_general | solution.py:723
  548.9 98.8 %shard_map.262 = f32[256,2048]{1,0:T(8,128)} custom-call(f32[2048,2048]{1,0:T(8,128)} %fusion.27.p_ref), custom_call_target="tpu_custom_call" | custom-call | tf_op jit(solution)/shard_map/pallas_call | solution.py:466
  647.7 89.1 %shard_map.260 = f32[256,2048]{1,0:T(8,128)} custom-call(f32[2048,2048]{1,0:T(8,128)} %convolution_add_fusion.1.p_ref), custom_call_target="tpu_custom_call" | custom-call | tf_op jit(solution)/shard_map/pallas_call | solution.py:466
  737.0 2.8 convert_element_type.225
  739.8 33.6 %shard_map.263 = bf16[8,64,1792]{2,1,0:T(8,128)(2,1)} custom-call(bf16[8,64,1792]{2,1,0:T(8,128)(2,1)} %bitcast.133), custom_call_target="tpu_custom_call" | custom-call | tf_op jit(solution)/shard_map/pallas_call | solution.py:531
  773.3 1.5 slice_convert_fusion.5
  774.8 2.4 slice_convert_fusion.6
  777.2 2.0 reshape.310
  779.2 2.8 copy.117
  782.0 2.5 copy.133
  784.5 2.6 reshape.309
  788.1 1.6 copy.132
  790.8 3.0 convert_reduce_fusion.4
  794.9 19.7 %shard_map.264 = f32[8,4,16,128]{3,2,1,0:T(8,128)} custom-call(f32[8,4,16,128]{3,2,1,0:T(8,128)} %copy_bitcast_fusion.3.x_ref), custom_call_target="tpu_custom_call" | custom-call | tf_op jit(solution)/shard_map/pallas_call | solution.py:531
  814.6 1.6 reduce_sum.158.x_ref
  816.2 5.1 shard_map.265
  824.3 1.9 copy.151
  (173 shorter events, 25.5 us)
Async XLA Ops:
  7.2 188.1 %all-gather.5.cloned.1.call-start = ((), (), s32[]{:S(2)}) async-start(), calls=%async_computation.3 | async-start | bytes 9175040 | tf_op jit(solution)/shard_map/all_gather | solution.py:628
  10.4 3.1 copy-start.26
  10.4 3.1 copy-start.28
  10.4 3.1 copy-start.29
  10.4 3.1 copy-start.30
  10.4 3.2 copy-start.31
  10.4 3.2 copy-start.27
  15.3 45.5 %copy-start.20 = (f32[64,2048]{1,0:T(8,128)S(1)}, f32[64,2048]{1,0:T(8,128)}, u32[]{:S(2)}) copy-start(f32[64,2048]{1,0:T(8,128)} %param.21) | copy-start | bytes 1572868
  60.7 253.9 %all-gather.7.cloned.1.call-start = ((), (), s32[]{:S(2)}) async-start(), calls=%async_computation.4 | async-start | bytes 1310720 | tf_op jit(solution)/shard_map/all_gather | solution.py:554
  60.8 0.7 collective-permute-start
  61.5 0.7 copy-start.21
  62.3 110.8 %copy-start.19 = (f32[256,2048]{1,0:T(8,128)S(1)}, f32[256,2048]{1,0:T(8,128)}, u32[]{:S(2)}) copy-start(f32[256,2048]{1,0:T(8,128)} %param.25) | copy-start | bytes 6291460
  62.3 252.3 %all-gather.11.cloned.1.call-start = ((), (), s32[]{:S(2)}) async-start(), calls=%async_computation.6 | async-start | bytes 9437184 | tf_op jit(solution)/shard_map/all_gather | solution.py:698
  173.0 265.6 %all-gather.9.cloned.1.call-start = ((), (), s32[]{:S(2)}) async-start(), calls=%async_computation.5 | async-start | bytes 5242880 | tf_op jit(solution)/shard_map/all_gather | solution.py:629
  174.2 354.0 %reduce-scatter.6.cloned.1.call-start = ((), (), s32[]{:S(2)}) async-start(), calls=%async_computation.8 | async-start | bytes 2621440 | tf_op jit(solution)/shard_map/reduce_scatter | solution.py:560
  183.8 5.8 copy-start
  189.6 2.5 copy-start.32
  192.4 26.1 %copy-start.22 = (s32[2048]{0:T(1024)}, s32[2048]{0:T(1024)S(1)}, u32[]{:S(2)}) copy-start(s32[2048]{0:T(1024)S(1)} %convert_reduce_fusion.5) | copy-start | bytes 24580
  252.1 7.2 copy-start.8
  252.1 7.2 copy-start.9
  259.3 5.2 copy-start.5
  331.4 7.4 copy-start.10
  338.9 398.1 %reduce-scatter.8.cloned.1.call-start = ((), (), s32[]{:S(2)}) async-start(), calls=%async_computation.9 | async-start | bytes 5242880 | tf_op jit(solution)/shard_map/reduce_scatter | solution.py:770
  358.1 381.6 %reduce-scatter.4.cloned.1.call-start = ((), (), s32[]{:S(2)}) async-start(), calls=%async_computation.7 | async-start | bytes 9175040 | tf_op jit(solution)/shard_map/reduce_scatter | solution.py:765
  411.7 3.4 copy-start.2
  411.7 5.4 copy-start.1
  421.4 5.1 copy-start.7
  438.7 18.4 %copy-start.12 = (bf16[2048,4,64]{0,2,1:T(8,128)(2,1)S(1)}, bf16[2048,4,64]{0,2,1:T(8,128)(2,1)}, u32[]{:S(2)}) copy-start(bf16[2048,4,64]{0,2,1:T(8,128)(2,1)} %copy.113) | copy-start | bytes 3145732
  438.7 18.4 %copy-start.15 = (bf16[2048,4,64]{0,2,1:T(8,128)(2,1)S(1)}, bf16[2048,4,64]{0,2,1:T(8,128)(2,1)}, u32[]{:S(2)}) copy-start(bf16[2048,4,64]{0,2,1:T(8,128)(2,1)} %copy.114) | copy-start | bytes 3145732
  485.8 0.7 copy-start.24
  485.8 0.8 copy-start.23
  485.8 1.2 copy-start.3
  487.7 18.1 %copy-start.13 = (bf16[2048,4,64]{0,2,1:T(8,128)(2,1)S(1)}, bf16[2048,4,64]{0,2,1:T(8,128)(2,1)}, u32[]{:S(2)}) copy-start(bf16[2048,4,64]{0,2,1:T(8,128)(2,1)} %copy.113) | copy-start | bytes 3145732
  487.7 18.1 %copy-start.16 = (bf16[2048,4,64]{0,2,1:T(8,128)(2,1)S(1)}, bf16[2048,4,64]{0,2,1:T(8,128)(2,1)}, u32[]{:S(2)}) copy-start(bf16[2048,4,64]{0,2,1:T(8,128)(2,1)} %copy.114) | copy-start | bytes 3145732
  487.7 18.1 %copy-start.33 = (bf16[2048,1024]{0,1:T(8,128)(2,1)S(1)}, bf16[2048,1024]{0,1:T(8,128)(2,1)}, u32[]{:S(2)}) copy-start(bf16[2048,1024]{0,1:T(8,128)(2,1)} %get-tuple-element.73) | copy-start | bytes 12582916
  505.8 28.0 %copy-start.11 = (bf16[2048,4,64]{0,2,1:T(8,128)(2,1)S(1)}, bf16[2048,4,64]{0,2,1:T(8,128)(2,1)}, u32[]{:S(2)}) copy-start(bf16[2048,4,64]{0,2,1:T(8,128)(2,1)} %copy-done.10) | copy-start | bytes 3145732
  528.2 19.8 %copy-start.14 = (bf16[2048,4,64]{0,2,1:T(8,128)(2,1)S(1)}, bf16[2048,4,64]{0,2,1:T(8,128)(2,1)}, u32[]{:S(2)}) copy-start(bf16[2048,4,64]{0,2,1:T(8,128)(2,1)} %copy.113) | copy-start | bytes 3145732
  528.2 19.8 %copy-start.17 = (bf16[2048,4,64]{0,2,1:T(8,128)(2,1)S(1)}, bf16[2048,4,64]{0,2,1:T(8,128)(2,1)}, u32[]{:S(2)}) copy-start(bf16[2048,4,64]{0,2,1:T(8,128)(2,1)} %copy.114) | copy-start | bytes 3145732
  528.2 208.7 %collective-permute-start.1 = (f32[64,2048]{1,0:T(8,128)}, f32[64,2048]{1,0:T(8,128)}, u32[]{:S(2)}, u32[]{:S(2)}) collective-permute-start(f32[64,2048]{1,0:T(8,128)} %reduce-scatter.6.cloned.1.call-done), channel_id=1, source_target_pairs={{0,0},{8,1},{16,2},{24,3},{1,4},{9,5},{17,6},{25,7},{2,8},{10,9},{... | collective-permute-start | bytes 1572872 | tf_op jit(solution)/shard_map/ppermute | solution.py:562
  787.1 2.6 copy-start.4
  787.1 3.6 copy-start.6
  787.1 3.6 copy-start.18
  822.6 3.5 copy-start.25
Sparse Core Ops, SparseCore 0:
  60.8 64.3 all-gather.4
  126.8 16.7 all-gather.6
  173.2 123.5 all-gather.10
  298.8 32.6 all-gather.8
  339.0 30.4 reduce-scatter.5
  372.0 44.5 reduce-scatter.7
  485.9 71.3 reduce-scatter.3

commit v21 on v17

--- a/solution.py
+++ b/solution.py
@@ -584,14 +584,10 @@
     return result
 
 
-def reduce_small(small):
-    n_dp = lax.axis_size("dp")
-    n_ctx = lax.axis_size("ctx")
-    count, width = small.shape
-    packed = jax.vmap(lambda row: pack_rows(row, 128))(small)
-    packed = packed.reshape((n_dp, n_ctx) + packed.shape[1:]).transpose(1, 0, 2, 3)
-    over_ctx = jnp.sum(exchange(packed, "ctx", 7), axis=0)
-    over_dp = jnp.sum(exchange(over_ctx, "dp", 9), axis=0)
+def reduce_small(over_ctx):
+    width = over_ctx.shape[1]
+    packed = jax.vmap(lambda row: pack_rows(row, 128))(over_ctx)
+    over_dp = jnp.sum(exchange(packed, "dp", 9), axis=0)
     return over_dp.reshape(-1)[:width]
 
 
@@ -619,18 +615,43 @@
     return (cols, fc2_rows, tokens)
 
 
-def return_heads(owned_parts):
+def split_wide(values):
+    high = values.astype(jnp.bfloat16)
+    low_part = (values - high.astype(jnp.float32)).astype(jnp.bfloat16)
+    return jnp.concatenate([high, low_part], axis=-1)
+
+
+def join_wide(values):
+    half = values.shape[-1] // 2
+    return values[..., :half].astype(jnp.float32) + values[..., half:].astype(jnp.float32)
+
+
+def return_heads(owned_parts, small):
     dp_count = lax.axis_size("dp")
     ctx_count = lax.axis_size("ctx")
     head_width = D // ctx_count
     unit = FF // (dp_count * ctx_count)
     rows_piece = owned_parts.shape[0] // ctx_count
-    got = exchange(owned_parts.reshape(ctx_count, rows_piece, -1), "ctx", 6)
+    width = owned_parts.shape[1]
+    small_width = small.shape[1]
+    small_by_ctx = small.reshape(dp_count, ctx_count, small_width).transpose(1, 0, 2)
+    coded = split_wide(small_by_ctx.reshape(ctx_count, -1))
+    extra = -(-coded.shape[1] // (8 * width)) * 8
+    coded = jnp.pad(coded, ((0, 0), (0, extra * width - coded.shape[1])))
+    payload = jnp.concatenate(
+        [owned_parts.reshape(ctx_count, rows_piece, width), coded.reshape(ctx_count, extra, width)],
+        axis=1,
+    )
+    got = exchange(payload, "ctx", 6)
+    small_got = got[:, rows_piece:, :].reshape(ctx_count, -1)[:, : 2 * dp_count * small_width]
+    over_ctx = jnp.sum(join_wide(small_got), axis=0).reshape(dp_count, small_width)
+    got = got[:, :rows_piece, :]
     qkv = got[:, :, : 3 * head_width].reshape(ctx_count, rows_piece, 3, head_width)
     fc1 = got[:, :, 3 * head_width :].reshape(ctx_count, rows_piece, dp_count, unit)
     return (
         qkv.transpose(1, 2, 0, 3).reshape(rows_piece, 3 * D).astype(jnp.float32),
         fc1.transpose(1, 2, 0, 3).reshape(rows_piece, FF).astype(jnp.float32),
+        over_ctx,
     )
 
 
@@ -683,9 +704,8 @@
     tokens_group = ring_all_gather(tokens, ring, 0)
     late_dy, tokens_group = lax.optimization_barrier((cotangent, tokens_group))
     dy_group = lax.all_gather(late_dy, "ctx", axis=0, tiled=True)
-    hidden_group = norm_parts(tokens_group.astype(jnp.float32), gain32, shift32)[2].astype(
-        jnp.bfloat16
-    )
+    normed_group, _, hidden32_group = norm_parts(tokens_group.astype(jnp.float32), gain32, shift32)
+    hidden_group = hidden32_group.astype(jnp.bfloat16)
     bias_cols = lax.dynamic_slice_in_dim(
         qkv_bias.reshape(3, D), here * head_width, head_width, 1
     ).reshape(3 * head_width)
@@ -743,17 +763,14 @@
     )
     d_both = jnp.concatenate([d_qkv, d_pre], axis=1)
     bias_part = jnp.sum(d_qkv.astype(jnp.float32), axis=0).reshape(3, head_width)
-    d_hidden = ring_reduce_scatter(
-        jnp.einsum("tc,dc->td", d_both, cols, preferred_element_type=jnp.float32), ring, 3
-    )
+    d_hidden_part = jnp.einsum("tc,dc->td", d_both, cols, preferred_element_type=jnp.float32)
+    gain_part = jnp.sum(d_hidden_part * normed_group, axis=0)
+    shift_part = jnp.sum(d_hidden_part, axis=0)
+    d_hidden = ring_reduce_scatter(d_hidden_part, ring, 3)
     weight_parts = jnp.einsum(
         "td,tc->dc", hidden_group, d_both, preferred_element_type=jnp.float32
     ).astype(jnp.bfloat16)
     owned_parts = lax.psum_scatter(weight_parts, "dp", scatter_dimension=0, tiled=True)
-    split_qkv, split_fc1 = return_heads(owned_parts)
-    d_hidden, split_qkv, split_fc1 = lax.optimization_barrier((d_hidden, split_qkv, split_fc1))
-    grad_gain, grad_shift, d_inputs = norm_back(d_hidden, normed, scaled, gain32)
-    grad_tokens = (grad_out32 + d_inputs).astype(jnp.bfloat16)
     owned_fc2 = lax.psum_scatter(
         grad_fc2_part.astype(jnp.bfloat16), "dp", scatter_dimension=0, tiled=True
     ).astype(jnp.float32)
@@ -770,13 +787,19 @@
         [
             full_bqkv.reshape(count, -1),
             grad_b_fc2.reshape(count, -1),
-            grad_gain.reshape(count, -1),
-            grad_shift.reshape(count, -1),
+            gain_part.reshape(count, -1),
+            shift_part.reshape(count, -1),
             full_bfc1.reshape(count, -1),
         ],
         axis=1,
     )
-    owned_small = reduce_small(small)
+    split_qkv, split_fc1, over_ctx = return_heads(owned_parts, small)
+    d_hidden, split_qkv, split_fc1, over_ctx = lax.optimization_barrier(
+        (d_hidden, split_qkv, split_fc1, over_ctx)
+    )
+    _, _, d_inputs = norm_back(d_hidden, normed, scaled, gain32)
+    grad_tokens = (grad_out32 + d_inputs).astype(jnp.bfloat16)
+    owned_small = reduce_small(over_ctx)
     cuts = [0, 3 * D // count, D // count, D // count, D // count, FF // count]
     bounds = [sum(cuts[: i + 1]) for i in range(len(cuts))]
     owned_bqkv, owned_bout, owned_gain, owned_shift, owned_bfc1 = [

time: 839 us -> 842 us (level); the launches traced: 833 us -> 825 us
  Pallas kernels: 513 us -> 498 us
    pallas_call x6 -> x5, Pallas kernels: 115 us -> 99.2 us  [exchange(): pl.pallas_call(functools.partial(_exchange_kernel, group=group), out_shap...]
  transfers between devices with their start and end apart: 9 -> 9, of which waited for: 0 -> 0; matrix products, arithmetic and copies ran while one was open for 31% -> 32% of each run, Pallas kernels for 50% -> 50%
where the time goes in v21:
time: 842 us; the launch traced here: 825 us
  Pallas kernels  498 us (59%)
  matrix products  155 us (18%)
  local copies, waits for them, and re-layouts  83.4 us (10%)
  other arithmetic  67.4 us (8%)
  between operations  15.2 us (2%)
    pallas_call x2, Pallas kernels, ring_reduce_scatter(): pl.pallas_call(functools.partial(_scatter_kernel, ring=ring, rows=rows, p...  188 us
    pallas_call x1, Pallas kernels, ring_all_gather(): pl.pallas_call(functools.partial(_gather_kernel, ring=ring, rows=rows), o...  109 us
    pallas_call x5, Pallas kernels, exchange(): pl.pallas_call(functools.partial(_exchange_kernel, group=group), out_shap...  99.2 us
    pallas_call x1, Pallas kernels, attention_backward(): pl.pallas_call(functools.partial(_bwd_kernel, tq=block, tk=block, scale=s...  53.8 us
    pallas_call x1, Pallas kernels, attention_forward(): pl.pallas_call(functools.partial(_fwd_kernel, tq=block, tk=block, scale=s...  48.1 us
    unnamed x84, local copies, waits for them, and re-layouts  33.1 us
    dot_general x1, matrix products, head_plan(): jnp.einsum('td,tc->dc', hidden_group, d_both, preferred_element_type=jnp....  28.5 us
    dot_general x1, matrix products, head_plan(): jnp.einsum('tc,dc->td', d_both, cols, preferred_element_type=jnp.float32)  24.8 us
  transfers between devices with their start and end apart: 9, of which 0 were waited for; matrix products, arithmetic and copies ran while one was open for 32% of the time, Pallas kernels for 50%

profile of v21, /device:TPU:0, one launch (start us, length us, event | category | flops | bytes accessed | tf_op | source)
XLA Modules:
  0.0 825.4 jit_solution(2765987263206085227)
XLA Ops:
  7.2 1.7 convert_element_type.194
  10.4 1.5 convert_element_type.193
  14.8 38.6 %shard_map.256 = bf16[8,64,1792]{2,1,0:T(8,128)(2,1)} custom-call(bf16[8,64,1792]{2,1,0:T(8,128)(2,1)} %pad_maximum_fusion.4.x_ref), custom_call_target="tpu_custom_call" | custom-call | tf_op jit(solution)/shard_map/pallas_call | solution.py:531
  55.0 108.6 %shard_map.257 = bf16[2048,2048]{1,0:T(8,128)(2,1)} custom-call(bf16[256,2048]{1,0:T(8,128)(2,1)} %x_ref), custom_call_target="tpu_custom_call" | custom-call | tf_op jit(solution)/shard_map/pallas_call | solution.py:395
  166.0 5.0 shard_map.258
  171.0 1.4 broadcast_in_dim.34.x_ref
  172.4 10.0 %shard_map.259 = bf16[8,4,16,128]{3,2,1,0:T(8,128)(2,1)} custom-call(bf16[8,4,16,128]{3,2,1,0:T(8,128)(2,1)} %broadcast_in_dim.34.x_ref), custom_call_target="tpu_custom_call" | custom-call | tf_op jit(solution)/shard_map/pallas_call | solution.py:531
  184.3 4.7 convert_reduce_fusion
  190.1 2.3 fusion.7
  195.8 23.2 %convolution_add_fusion = f32[2048,1792]{0,1:T(8,128)} fusion(bf16[2048,1792]{1,0:T(8,128)(2,1)} %all-gather.5.cloned.1.call-done, f32[1792]{0:T(1024)S(1)} %maximum_convert_fusion, bf16[2048,2048]{1,0:T(8,128)(2,1)} %shard_map.257, f32[2048]{0:T(1024)S(1)} %reshape.312, f32[2048]{0:T(1024)S(1)} %reshape.311, f32[2048]{0:T(1024)S(1)} %add_rsqrt_fusion, ...), kind=kOutput, calls=%fused_computation.12 | convolution fusion | flops 15061221376 | bytes 30448640 | tf_op jit(solution)/shard_map/dot_general | solution.py:712
  218.9 1.7 slice.218
  220.7 3.9 fusion.38
  226.5 3.5 copy.125
  230.0 3.6 copy.126
  233.6 2.1 slice.219
  235.7 2.3 fusion.39
  237.9 3.7 copy.128
  241.6 3.6 copy.129
  245.2 3.0 copy.127
  248.2 2.6 copy.130
  250.9 1.8 copy.111
  252.6 7.3 subtract_convert_fusion.2
  259.9 5.2 maximum_bitcast_fusion
  265.1 2.0 maximum_maximum_fusion.v_ref
  267.1 48.1 %shard_map.260 = (f32[4,2048,64]{2,1,0:T(8,128)}, f32[4,2048,1]{2,1,0:T(8,128)}) custom-call(s32[10]{0:T(128)} %constant.61.clone.qi_ref, s32[10]{0:T(128)} %constant.62.clone.kj_ref, bf16[4,2048,64]{2,1,0:T(8,128)(2,1)} %get-tuple-element.78.q_ref, bf16[4,2048,64]{2,1,0:T(8,128)(2,1)} %get-tuple-element.79.k_ref, ...), custom_call_target="tpu_custom_call" | custom-call | flops 2147483648 | bytes 5242880 | tf_op jit(solution)/shard_map/pallas_call | solution.py:168
  315.2 6.0 convolution_convert_fusion.2
  321.3 1.8 copy.114
  323.1 6.8 multiply_reduce_fusion
  329.9 2.1 copy.113
  332.0 7.4 fusion.42
  339.5 2.7 copy.115.delta_ref
  342.2 15.6 %convolution_convert_fusion.1 = bf16[1024,2048]{1,0:T(8,128)(2,1)} fusion(bf16[2048,2048]{1,0:T(8,128)(2,1)} %all-gather.11.cloned.1.call-done, f32[2048,1792]{0,1:T(8,128)} %convolution_add_fusion), kind=kOutput, calls=%fused_computation.37 | convolution fusion | flops 8610906112 | bytes 20971520 | tf_op jit(solution)/shard_map/tf,td->fd/dot_general | solution.py:740
  357.9 53.8 %shard_map.262 = (f32[4,2048,64]{2,1,0:T(8,128)}, f32[4,2048,64]{2,1,0:T(8,128)}, f32[4,2048,64]{2,1,0:T(8,128)}) custom-call(s32[10]{0:T(128)} %constant.63.clone.qi_ref, s32[10]{0:T(128)} %constant.64.clone.kj_ref, bf16[4,2048,64]{2,1,0:T(8,128)(2,1)} %get-tuple-element.78.q_ref, bf16[4,2048,64]{2,1,0:T(8,128)(2,1)} %get-tuple-element.79.k_ref, ...), custom_call_target="tpu_custom_call" | custom-call | flops 5368709120 | bytes 12582912 | tf_op jit(solution)/shard_map/pallas_call | solution.py:258
  411.7 2.9 slice.217
  415.2 1.9 slice.216
  417.1 4.3 add_convert_fusion.1
  421.4 3.2 pad_maximum_fusion.1
  424.7 1.9 copy.117
  426.6 5.4 pad_maximum_fusion.2
  432.0 2.7 copy.118
  434.7 2.5 convert_bitcast_fusion
  437.2 1.6 copy.119
  438.8 18.4 %convert_reduce_fusion.1 = (f32[1024]{0:T(1024)S(1)}, bf16[2048,1024]{0,1:T(8,128)(2,1)}) fusion(f32[2048,1792]{0,1:T(8,128)} %convolution_add_fusion, bf16[2048,2048]{1,0:T(8,128)(2,1)} %all-gather.11.cloned.1.call-done, bf16[1024,2048]{1,0:T(8,128)(2,1)} %all-gather.9.cloned.1.call-done), kind=kOutput, calls=%fused_computation.21 | convolution fusion | flops 8633973760 | bytes 25169920 | tf_op jit(solution)/shard_map/td,fd->tf/dot_general | solution.py:741
  457.1 28.5 %convolution_convert_fusion = bf16[2048,1792]{1,0:T(8,128)(2,1)} fusion(bf16[2048,1024]{0,1:T(8,128)(2,1)} %get-tuple-element.77, bf16[2048,256]{0,1:T(8,128)(2,1)S(1)} %bitcast.127, bf16[2048,256]{0,1:T(8,128)(2,1)S(1)} %bitcast.124, bf16[2048,256]{0,1:T(8,128)(2,1)S(1)} %bitcast.120, bf16[2048,2048]{1,0:T(8,128)(2,1)} %shard_map.257, ...), kind=kOutput, calls=%fused_computation.23 | convolution fusion | flops 15090581504 | bytes 23101440 | tf_op jit(solution)/shard_map/td,tc->dc/dot_general | solution.py:770
  488.0 16.8 %fusion.34 = f32[2048,2048]{1,0:T(8,128)} fusion(bf16[1024,2048]{1,0:T(8,128)(2,1)} %all-gather.9.cloned.1.call-done, f32[2048,1792]{0,1:T(8,128)} %convolution_add_fusion), kind=kOutput, calls=%fused_computation.116 | convolution fusion | flops 8608808960 | bytes 29360128 | tf_op jit(solution)/shard_map/dot_general | solution.py:731
  505.5 24.8 %fusion.37 = (f32[2048]{0:T(1024)S(1)}, f32[2048]{0:T(1024)S(1)}, f32[2048,2048]{1,0:T(8,128)}) fusion(f32[2048]{0:T(1024)S(1)} %add_rsqrt_fusion, f32[2048]{0:T(1024)S(1)} %broadcast_multiply_fusion, bf16[2048,2048]{1,0:T(8,128)(2,1)} %shard_map.257, bf16[2048,1792]{1,0:T(8,128)(2,1)} %all-gather.5.cloned.1.call-done, ...), kind=kOutput, calls=%fused_computation.117 | convolution fusion | flops 15086907392 | bytes 39878656 | tf_op jit(solution)/shard_map/tc,dc->td/dot_general | solution.py:766
  530.7 5.6 collective-permute-start.1
  536.3 14.3 %convolution_add_fusion.1.p_ref = f32[2048,2048]{1,0:T(8,128)} fusion(f32[2048,2048]{1,0:T(8,128)} %fusion.34, bf16[2048,256]{0,1:T(8,128)(2,1)S(1)} %bitcast.114, bf16[256,2048]{1,0:T(8,128)(2,1)} %all-gather.7.cloned.1.call-done), kind=kOutput, calls=%fused_computation.13 | convolution fusion | flops 2151677952 | bytes 35651584 | tf_op jit(solution)/shard_map/dot_general | solution.py:730
  550.6 99.4 %shard_map.263 = f32[256,2048]{1,0:T(8,128)} custom-call(f32[2048,2048]{1,0:T(8,128)} %get-tuple-element.75.p_ref), custom_call_target="tpu_custom_call" | custom-call | tf_op jit(solution)/shard_map/pallas_call | solution.py:466
  650.0 88.4 %shard_map.261 = f32[256,2048]{1,0:T(8,128)} custom-call(f32[2048,2048]{1,0:T(8,128)} %convolution_add_fusion.1.p_ref), custom_call_target="tpu_custom_call" | custom-call | tf_op jit(solution)/shard_map/pallas_call | solution.py:466
  738.4 2.8 convert_element_type.245
  741.2 2.9 pad_maximum_fusion.3.x_ref
  744.1 36.9 %shard_map.264 = bf16[8,72,1792]{2,1,0:T(8,128)(2,1)} custom-call(bf16[8,72,1792]{2,1,0:T(8,128)(2,1)} %pad_maximum_fusion.3.x_ref), custom_call_target="tpu_custom_call" | custom-call | tf_op jit(solution)/shard_map/pallas_call | solution.py:531
  781.0 1.5 slice_convert_fusion.5
  782.5 2.4 slice_convert_fusion.6
  785.9 2.0 reshape.318
  787.9 2.9 copy.122
  790.8 2.5 copy.137
  793.3 1.9 reshape.317
  795.2 2.7 copy.121
  797.9 1.6 copy.136
  800.2 8.7 %shard_map.265 = f32[4,16,128]{2,1,0:T(8,128)} custom-call(f32[4,16,128]{2,1,0:T(8,128)} %bitcast.148), custom_call_target="tpu_custom_call" | custom-call | tf_op jit(solution)/shard_map/pallas_call | solution.py:531
  812.0 3.9 fusion.23
  816.4 1.9 copy.156
  (172 shorter events, 25.4 us)
Async XLA Ops:
  7.2 188.6 %all-gather.5.cloned.1.call-start = ((), (), s32[]{:S(2)}) async-start(), calls=%async_computation.3 | async-start | bytes 9175040 | tf_op jit(solution)/shard_map/all_gather | solution.py:612
  13.4 40.1 %copy-start.19 = (f32[64,2048]{1,0:T(8,128)S(1)}, f32[64,2048]{1,0:T(8,128)}, u32[]{:S(2)}) copy-start(f32[64,2048]{1,0:T(8,128)} %param.21) | copy-start | bytes 1572868
  53.4 261.8 %all-gather.7.cloned.1.call-start = ((), (), s32[]{:S(2)}) async-start(), calls=%async_computation.4 | async-start | bytes 1310720 | tf_op jit(solution)/shard_map/all_gather | solution.py:554
  53.5 0.7 collective-permute-start
  54.2 0.7 copy-start.20
  54.9 108.8 %copy-start.18 = (f32[256,2048]{1,0:T(8,128)S(1)}, f32[256,2048]{1,0:T(8,128)}, u32[]{:S(2)}) copy-start(f32[256,2048]{1,0:T(8,128)} %param.25) | copy-start | bytes 6291460
  54.9 260.3 %all-gather.11.cloned.1.call-start = ((), (), s32[]{:S(2)}) async-start(), calls=%async_computation.6 | async-start | bytes 9437184 | tf_op jit(solution)/shard_map/all_gather | solution.py:706
  163.6 1.5 copy-start.25
  163.6 1.5 copy-start.27
  163.6 1.5 copy-start.28
  163.6 1.6 copy-start.29
  163.6 1.6 copy-start.30
  163.7 1.6 copy-start.26
  163.7 275.1 %all-gather.9.cloned.1.call-start = ((), (), s32[]{:S(2)}) async-start(), calls=%async_computation.5 | async-start | bytes 5242880 | tf_op jit(solution)/shard_map/all_gather | solution.py:613
  164.9 365.8 %reduce-scatter.6.cloned.1.call-start = ((), (), s32[]{:S(2)}) async-start(), calls=%async_computation.8 | async-start | bytes 2621440 | tf_op jit(solution)/shard_map/reduce_scatter | solution.py:560
  184.3 5.8 copy-start
  190.1 2.5 copy-start.31
  192.9 26.0 %copy-start.21 = (s32[2048]{0:T(1024)}, s32[2048]{0:T(1024)S(1)}, u32[]{:S(2)}) copy-start(s32[2048]{0:T(1024)S(1)} %convert_reduce_fusion.5) | copy-start | bytes 24580
  252.6 7.3 copy-start.9
  252.6 7.3 copy-start.10
  259.9 5.2 copy-start.7
  331.9 7.4 copy-start.11
  339.4 399.0 %reduce-scatter.8.cloned.1.call-start = ((), (), s32[]{:S(2)}) async-start(), calls=%async_computation.9 | async-start | bytes 5242880 | tf_op jit(solution)/shard_map/reduce_scatter | solution.py:774
  357.8 383.4 %reduce-scatter.4.cloned.1.call-start = ((), (), s32[]{:S(2)}) async-start(), calls=%async_computation.7 | async-start | bytes 9175040 | tf_op jit(solution)/shard_map/reduce_scatter | solution.py:773
  411.7 3.5 copy-start.3
  411.7 5.4 copy-start.2
  421.4 5.1 copy-start.8
  438.8 18.4 %copy-start.14 = (bf16[2048,4,64]{0,2,1:T(8,128)(2,1)S(1)}, bf16[2048,4,64]{0,2,1:T(8,128)(2,1)}, u32[]{:S(2)}) copy-start(bf16[2048,4,64]{0,2,1:T(8,128)(2,1)} %copy.118) | copy-start | bytes 3145732
  438.8 18.4 %copy-start.16 = (bf16[2048,4,64]{0,2,1:T(8,128)(2,1)S(1)}, bf16[2048,4,64]{0,2,1:T(8,128)(2,1)}, u32[]{:S(2)}) copy-start(bf16[2048,4,64]{0,2,1:T(8,128)(2,1)} %copy.119) | copy-start | bytes 3145732
  485.7 1.2 copy-start.5
  485.7 1.5 copy-start.23
  485.7 1.5 copy-start.22
  485.7 1.6 copy-start.1
  488.0 16.8 %copy-start.15 = (bf16[2048,4,64]{0,2,1:T(8,128)(2,1)S(1)}, bf16[2048,4,64]{0,2,1:T(8,128)(2,1)}, u32[]{:S(2)}) copy-start(bf16[2048,4,64]{0,2,1:T(8,128)(2,1)} %copy.118) | copy-start | bytes 3145732
  488.0 16.8 %copy-start.17 = (bf16[2048,4,64]{0,2,1:T(8,128)(2,1)S(1)}, bf16[2048,4,64]{0,2,1:T(8,128)(2,1)}, u32[]{:S(2)}) copy-start(bf16[2048,4,64]{0,2,1:T(8,128)(2,1)} %copy.119) | copy-start | bytes 3145732
  505.5 30.7 %copy-start.12 = (bf16[2048,4,64]{0,2,1:T(8,128)(2,1)S(1)}, bf16[2048,4,64]{0,2,1:T(8,128)(2,1)}, u32[]{:S(2)}) copy-start(bf16[2048,4,64]{0,2,1:T(8,128)(2,1)} %copy-done.11) | copy-start | bytes 3145732
  530.7 207.7 %collective-permute-start.1 = (f32[64,2048]{1,0:T(8,128)}, f32[64,2048]{1,0:T(8,128)}, u32[]{:S(2)}, u32[]{:S(2)}) collective-permute-start(f32[64,2048]{1,0:T(8,128)} %reduce-scatter.6.cloned.1.call-done), channel_id=1, source_target_pairs={{0,0},{8,1},{16,2},{24,3},{1,4},{9,5},{17,6},{25,7},{2,8},{10,9},{... | collective-permute-start | bytes 1572872 | tf_op jit(solution)/shard_map/ppermute | solution.py:562
  787.9 5.4 copy-start.13
  795.2 16.2 %copy-start.4 = (f32[256,2048]{1,0:T(8,128)S(1)}, f32[256,2048]{1,0:T(8,128)}, u32[]{:S(2)}) copy-start(f32[256,2048]{1,0:T(8,128)} %shard_map.263) | copy-start | bytes 6291460
  809.6 2.4 copy-start.6
  810.2 5.7 copy-start.24
Sparse Core Ops, SparseCore 0:
  53.5 63.1 all-gather.4
  118.3 16.7 all-gather.6
  163.8 126.5 all-gather.10
  292.4 32.6 all-gather.8
  339.5 33.8 reduce-scatter.5
  376.0 44.5 reduce-scatter.7
  485.9 75.3 reduce-scatter.3

commit v22 on v17

--- a/solution.py
+++ b/solution.py
@@ -151,7 +151,7 @@
     )
 
 
-def attention_forward(q, k, v, seg, block=512):
+def attention_forward(q, k, v, seg, block=1024):
     heads, total, dim = q.shape
     count = total // block
     scale = 1.0 / math.sqrt(dim)
@@ -240,7 +240,7 @@
         dv_ref[0] = dv_sc[...].T
 
 
-def attention_backward(q, k, v, do, lse, delta, seg, block=512):
+def attention_backward(q, k, v, do, lse, delta, seg, block=1024):
     heads, total, dim = q.shape
     count = total // block
     scale = 1.0 / math.sqrt(dim)

time: 839 us -> 817 us (0.974)
  Pallas kernels: 513 us -> 491 us
    pallas_call x1, Pallas kernels: 48.1 us -> 34.9 us  [attention_forward(): pl.pallas_call(functools.partial(_fwd_kernel, tq=block, tk=block, scale=s...]
    pallas_call x1, Pallas kernels: 53.9 us -> 44.7 us  [attention_backward(): pl.pallas_call(functools.partial(_bwd_kernel, tq=block, tk=block, scale=s...]
  transfers between devices with their start and end apart: 9 -> 9, of which waited for: 0 -> 0; matrix products, arithmetic and copies ran while one was open for 31% -> 32% of each run, Pallas kernels for 50% -> 48%
where the time goes in v22:
time: 817 us; the launch traced here: 812 us
  Pallas kernels  491 us (60%)
  matrix products  152 us (19%)
  local copies, waits for them, and re-layouts  81.5 us (10%)
  other arithmetic  65.6 us (8%)
  between operations  15.2 us (2%)
    pallas_call x2, Pallas kernels, ring_reduce_scatter(): pl.pallas_call(functools.partial(_scatter_kernel, ring=ring, rows=rows, p...  186 us
    pallas_call x6, Pallas kernels, exchange(): pl.pallas_call(functools.partial(_exchange_kernel, group=group), out_shap...  116 us
    pallas_call x1, Pallas kernels, ring_all_gather(): pl.pallas_call(functools.partial(_gather_kernel, ring=ring, rows=rows), o...  109 us
    pallas_call x1, Pallas kernels, attention_backward(): pl.pallas_call(functools.partial(_bwd_kernel, tq=block, tk=block, scale=s...  44.7 us
    pallas_call x1, Pallas kernels, attention_forward(): pl.pallas_call(functools.partial(_fwd_kernel, tq=block, tk=block, scale=s...  34.9 us
    unnamed x84, local copies, waits for them, and re-layouts  31.1 us
    dot_general x1, matrix products, head_plan(): jnp.einsum('td,tc->dc', hidden_group, d_both, preferred_element_type=jnp....  29.1 us
    dot_general x1, matrix products, head_plan(): jnp.dot(hidden_group, cols, preferred_element_type=jnp.float32)  23.3 us
  transfers between devices with their start and end apart: 9, of which 0 were waited for; matrix products, arithmetic and copies ran while one was open for 32% of the time, Pallas kernels for 48%

profile of v22, /device:TPU:0, one launch (start us, length us, event | category | flops | bytes accessed | tf_op | source)
XLA Modules:
  0.0 811.7 jit_solution(7745302386253228441)
XLA Ops:
  7.2 1.7 convert_element_type.177
  10.4 1.5 convert_element_type.176
  14.8 38.6 %shard_map.256 = bf16[8,64,1792]{2,1,0:T(8,128)(2,1)} custom-call(bf16[8,64,1792]{2,1,0:T(8,128)(2,1)} %pad_maximum_fusion.3.x_ref), custom_call_target="tpu_custom_call" | custom-call | tf_op jit(solution)/shard_map/pallas_call | solution.py:531
  55.0 108.6 %shard_map.257 = bf16[2048,2048]{1,0:T(8,128)(2,1)} custom-call(bf16[256,2048]{1,0:T(8,128)(2,1)} %x_ref), custom_call_target="tpu_custom_call" | custom-call | tf_op jit(solution)/shard_map/pallas_call | solution.py:395
  166.0 5.0 shard_map.258
  171.0 1.4 broadcast_in_dim.34.x_ref
  172.4 10.0 %shard_map.259 = bf16[8,4,16,128]{3,2,1,0:T(8,128)(2,1)} custom-call(bf16[8,4,16,128]{3,2,1,0:T(8,128)(2,1)} %broadcast_in_dim.34.x_ref), custom_call_target="tpu_custom_call" | custom-call | tf_op jit(solution)/shard_map/pallas_call | solution.py:531
  184.3 4.7 convert_reduce_fusion
  190.1 2.3 fusion.2
  195.7 23.3 %convolution_add_fusion = f32[2048,1792]{0,1:T(8,128)} fusion(bf16[2048,1792]{1,0:T(8,128)(2,1)} %all-gather.5.cloned.1.call-done, f32[1792]{0:T(1024)S(1)} %maximum_convert_fusion, bf16[2048,2048]{1,0:T(8,128)(2,1)} %shard_map.257, f32[2048]{0:T(1024)S(1)} %reshape.300, f32[2048]{0:T(1024)S(1)} %reshape.299, f32[2048]{0:T(1024)S(1)} %add_rsqrt_fusion, ...), kind=kOutput, calls=%fused_computation.10 | convolution fusion | flops 15061221376 | bytes 30448640 | tf_op jit(solution)/shard_map/dot_general | solution.py:692
  219.0 1.7 slice.195
  220.7 3.9 fusion.34
  226.6 3.5 copy.129
  230.1 3.5 copy.130
  233.7 2.1 slice.196
  235.7 2.3 fusion.35
  238.0 3.7 copy.132
  241.7 3.6 copy.133
  245.2 2.8 copy.131
  248.0 2.6 copy.134
  250.7 1.8 copy.114
  252.4 7.3 subtract_convert_fusion.2
  259.7 5.2 maximum_bitcast_fusion
  264.9 2.0 maximum_maximum_fusion.v_ref
  266.9 34.9 %shard_map.260 = (f32[4,2048,64]{2,1,0:T(8,128)}, f32[4,2048,1]{2,1,0:T(8,128)}) custom-call(s32[3]{0:T(128)} %constant.57.clone.qi_ref, s32[3]{0:T(128)} %constant.58.clone.kj_ref, bf16[4,2048,64]{2,1,0:T(8,128)(2,1)} %get-tuple-element.74.q_ref, bf16[4,2048,64]{2,1,0:T(8,128)(2,1)} %get-tuple-element.75.k_ref, ...), custom_call_target="tpu_custom_call" | custom-call | flops 2147483648 | bytes 5242880 | tf_op jit(solution)/shard_map/pallas_call | solution.py:168
  301.8 6.0 convolution_convert_fusion.2
  307.8 2.2 copy.117
  310.0 6.8 multiply_reduce_fusion
  316.8 1.9 copy.116
  318.7 7.5 fusion.38
  326.3 2.8 copy.118.delta_ref
  329.0 15.6 %convolution_convert_fusion.1 = bf16[1024,2048]{1,0:T(8,128)(2,1)} fusion(bf16[2048,2048]{1,0:T(8,128)(2,1)} %all-gather.11.cloned.1.call-done, f32[2048,1792]{0,1:T(8,128)} %convolution_add_fusion), kind=kOutput, calls=%fused_computation.35 | convolution fusion | flops 8610906112 | bytes 20971520 | tf_op jit(solution)/shard_map/tf,td->fd/dot_general | solution.py:720
  344.7 44.7 %shard_map.262 = (f32[4,2048,64]{2,1,0:T(8,128)}, f32[4,2048,64]{2,1,0:T(8,128)}, f32[4,2048,64]{2,1,0:T(8,128)}) custom-call(s32[3]{0:T(128)} %constant.57.clone.qi_ref, s32[3]{0:T(128)} %constant.58.clone.kj_ref, bf16[4,2048,64]{2,1,0:T(8,128)(2,1)} %get-tuple-element.74.q_ref, bf16[4,2048,64]{2,1,0:T(8,128)(2,1)} %get-tuple-element.75.k_ref, ...), custom_call_target="tpu_custom_call" | custom-call | flops 5368709120 | bytes 12582912 | tf_op jit(solution)/shard_map/pallas_call | solution.py:258
  389.4 3.0 slice.194
  392.9 1.9 slice.193
  394.8 4.3 add_convert_fusion.1
  399.1 3.2 pad_maximum_fusion.1
  402.3 2.1 copy.120
  404.5 5.4 pad_maximum_fusion.2
  409.9 2.7 copy.121
  412.6 2.5 convert_bitcast_fusion
  415.1 1.6 copy.122
  416.7 17.9 %convert_reduce_fusion.1 = (f32[1024]{0:T(1024)S(1)}, bf16[2048,1024]{0,1:T(8,128)(2,1)}) fusion(f32[2048,1792]{0,1:T(8,128)} %convolution_add_fusion, bf16[2048,2048]{1,0:T(8,128)(2,1)} %all-gather.11.cloned.1.call-done, bf16[1024,2048]{1,0:T(8,128)(2,1)} %all-gather.9.cloned.1.call-done), kind=kOutput, calls=%fused_computation.19 | convolution fusion | flops 8633973760 | bytes 25169920 | tf_op jit(solution)/shard_map/td,fd->tf/dot_general | solution.py:721
  434.6 29.1 %convolution_convert_fusion = bf16[2048,1792]{1,0:T(8,128)(2,1)} fusion(bf16[2048,1024]{0,1:T(8,128)(2,1)} %get-tuple-element.73, bf16[2048,256]{0,1:T(8,128)(2,1)S(1)} %bitcast.120, bf16[2048,256]{0,1:T(8,128)(2,1)S(1)} %bitcast.117, bf16[2048,256]{0,1:T(8,128)(2,1)S(1)} %bitcast.114, bf16[2048,2048]{1,0:T(8,128)(2,1)} %shard_map.257, ...), kind=kOutput, calls=%fused_computation.21 | convolution fusion | flops 15090581504 | bytes 23101440 | tf_op jit(solution)/shard_map/td,tc->dc/dot_general | solution.py:749
  465.7 16.8 %fusion.31 = f32[2048,2048]{1,0:T(8,128)} fusion(bf16[1024,2048]{1,0:T(8,128)(2,1)} %all-gather.9.cloned.1.call-done, f32[2048,1792]{0,1:T(8,128)} %convolution_add_fusion), kind=kOutput, calls=%fused_computation.108 | convolution fusion | flops 8608808960 | bytes 29360128 | tf_op jit(solution)/shard_map/dot_general | solution.py:711
  482.5 21.4 %fusion.27.p_ref = f32[2048,2048]{1,0:T(8,128)} fusion(bf16[2048,1792]{1,0:T(8,128)(2,1)} %all-gather.5.cloned.1.call-done, bf16[2048,1024]{0,1:T(8,128)(2,1)S(1)} %copy-done.33, bf16[2048,256]{0,1:T(8,128)(2,1)S(1)} %bitcast.121, bf16[2048,256]{0,1:T(8,128)(2,1)S(1)} %bitcast.118, bf16[2048,256]{0,1:T(8,128)(2,1)S(1)} %bitcast.115), kind=kOutput, calls=%fused_computation.66 | convolution fusion | flops 15061745664 | bytes 31457280 | tf_op jit(solution)/shard_map/tc,dc->td/dot_general | solution.py:747
  503.9 5.5 collective-permute-start.1
  509.4 14.4 %convolution_add_fusion.1.p_ref = f32[2048,2048]{1,0:T(8,128)} fusion(f32[2048,2048]{1,0:T(8,128)} %fusion.31, bf16[2048,256]{0,1:T(8,128)(2,1)S(1)} %bitcast.108, bf16[256,2048]{1,0:T(8,128)(2,1)} %all-gather.7.cloned.1.call-done), kind=kOutput, calls=%fused_computation.11 | convolution fusion | flops 2151677952 | bytes 35651584 | tf_op jit(solution)/shard_map/dot_general | solution.py:710
  524.7 98.4 %shard_map.263 = f32[256,2048]{1,0:T(8,128)} custom-call(f32[2048,2048]{1,0:T(8,128)} %fusion.27.p_ref), custom_call_target="tpu_custom_call" | custom-call | tf_op jit(solution)/shard_map/pallas_call | solution.py:466
  623.2 88.0 %shard_map.261 = f32[256,2048]{1,0:T(8,128)} custom-call(f32[2048,2048]{1,0:T(8,128)} %convolution_add_fusion.1.p_ref), custom_call_target="tpu_custom_call" | custom-call | tf_op jit(solution)/shard_map/pallas_call | solution.py:466
  711.3 2.8 convert_element_type.223
  714.0 32.4 %shard_map.264 = bf16[8,64,1792]{2,1,0:T(8,128)(2,1)} custom-call(bf16[8,64,1792]{2,1,0:T(8,128)(2,1)} %bitcast.131), custom_call_target="tpu_custom_call" | custom-call | tf_op jit(solution)/shard_map/pallas_call | solution.py:531
  746.4 1.5 slice_convert_fusion.5
  747.9 2.4 slice_convert_fusion.6
  750.3 2.0 reshape.306
  752.3 2.8 copy.125
  755.1 2.5 copy.140
  757.6 2.6 reshape.305
  761.2 1.6 copy.139
  763.9 3.0 convert_reduce_fusion.4
  768.0 19.7 %shard_map.265 = f32[8,4,16,128]{3,2,1,0:T(8,128)} custom-call(f32[8,4,16,128]{3,2,1,0:T(8,128)} %copy_bitcast_fusion.3.x_ref), custom_call_target="tpu_custom_call" | custom-call | tf_op jit(solution)/shard_map/pallas_call | solution.py:531
  787.7 1.6 reduce_sum.158.x_ref
  789.3 10.5 %shard_map.266 = f32[4,16,128]{2,1,0:T(8,128)} custom-call(f32[4,16,128]{2,1,0:T(8,128)} %reduce_sum.158.x_ref), custom_call_target="tpu_custom_call" | custom-call | tf_op jit(solution)/shard_map/pallas_call | solution.py:531
  802.8 1.9 copy.157
  (169 shorter events, 25.7 us)
Async XLA Ops:
  7.2 188.6 %all-gather.5.cloned.1.call-start = ((), (), s32[]{:S(2)}) async-start(), calls=%async_computation.3 | async-start | bytes 9175040 | tf_op jit(solution)/shard_map/all_gather | solution.py:616
  13.4 40.1 %copy-start.20 = (f32[64,2048]{1,0:T(8,128)S(1)}, f32[64,2048]{1,0:T(8,128)}, u32[]{:S(2)}) copy-start(f32[64,2048]{1,0:T(8,128)} %param.21) | copy-start | bytes 1572868
  53.4 248.4 %all-gather.7.cloned.1.call-start = ((), (), s32[]{:S(2)}) async-start(), calls=%async_computation.4 | async-start | bytes 1310720 | tf_op jit(solution)/shard_map/all_gather | solution.py:554
  53.5 0.7 collective-permute-start
  54.2 0.7 copy-start.21
  54.9 108.8 %copy-start.19 = (f32[256,2048]{1,0:T(8,128)S(1)}, f32[256,2048]{1,0:T(8,128)}, u32[]{:S(2)}) copy-start(f32[256,2048]{1,0:T(8,128)} %param.25) | copy-start | bytes 6291460
  54.9 246.9 %all-gather.11.cloned.1.call-start = ((), (), s32[]{:S(2)}) async-start(), calls=%async_computation.6 | async-start | bytes 9437184 | tf_op jit(solution)/shard_map/all_gather | solution.py:685
  163.6 1.5 copy-start.26
  163.6 1.5 copy-start.28
  163.6 1.5 copy-start.29
  163.7 1.6 copy-start.30
  163.7 1.6 copy-start.31
  163.7 1.6 copy-start.27
  163.7 253.0 %all-gather.9.cloned.1.call-start = ((), (), s32[]{:S(2)}) async-start(), calls=%async_computation.5 | async-start | bytes 5242880 | tf_op jit(solution)/shard_map/all_gather | solution.py:617
  164.9 339.0 %reduce-scatter.6.cloned.1.call-start = ((), (), s32[]{:S(2)}) async-start(), calls=%async_computation.8 | async-start | bytes 2621440 | tf_op jit(solution)/shard_map/reduce_scatter | solution.py:560
  184.3 5.8 copy-start
  190.1 2.5 copy-start.32
  192.9 26.1 %copy-start.22 = (s32[2048]{0:T(1024)}, s32[2048]{0:T(1024)S(1)}, u32[]{:S(2)}) copy-start(s32[2048]{0:T(1024)S(1)} %convert_reduce_fusion.5) | copy-start | bytes 24580
  252.4 7.3 copy-start.8
  252.4 7.3 copy-start.9
  259.7 5.2 copy-start.5
  318.7 7.5 copy-start.10
  326.2 385.0 %reduce-scatter.8.cloned.1.call-start = ((), (), s32[]{:S(2)}) async-start(), calls=%async_computation.9 | async-start | bytes 5242880 | tf_op jit(solution)/shard_map/reduce_scatter | solution.py:757
  344.6 369.4 %reduce-scatter.4.cloned.1.call-start = ((), (), s32[]{:S(2)}) async-start(), calls=%async_computation.7 | async-start | bytes 9175040 | tf_op jit(solution)/shard_map/reduce_scatter | solution.py:752
  389.3 3.5 copy-start.2
  389.4 5.5 copy-start.1
  399.1 5.4 copy-start.7
  416.7 17.9 %copy-start.12 = (bf16[2048,4,64]{0,2,1:T(8,128)(2,1)S(1)}, bf16[2048,4,64]{0,2,1:T(8,128)(2,1)}, u32[]{:S(2)}) copy-start(bf16[2048,4,64]{0,2,1:T(8,128)(2,1)} %copy.121) | copy-start | bytes 3145732
  416.7 17.9 %copy-start.15 = (bf16[2048,4,64]{0,2,1:T(8,128)(2,1)S(1)}, bf16[2048,4,64]{0,2,1:T(8,128)(2,1)}, u32[]{:S(2)}) copy-start(bf16[2048,4,64]{0,2,1:T(8,128)(2,1)} %copy.122) | copy-start | bytes 3145732
  463.7 0.7 copy-start.24
  463.8 0.8 copy-start.23
  463.8 1.2 copy-start.3
  465.7 16.9 %copy-start.13 = (bf16[2048,4,64]{0,2,1:T(8,128)(2,1)S(1)}, bf16[2048,4,64]{0,2,1:T(8,128)(2,1)}, u32[]{:S(2)}) copy-start(bf16[2048,4,64]{0,2,1:T(8,128)(2,1)} %copy.121) | copy-start | bytes 3145732
  465.7 16.8 %copy-start.16 = (bf16[2048,4,64]{0,2,1:T(8,128)(2,1)S(1)}, bf16[2048,4,64]{0,2,1:T(8,128)(2,1)}, u32[]{:S(2)}) copy-start(bf16[2048,4,64]{0,2,1:T(8,128)(2,1)} %copy.122) | copy-start | bytes 3145732
  465.7 16.8 %copy-start.33 = (bf16[2048,1024]{0,1:T(8,128)(2,1)S(1)}, bf16[2048,1024]{0,1:T(8,128)(2,1)}, u32[]{:S(2)}) copy-start(bf16[2048,1024]{0,1:T(8,128)(2,1)} %get-tuple-element.73) | copy-start | bytes 12582916
  482.5 26.9 %copy-start.11 = (bf16[2048,4,64]{0,2,1:T(8,128)(2,1)S(1)}, bf16[2048,4,64]{0,2,1:T(8,128)(2,1)}, u32[]{:S(2)}) copy-start(bf16[2048,4,64]{0,2,1:T(8,128)(2,1)} %copy-done.10) | copy-start | bytes 3145732
  503.9 19.9 %copy-start.14 = (bf16[2048,4,64]{0,2,1:T(8,128)(2,1)S(1)}, bf16[2048,4,64]{0,2,1:T(8,128)(2,1)}, u32[]{:S(2)}) copy-start(bf16[2048,4,64]{0,2,1:T(8,128)(2,1)} %copy.121) | copy-start | bytes 3145732
  503.9 19.9 %copy-start.17 = (bf16[2048,4,64]{0,2,1:T(8,128)(2,1)S(1)}, bf16[2048,4,64]{0,2,1:T(8,128)(2,1)}, u32[]{:S(2)}) copy-start(bf16[2048,4,64]{0,2,1:T(8,128)(2,1)} %copy.122) | copy-start | bytes 3145732
  503.9 207.3 %collective-permute-start.1 = (f32[64,2048]{1,0:T(8,128)}, f32[64,2048]{1,0:T(8,128)}, u32[]{:S(2)}, u32[]{:S(2)}) collective-permute-start(f32[64,2048]{1,0:T(8,128)} %reduce-scatter.6.cloned.1.call-done), channel_id=1, source_target_pairs={{0,0},{8,1},{16,2},{24,3},{1,4},{9,5},{17,6},{25,7},{2,8},{10,9},{... | collective-permute-start | bytes 1572872 | tf_op jit(solution)/shard_map/ppermute | solution.py:562
  760.2 2.6 copy-start.4
  760.2 3.6 copy-start.6
  760.2 3.6 copy-start.18
  801.1 3.5 copy-start.25
Sparse Core Ops, SparseCore 0:
  53.5 63.1 all-gather.4
  118.3 16.7 all-gather.6
  163.8 126.5 all-gather.10
  292.4 32.6 all-gather.8
  327.5 32.7 reduce-scatter.5
  362.8 44.5 reduce-scatter.7
  463.9 75.5 reduce-scatter.3

commit v23 on v22

--- a/solution.py
+++ b/solution.py
@@ -151,7 +151,7 @@
     )
 
 
-def attention_forward(q, k, v, seg, block=1024):
+def attention_forward(q, k, v, seg, block=2048):
     heads, total, dim = q.shape
     count = total // block
     scale = 1.0 / math.sqrt(dim)
@@ -240,7 +240,7 @@
         dv_ref[0] = dv_sc[...].T
 
 
-def attention_backward(q, k, v, do, lse, delta, seg, block=1024):
+def attention_backward(q, k, v, do, lse, delta, seg, block=2048):
     heads, total, dim = q.shape
     count = total // block
     scale = 1.0 / math.sqrt(dim)

time: 817 us -> 826 us (1.011)
  Pallas kernels: 491 us -> 501 us
    pallas_call x1, Pallas kernels: 44.7 us -> 54.5 us  [attention_backward(): pl.pallas_call(functools.partial(_bwd_kernel, tq=block, tk=block, scale=s...]
  transfers between devices with their start and end apart: 9 -> 9, of which waited for: 0 -> 0; matrix products, arithmetic and copies ran while one was open for 32% -> 32% of each run, Pallas kernels for 48% -> 49%
where the time goes in v23:
time: 826 us; the launch traced here: 821 us
  Pallas kernels  501 us (61%)
  matrix products  152 us (18%)
  local copies, waits for them, and re-layouts  81.1 us (10%)
  other arithmetic  65.6 us (8%)
  between operations  15.2 us (2%)
    pallas_call x2, Pallas kernels, ring_reduce_scatter(): pl.pallas_call(functools.partial(_scatter_kernel, ring=ring, rows=rows, p...  186 us
    pallas_call x6, Pallas kernels, exchange(): pl.pallas_call(functools.partial(_exchange_kernel, group=group), out_shap...  116 us
    pallas_call x1, Pallas kernels, ring_all_gather(): pl.pallas_call(functools.partial(_gather_kernel, ring=ring, rows=rows), o...  109 us
    pallas_call x1, Pallas kernels, attention_backward(): pl.pallas_call(functools.partial(_bwd_kernel, tq=block, tk=block, scale=s...  54.5 us
    pallas_call x1, Pallas kernels, attention_forward(): pl.pallas_call(functools.partial(_fwd_kernel, tq=block, tk=block, scale=s...  35.1 us
    unnamed x84, local copies, waits for them, and re-layouts  31.4 us
    dot_general x1, matrix products, head_plan(): jnp.einsum('td,tc->dc', hidden_group, d_both, preferred_element_type=jnp....  29.1 us
    dot_general x1, matrix products, head_plan(): jnp.dot(hidden_group, cols, preferred_element_type=jnp.float32)  23.2 us
  transfers between devices with their start and end apart: 9, of which 0 were waited for; matrix products, arithmetic and copies ran while one was open for 32% of the time, Pallas kernels for 49%

profile of v23, /device:TPU:0, one launch (start us, length us, event | category | flops | bytes accessed | tf_op | source)
XLA Modules:
  0.0 821.3 jit_solution(2493205591870310044)
XLA Ops:
  7.2 1.7 convert_element_type.177
  10.4 1.5 convert_element_type.176
  14.8 38.6 %shard_map.256 = bf16[8,64,1792]{2,1,0:T(8,128)(2,1)} custom-call(bf16[8,64,1792]{2,1,0:T(8,128)(2,1)} %pad_maximum_fusion.3.x_ref), custom_call_target="tpu_custom_call" | custom-call | tf_op jit(solution)/shard_map/pallas_call | solution.py:531
  55.0 108.6 %shard_map.257 = bf16[2048,2048]{1,0:T(8,128)(2,1)} custom-call(bf16[256,2048]{1,0:T(8,128)(2,1)} %x_ref), custom_call_target="tpu_custom_call" | custom-call | tf_op jit(solution)/shard_map/pallas_call | solution.py:395
  166.0 5.0 shard_map.258
  171.0 1.4 broadcast_in_dim.34.x_ref
  172.4 10.0 %shard_map.259 = bf16[8,4,16,128]{3,2,1,0:T(8,128)(2,1)} custom-call(bf16[8,4,16,128]{3,2,1,0:T(8,128)(2,1)} %broadcast_in_dim.34.x_ref), custom_call_target="tpu_custom_call" | custom-call | tf_op jit(solution)/shard_map/pallas_call | solution.py:531
  184.3 4.7 convert_reduce_fusion
  190.2 2.3 fusion.2
  195.8 23.2 %convolution_add_fusion = f32[2048,1792]{0,1:T(8,128)} fusion(bf16[2048,1792]{1,0:T(8,128)(2,1)} %all-gather.5.cloned.1.call-done, f32[1792]{0:T(1024)S(1)} %maximum_convert_fusion, bf16[2048,2048]{1,0:T(8,128)(2,1)} %shard_map.257, f32[2048]{0:T(1024)S(1)} %reshape.300, f32[2048]{0:T(1024)S(1)} %reshape.299, f32[2048]{0:T(1024)S(1)} %add_rsqrt_fusion, ...), kind=kOutput, calls=%fused_computation.10 | convolution fusion | flops 15061221376 | bytes 30448640 | tf_op jit(solution)/shard_map/dot_general | solution.py:692
  219.0 1.7 slice.195
  220.7 3.9 fusion.34
  226.5 3.5 copy.129
  230.1 3.5 copy.130
  233.6 2.1 slice.196
  235.7 2.3 fusion.35
  238.0 3.7 copy.132
  241.6 3.6 copy.133
  245.2 3.0 copy.131
  248.2 2.6 copy.134
  250.8 1.8 copy.114
  252.6 7.3 subtract_convert_fusion.2
  259.9 5.2 maximum_bitcast_fusion
  265.1 2.0 maximum_maximum_fusion.v_ref
  267.1 35.1 %shard_map.260 = (f32[4,2048,64]{2,1,0:T(8,128)}, f32[4,2048,1]{2,1,0:T(8,128)}) custom-call(s32[1]{0:T(128)} %constant.55.clone.qi_ref.kj_ref, s32[1]{0:T(128)} %constant.55.clone.qi_ref.kj_ref, bf16[4,2048,64]{2,1,0:T(8,128)(2,1)} %get-tuple-element.74.q_ref, bf16[4,2048,64]{2,1,0:T(8,128)(2,1)} %get-tuple-element.75.k_ref, ...), custom_call_target="tpu_custom_call" | custom-call | flops 2147483648 | bytes 5242880 | tf_op jit(solution)/shard_map/pallas_call | solution.py:168
  302.2 6.0 convolution_convert_fusion.2
  308.3 1.8 copy.117
  310.1 6.8 multiply_reduce_fusion
  316.9 1.9 copy.116
  318.8 7.5 fusion.38
  326.3 2.8 copy.118.delta_ref
  329.1 15.6 %convolution_convert_fusion.1 = bf16[1024,2048]{1,0:T(8,128)(2,1)} fusion(bf16[2048,2048]{1,0:T(8,128)(2,1)} %all-gather.11.cloned.1.call-done, f32[2048,1792]{0,1:T(8,128)} %convolution_add_fusion), kind=kOutput, calls=%fused_computation.35 | convolution fusion | flops 8610906112 | bytes 20971520 | tf_op jit(solution)/shard_map/tf,td->fd/dot_general | solution.py:720
  344.7 54.5 %shard_map.262 = (f32[4,2048,64]{2,1,0:T(8,128)}, f32[4,2048,64]{2,1,0:T(8,128)}, f32[4,2048,64]{2,1,0:T(8,128)}) custom-call(s32[1]{0:T(128)} %constant.55.clone.qi_ref.kj_ref, s32[1]{0:T(128)} %constant.55.clone.qi_ref.kj_ref, bf16[4,2048,64]{2,1,0:T(8,128)(2,1)} %get-tuple-element.74.q_ref, bf16[4,2048,64]{2,1,0:T(8,128)(2,1)} %get-tuple-element.75.k_ref, ...), custom_call_target="tpu_custom_call" | custom-call | flops 5368709120 | bytes 12582912 | tf_op jit(solution)/shard_map/pallas_call | solution.py:258
  399.2 2.9 slice.194
  402.8 1.9 slice.193
  404.7 4.3 add_convert_fusion.1
  409.0 3.2 pad_maximum_fusion.1
  412.2 1.9 copy.120
  414.1 5.4 pad_maximum_fusion.2
  419.6 2.7 copy.121
  422.3 2.5 convert_bitcast_fusion
  424.7 1.6 copy.122
  426.3 17.9 %convert_reduce_fusion.1 = (f32[1024]{0:T(1024)S(1)}, bf16[2048,1024]{0,1:T(8,128)(2,1)}) fusion(f32[2048,1792]{0,1:T(8,128)} %convolution_add_fusion, bf16[2048,2048]{1,0:T(8,128)(2,1)} %all-gather.11.cloned.1.call-done, bf16[1024,2048]{1,0:T(8,128)(2,1)} %all-gather.9.cloned.1.call-done), kind=kOutput, calls=%fused_computation.19 | convolution fusion | flops 8633973760 | bytes 25169920 | tf_op jit(solution)/shard_map/td,fd->tf/dot_general | solution.py:721
  444.3 29.1 %convolution_convert_fusion = bf16[2048,1792]{1,0:T(8,128)(2,1)} fusion(bf16[2048,1024]{0,1:T(8,128)(2,1)} %get-tuple-element.73, bf16[2048,256]{0,1:T(8,128)(2,1)S(1)} %bitcast.120, bf16[2048,256]{0,1:T(8,128)(2,1)S(1)} %bitcast.117, bf16[2048,256]{0,1:T(8,128)(2,1)S(1)} %bitcast.114, bf16[2048,2048]{1,0:T(8,128)(2,1)} %shard_map.257, ...), kind=kOutput, calls=%fused_computation.21 | convolution fusion | flops 15090581504 | bytes 23101440 | tf_op jit(solution)/shard_map/td,tc->dc/dot_general | solution.py:749
  475.4 16.8 %fusion.31 = f32[2048,2048]{1,0:T(8,128)} fusion(bf16[1024,2048]{1,0:T(8,128)(2,1)} %all-gather.9.cloned.1.call-done, f32[2048,1792]{0,1:T(8,128)} %convolution_add_fusion), kind=kOutput, calls=%fused_computation.108 | convolution fusion | flops 8608808960 | bytes 29360128 | tf_op jit(solution)/shard_map/dot_general | solution.py:711
  492.2 21.4 %fusion.27.p_ref = f32[2048,2048]{1,0:T(8,128)} fusion(bf16[2048,1792]{1,0:T(8,128)(2,1)} %all-gather.5.cloned.1.call-done, bf16[2048,1024]{0,1:T(8,128)(2,1)S(1)} %copy-done.33, bf16[2048,256]{0,1:T(8,128)(2,1)S(1)} %bitcast.121, bf16[2048,256]{0,1:T(8,128)(2,1)S(1)} %bitcast.118, bf16[2048,256]{0,1:T(8,128)(2,1)S(1)} %bitcast.115), kind=kOutput, calls=%fused_computation.66 | convolution fusion | flops 15061745664 | bytes 31457280 | tf_op jit(solution)/shard_map/tc,dc->td/dot_general | solution.py:747
  513.6 5.5 collective-permute-start.1
  519.1 14.4 %convolution_add_fusion.1.p_ref = f32[2048,2048]{1,0:T(8,128)} fusion(f32[2048,2048]{1,0:T(8,128)} %fusion.31, bf16[2048,256]{0,1:T(8,128)(2,1)S(1)} %bitcast.108, bf16[256,2048]{1,0:T(8,128)(2,1)} %all-gather.7.cloned.1.call-done), kind=kOutput, calls=%fused_computation.11 | convolution fusion | flops 2151677952 | bytes 35651584 | tf_op jit(solution)/shard_map/dot_general | solution.py:710
  534.4 98.4 %shard_map.263 = f32[256,2048]{1,0:T(8,128)} custom-call(f32[2048,2048]{1,0:T(8,128)} %fusion.27.p_ref), custom_call_target="tpu_custom_call" | custom-call | tf_op jit(solution)/shard_map/pallas_call | solution.py:466
  632.8 88.1 %shard_map.261 = f32[256,2048]{1,0:T(8,128)} custom-call(f32[2048,2048]{1,0:T(8,128)} %convolution_add_fusion.1.p_ref), custom_call_target="tpu_custom_call" | custom-call | tf_op jit(solution)/shard_map/pallas_call | solution.py:466
  721.0 2.8 convert_element_type.223
  723.8 32.4 %shard_map.264 = bf16[8,64,1792]{2,1,0:T(8,128)(2,1)} custom-call(bf16[8,64,1792]{2,1,0:T(8,128)(2,1)} %bitcast.131), custom_call_target="tpu_custom_call" | custom-call | tf_op jit(solution)/shard_map/pallas_call | solution.py:531
  756.2 1.5 slice_convert_fusion.5
  757.7 2.4 slice_convert_fusion.6
  760.1 2.0 reshape.306
  762.1 2.8 copy.125
  764.9 2.5 copy.140
  767.4 2.6 reshape.305
  771.0 1.6 copy.139
  773.7 3.0 convert_reduce_fusion.4
  777.8 19.7 %shard_map.265 = f32[8,4,16,128]{3,2,1,0:T(8,128)} custom-call(f32[8,4,16,128]{3,2,1,0:T(8,128)} %copy_bitcast_fusion.3.x_ref), custom_call_target="tpu_custom_call" | custom-call | tf_op jit(solution)/shard_map/pallas_call | solution.py:531
  797.5 1.6 reduce_sum.158.x_ref
  799.1 10.3 %shard_map.266 = f32[4,16,128]{2,1,0:T(8,128)} custom-call(f32[4,16,128]{2,1,0:T(8,128)} %reduce_sum.158.x_ref), custom_call_target="tpu_custom_call" | custom-call | tf_op jit(solution)/shard_map/pallas_call | solution.py:531
  812.3 1.9 copy.157
  (169 shorter events, 25.8 us)
Async XLA Ops:
  7.2 188.6 %all-gather.5.cloned.1.call-start = ((), (), s32[]{:S(2)}) async-start(), calls=%async_computation.3 | async-start | bytes 9175040 | tf_op jit(solution)/shard_map/all_gather | solution.py:616
  13.4 40.1 %copy-start.20 = (f32[64,2048]{1,0:T(8,128)S(1)}, f32[64,2048]{1,0:T(8,128)}, u32[]{:S(2)}) copy-start(f32[64,2048]{1,0:T(8,128)} %param.21) | copy-start | bytes 1572868
  53.4 248.8 %all-gather.7.cloned.1.call-start = ((), (), s32[]{:S(2)}) async-start(), calls=%async_computation.4 | async-start | bytes 1310720 | tf_op jit(solution)/shard_map/all_gather | solution.py:554
  53.5 0.7 collective-permute-start
  54.2 0.7 copy-start.21
  54.9 108.8 %copy-start.19 = (f32[256,2048]{1,0:T(8,128)S(1)}, f32[256,2048]{1,0:T(8,128)}, u32[]{:S(2)}) copy-start(f32[256,2048]{1,0:T(8,128)} %param.25) | copy-start | bytes 6291460
  54.9 247.3 %all-gather.11.cloned.1.call-start = ((), (), s32[]{:S(2)}) async-start(), calls=%async_computation.6 | async-start | bytes 9437184 | tf_op jit(solution)/shard_map/all_gather | solution.py:685
  163.6 1.5 copy-start.26
  163.6 1.5 copy-start.28
  163.6 1.5 copy-start.29
  163.7 1.6 copy-start.30
  163.7 1.6 copy-start.31
  163.7 1.6 copy-start.27
  163.7 262.6 %all-gather.9.cloned.1.call-start = ((), (), s32[]{:S(2)}) async-start(), calls=%async_computation.5 | async-start | bytes 5242880 | tf_op jit(solution)/shard_map/all_gather | solution.py:617
  164.9 348.7 %reduce-scatter.6.cloned.1.call-start = ((), (), s32[]{:S(2)}) async-start(), calls=%async_computation.8 | async-start | bytes 2621440 | tf_op jit(solution)/shard_map/reduce_scatter | solution.py:560
  184.3 5.8 copy-start
  190.2 2.5 copy-start.32
  192.9 26.1 %copy-start.22 = (s32[2048]{0:T(1024)}, s32[2048]{0:T(1024)S(1)}, u32[]{:S(2)}) copy-start(s32[2048]{0:T(1024)S(1)} %convert_reduce_fusion.5) | copy-start | bytes 24580
  252.6 7.3 copy-start.8
  252.6 7.3 copy-start.9
  259.9 5.2 copy-start.5
  318.8 7.5 copy-start.10
  326.3 394.7 %reduce-scatter.8.cloned.1.call-start = ((), (), s32[]{:S(2)}) async-start(), calls=%async_computation.9 | async-start | bytes 5242880 | tf_op jit(solution)/shard_map/reduce_scatter | solution.py:757
  344.7 379.1 %reduce-scatter.4.cloned.1.call-start = ((), (), s32[]{:S(2)}) async-start(), calls=%async_computation.7 | async-start | bytes 9175040 | tf_op jit(solution)/shard_map/reduce_scatter | solution.py:752
  399.2 3.5 copy-start.2
  399.2 5.5 copy-start.1
  409.0 5.2 copy-start.7
  426.3 17.9 %copy-start.12 = (bf16[2048,4,64]{0,2,1:T(8,128)(2,1)S(1)}, bf16[2048,4,64]{0,2,1:T(8,128)(2,1)}, u32[]{:S(2)}) copy-start(bf16[2048,4,64]{0,2,1:T(8,128)(2,1)} %copy.121) | copy-start | bytes 3145732
  426.3 17.9 %copy-start.15 = (bf16[2048,4,64]{0,2,1:T(8,128)(2,1)S(1)}, bf16[2048,4,64]{0,2,1:T(8,128)(2,1)}, u32[]{:S(2)}) copy-start(bf16[2048,4,64]{0,2,1:T(8,128)(2,1)} %copy.122) | copy-start | bytes 3145732
  473.4 0.7 copy-start.24
  473.4 0.8 copy-start.23
  473.4 1.2 copy-start.3
  475.3 16.9 %copy-start.13 = (bf16[2048,4,64]{0,2,1:T(8,128)(2,1)S(1)}, bf16[2048,4,64]{0,2,1:T(8,128)(2,1)}, u32[]{:S(2)}) copy-start(bf16[2048,4,64]{0,2,1:T(8,128)(2,1)} %copy.121) | copy-start | bytes 3145732
  475.3 16.8 %copy-start.16 = (bf16[2048,4,64]{0,2,1:T(8,128)(2,1)S(1)}, bf16[2048,4,64]{0,2,1:T(8,128)(2,1)}, u32[]{:S(2)}) copy-start(bf16[2048,4,64]{0,2,1:T(8,128)(2,1)} %copy.122) | copy-start | bytes 3145732
  475.3 16.8 %copy-start.33 = (bf16[2048,1024]{0,1:T(8,128)(2,1)S(1)}, bf16[2048,1024]{0,1:T(8,128)(2,1)}, u32[]{:S(2)}) copy-start(bf16[2048,1024]{0,1:T(8,128)(2,1)} %get-tuple-element.73) | copy-start | bytes 12582916
  492.2 26.9 %copy-start.11 = (bf16[2048,4,64]{0,2,1:T(8,128)(2,1)S(1)}, bf16[2048,4,64]{0,2,1:T(8,128)(2,1)}, u32[]{:S(2)}) copy-start(bf16[2048,4,64]{0,2,1:T(8,128)(2,1)} %copy-done.10) | copy-start | bytes 3145732
  513.6 19.9 %copy-start.14 = (bf16[2048,4,64]{0,2,1:T(8,128)(2,1)S(1)}, bf16[2048,4,64]{0,2,1:T(8,128)(2,1)}, u32[]{:S(2)}) copy-start(bf16[2048,4,64]{0,2,1:T(8,128)(2,1)} %copy.121) | copy-start | bytes 3145732
  513.6 19.9 %copy-start.17 = (bf16[2048,4,64]{0,2,1:T(8,128)(2,1)S(1)}, bf16[2048,4,64]{0,2,1:T(8,128)(2,1)}, u32[]{:S(2)}) copy-start(bf16[2048,4,64]{0,2,1:T(8,128)(2,1)} %copy.122) | copy-start | bytes 3145732
  513.6 207.4 %collective-permute-start.1 = (f32[64,2048]{1,0:T(8,128)}, f32[64,2048]{1,0:T(8,128)}, u32[]{:S(2)}, u32[]{:S(2)}) collective-permute-start(f32[64,2048]{1,0:T(8,128)} %reduce-scatter.6.cloned.1.call-done), channel_id=1, source_target_pairs={{0,0},{8,1},{16,2},{24,3},{1,4},{9,5},{17,6},{25,7},{2,8},{10,9},{... | collective-permute-start | bytes 1572872 | tf_op jit(solution)/shard_map/ppermute | solution.py:562
  770.0 2.6 copy-start.4
  770.0 3.6 copy-start.6
  770.1 3.6 copy-start.18
  810.7 3.5 copy-start.25
Sparse Core Ops, SparseCore 0:
  53.5 63.1 all-gather.4
  118.3 16.7 all-gather.6
  163.8 126.5 all-gather.10
  292.4 32.6 all-gather.8
  327.5 32.8 reduce-scatter.5
  362.9 44.5 reduce-scatter.7
  473.6 75.3 reduce-scatter.3

commit v24 on v16

--- a/solution.py
+++ b/solution.py
@@ -115,7 +115,11 @@
         s = lax.dot_general(q, k, TRANS_B, preferred_element_type=jnp.float32) * scale
         s = jnp.where(_allowed(segq_ref, segk_ref, i, j, tq, tk, causal), s, -jnp.inf)
         m_prev = m_sc[...]
-        m_new = jnp.maximum(m_prev, jnp.max(s, axis=1, keepdims=True))
+        lanes = s.shape[1]
+        folded = s[:, :128]
+        for start in range(128, lanes, 128):
+            folded = jnp.maximum(folded, s[:, start : start + 128])
+        m_new = jnp.maximum(m_prev, jnp.max(folded, axis=1, keepdims=True))
         factor = jnp.exp(m_prev - m_new)
         p = jnp.exp(s - m_new)
         acc_sc[...] = acc_sc[...] * factor + jnp.dot(
@@ -147,7 +151,7 @@
     )
 
 
-def attention_forward(q, k, v, seg, block=512):
+def attention_forward(q, k, v, seg, block=1024):
     heads, total, dim = q.shape
     count = total // block
     scale = 1.0 / math.sqrt(dim)
@@ -236,7 +240,7 @@
         dv_ref[0] = dv_sc[...].T
 
 
-def attention_backward(q, k, v, do, lse, delta, seg, block=512):
+def attention_backward(q, k, v, do, lse, delta, seg, block=1024):
     heads, total, dim = q.shape
     count = total // block
     scale = 1.0 / math.sqrt(dim)

time: 841 us -> 819 us (0.974)
  Pallas kernels: 522 us -> 500 us
    pallas_call x1, Pallas kernels: 48.1 us -> 34.9 us  [attention_forward(): pl.pallas_call(functools.partial(_fwd_kernel, tq=block, tk=block, scale=s...]
    pallas_call x1, Pallas kernels: 53.7 us -> 44.5 us  [attention_backward(): pl.pallas_call(functools.partial(_bwd_kernel, tq=block, tk=block, scale=s...]
  transfers between devices with their start and end apart: 9 -> 9, of which waited for: 0 -> 0; matrix products, arithmetic and copies ran while one was open for 30% -> 31% of each run, Pallas kernels for 50% -> 49%
where the time goes in v24:
time: 819 us; the launch traced here: 814 us
  Pallas kernels  500 us (61%)
  matrix products  166 us (20%)
  other arithmetic  69 us (8%)
  local copies, waits for them, and re-layouts  56.3 us (7%)
  between operations  15.4 us (2%)
    pallas_call x2, Pallas kernels, ring_reduce_scatter(): pl.pallas_call(functools.partial(_scatter_kernel, ring=ring, rows=rows, p...  180 us
    pallas_call x6, Pallas kernels, exchange(): pl.pallas_call(functools.partial(_exchange_kernel, group=group), out_shap...  146 us
    pallas_call x1, Pallas kernels, ring_all_gather(): pl.pallas_call(functools.partial(_gather_kernel, ring=ring, rows=rows), o...  95 us
    pallas_call x1, Pallas kernels, attention_backward(): pl.pallas_call(functools.partial(_bwd_kernel, tq=block, tk=block, scale=s...  44.5 us
    pallas_call x1, Pallas kernels, attention_forward(): pl.pallas_call(functools.partial(_fwd_kernel, tq=block, tk=block, scale=s...  34.9 us
    dot_general x1, matrix products, head_plan(): jnp.einsum('td,tc->dc', hidden_group, d_both, preferred_element_type=jnp....  28.3 us
    dot_general x1, matrix products, head_plan(): jnp.einsum('tc,dc->td', d_both, cols, preferred_element_type=jnp.float32)  22.3 us
    dot_general x1, matrix products, head_plan(): jnp.einsum('td,fd->tf', dy_group, fc2_rows, preferred_element_type=jnp.fl...  20.9 us
  transfers between devices with their start and end apart: 9, of which 0 were waited for; matrix products, arithmetic and copies ran while one was open for 31% of the time, Pallas kernels for 49%

profile of v24, /device:TPU:0, one launch (start us, length us, event | category | flops | bytes accessed | tf_op | source)
XLA Modules:
  0.0 813.8 jit_solution(15139101981849119181)
XLA Ops:
  7.2 1.7 convert_element_type.183
  10.4 1.5 convert_element_type.182
  13.4 1.4 pad_maximum_fusion.5.x_ref
  14.7 38.6 %shard_map.256 = bf16[8,64,1792]{2,1,0:T(8,128)(2,1)} custom-call(bf16[8,64,1792]{2,1,0:T(8,128)(2,1)} %pad_maximum_fusion.5.x_ref), custom_call_target="tpu_custom_call" | custom-call | tf_op jit(solution)/shard_map/pallas_call | solution.py:531
  53.5 95.0 %shard_map.257 = bf16[2048,2048]{1,0:T(8,128)(2,1)} custom-call(bf16[256,2048]{1,0:T(8,128)(2,1)} %x_ref), custom_call_target="tpu_custom_call" | custom-call | tf_op jit(solution)/shard_map/pallas_call | solution.py:395
  150.1 1.1 convert_element_type.206
  152.4 19.1 %shard_map.258 = bf16[4,16,128]{2,1,0:T(8,128)(2,1)} custom-call(bf16[4,16,128]{2,1,0:T(8,128)(2,1)} %broadcast_in_dim.33.x_ref), custom_call_target="tpu_custom_call" | custom-call | tf_op jit(solution)/shard_map/pallas_call | solution.py:531
  171.5 1.4 broadcast_in_dim.34.x_ref
  172.9 25.7 %shard_map.259 = bf16[8,4,16,128]{3,2,1,0:T(8,128)(2,1)} custom-call(bf16[8,4,16,128]{3,2,1,0:T(8,128)(2,1)} %broadcast_in_dim.34.x_ref), custom_call_target="tpu_custom_call" | custom-call | tf_op jit(solution)/shard_map/pallas_call | solution.py:531
  200.3 4.7 convert_reduce_fusion
  205.0 1.1 copy-done
  206.1 2.3 fusion.2
  209.3 1.3 copy.102.segq_ref
  210.7 5.5 multiply_cosine_fusion
  216.2 1.9 slice-done
  218.1 3.0 copy.99
  221.1 17.2 %fusion.52 = (bf16[12,2048,64]{2,1,0:T(8,128)(2,1)S(1)}, f32[12,2048,64]{2,1,0:T(8,128)S(1)}) fusion(f32[12,64]{1,0:T(8,128)S(1)} %reshape.350, bf16[2048,12,64]{0,2,1:T(8,128)(2,1)} %bitcast.122, f32[2048]{0:T(1024)S(1)} %reshape.349, f32[2048]{0:T(1024)S(1)} %reshape.348, f32[2048]{0:T(1024)S(1)} %add_rsqrt_fusion, f32[2048]{0:T(1024)S(1)} %broadcast_multiply_fusion, ...), kind=kOutput, calls=%fused_computation.116 | convolution fusion | flops 6470762496 | bytes 21007360 | tf_op jit(solution)/shard_map/td,dhe->hte/dot_general | solution.py:696
  238.5 1.2 fusion.50
  240.8 5.0 subtract_convert_fusion.2
  245.8 7.0 pad_maximum_fusion.1
  252.9 2.0 maximum_maximum_fusion.v_ref
  254.8 34.9 %shard_map.260 = (f32[4,2048,64]{2,1,0:T(8,128)}, f32[4,2048,1]{2,1,0:T(8,128)}) custom-call(s32[3]{0:T(128)} %constant.57.clone.qi_ref, s32[3]{0:T(128)} %constant.58.clone.kj_ref, bf16[4,2048,64]{2,1,0:T(8,128)(2,1)} %get-tuple-element.68.q_ref, bf16[4,2048,64]{2,1,0:T(8,128)(2,1)} %get-tuple-element.69.k_ref, ...), custom_call_target="tpu_custom_call" | custom-call | flops 2147483648 | bytes 5242880 | tf_op jit(solution)/shard_map/pallas_call | solution.py:168
  289.7 8.4 %fusion.13 = f32[4,64,2048]{2,1,0:T(8,128)} fusion(bf16[2048,2048]{1,0:T(8,128)(2,1)} %all-gather.11.cloned.1.call-done, f32[4,2048,64]{2,1,0:T(8,128)} %get-tuple-element.27), kind=kOutput, calls=%fused_computation.19 | convolution fusion | flops 2148007936 | bytes 12582912 | tf_op jit(solution)/shard_map/hte,td->hed/dot_general | solution.py:728
  298.2 14.7 %fusion.21 = f32[2048,1024]{1,0:T(8,128)} fusion(bf16[2048,1792]{1,0:T(8,128)(2,1)} %all-gather.5.cloned.1.call-done, bf16[2048,2048]{1,0:T(8,128)(2,1)} %shard_map.257, f32[2048]{0:T(1024)S(1)} %reshape.349, f32[2048]{0:T(1024)S(1)} %reshape.348, f32[2048]{0:T(1024)S(1)} %add_rsqrt_fusion, f32[2048]{0:T(1024)S(1)} %broadcast_multiply_fusion), kind=kOutput, calls=%fused_computation.32 | convolution fusion | flops 8615100416 | bytes 21004288 | tf_op jit(solution)/shard_map/dot_general | solution.py:699
  312.9 6.0 fusion.23
  318.9 1.8 copy.104
  320.7 16.5 %convolution_convert_fusion.1 = bf16[1024,2048]{1,0:T(8,128)(2,1)} fusion(bf16[2048,2048]{1,0:T(8,128)(2,1)} %all-gather.11.cloned.1.call-done, f32[2048,1024]{1,0:T(8,128)} %fusion.21, f32[1024]{0:T(1024)S(1)} %bitcast.137), kind=kOutput, calls=%fused_computation.43 | convolution fusion | flops 8613003264 | bytes 20975616 | tf_op jit(solution)/shard_map/tf,td->fd/dot_general | solution.py:724
  337.3 4.0 multiply_reduce_fusion
  341.3 2.9 copy.105.delta_ref
  344.2 44.5 %shard_map.262 = (f32[4,2048,64]{2,1,0:T(8,128)}, f32[4,2048,64]{2,1,0:T(8,128)}, f32[4,2048,64]{2,1,0:T(8,128)}) custom-call(s32[3]{0:T(128)} %constant.57.clone.qi_ref, s32[3]{0:T(128)} %constant.58.clone.kj_ref, bf16[4,2048,64]{2,1,0:T(8,128)(2,1)} %get-tuple-element.68.q_ref, bf16[4,2048,64]{2,1,0:T(8,128)(2,1)} %get-tuple-element.69.k_ref, ...), custom_call_target="tpu_custom_call" | custom-call | flops 5368709120 | bytes 12582912 | tf_op jit(solution)/shard_map/pallas_call | solution.py:258
  388.8 3.1 slice.191
  392.5 1.9 slice.190
  394.4 4.3 add_convert_fusion.1
  398.7 3.2 pad_maximum_fusion.3
  401.9 2.3 copy.107
  404.2 6.1 pad_maximum_fusion.4
  410.3 1.9 copy.108
  412.2 3.8 convert_bitcast_fusion
  416.0 1.9 copy.109
  417.9 1.3 copy.110
  419.2 1.3 copy.111
  420.5 1.3 copy.112
  421.8 20.9 %convert_reduce_fusion.1 = (f32[1024]{0:T(1024)S(1)}, bf16[2048,1024]{1,0:T(8,128)(2,1)}) fusion(f32[2048,1024]{1,0:T(8,128)} %fusion.21, f32[1024]{0:T(1024)S(1)} %bitcast.138, bf16[2048,2048]{1,0:T(8,128)(2,1)} %all-gather.11.cloned.1.call-done, bf16[1024,2048]{1,0:T(8,128)(2,1)} %all-gather.9.cloned.1.call-done), kind=kOutput, calls=%fused_computation.25 | convolution fusion | flops 8636070912 | bytes 25174016 | tf_op jit(solution)/shard_map/td,fd->tf/dot_general | solution.py:725
  442.8 28.3 %convolution_convert_fusion = bf16[2048,1792]{1,0:T(8,128)(2,1)} fusion(bf16[2048,1024]{1,0:T(8,128)(2,1)} %get-tuple-element.67, bf16[2048,256]{1,0:T(8,128)(2,1)} %copy.112, bf16[2048,256]{1,0:T(8,128)(2,1)} %copy.111, bf16[2048,256]{1,0:T(8,128)(2,1)} %copy.110, bf16[2048,2048]{1,0:T(8,128)(2,1)} %shard_map.257, f32[2048]{0:T(1024)S(1)} %reshape.349, ...), kind=kOutput, calls=%fused_computation.27 | convolution fusion | flops 15090581504 | bytes 23101440 | tf_op jit(solution)/shard_map/td,tc->dc/dot_general | solution.py:749
  473.0 16.9 %fusion.46 = f32[2048,2048]{1,0:T(8,128)} fusion(bf16[1024,2048]{1,0:T(8,128)(2,1)} %all-gather.9.cloned.1.call-done, f32[2048,1024]{1,0:T(8,128)} %fusion.21, f32[1024]{0:T(1024)S(1)} %bitcast.139), kind=kOutput, calls=%fused_computation.113 | convolution fusion | flops 8610906112 | bytes 29364224 | tf_op jit(solution)/shard_map/dot_general | solution.py:715
  489.9 14.3 %bitcast_add_fusion.p_ref = f32[2048,2048]{1,0:T(8,128)} fusion(f32[2048,2048]{1,0:T(8,128)} %fusion.46, bf16[4,64,2048]{2,1,0:T(8,128)(2,1)S(1)} %bitcast.128, f32[4,2048,64]{2,1,0:T(8,128)S(1)} %copy-done.1), kind=kOutput, calls=%fused_computation.8 | convolution fusion | flops 2152202240 | bytes 36700160 | tf_op jit(solution)/shard_map/hte,hed->td/dot_general | solution.py:714
  504.2 90.0 %shard_map.261 = f32[256,2048]{1,0:T(8,128)} custom-call(f32[2048,2048]{1,0:T(8,128)} %bitcast_add_fusion.p_ref), custom_call_target="tpu_custom_call" | custom-call | tf_op jit(solution)/shard_map/pallas_call | solution.py:466
  594.3 5.5 collective-permute-start.1
  599.8 22.3 %fusion.40.p_ref = f32[2048,2048]{1,0:T(8,128)} fusion(bf16[2048,1792]{1,0:T(8,128)(2,1)} %all-gather.5.cloned.1.call-done, bf16[2048,1024]{1,0:T(8,128)(2,1)} %get-tuple-element.67, bf16[2048,256]{1,0:T(8,128)(2,1)} %copy.112, bf16[2048,256]{1,0:T(8,128)(2,1)} %copy.111, bf16[2048,256]{1,0:T(8,128)(2,1)} %copy.110), kind=kOutput, calls=%fused_computation.74 | convolution fusion | flops 15061745664 | bytes 31457280 | tf_op jit(solution)/shard_map/tc,dc->td/dot_general | solution.py:747
  622.9 90.2 %shard_map.263 = f32[256,2048]{1,0:T(8,128)} custom-call(f32[2048,2048]{1,0:T(8,128)} %fusion.40.p_ref), custom_call_target="tpu_custom_call" | custom-call | tf_op jit(solution)/shard_map/pallas_call | solution.py:466
  713.2 2.8 convert_element_type.230
  716.0 34.2 %shard_map.264 = bf16[8,64,1792]{2,1,0:T(8,128)(2,1)} custom-call(bf16[8,64,1792]{2,1,0:T(8,128)(2,1)} %bitcast.125), custom_call_target="tpu_custom_call" | custom-call | tf_op jit(solution)/shard_map/pallas_call | solution.py:531
  750.2 1.5 slice_convert_fusion.2
  751.6 2.4 slice_convert_fusion.3
  754.1 2.0 reshape.357
  756.0 2.8 copy.114
  758.8 2.5 copy.124
  761.4 2.6 reshape.356
  764.9 1.6 copy.123
  767.6 3.0 convert_reduce_fusion.4
  771.7 19.7 %shard_map.265 = f32[8,4,16,128]{3,2,1,0:T(8,128)} custom-call(f32[8,4,16,128]{3,2,1,0:T(8,128)} %copy_bitcast_fusion.3.x_ref), custom_call_target="tpu_custom_call" | custom-call | tf_op jit(solution)/shard_map/pallas_call | solution.py:531
  791.5 1.6 reduce_sum.158.x_ref
  793.1 8.5 %shard_map.266 = f32[4,16,128]{2,1,0:T(8,128)} custom-call(f32[4,16,128]{2,1,0:T(8,128)} %reduce_sum.158.x_ref), custom_call_target="tpu_custom_call" | custom-call | tf_op jit(solution)/shard_map/pallas_call | solution.py:531
  804.6 1.9 copy.141
  (148 shorter events, 18.9 us)
Async XLA Ops:
  7.2 209.0 %all-gather.5.cloned.1.call-start = ((), (), s32[]{:S(2)}) async-start(), calls=%async_computation.3 | async-start | bytes 9175040 | tf_op jit(solution)/shard_map/all_gather | solution.py:616
  53.4 95.2 %copy-start.15 = (f32[64,2048]{1,0:T(8,128)S(1)}, f32[64,2048]{1,0:T(8,128)}, u32[]{:S(2)}) copy-start(f32[64,2048]{1,0:T(8,128)} %param.21) | copy-start | bytes 1572868
  53.4 96.7 %copy-start.13 = (f32[256,2048]{1,0:T(8,128)S(1)}, f32[256,2048]{1,0:T(8,128)}, u32[]{:S(2)}) copy-start(f32[256,2048]{1,0:T(8,128)} %param.25) | copy-start | bytes 6291460
  53.4 236.3 %all-gather.11.cloned.1.call-start = ((), (), s32[]{:S(2)}) async-start(), calls=%async_computation.6 | async-start | bytes 9437184 | tf_op jit(solution)/shard_map/all_gather | solution.py:685
  148.4 3.1 copy-start.21
  148.5 3.1 copy-start.23
  148.5 3.1 copy-start.24
  148.5 3.1 copy-start.25
  148.5 3.1 copy-start.26
  148.5 3.1 copy-start.22
  148.5 164.4 %all-gather.7.cloned.1.call-start = ((), (), s32[]{:S(2)}) async-start(), calls=%async_computation.4 | async-start | bytes 1310720 | tf_op jit(solution)/shard_map/all_gather | solution.py:554
  148.6 0.7 collective-permute-start
  149.3 0.7 copy-start.16
  150.1 271.8 %all-gather.9.cloned.1.call-start = ((), (), s32[]{:S(2)}) async-start(), calls=%async_computation.5 | async-start | bytes 5242880 | tf_op jit(solution)/shard_map/all_gather | solution.py:617
  151.3 443.0 %reduce-scatter.6.cloned.1.call-start = ((), (), s32[]{:S(2)}) async-start(), calls=%async_computation.8 | async-start | bytes 2621440 | tf_op jit(solution)/shard_map/reduce_scatter | solution.py:560
  200.3 5.8 copy-start
  206.1 2.7 copy-start.27
  209.1 7.2 copy-start.17
  216.2 1.9 slice-start
  238.5 14.4 %copy-start.10 = (bf16[4,2048,64]{2,1,0:T(8,128)(2,1)}, bf16[4,2048,64]{2,1,0:T(8,128)(2,1)S(1)}, u32[]{:S(2)}) copy-start(bf16[4,2048,64]{2,1,0:T(8,128)(2,1)S(1)} %slice.148.v_ref) | copy-start | bytes 3145732
  238.5 2.0 copy-start.8
  238.5 2.3 copy-start.9
  298.2 415.0 %reduce-scatter.8.cloned.1.call-start = ((), (), s32[]{:S(2)}) async-start(), calls=%async_computation.9 | async-start | bytes 5242880 | tf_op jit(solution)/shard_map/reduce_scatter | solution.py:757
  337.3 378.7 %reduce-scatter.4.cloned.1.call-start = ((), (), s32[]{:S(2)}) async-start(), calls=%async_computation.7 | async-start | bytes 9175040 | tf_op jit(solution)/shard_map/reduce_scatter | solution.py:752
  388.8 3.7 copy-start.3
  388.8 5.6 copy-start.2
  417.9 24.9 %copy-start.6 = (bf16[2048,4,64]{0,2,1:T(8,128)(2,1)}, bf16[2048,4,64]{0,2,1:T(8,128)(2,1)S(1)}, u32[]{:S(2)}) copy-start(bf16[2048,4,64]{0,2,1:T(8,128)(2,1)S(1)} %copy.109) | copy-start | bytes 3145732
  471.1 0.7 copy-start.19
  471.1 0.8 copy-start.18
  471.1 1.3 copy-start.4
  473.0 16.9 %copy-start.1 = (f32[4,2048,64]{2,1,0:T(8,128)S(1)}, f32[4,2048,64]{2,1,0:T(8,128)}, u32[]{:S(2)}) copy-start(f32[4,2048,64]{2,1,0:T(8,128)} %get-tuple-element.27) | copy-start | bytes 6291460
  473.0 16.9 %copy-start.14 = (bf16[256,2048]{1,0:T(8,128)(2,1)S(1)}, bf16[256,2048]{1,0:T(8,128)(2,1)}, u32[]{:S(2)}) copy-start(bf16[256,2048]{1,0:T(8,128)(2,1)} %all-gather.7.cloned.1.call-done) | copy-start | bytes 3145732
  594.3 27.9 %copy-start.7 = (bf16[2048,4,64]{0,2,1:T(8,128)(2,1)S(1)}, bf16[2048,4,64]{0,2,1:T(8,128)(2,1)}, u32[]{:S(2)}) copy-start(bf16[2048,4,64]{0,2,1:T(8,128)(2,1)} %copy-done.6) | copy-start | bytes 3145732
  594.3 118.9 %collective-permute-start.1 = (f32[64,2048]{1,0:T(8,128)}, f32[64,2048]{1,0:T(8,128)}, u32[]{:S(2)}, u32[]{:S(2)}) collective-permute-start(f32[64,2048]{1,0:T(8,128)} %reduce-scatter.6.cloned.1.call-done), channel_id=1, source_target_pairs={{0,0},{8,1},{16,2},{24,3},{1,4},{9,5},{17,6},{25,7},{2,8},{10,9},{... | collective-permute-start | bytes 1572872 | tf_op jit(solution)/shard_map/ppermute | solution.py:562
  764.0 2.6 copy-start.5
  764.0 3.6 copy-start.11
  764.0 3.6 copy-start.12
  803.0 3.5 copy-start.20
Sparse Core Ops, SparseCore 0:
  53.5 63.1 all-gather.4
  148.7 131.5 all-gather.10
  282.4 14.9 all-gather.6
  299.3 34.4 all-gather.8
  336.2 31.4 reduce-scatter.5
  370.2 44.5 reduce-scatter.7
  471.3 67.2 reduce-scatter.3

commit v25 on v22

--- a/solution.py
+++ b/solution.py
@@ -345,9 +345,10 @@
     pl.semaphore_wait(barrier, 2)
 
 
-def _gather_kernel(x_ref, y_ref, own_sem, send_sem, recv_sem, *, ring, rows):
+def _gather_kernel(x_ref, y_ref, own_sem, send_sem, recv_sem, *, ring, rows, parts):
     n = ring.size
     half = rows // 2
+    piece = half // parts
     g = lax.axis_index("dp")
     c = lax.axis_index("ctx")
     pos = ring.position(c)
@@ -357,13 +358,13 @@
     own.start()
     _barrier(g, left, right)
 
-    def link(direction, step, origin, source):
-        offset = origin * rows + direction * half
+    def link(direction, step, part, origin, source):
+        offset = origin * rows + direction * half + part * piece
         return pltpu.make_async_remote_copy(
             src_ref=source,
-            dst_ref=y_ref.at[pl.ds(offset, half)],
-            send_sem=send_sem.at[direction, step],
-            recv_sem=recv_sem.at[direction, step],
+            dst_ref=y_ref.at[pl.ds(offset, piece)],
+            send_sem=send_sem.at[direction, step, part],
+            recv_sem=recv_sem.at[direction, step, part],
             device_id=(g, right if direction == 0 else left),
             device_id_type=MESH_ID,
         )
@@ -371,19 +372,23 @@
     sent = []
     for step in range(n - 1):
         origins = (ring.device(pos - step + n), ring.device(pos + step))
-        for direction in (0, 1):
-            origin = origins[direction]
-            if step == 0:
-                source = x_ref.at[pl.ds(direction * half, half)]
-            else:
-                link(direction, step - 1, origin, None if False else y_ref.at[pl.ds(origin * rows + direction * half, half)]).wait_recv()
-                source = y_ref.at[pl.ds(origin * rows + direction * half, half)]
-            copy = link(direction, step, origin, source)
-            copy.start()
-            sent.append(copy)
+        for part in range(parts):
+            for direction in (0, 1):
+                origin = origins[direction]
+                here_rows = y_ref.at[pl.ds(origin * rows + direction * half + part * piece, piece)]
+                if step == 0:
+                    source = x_ref.at[pl.ds(direction * half + part * piece, piece)]
+                else:
+                    link(direction, step - 1, part, origin, here_rows).wait_recv()
+                    source = here_rows
+                copy = link(direction, step, part, origin, source)
+                copy.start()
+                sent.append(copy)
     last = n - 2
-    for direction, origin in ((0, ring.device(pos - last - 1 + n)), (1, ring.device(pos + last + 1))):
-        link(direction, last, origin, y_ref.at[pl.ds(origin * rows + direction * half, half)]).wait_recv()
+    for part in range(parts):
+        for direction, origin in ((0, ring.device(pos - last - 1 + n)), (1, ring.device(pos + last + 1))):
+            rows_at = y_ref.at[pl.ds(origin * rows + direction * half + part * piece, piece)]
+            link(direction, last, part, origin, rows_at).wait_recv()
     for copy in sent:
         copy.wait_send()
     own.wait()
@@ -393,14 +398,14 @@
     rows, cols = x.shape
     n = ring.size
     return pl.pallas_call(
-        functools.partial(_gather_kernel, ring=ring, rows=rows),
+        functools.partial(_gather_kernel, ring=ring, rows=rows, parts=2),
         out_shape=jax.ShapeDtypeStruct((n * rows, cols), x.dtype),
         in_specs=[pl.BlockSpec(memory_space=pl.ANY)],
         out_specs=pl.BlockSpec(memory_space=pl.ANY),
         scratch_shapes=[
             pltpu.SemaphoreType.DMA(()),
-            pltpu.SemaphoreType.DMA((2, n - 1)),
-            pltpu.SemaphoreType.DMA((2, n - 1)),
+            pltpu.SemaphoreType.DMA((2, n - 1, 2)),
+            pltpu.SemaphoreType.DMA((2, n - 1, 2)),
         ],
         compiler_params=pltpu.CompilerParams(collective_id=collective_id, has_side_effects=True),
     )(x)

time: 817 us -> 814 us (level)
  no operation moved by 1% of the time
where the time goes in v25:
time: 814 us; the launch traced here: 809 us
  Pallas kernels  488 us (60%)
  matrix products  152 us (19%)
  local copies, waits for them, and re-layouts  81.6 us (10%)
  other arithmetic  65.5 us (8%)
  between operations  15.2 us (2%)
    pallas_call x2, Pallas kernels, ring_reduce_scatter(): pl.pallas_call(functools.partial(_scatter_kernel, ring=ring, rows=rows, p...  187 us
    pallas_call x6, Pallas kernels, exchange(): pl.pallas_call(functools.partial(_exchange_kernel, group=group), out_shap...  116 us
    pallas_call x1, Pallas kernels, ring_all_gather(): pl.pallas_call(functools.partial(_gather_kernel, ring=ring, rows=rows, pa...  106 us
    pallas_call x1, Pallas kernels, attention_backward(): pl.pallas_call(functools.partial(_bwd_kernel, tq=block, tk=block, scale=s...  44.8 us
    pallas_call x1, Pallas kernels, attention_forward(): pl.pallas_call(functools.partial(_fwd_kernel, tq=block, tk=block, scale=s...  34.9 us
    unnamed x84, local copies, waits for them, and re-layouts  31.1 us
    dot_general x1, matrix products, head_plan(): jnp.einsum('td,tc->dc', hidden_group, d_both, preferred_element_type=jnp....  29.1 us
    dot_general x1, matrix products, head_plan(): jnp.dot(hidden_group, cols, preferred_element_type=jnp.float32)  23.3 us
  transfers between devices with their start and end apart: 9, of which 0 were waited for; matrix products, arithmetic and copies ran while one was open for 32% of the time, Pallas kernels for 48%

profile of v25, /device:TPU:0, one launch (start us, length us, event | category | flops | bytes accessed | tf_op | source)
XLA Modules:
  0.0 809.4 jit_solution(7514450501381541911)
XLA Ops:
  7.2 1.7 convert_element_type.177
  10.4 1.5 convert_element_type.176
  14.8 38.6 %shard_map.256 = bf16[8,64,1792]{2,1,0:T(8,128)(2,1)} custom-call(bf16[8,64,1792]{2,1,0:T(8,128)(2,1)} %pad_maximum_fusion.3.x_ref), custom_call_target="tpu_custom_call" | custom-call | tf_op jit(solution)/shard_map/pallas_call | solution.py:536
  55.0 105.9 %shard_map.257 = bf16[2048,2048]{1,0:T(8,128)(2,1)} custom-call(bf16[256,2048]{1,0:T(8,128)(2,1)} %x_ref), custom_call_target="tpu_custom_call" | custom-call | tf_op jit(solution)/shard_map/pallas_call | solution.py:400
  163.3 5.0 shard_map.258
  168.3 1.4 broadcast_in_dim.34.x_ref
  169.7 9.0 %shard_map.259 = bf16[8,4,16,128]{3,2,1,0:T(8,128)(2,1)} custom-call(bf16[8,4,16,128]{3,2,1,0:T(8,128)(2,1)} %broadcast_in_dim.34.x_ref), custom_call_target="tpu_custom_call" | custom-call | tf_op jit(solution)/shard_map/pallas_call | solution.py:536
  180.7 4.7 convert_reduce_fusion
  186.5 2.3 fusion.2
  192.1 23.3 %convolution_add_fusion = f32[2048,1792]{0,1:T(8,128)} fusion(bf16[2048,1792]{1,0:T(8,128)(2,1)} %all-gather.5.cloned.1.call-done, f32[1792]{0:T(1024)S(1)} %maximum_convert_fusion, bf16[2048,2048]{1,0:T(8,128)(2,1)} %shard_map.257, f32[2048]{0:T(1024)S(1)} %reshape.300, f32[2048]{0:T(1024)S(1)} %reshape.299, f32[2048]{0:T(1024)S(1)} %add_rsqrt_fusion, ...), kind=kOutput, calls=%fused_computation.10 | convolution fusion | flops 15061221376 | bytes 30448640 | tf_op jit(solution)/shard_map/dot_general | solution.py:697
  215.4 1.8 slice.195
  217.1 3.9 fusion.34
  223.0 3.5 copy.129
  226.5 3.5 copy.130
  230.1 2.1 slice.196
  232.2 2.3 fusion.35
  234.4 3.7 copy.132
  238.1 3.6 copy.133
  241.6 2.8 copy.131
  244.5 2.6 copy.134
  247.1 1.8 copy.114
  248.8 7.3 subtract_convert_fusion.2
  256.1 5.2 maximum_bitcast_fusion
  261.3 2.0 maximum_maximum_fusion.v_ref
  263.3 34.9 %shard_map.260 = (f32[4,2048,64]{2,1,0:T(8,128)}, f32[4,2048,1]{2,1,0:T(8,128)}) custom-call(s32[3]{0:T(128)} %constant.57.clone.qi_ref, s32[3]{0:T(128)} %constant.58.clone.kj_ref, bf16[4,2048,64]{2,1,0:T(8,128)(2,1)} %get-tuple-element.74.q_ref, bf16[4,2048,64]{2,1,0:T(8,128)(2,1)} %get-tuple-element.75.k_ref, ...), custom_call_target="tpu_custom_call" | custom-call | flops 2147483648 | bytes 5242880 | tf_op jit(solution)/shard_map/pallas_call | solution.py:168
  298.2 6.0 convolution_convert_fusion.2
  304.2 2.2 copy.117
  306.4 6.8 multiply_reduce_fusion
  313.2 1.9 copy.116
  315.1 7.4 fusion.38
  322.6 2.8 copy.118.delta_ref
  325.4 15.6 %convolution_convert_fusion.1 = bf16[1024,2048]{1,0:T(8,128)(2,1)} fusion(bf16[2048,2048]{1,0:T(8,128)(2,1)} %all-gather.11.cloned.1.call-done, f32[2048,1792]{0,1:T(8,128)} %convolution_add_fusion), kind=kOutput, calls=%fused_computation.35 | convolution fusion | flops 8610906112 | bytes 20971520 | tf_op jit(solution)/shard_map/tf,td->fd/dot_general | solution.py:725
  341.0 44.8 %shard_map.262 = (f32[4,2048,64]{2,1,0:T(8,128)}, f32[4,2048,64]{2,1,0:T(8,128)}, f32[4,2048,64]{2,1,0:T(8,128)}) custom-call(s32[3]{0:T(128)} %constant.57.clone.qi_ref, s32[3]{0:T(128)} %constant.58.clone.kj_ref, bf16[4,2048,64]{2,1,0:T(8,128)(2,1)} %get-tuple-element.74.q_ref, bf16[4,2048,64]{2,1,0:T(8,128)(2,1)} %get-tuple-element.75.k_ref, ...), custom_call_target="tpu_custom_call" | custom-call | flops 5368709120 | bytes 12582912 | tf_op jit(solution)/shard_map/pallas_call | solution.py:258
  385.9 3.0 slice.194
  389.4 1.9 slice.193
  391.3 4.3 add_convert_fusion.1
  395.6 3.2 pad_maximum_fusion.1
  398.8 2.1 copy.120
  401.0 5.4 pad_maximum_fusion.2
  406.4 2.7 copy.121
  409.1 2.5 convert_bitcast_fusion
  411.5 1.6 copy.122
  413.2 17.9 %convert_reduce_fusion.1 = (f32[1024]{0:T(1024)S(1)}, bf16[2048,1024]{0,1:T(8,128)(2,1)}) fusion(f32[2048,1792]{0,1:T(8,128)} %convolution_add_fusion, bf16[2048,2048]{1,0:T(8,128)(2,1)} %all-gather.11.cloned.1.call-done, bf16[1024,2048]{1,0:T(8,128)(2,1)} %all-gather.9.cloned.1.call-done), kind=kOutput, calls=%fused_computation.19 | convolution fusion | flops 8633973760 | bytes 25169920 | tf_op jit(solution)/shard_map/td,fd->tf/dot_general | solution.py:726
  431.1 29.1 %convolution_convert_fusion = bf16[2048,1792]{1,0:T(8,128)(2,1)} fusion(bf16[2048,1024]{0,1:T(8,128)(2,1)} %get-tuple-element.73, bf16[2048,256]{0,1:T(8,128)(2,1)S(1)} %bitcast.120, bf16[2048,256]{0,1:T(8,128)(2,1)S(1)} %bitcast.117, bf16[2048,256]{0,1:T(8,128)(2,1)S(1)} %bitcast.114, bf16[2048,2048]{1,0:T(8,128)(2,1)} %shard_map.257, ...), kind=kOutput, calls=%fused_computation.21 | convolution fusion | flops 15090581504 | bytes 23101440 | tf_op jit(solution)/shard_map/td,tc->dc/dot_general | solution.py:754
  462.2 16.8 %fusion.31 = f32[2048,2048]{1,0:T(8,128)} fusion(bf16[1024,2048]{1,0:T(8,128)(2,1)} %all-gather.9.cloned.1.call-done, f32[2048,1792]{0,1:T(8,128)} %convolution_add_fusion), kind=kOutput, calls=%fused_computation.108 | convolution fusion | flops 8608808960 | bytes 29360128 | tf_op jit(solution)/shard_map/dot_general | solution.py:716
  479.0 21.4 %fusion.27.p_ref = f32[2048,2048]{1,0:T(8,128)} fusion(bf16[2048,1792]{1,0:T(8,128)(2,1)} %all-gather.5.cloned.1.call-done, bf16[2048,1024]{0,1:T(8,128)(2,1)S(1)} %copy-done.33, bf16[2048,256]{0,1:T(8,128)(2,1)S(1)} %bitcast.121, bf16[2048,256]{0,1:T(8,128)(2,1)S(1)} %bitcast.118, bf16[2048,256]{0,1:T(8,128)(2,1)S(1)} %bitcast.115), kind=kOutput, calls=%fused_computation.66 | convolution fusion | flops 15061745664 | bytes 31457280 | tf_op jit(solution)/shard_map/tc,dc->td/dot_general | solution.py:752
  500.4 5.5 collective-permute-start.1
  505.9 14.4 %convolution_add_fusion.1.p_ref = f32[2048,2048]{1,0:T(8,128)} fusion(f32[2048,2048]{1,0:T(8,128)} %fusion.31, bf16[2048,256]{0,1:T(8,128)(2,1)S(1)} %bitcast.108, bf16[256,2048]{1,0:T(8,128)(2,1)} %all-gather.7.cloned.1.call-done), kind=kOutput, calls=%fused_computation.11 | convolution fusion | flops 2151677952 | bytes 35651584 | tf_op jit(solution)/shard_map/dot_general | solution.py:715
  521.2 99.5 %shard_map.263 = f32[256,2048]{1,0:T(8,128)} custom-call(f32[2048,2048]{1,0:T(8,128)} %fusion.27.p_ref), custom_call_target="tpu_custom_call" | custom-call | tf_op jit(solution)/shard_map/pallas_call | solution.py:471
  620.7 87.8 %shard_map.261 = f32[256,2048]{1,0:T(8,128)} custom-call(f32[2048,2048]{1,0:T(8,128)} %convolution_add_fusion.1.p_ref), custom_call_target="tpu_custom_call" | custom-call | tf_op jit(solution)/shard_map/pallas_call | solution.py:471
  708.6 2.8 convert_element_type.223
  711.4 32.2 %shard_map.264 = bf16[8,64,1792]{2,1,0:T(8,128)(2,1)} custom-call(bf16[8,64,1792]{2,1,0:T(8,128)(2,1)} %bitcast.131), custom_call_target="tpu_custom_call" | custom-call | tf_op jit(solution)/shard_map/pallas_call | solution.py:536
  743.6 1.5 slice_convert_fusion.5
  745.0 2.4 slice_convert_fusion.6
  747.4 2.0 reshape.306
  749.4 2.8 copy.125
  752.2 2.5 copy.140
  754.7 2.6 reshape.305
  758.3 1.6 copy.139
  761.0 3.0 convert_reduce_fusion.4
  765.1 19.7 %shard_map.265 = f32[8,4,16,128]{3,2,1,0:T(8,128)} custom-call(f32[8,4,16,128]{3,2,1,0:T(8,128)} %copy_bitcast_fusion.3.x_ref), custom_call_target="tpu_custom_call" | custom-call | tf_op jit(solution)/shard_map/pallas_call | solution.py:536
  784.8 1.6 reduce_sum.158.x_ref
  786.4 11.1 %shard_map.266 = f32[4,16,128]{2,1,0:T(8,128)} custom-call(f32[4,16,128]{2,1,0:T(8,128)} %reduce_sum.158.x_ref), custom_call_target="tpu_custom_call" | custom-call | tf_op jit(solution)/shard_map/pallas_call | solution.py:536
  800.5 1.9 copy.157
  (169 shorter events, 25.7 us)
Async XLA Ops:
  7.2 184.9 %all-gather.5.cloned.1.call-start = ((), (), s32[]{:S(2)}) async-start(), calls=%async_computation.3 | async-start | bytes 9175040 | tf_op jit(solution)/shard_map/all_gather | solution.py:621
  13.4 40.1 %copy-start.20 = (f32[64,2048]{1,0:T(8,128)S(1)}, f32[64,2048]{1,0:T(8,128)}, u32[]{:S(2)}) copy-start(f32[64,2048]{1,0:T(8,128)} %param.21) | copy-start | bytes 1572868
  53.4 244.8 %all-gather.7.cloned.1.call-start = ((), (), s32[]{:S(2)}) async-start(), calls=%async_computation.4 | async-start | bytes 1310720 | tf_op jit(solution)/shard_map/all_gather | solution.py:559
  53.5 0.7 collective-permute-start
  54.2 0.7 copy-start.21
  54.9 106.1 %copy-start.19 = (f32[256,2048]{1,0:T(8,128)S(1)}, f32[256,2048]{1,0:T(8,128)}, u32[]{:S(2)}) copy-start(f32[256,2048]{1,0:T(8,128)} %param.25) | copy-start | bytes 6291460
  54.9 243.3 %all-gather.11.cloned.1.call-start = ((), (), s32[]{:S(2)}) async-start(), calls=%async_computation.6 | async-start | bytes 9437184 | tf_op jit(solution)/shard_map/all_gather | solution.py:690
  160.9 1.5 copy-start.26
  160.9 1.5 copy-start.28
  160.9 1.5 copy-start.29
  160.9 1.6 copy-start.30
  161.0 1.6 copy-start.31
  161.0 1.6 copy-start.27
  161.0 252.2 %all-gather.9.cloned.1.call-start = ((), (), s32[]{:S(2)}) async-start(), calls=%async_computation.5 | async-start | bytes 5242880 | tf_op jit(solution)/shard_map/all_gather | solution.py:622
  162.2 338.2 %reduce-scatter.6.cloned.1.call-start = ((), (), s32[]{:S(2)}) async-start(), calls=%async_computation.8 | async-start | bytes 2621440 | tf_op jit(solution)/shard_map/reduce_scatter | solution.py:565
  180.7 5.8 copy-start
  186.5 2.5 copy-start.32
  189.2 26.1 %copy-start.22 = (s32[2048]{0:T(1024)}, s32[2048]{0:T(1024)S(1)}, u32[]{:S(2)}) copy-start(s32[2048]{0:T(1024)S(1)} %convert_reduce_fusion.5) | copy-start | bytes 24580
  248.8 7.3 copy-start.8
  248.8 7.3 copy-start.9
  256.1 5.2 copy-start.5
  315.1 7.4 copy-start.10
  322.6 386.0 %reduce-scatter.8.cloned.1.call-start = ((), (), s32[]{:S(2)}) async-start(), calls=%async_computation.9 | async-start | bytes 5242880 | tf_op jit(solution)/shard_map/reduce_scatter | solution.py:762
  341.0 370.4 %reduce-scatter.4.cloned.1.call-start = ((), (), s32[]{:S(2)}) async-start(), calls=%async_computation.7 | async-start | bytes 9175040 | tf_op jit(solution)/shard_map/reduce_scatter | solution.py:757
  385.8 3.5 copy-start.2
  385.8 5.5 copy-start.1
  395.6 5.4 copy-start.7
  413.2 17.9 %copy-start.12 = (bf16[2048,4,64]{0,2,1:T(8,128)(2,1)S(1)}, bf16[2048,4,64]{0,2,1:T(8,128)(2,1)}, u32[]{:S(2)}) copy-start(bf16[2048,4,64]{0,2,1:T(8,128)(2,1)} %copy.121) | copy-start | bytes 3145732
  413.2 17.9 %copy-start.15 = (bf16[2048,4,64]{0,2,1:T(8,128)(2,1)S(1)}, bf16[2048,4,64]{0,2,1:T(8,128)(2,1)}, u32[]{:S(2)}) copy-start(bf16[2048,4,64]{0,2,1:T(8,128)(2,1)} %copy.122) | copy-start | bytes 3145732
  460.2 0.7 copy-start.24
  460.2 0.8 copy-start.23
  460.3 1.2 copy-start.3
  462.2 16.9 %copy-start.13 = (bf16[2048,4,64]{0,2,1:T(8,128)(2,1)S(1)}, bf16[2048,4,64]{0,2,1:T(8,128)(2,1)}, u32[]{:S(2)}) copy-start(bf16[2048,4,64]{0,2,1:T(8,128)(2,1)} %copy.121) | copy-start | bytes 3145732
  462.2 16.8 %copy-start.16 = (bf16[2048,4,64]{0,2,1:T(8,128)(2,1)S(1)}, bf16[2048,4,64]{0,2,1:T(8,128)(2,1)}, u32[]{:S(2)}) copy-start(bf16[2048,4,64]{0,2,1:T(8,128)(2,1)} %copy.122) | copy-start | bytes 3145732
  462.2 16.8 %copy-start.33 = (bf16[2048,1024]{0,1:T(8,128)(2,1)S(1)}, bf16[2048,1024]{0,1:T(8,128)(2,1)}, u32[]{:S(2)}) copy-start(bf16[2048,1024]{0,1:T(8,128)(2,1)} %get-tuple-element.73) | copy-start | bytes 12582916
  479.0 26.9 %copy-start.11 = (bf16[2048,4,64]{0,2,1:T(8,128)(2,1)S(1)}, bf16[2048,4,64]{0,2,1:T(8,128)(2,1)}, u32[]{:S(2)}) copy-start(bf16[2048,4,64]{0,2,1:T(8,128)(2,1)} %copy-done.10) | copy-start | bytes 3145732
  500.4 19.9 %copy-start.14 = (bf16[2048,4,64]{0,2,1:T(8,128)(2,1)S(1)}, bf16[2048,4,64]{0,2,1:T(8,128)(2,1)}, u32[]{:S(2)}) copy-start(bf16[2048,4,64]{0,2,1:T(8,128)(2,1)} %copy.121) | copy-start | bytes 3145732
  500.4 19.9 %copy-start.17 = (bf16[2048,4,64]{0,2,1:T(8,128)(2,1)S(1)}, bf16[2048,4,64]{0,2,1:T(8,128)(2,1)}, u32[]{:S(2)}) copy-start(bf16[2048,4,64]{0,2,1:T(8,128)(2,1)} %copy.122) | copy-start | bytes 3145732
  500.4 208.2 %collective-permute-start.1 = (f32[64,2048]{1,0:T(8,128)}, f32[64,2048]{1,0:T(8,128)}, u32[]{:S(2)}, u32[]{:S(2)}) collective-permute-start(f32[64,2048]{1,0:T(8,128)} %reduce-scatter.6.cloned.1.call-done), channel_id=1, source_target_pairs={{0,0},{8,1},{16,2},{24,3},{1,4},{9,5},{17,6},{25,7},{2,8},{10,9},{... | collective-permute-start | bytes 1572872 | tf_op jit(solution)/shard_map/ppermute | solution.py:567
  757.4 2.6 copy-start.4
  757.4 3.6 copy-start.6
  757.4 3.6 copy-start.18
  798.8 3.5 copy-start.25
Sparse Core Ops, SparseCore 0:
  53.5 63.1 all-gather.4
  118.3 16.7 all-gather.6
  161.1 126.0 all-gather.10
  289.2 32.6 all-gather.8
  324.3 32.6 reduce-scatter.5
  359.5 44.5 reduce-scatter.7
  460.4 75.7 reduce-scatter.3

commit v26 on v25

--- a/solution.py
+++ b/solution.py
@@ -398,14 +398,14 @@
     rows, cols = x.shape
     n = ring.size
     return pl.pallas_call(
-        functools.partial(_gather_kernel, ring=ring, rows=rows, parts=2),
+        functools.partial(_gather_kernel, ring=ring, rows=rows, parts=4),
         out_shape=jax.ShapeDtypeStruct((n * rows, cols), x.dtype),
         in_specs=[pl.BlockSpec(memory_space=pl.ANY)],
         out_specs=pl.BlockSpec(memory_space=pl.ANY),
         scratch_shapes=[
             pltpu.SemaphoreType.DMA(()),
-            pltpu.SemaphoreType.DMA((2, n - 1, 2)),
-            pltpu.SemaphoreType.DMA((2, n - 1, 2)),
+            pltpu.SemaphoreType.DMA((2, n - 1, 4)),
+            pltpu.SemaphoreType.DMA((2, n - 1, 4)),
         ],
         compiler_params=pltpu.CompilerParams(collective_id=collective_id, has_side_effects=True),
     )(x)

time: 814 us -> 815 us (level)
  no operation moved by 1% of the time
where the time goes in v26:
time: 815 us; the launch traced here: 810 us
  Pallas kernels  489 us (60%)
  matrix products  152 us (19%)
  local copies, waits for them, and re-layouts  81.6 us (10%)
  other arithmetic  65.5 us (8%)
  between operations  15.2 us (2%)
    pallas_call x2, Pallas kernels, ring_reduce_scatter(): pl.pallas_call(functools.partial(_scatter_kernel, ring=ring, rows=rows, p...  187 us
    pallas_call x6, Pallas kernels, exchange(): pl.pallas_call(functools.partial(_exchange_kernel, group=group), out_shap...  115 us
    pallas_call x1, Pallas kernels, ring_all_gather(): pl.pallas_call(functools.partial(_gather_kernel, ring=ring, rows=rows, pa...  106 us
    pallas_call x1, Pallas kernels, attention_backward(): pl.pallas_call(functools.partial(_bwd_kernel, tq=block, tk=block, scale=s...  44.8 us
    pallas_call x1, Pallas kernels, attention_forward(): pl.pallas_call(functools.partial(_fwd_kernel, tq=block, tk=block, scale=s...  34.9 us
    unnamed x84, local copies, waits for them, and re-layouts  31.1 us
    dot_general x1, matrix products, head_plan(): jnp.einsum('td,tc->dc', hidden_group, d_both, preferred_element_type=jnp....  29.1 us
    dot_general x1, matrix products, head_plan(): jnp.dot(hidden_group, cols, preferred_element_type=jnp.float32)  23.2 us
  transfers between devices with their start and end apart: 9, of which 0 were waited for; matrix products, arithmetic and copies ran while one was open for 32% of the time, Pallas kernels for 48%

profile of v26, /device:TPU:0, one launch (start us, length us, event | category | flops | bytes accessed | tf_op | source)
XLA Modules:
  0.0 809.9 jit_solution(15117924499090132315)
XLA Ops:
  7.2 1.7 convert_element_type.177
  10.4 1.5 convert_element_type.176
  14.8 38.6 %shard_map.256 = bf16[8,64,1792]{2,1,0:T(8,128)(2,1)} custom-call(bf16[8,64,1792]{2,1,0:T(8,128)(2,1)} %pad_maximum_fusion.3.x_ref), custom_call_target="tpu_custom_call" | custom-call | tf_op jit(solution)/shard_map/pallas_call | solution.py:536
  55.0 106.4 %shard_map.257 = bf16[2048,2048]{1,0:T(8,128)(2,1)} custom-call(bf16[256,2048]{1,0:T(8,128)(2,1)} %x_ref), custom_call_target="tpu_custom_call" | custom-call | tf_op jit(solution)/shard_map/pallas_call | solution.py:400
  163.8 5.0 shard_map.258
  168.8 1.4 broadcast_in_dim.34.x_ref
  170.2 9.0 %shard_map.259 = bf16[8,4,16,128]{3,2,1,0:T(8,128)(2,1)} custom-call(bf16[8,4,16,128]{3,2,1,0:T(8,128)(2,1)} %broadcast_in_dim.34.x_ref), custom_call_target="tpu_custom_call" | custom-call | tf_op jit(solution)/shard_map/pallas_call | solution.py:536
  181.2 4.7 convert_reduce_fusion
  187.0 2.3 fusion.2
  192.6 23.2 %convolution_add_fusion = f32[2048,1792]{0,1:T(8,128)} fusion(bf16[2048,1792]{1,0:T(8,128)(2,1)} %all-gather.5.cloned.1.call-done, f32[1792]{0:T(1024)S(1)} %maximum_convert_fusion, bf16[2048,2048]{1,0:T(8,128)(2,1)} %shard_map.257, f32[2048]{0:T(1024)S(1)} %reshape.300, f32[2048]{0:T(1024)S(1)} %reshape.299, f32[2048]{0:T(1024)S(1)} %add_rsqrt_fusion, ...), kind=kOutput, calls=%fused_computation.10 | convolution fusion | flops 15061221376 | bytes 30448640 | tf_op jit(solution)/shard_map/dot_general | solution.py:697
  215.9 1.8 slice.195
  217.7 3.9 fusion.34
  223.5 3.5 copy.129
  227.0 3.5 copy.130
  230.6 2.1 slice.196
  232.7 2.3 fusion.35
  234.9 3.7 copy.132
  238.6 3.6 copy.133
  242.2 2.8 copy.131
  245.0 2.6 copy.134
  247.6 1.8 copy.114
  249.4 7.3 subtract_convert_fusion.2
  256.7 5.2 maximum_bitcast_fusion
  261.8 2.0 maximum_maximum_fusion.v_ref
  263.9 34.9 %shard_map.260 = (f32[4,2048,64]{2,1,0:T(8,128)}, f32[4,2048,1]{2,1,0:T(8,128)}) custom-call(s32[3]{0:T(128)} %constant.57.clone.qi_ref, s32[3]{0:T(128)} %constant.58.clone.kj_ref, bf16[4,2048,64]{2,1,0:T(8,128)(2,1)} %get-tuple-element.74.q_ref, bf16[4,2048,64]{2,1,0:T(8,128)(2,1)} %get-tuple-element.75.k_ref, ...), custom_call_target="tpu_custom_call" | custom-call | flops 2147483648 | bytes 5242880 | tf_op jit(solution)/shard_map/pallas_call | solution.py:168
  298.8 6.0 convolution_convert_fusion.2
  304.7 2.2 copy.117
  306.9 6.8 multiply_reduce_fusion
  313.7 1.9 copy.116
  315.6 7.4 fusion.38
  323.1 2.8 copy.118.delta_ref
  325.9 15.6 %convolution_convert_fusion.1 = bf16[1024,2048]{1,0:T(8,128)(2,1)} fusion(bf16[2048,2048]{1,0:T(8,128)(2,1)} %all-gather.11.cloned.1.call-done, f32[2048,1792]{0,1:T(8,128)} %convolution_add_fusion), kind=kOutput, calls=%fused_computation.35 | convolution fusion | flops 8610906112 | bytes 20971520 | tf_op jit(solution)/shard_map/tf,td->fd/dot_general | solution.py:725
  341.5 44.8 %shard_map.262 = (f32[4,2048,64]{2,1,0:T(8,128)}, f32[4,2048,64]{2,1,0:T(8,128)}, f32[4,2048,64]{2,1,0:T(8,128)}) custom-call(s32[3]{0:T(128)} %constant.57.clone.qi_ref, s32[3]{0:T(128)} %constant.58.clone.kj_ref, bf16[4,2048,64]{2,1,0:T(8,128)(2,1)} %get-tuple-element.74.q_ref, bf16[4,2048,64]{2,1,0:T(8,128)(2,1)} %get-tuple-element.75.k_ref, ...), custom_call_target="tpu_custom_call" | custom-call | flops 5368709120 | bytes 12582912 | tf_op jit(solution)/shard_map/pallas_call | solution.py:258
  386.4 3.0 slice.194
  389.9 1.9 slice.193
  391.8 4.3 add_convert_fusion.1
  396.1 3.2 pad_maximum_fusion.1
  399.4 2.1 copy.120
  401.5 5.4 pad_maximum_fusion.2
  406.9 2.7 copy.121
  409.6 2.5 convert_bitcast_fusion
  412.1 1.6 copy.122
  413.7 17.9 %convert_reduce_fusion.1 = (f32[1024]{0:T(1024)S(1)}, bf16[2048,1024]{0,1:T(8,128)(2,1)}) fusion(f32[2048,1792]{0,1:T(8,128)} %convolution_add_fusion, bf16[2048,2048]{1,0:T(8,128)(2,1)} %all-gather.11.cloned.1.call-done, bf16[1024,2048]{1,0:T(8,128)(2,1)} %all-gather.9.cloned.1.call-done), kind=kOutput, calls=%fused_computation.19 | convolution fusion | flops 8633973760 | bytes 25169920 | tf_op jit(solution)/shard_map/td,fd->tf/dot_general | solution.py:726
  431.6 29.1 %convolution_convert_fusion = bf16[2048,1792]{1,0:T(8,128)(2,1)} fusion(bf16[2048,1024]{0,1:T(8,128)(2,1)} %get-tuple-element.73, bf16[2048,256]{0,1:T(8,128)(2,1)S(1)} %bitcast.120, bf16[2048,256]{0,1:T(8,128)(2,1)S(1)} %bitcast.117, bf16[2048,256]{0,1:T(8,128)(2,1)S(1)} %bitcast.114, bf16[2048,2048]{1,0:T(8,128)(2,1)} %shard_map.257, ...), kind=kOutput, calls=%fused_computation.21 | convolution fusion | flops 15090581504 | bytes 23101440 | tf_op jit(solution)/shard_map/td,tc->dc/dot_general | solution.py:754
  462.7 16.8 %fusion.31 = f32[2048,2048]{1,0:T(8,128)} fusion(bf16[1024,2048]{1,0:T(8,128)(2,1)} %all-gather.9.cloned.1.call-done, f32[2048,1792]{0,1:T(8,128)} %convolution_add_fusion), kind=kOutput, calls=%fused_computation.108 | convolution fusion | flops 8608808960 | bytes 29360128 | tf_op jit(solution)/shard_map/dot_general | solution.py:716
  479.6 21.4 %fusion.27.p_ref = f32[2048,2048]{1,0:T(8,128)} fusion(bf16[2048,1792]{1,0:T(8,128)(2,1)} %all-gather.5.cloned.1.call-done, bf16[2048,1024]{0,1:T(8,128)(2,1)S(1)} %copy-done.33, bf16[2048,256]{0,1:T(8,128)(2,1)S(1)} %bitcast.121, bf16[2048,256]{0,1:T(8,128)(2,1)S(1)} %bitcast.118, bf16[2048,256]{0,1:T(8,128)(2,1)S(1)} %bitcast.115), kind=kOutput, calls=%fused_computation.66 | convolution fusion | flops 15061745664 | bytes 31457280 | tf_op jit(solution)/shard_map/tc,dc->td/dot_general | solution.py:752
  500.9 5.5 collective-permute-start.1
  506.4 14.4 %convolution_add_fusion.1.p_ref = f32[2048,2048]{1,0:T(8,128)} fusion(f32[2048,2048]{1,0:T(8,128)} %fusion.31, bf16[2048,256]{0,1:T(8,128)(2,1)S(1)} %bitcast.108, bf16[256,2048]{1,0:T(8,128)(2,1)} %all-gather.7.cloned.1.call-done), kind=kOutput, calls=%fused_computation.11 | convolution fusion | flops 2151677952 | bytes 35651584 | tf_op jit(solution)/shard_map/dot_general | solution.py:715
  521.8 99.5 %shard_map.263 = f32[256,2048]{1,0:T(8,128)} custom-call(f32[2048,2048]{1,0:T(8,128)} %fusion.27.p_ref), custom_call_target="tpu_custom_call" | custom-call | tf_op jit(solution)/shard_map/pallas_call | solution.py:471
  621.3 87.8 %shard_map.261 = f32[256,2048]{1,0:T(8,128)} custom-call(f32[2048,2048]{1,0:T(8,128)} %convolution_add_fusion.1.p_ref), custom_call_target="tpu_custom_call" | custom-call | tf_op jit(solution)/shard_map/pallas_call | solution.py:471
  709.2 2.8 convert_element_type.223
  712.0 32.2 %shard_map.264 = bf16[8,64,1792]{2,1,0:T(8,128)(2,1)} custom-call(bf16[8,64,1792]{2,1,0:T(8,128)(2,1)} %bitcast.131), custom_call_target="tpu_custom_call" | custom-call | tf_op jit(solution)/shard_map/pallas_call | solution.py:536
  744.1 1.5 slice_convert_fusion.5
  745.6 2.4 slice_convert_fusion.6
  748.0 2.0 reshape.306
  750.0 2.8 copy.125
  752.8 2.5 copy.140
  755.3 2.6 reshape.305
  758.9 1.6 copy.139
  761.6 3.0 convert_reduce_fusion.4
  765.7 19.7 %shard_map.265 = f32[8,4,16,128]{3,2,1,0:T(8,128)} custom-call(f32[8,4,16,128]{3,2,1,0:T(8,128)} %copy_bitcast_fusion.3.x_ref), custom_call_target="tpu_custom_call" | custom-call | tf_op jit(solution)/shard_map/pallas_call | solution.py:536
  785.4 1.6 reduce_sum.158.x_ref
  787.0 10.9 %shard_map.266 = f32[4,16,128]{2,1,0:T(8,128)} custom-call(f32[4,16,128]{2,1,0:T(8,128)} %reduce_sum.158.x_ref), custom_call_target="tpu_custom_call" | custom-call | tf_op jit(solution)/shard_map/pallas_call | solution.py:536
  800.9 1.9 copy.157
  (169 shorter events, 25.7 us)
Async XLA Ops:
  7.2 185.4 %all-gather.5.cloned.1.call-start = ((), (), s32[]{:S(2)}) async-start(), calls=%async_computation.3 | async-start | bytes 9175040 | tf_op jit(solution)/shard_map/all_gather | solution.py:621
  13.4 40.1 %copy-start.20 = (f32[64,2048]{1,0:T(8,128)S(1)}, f32[64,2048]{1,0:T(8,128)}, u32[]{:S(2)}) copy-start(f32[64,2048]{1,0:T(8,128)} %param.21) | copy-start | bytes 1572868
  53.4 245.3 %all-gather.7.cloned.1.call-start = ((), (), s32[]{:S(2)}) async-start(), calls=%async_computation.4 | async-start | bytes 1310720 | tf_op jit(solution)/shard_map/all_gather | solution.py:559
  53.5 0.7 collective-permute-start
  54.2 0.7 copy-start.21
  54.9 106.7 %copy-start.19 = (f32[256,2048]{1,0:T(8,128)S(1)}, f32[256,2048]{1,0:T(8,128)}, u32[]{:S(2)}) copy-start(f32[256,2048]{1,0:T(8,128)} %param.25) | copy-start | bytes 6291460
  54.9 243.8 %all-gather.11.cloned.1.call-start = ((), (), s32[]{:S(2)}) async-start(), calls=%async_computation.6 | async-start | bytes 9437184 | tf_op jit(solution)/shard_map/all_gather | solution.py:690
  161.4 1.5 copy-start.26
  161.5 1.5 copy-start.28
  161.5 1.5 copy-start.29
  161.5 1.6 copy-start.30
  161.5 1.6 copy-start.31
  161.5 1.6 copy-start.27
  161.5 252.2 %all-gather.9.cloned.1.call-start = ((), (), s32[]{:S(2)}) async-start(), calls=%async_computation.5 | async-start | bytes 5242880 | tf_op jit(solution)/shard_map/all_gather | solution.py:622
  162.7 338.2 %reduce-scatter.6.cloned.1.call-start = ((), (), s32[]{:S(2)}) async-start(), calls=%async_computation.8 | async-start | bytes 2621440 | tf_op jit(solution)/shard_map/reduce_scatter | solution.py:565
  181.2 5.8 copy-start
  187.0 2.5 copy-start.32
  189.8 26.1 %copy-start.22 = (s32[2048]{0:T(1024)}, s32[2048]{0:T(1024)S(1)}, u32[]{:S(2)}) copy-start(s32[2048]{0:T(1024)S(1)} %convert_reduce_fusion.5) | copy-start | bytes 24580
  249.4 7.3 copy-start.8
  249.4 7.3 copy-start.9
  256.6 5.2 copy-start.5
  315.6 7.4 copy-start.10
  323.1 386.1 %reduce-scatter.8.cloned.1.call-start = ((), (), s32[]{:S(2)}) async-start(), calls=%async_computation.9 | async-start | bytes 5242880 | tf_op jit(solution)/shard_map/reduce_scatter | solution.py:762
  341.5 370.5 %reduce-scatter.4.cloned.1.call-start = ((), (), s32[]{:S(2)}) async-start(), calls=%async_computation.7 | async-start | bytes 9175040 | tf_op jit(solution)/shard_map/reduce_scatter | solution.py:757
  386.4 3.5 copy-start.2
  386.4 5.5 copy-start.1
  396.1 5.4 copy-start.7
  413.7 17.9 %copy-start.12 = (bf16[2048,4,64]{0,2,1:T(8,128)(2,1)S(1)}, bf16[2048,4,64]{0,2,1:T(8,128)(2,1)}, u32[]{:S(2)}) copy-start(bf16[2048,4,64]{0,2,1:T(8,128)(2,1)} %copy.121) | copy-start | bytes 3145732
  413.7 17.9 %copy-start.15 = (bf16[2048,4,64]{0,2,1:T(8,128)(2,1)S(1)}, bf16[2048,4,64]{0,2,1:T(8,128)(2,1)}, u32[]{:S(2)}) copy-start(bf16[2048,4,64]{0,2,1:T(8,128)(2,1)} %copy.122) | copy-start | bytes 3145732
  460.8 0.7 copy-start.24
  460.8 0.8 copy-start.23
  460.8 1.2 copy-start.3
  462.7 16.9 %copy-start.13 = (bf16[2048,4,64]{0,2,1:T(8,128)(2,1)S(1)}, bf16[2048,4,64]{0,2,1:T(8,128)(2,1)}, u32[]{:S(2)}) copy-start(bf16[2048,4,64]{0,2,1:T(8,128)(2,1)} %copy.121) | copy-start | bytes 3145732
  462.7 16.9 %copy-start.16 = (bf16[2048,4,64]{0,2,1:T(8,128)(2,1)S(1)}, bf16[2048,4,64]{0,2,1:T(8,128)(2,1)}, u32[]{:S(2)}) copy-start(bf16[2048,4,64]{0,2,1:T(8,128)(2,1)} %copy.122) | copy-start | bytes 3145732
  462.7 16.8 %copy-start.33 = (bf16[2048,1024]{0,1:T(8,128)(2,1)S(1)}, bf16[2048,1024]{0,1:T(8,128)(2,1)}, u32[]{:S(2)}) copy-start(bf16[2048,1024]{0,1:T(8,128)(2,1)} %get-tuple-element.73) | copy-start | bytes 12582916
  479.6 26.9 %copy-start.11 = (bf16[2048,4,64]{0,2,1:T(8,128)(2,1)S(1)}, bf16[2048,4,64]{0,2,1:T(8,128)(2,1)}, u32[]{:S(2)}) copy-start(bf16[2048,4,64]{0,2,1:T(8,128)(2,1)} %copy-done.10) | copy-start | bytes 3145732
  500.9 19.9 %copy-start.14 = (bf16[2048,4,64]{0,2,1:T(8,128)(2,1)S(1)}, bf16[2048,4,64]{0,2,1:T(8,128)(2,1)}, u32[]{:S(2)}) copy-start(bf16[2048,4,64]{0,2,1:T(8,128)(2,1)} %copy.121) | copy-start | bytes 3145732
  500.9 19.9 %copy-start.17 = (bf16[2048,4,64]{0,2,1:T(8,128)(2,1)S(1)}, bf16[2048,4,64]{0,2,1:T(8,128)(2,1)}, u32[]{:S(2)}) copy-start(bf16[2048,4,64]{0,2,1:T(8,128)(2,1)} %copy.122) | copy-start | bytes 3145732
  500.9 208.2 %collective-permute-start.1 = (f32[64,2048]{1,0:T(8,128)}, f32[64,2048]{1,0:T(8,128)}, u32[]{:S(2)}, u32[]{:S(2)}) collective-permute-start(f32[64,2048]{1,0:T(8,128)} %reduce-scatter.6.cloned.1.call-done), channel_id=1, source_target_pairs={{0,0},{8,1},{16,2},{24,3},{1,4},{9,5},{17,6},{25,7},{2,8},{10,9},{... | collective-permute-start | bytes 1572872 | tf_op jit(solution)/shard_map/ppermute | solution.py:567
  757.9 2.6 copy-start.4
  757.9 3.6 copy-start.6
  757.9 3.6 copy-start.18
  799.3 3.5 copy-start.25
Sparse Core Ops, SparseCore 0:
  53.5 63.1 all-gather.4
  118.3 16.7 all-gather.6
  161.7 126.0 all-gather.10
  289.8 32.6 all-gather.8
  324.8 32.6 reduce-scatter.5
  360.1 44.5 reduce-scatter.7
  460.9 75.7 reduce-scatter.3
